TPU v7x, 32 devices: a whole 2x2x4 slice. The times are simulated.
32 devices in a mesh: row: 16 (over z, y, core), col: 2 (over x).
Axes of the slice: x: 2, y: 2, z: 4, core: 2. Of those that a mesh axis runs over, the one named last changes fastest.
Arguments:
- specimen_slices: float32 [2, 2, 4096, 512], P(None, None, 'row', 'col'), may hold values from -6 to 6
- illumination_probe: float32 [2, 128, 128], replicated, may hold values from -6 to 6
- propagation_phase: float32 [128, 128], replicated, may hold values from -3.140625 to 3.140625
- amplitudes: float32 [16, 2, 4, 128, 128], P('row', 'col'), may hold values from 0.5 to 4
- positions: int32 [16, 2, 4, 2], P('row', 'col'), may hold values from 0 to 255
- counts: int32 [16, 2], P('row', 'col'), may hold values from 1 to 4, as said below
- measurement_index: int32 [16, 2, 4], P('row', 'col'), may hold values from 0 to 3, each once within a row
Outputs:
- updated: float32 [2, 2, 4096, 512], P(None, None, 'row', 'col')
Inputs may be any that keep to these rules, and one draw needn't show every extreme that they name: `counts`: some tile holds exactly 4 probe positions.
All inputs are finite; a program needn't handle non-finite values.
Results may differ from a plain program's by a relative error of at most 0.0001.
Values sent between devices are 32-bit elements; how exact they have to be, the bound alone decides.
No kernel may reach another device: no remote copies, remote signals or barrier semaphores. Data moves between devices by JAX's collectives and lax.ppermute only.
A program may use at most 64 MiB of HBM per device.

v0:
```python
import functools
import math

import jax
import jax.numpy as jnp
import ml_dtypes
import numpy as np
from jax import lax
from jax.experimental import pallas as pl
from jax.experimental.pallas import tpu as pltpu
from jax.sharding import PartitionSpec as P


ITERS = 2
LANES = 128

step_size = 0.02
floor_amp = 0.5


def send_corner(block, distance):
    count = lax.axis_size("row")
    route = [(i, i + distance) for i in range(count) if 0 <= i + distance < count]
    return lax.ppermute(block, "row", route)


def send_wrap(block, distance):
    rows, cols = lax.axis_size("row"), lax.axis_size("col")
    start, end = (rows - 1, 0) if distance > 0 else (0, rows - 1)
    route = [(start * cols + c, end * cols + (c + distance) % cols) for c in range(cols)]
    return lax.ppermute(block, ("row", "col"), route)


def from_behind(block, axis, distance):
    devices = range(lax.axis_size(axis))
    route = [((i - distance) % len(devices), i) for i in devices]
    return lax.ppermute(block, axis, route)


def two_parts(value):
    high = value.astype(ml_dtypes.bfloat16)
    low = (value - high.astype(np.float64)).astype(ml_dtypes.bfloat16)
    return high, low


def dft_operands(width):
    index = np.arange(width)
    angle = (index[:, None] * index[None, :] % width) * (2.0 * math.pi / width)
    real = np.cos(angle) / math.sqrt(width)
    imag = -np.sin(angle) / math.sqrt(width)
    right = np.block([[real, imag], [-imag, real]])
    right_high, right_low = two_parts(right)
    left_high, left_low = two_parts(right.T)
    return np.stack([right_high, right_low, left_high, left_low])


def split(value):
    high = value.astype(jnp.bfloat16)
    low = (value - high.astype(jnp.float32)).astype(jnp.bfloat16)
    return high, low


def rows_of(j, width):
    return slice(j * width, (j + 1) * width)


def product(left, right):
    return jnp.dot(left, right, preferred_element_type=jnp.float32)


def right_side(pairs, table_ref):
    high, low = split(jnp.concatenate([jnp.concatenate(pair, 1) for pair in pairs], 0))
    return product(high, table_ref[0]) + product(low, table_ref[0]) + product(high, table_ref[1])


def left_side(half, table_ref, width):
    count = half.shape[0] // width
    parts = [half[rows_of(k, width)] for k in range(count)]
    tall = [jnp.concatenate([part[:, :width], part[:, width:]], 0) for part in parts]
    high, low = split(jnp.concatenate(tall, 1))
    full = product(table_ref[2], high) + product(table_ref[2], low) + product(table_ref[3], high)
    return [(full[:width, rows_of(k, width)], full[width:, rows_of(k, width)]) for k in range(count)]


def interleave(chains, lag):
    waiting = [(n * lag, chain) for n, chain in enumerate(chains)]
    while waiting:
        after = []
        for delay, chain in waiting:
            if delay:
                after.append((delay - 1, chain))
            elif next(chain, None) is not None:
                after.append((0, chain))
        waiting = after


def fill_ext(ext_ref, pieces):
    for row, col, *sources in pieces:
        height, across = sources[0].shape[1:]
        for c in range(2):
            for b in range(across // LANES):
                lanes = slice(b * LANES, (b + 1) * LANES)
                value = sources[0][c, :, lanes]
                for source in sources[1:]:
                    value += source[c, :, lanes]
                ext_ref[c, col // LANES + b, row:row + height, :] = value


def place(scalar_ref, j):
    col = scalar_ref[2 * j + 1]
    return scalar_ref[2 * j], col // LANES, col % LANES


def window(ext_ref, c, spot, width, lane):
    row, block, shift = spot
    near = ext_ref[c, block, pl.ds(row, width), :]
    far = ext_ref[c, block + 1, pl.ds(row, width), :]
    return pltpu.roll(jnp.where(lane >= shift, near, far), LANES - shift, 1)


def scatter(grad_ref, c, spot, width, lane, used, update):
    row, block, shift = spot
    turned = pltpu.roll(jnp.where(used, update, 0.0), shift, 1)
    near = lane >= shift
    grad_ref[c, block, pl.ds(row, width), :] += jnp.where(near, turned, 0.0)
    grad_ref[c, block + 1, pl.ds(row, width), :] += jnp.where(near, 0.0, turned)


def emit(grad_ref, own_ref, down_ref, upper_ref, lower_ref, diag_ref, width):
    tile_px = own_ref.shape[1]
    blocks = tile_px // LANES
    for c in range(2):
        for b in range(blocks):
            lanes = slice(b * LANES, (b + 1) * LANES)
            own_ref[c, :, lanes] = grad_ref[c, b, :tile_px, :]
            down_ref[c, :, lanes] = grad_ref[c, b, tile_px:, :]
        upper_ref[c] = grad_ref[c, blocks, :width, :]
        lower_ref[c] = grad_ref[c, blocks, width:tile_px, :]
        diag_ref[c] = grad_ref[c, blocks, tile_px:, :]


def lanes_of(width):
    return lax.broadcasted_iota(jnp.int32, (width, LANES), 1)


LAG = 1


def groups_of(spots):
    return [range(j, min(j + 2, spots)) for j in range(0, spots, 2)]


def forward_steps(group, enter_ref, leave_ref, cos_ref, sin_ref, table_ref, width):
    half = right_side([(enter_ref[j, 0], enter_ref[j, 1]) for j in group], table_ref)
    yield True
    pairs = left_side(half, table_ref, width)
    yield True
    half = right_side([
        (cos_ref[...] * real - sin_ref[...] * imag, -(cos_ref[...] * imag + sin_ref[...] * real))
        for real, imag in pairs
    ], table_ref)
    yield True
    pairs = left_side(half, table_ref, width)
    yield True
    for j, (real, negative) in zip(group, pairs):
        leave_ref[j, 0] = real
        leave_ref[j, 1] = -negative


def residual_steps(group, moved_ref, win_ref, measured_of, finish, table_ref, width):
    half = right_side([
        (
            moved_ref[j, 0] * win_ref[j, 0] - moved_ref[j, 1] * win_ref[j, 1],
            moved_ref[j, 0] * win_ref[j, 1] + moved_ref[j, 1] * win_ref[j, 0],
        )
        for j in group
    ], table_ref)
    yield True
    pairs = left_side(half, table_ref, width)
    yield True
    residuals = []
    for j, (real, imag) in zip(group, pairs):
        power = jnp.maximum(real * real + imag * imag, floor_amp * floor_amp)
        factor = 1.0 - measured_of(j) * lax.rsqrt(power)
        residuals.append((real * factor, -(imag * factor)))
    half = right_side(residuals, table_ref)
    yield True
    pairs = left_side(half, table_ref, width)
    yield True
    for j, (real, negative) in zip(group, pairs):
        finish(j, real, -negative)


def joined(*parts):
    for part in parts:
        yield from part


def whole_pieces(refs, s, tile_px, width):
    tile_ref, below_ref, upper_ref, lower_ref, corner_ref, wrapped_ref = refs
    both = pl.ds(2 * s, 2)
    return [
        (0, 0, tile_ref.at[s]),
        (tile_px, 0, below_ref.at[both]),
        (0, tile_px, upper_ref.at[both]),
        (width, tile_px, lower_ref.at[both]),
        (tile_px, tile_px, corner_ref.at[both], wrapped_ref.at[both]),
    ]


def slice_pieces(refs, s, tile_px, width):
    (
        rest_ref, quad_ref, below_left_ref, below_right_ref, upper_ref, lower_ref, corner_ref, wrapped_ref,
    ) = refs
    both = pl.ds(2 * s, 2)
    across = tile_px - width
    return [
        (width, 0, rest_ref.at[:, pl.ds(width, across), :]),
        (0, width, rest_ref.at[:, pl.ds(0, width), pl.ds(width, across)]),
        (0, 0, quad_ref),
        (tile_px, 0, below_left_ref.at[both]),
        (tile_px, width, below_right_ref.at[both]),
        (0, tile_px, upper_ref),
        (width, tile_px, lower_ref),
        (tile_px, tile_px, corner_ref, wrapped_ref.at[both]),
    ]


def take_windows(ext_ref, spot_list, win_ref, width, lane):
    for j, spot in enumerate(spot_list):
        win_ref[j, 0] = window(ext_ref, 0, spot, width, lane)
        win_ref[j, 1] = window(ext_ref, 1, spot, width, lane)


def light(ext_ref, spot_list, probe_ref, enter_ref, width, lane):
    for j, spot in enumerate(spot_list):
        real = window(ext_ref, 0, spot, width, lane)
        imag = window(ext_ref, 1, spot, width, lane)
        enter_ref[j, 0] = probe_ref[0] * real - probe_ref[1] * imag
        enter_ref[j, 1] = probe_ref[0] * imag + probe_ref[1] * real


def residual_end(scalar_ref, spots, spot_list, ext_ref, moved_ref, win_ref, back_ref, width, lane):
    total = scalar_ref[2 * spots]

    def finish(j, real, imag):
        used = j < total
        scatter(ext_ref, 0, spot_list[j], width, lane, used, moved_ref[j, 0] * real + moved_ref[j, 1] * imag)
        scatter(ext_ref, 1, spot_list[j], width, lane, used, moved_ref[j, 0] * imag - moved_ref[j, 1] * real)
        back_ref[j, 0] = win_ref[j, 0] * real + win_ref[j, 1] * imag
        back_ref[j, 1] = win_ref[j, 0] * imag - win_ref[j, 1] * real

    return finish


def wave_kernel(
    scalar_ref, tile_ref, below_ref, upper_ref, lower_ref, corner_ref, wrapped_ref,
    cos_ref, sin_ref, probe_ref, amp_ref, table_ref,
    own_ref, down_ref, up_out_ref, low_out_ref, diag_ref, back_ref,
    ext_ref, win_ref, moved_ref, *, spots, width,
):
    lane = lanes_of(width)
    tile_px = own_ref.shape[1]
    spot_list = [place(scalar_ref, j) for j in range(spots)]
    halo = (tile_ref, below_ref, upper_ref, lower_ref, corner_ref, wrapped_ref)
    fill_ext(ext_ref, whole_pieces(halo, 0, tile_px, width))
    light(ext_ref, spot_list, probe_ref, back_ref, width, lane)
    fill_ext(ext_ref, whole_pieces(halo, 1, tile_px, width))
    take_windows(ext_ref, spot_list, win_ref, width, lane)
    ext_ref[...] = jnp.zeros(ext_ref.shape, jnp.float32)
    finish = residual_end(scalar_ref, spots, spot_list, ext_ref, moved_ref, win_ref, back_ref, width, lane)
    interleave([
        joined(
            forward_steps(group, back_ref, moved_ref, cos_ref, sin_ref, table_ref, width),
            residual_steps(
                group, moved_ref, win_ref, lambda j: amp_ref[scalar_ref[2 * spots + 1 + j]],
                finish, table_ref, width,
            ),
        )
        for group in groups_of(spots)
    ], LAG)
    emit(ext_ref, own_ref, down_ref, up_out_ref, low_out_ref, diag_ref, width)


def forward_kernel(
    scalar_ref, rest_ref, quad_ref, left_ref, right_ref, upper_ref, lower_ref, corner_ref, wrapped_ref,
    cos_ref, sin_ref, probe_ref, table_ref, moved_ref, ext_ref, enter_ref, *, spots, width,
):
    lane = lanes_of(width)
    spot_list = [place(scalar_ref, j) for j in range(spots)]
    halo = (rest_ref, quad_ref, left_ref, right_ref, upper_ref, lower_ref, corner_ref, wrapped_ref)
    fill_ext(ext_ref, slice_pieces(halo, 0, rest_ref.shape[1], width))
    light(ext_ref, spot_list, probe_ref, enter_ref, width, lane)
    interleave([
        forward_steps(group, enter_ref, moved_ref, cos_ref, sin_ref, table_ref, width)
        for group in groups_of(spots)
    ], LAG)


def residual_kernel(
    scalar_ref, rest_ref, quad_ref, left_ref, right_ref, upper_ref, lower_ref, corner_ref, wrapped_ref,
    moved_ref, amp_ref, table_ref,
    own_ref, down_ref, up_out_ref, low_out_ref, diag_ref, back_ref,
    ext_ref, win_ref, *, spots, width,
):
    lane = lanes_of(width)
    spot_list = [place(scalar_ref, j) for j in range(spots)]
    halo = (rest_ref, quad_ref, left_ref, right_ref, upper_ref, lower_ref, corner_ref, wrapped_ref)
    fill_ext(ext_ref, slice_pieces(halo, 1, rest_ref.shape[1], width))
    take_windows(ext_ref, spot_list, win_ref, width, lane)
    ext_ref[...] = jnp.zeros(ext_ref.shape, jnp.float32)
    finish = residual_end(scalar_ref, spots, spot_list, ext_ref, moved_ref, win_ref, back_ref, width, lane)
    interleave([
        residual_steps(
            group, moved_ref, win_ref, lambda j: amp_ref[scalar_ref[2 * spots + 1 + j]],
            finish, table_ref, width,
        )
        for group in groups_of(spots)
    ], LAG)
    emit(ext_ref, own_ref, down_ref, up_out_ref, low_out_ref, diag_ref, width)


def backward_kernel(
    scalar_ref, back_ref, other_diag_ref, cos_ref, sin_ref, probe_ref, table_ref,
    own_ref, down_ref, up_out_ref, low_out_ref, diag_ref, diags_ref, ext_ref, *, spots, width,
):
    lane = lanes_of(width)
    total = scalar_ref[2 * spots]
    ext_ref[...] = jnp.zeros(ext_ref.shape, jnp.float32)

    def chain(group):
        half = right_side([(back_ref[j, 0], back_ref[j, 1]) for j in group], table_ref)
        yield True
        pairs = left_side(half, table_ref, width)
        yield True
        half = right_side([
            (cos_ref[...] * real + sin_ref[...] * imag, -(cos_ref[...] * imag - sin_ref[...] * real))
            for real, imag in pairs
        ], table_ref)
        yield True
        pairs = left_side(half, table_ref, width)
        yield True
        for j, (real, negative) in zip(group, pairs):
            imag = -negative
            spot = place(scalar_ref, j)
            used = j < total
            scatter(ext_ref, 0, spot, width, lane, used, probe_ref[0] * real + probe_ref[1] * imag)
            scatter(ext_ref, 1, spot, width, lane, used, probe_ref[0] * imag - probe_ref[1] * real)

    interleave([chain(group) for group in groups_of(spots)], LAG)
    emit(ext_ref, own_ref, down_ref, up_out_ref, low_out_ref, diag_ref, width)
    diags_ref[:2] = diag_ref[...]
    diags_ref[2:] = other_diag_ref[...]


def step(value, gradient):
    return value - step_size * gradient


def rest_values(tile_ref, own_ref, above_ref, lower_ref, c, width):
    tile_px = own_ref.shape[1]
    top, low = slice(0, width), slice(width, tile_px)
    left, right = slice(0, width), slice(width, tile_px)
    yield top, right, step(tile_ref[c, top, right], own_ref[c, top, right] + above_ref[c, :, right])
    yield low, left, step(tile_ref[c, low, left], own_ref[c, low, left] + lower_ref[c])
    yield low, right, step(tile_ref[c, low, right], own_ref[c, low, right])


def quad_value(quad_ref, own_ref, above_ref, upper_ref, wrap_ref, c, width):
    top, left = slice(0, width), slice(0, width)
    received = above_ref[c, :, left] + upper_ref[c] + wrap_ref[c]
    return step(quad_ref[c, top, left], own_ref[c, top, left] + received)


def update_second_kernel(
    tile_ref, own_ref, above_ref, low_ref, rest_ref, left_ref, right_ref, *, width,
):
    for c in range(2):
        pieces = list(rest_values(tile_ref.at[1], own_ref, above_ref, low_ref, c, width))
        for rows, lanes, value in pieces:
            rest_ref[c, rows, lanes] = value
        right_ref[c] = pieces[0][2]
        left_ref[c] = pieces[1][2]


def update_first_kernel(
    tile_ref, own_ref, above_ref, low_ref, second_ref, rest_ref, left_ref, right_ref, *, width,
):
    for c in range(2):
        pieces = list(rest_values(tile_ref.at[0], own_ref, above_ref, low_ref, c, width))
        for rows, lanes, value in pieces:
            rest_ref[c, rows, lanes] = value
        right_ref[c] = pieces[0][2]
        right_ref[2 + c] = second_ref[c]
        left_ref[c] = pieces[1][2]


def update_quad_kernel(
    tile_ref, own_one, own_two, above_one, above_two, up_one, up_two, wrap_ref,
    quad_one, quad_two, left_ref, *, width,
):
    parts = ((own_one, above_one, up_one, quad_one), (own_two, above_two, up_two, quad_two))
    for s, (own_ref, above_ref, up_ref, quad_ref) in enumerate(parts):
        for c in range(2):
            wrap = wrap_ref.at[pl.ds(2 * s, 2)]
            value = quad_value(tile_ref.at[s], own_ref, above_ref, up_ref, wrap, c, width)
            quad_ref[c] = value
            left_ref[2 * s + c] = value


def finish_rest_kernel(rest_ref, own_ref, above_ref, low_ref, *refs, width, part):
    out_ref, tile_ref, sem = refs[-3:]
    for c in range(2):
        for rows, lanes, value in rest_values(rest_ref, own_ref, above_ref, low_ref, c, width):
            tile_ref[c, rows, lanes] = value
        tile_ref[c, :width, :width] = jnp.zeros((width, width), jnp.float32)
    copy = pltpu.make_async_copy(tile_ref, out_ref.at[part], sem)
    copy.start()
    copy.wait()


def finish_quad_kernel(
    quad_one, quad_two, own_one, own_two, above_one, above_two, up_one, up_two, wrap_ref, part_ref, out_ref,
    quads_ref, sem, *, width,
):
    del part_ref
    parts = ((quad_one, own_one, above_one, up_one), (quad_two, own_two, above_two, up_two))
    for s, refs in enumerate(parts):
        for c in range(2):
            quads_ref[s, c] = quad_value(*refs, wrap_ref.at[pl.ds(2 * s, 2)], c, width)
    copy = pltpu.make_async_copy(quads_ref, out_ref.at[:, :, pl.ds(0, width), pl.ds(0, width)], sem)
    copy.start()
    copy.wait()


def stage_kernel(*refs):
    sems = refs[-1]
    count = (len(refs) - 1) // 2
    copies = [pltpu.make_async_copy(refs[k], refs[count + k], sems.at[k]) for k in range(count)]
    for copy in copies:
        copy.start()
    for copy in copies:
        copy.wait()


F32 = functools.partial(jax.ShapeDtypeStruct, dtype=jnp.float32)
SMEM = pl.BlockSpec(memory_space=pltpu.SMEM)
VMEM = pl.BlockSpec(memory_space=pltpu.VMEM)
LIMIT = pltpu.CompilerParams(vmem_limit_bytes=16 * 1024 * 1024)


FAR = pl.BlockSpec(memory_space=pltpu.MemorySpace.HBM)


def call(kernel, scalars, arrays, outs, scratch, **static):
    return pl.pallas_call(
        functools.partial(kernel, **static),
        in_specs=[SMEM] * len(scalars) + [VMEM] * len(arrays),
        out_specs=[VMEM] * len(outs),
        out_shape=outs,
        scratch_shapes=scratch,
        compiler_params=LIMIT,
    )(*scalars, *arrays)


def pack_kernel(whole_ref, *refs, boxes):
    outs, sems = refs[:-1], refs[-1]
    copies = []
    for (rows, lanes), out_ref in zip(boxes, outs):
        for s in range(2):
            source = whole_ref.at[s, :, pl.ds(*rows), pl.ds(*lanes)]
            copies.append(pltpu.make_async_copy(source, out_ref.at[pl.ds(2 * s, 2)], sems.at[len(copies)]))
    for copy in copies:
        copy.start()
    for copy in copies:
        copy.wait()


def pack(whole, boxes):
    return pl.pallas_call(
        functools.partial(pack_kernel, boxes=boxes),
        in_specs=[FAR],
        out_specs=[VMEM] * len(boxes),
        out_shape=[F32((4, rows[1], lanes[1])) for rows, lanes in boxes],
        scratch_shapes=[pltpu.SemaphoreType.DMA((2 * len(boxes),))],
        compiler_params=LIMIT,
    )(in_hbm(whole))


def in_hbm(array):
    return pltpu.with_memory_space_constraint(array, pltpu.MemorySpace.HBM)


def body(
    specimen_slices,
    illumination_probe,
    propagation_phase,
    amplitudes,
    positions,
    counts,
    measurement_index,
):
    tile_px = specimen_slices.shape[2]
    width = illumination_probe.shape[1]
    spots = positions.shape[2]
    ext = tile_px + width
    across = tile_px - width
    cos, sin = jnp.cos(propagation_phase), jnp.sin(propagation_phase)
    scalars = (jnp.concatenate([positions.reshape(-1), counts.reshape(-1), measurement_index.reshape(-1)]),)
    static = dict(spots=spots, width=width)
    ext_space = pltpu.VMEM((2, ext // LANES, ext, LANES), jnp.float32)
    wave_space = pltpu.VMEM((spots, 2, width, width), jnp.float32)
    wave = F32((spots, 2, width, width))
    square = F32((2, width, width))
    squares = F32((4, width, width))
    whole = F32((2, tile_px, tile_px))
    strip = F32((2, width, tile_px))
    gradient = [whole, strip, square, square, square]

    (left_up,) = pack(specimen_slices, [((0, width), (0, width))])
    upper = from_behind(left_up, "col", -1)
    left_low, top = pack(specimen_slices, [((width, across), (0, width)), ((0, width), (0, tile_px))])
    lower = from_behind(left_low, "col", -1)
    below = from_behind(top, "row", -1)
    wrapped = send_wrap(left_up, -1)
    far = (specimen_slices, illumination_probe, amplitudes[0, 0], jnp.asarray(dft_operands(width)))
    tile, probe, measured, table = pl.pallas_call(
        stage_kernel,
        in_specs=[FAR] * len(far),
        out_specs=[VMEM] * len(far),
        out_shape=[jax.ShapeDtypeStruct(x.shape, x.dtype) for x in far],
        scratch_shapes=[pltpu.SemaphoreType.DMA((len(far),))],
        compiler_params=LIMIT,
        name="stage",
    )(*[in_hbm(x) for x in far])
    corner = send_corner(upper, -1)
    for i in range(ITERS):
        if i == 0:
            own_two, down_two, up_two, low_two, diag_two, back = call(
                wave_kernel, scalars,
                (tile, below, upper, lower, corner, wrapped, cos, sin, probe, measured, table),
                [*gradient, wave], [ext_space, wave_space, wave_space], **static,
            )
        else:
            (moved,) = call(
                forward_kernel, scalars, (*halo[0], cos, sin, probe, table),
                [wave], [ext_space, wave_space], **static,
            )
            own_two, down_two, up_two, low_two, diag_two, back = call(
                residual_kernel, scalars, (*halo[1], moved, measured, table),
                [*gradient, wave], [ext_space, wave_space], **static,
            )
        low_two = from_behind(low_two, "col", 1)
        corner_two = send_corner(diag_two, 1)
        above_two = from_behind(down_two, "row", 1)
        own_one, down_one, up_one, low_one, diag_one, diags = call(
            backward_kernel, scalars, (back, diag_two, cos, sin, probe, table),
            [*gradient, squares], [ext_space], **static,
        )
        low_one = from_behind(low_one, "col", 1)
        corner_one = send_corner(diag_one, 1)
        above_one = from_behind(down_one, "row", 1)
        up_two = up_two + corner_two
        up_one = up_one + corner_one
        up_two = from_behind(up_two, "col", 1)
        up_one = from_behind(up_one, "col", 1)
        from_wrap = send_wrap(diags, 1)
        if i + 1 < ITERS:
            rest_two, left_two, right = call(
                update_second_kernel, (), (tile, own_two, above_two, low_two),
                [whole, square, F32((2, width, across))], [], width=width,
            )
            rest_one, left_one, right = call(
                update_first_kernel, (), (tile, own_one, above_one, low_one, right),
                [whole, square, F32((4, width, across))], [], width=width,
            )
            lower_one = from_behind(left_one, "col", -1)
            below_right = from_behind(right, "row", -1)
            quad_one, quad_two, left = call(
                update_quad_kernel, (),
                (tile, own_one, own_two, above_one, above_two, up_one, up_two, from_wrap),
                [square, square, squares], [], width=width,
            )
            upper_one = from_behind(quad_one, "col", -1)
            upper_two = from_behind(quad_two, "col", -1)
            below_left = from_behind(left, "row", -1)
            lower_two = from_behind(left_two, "col", -1)
            wrapped = send_wrap(left, -1)
            corner_one = send_corner(upper_one, -1)
            corner_two = send_corner(upper_two, -1)
            halo = (
                (rest_one, quad_one, below_left, below_right, upper_one, lower_one, corner_one, wrapped),
                (rest_two, quad_two, below_left, below_right, upper_two, lower_two, corner_two, wrapped),
            )
        else:
            part = []
            for slice_at, operands in (
                (1, (rest_two, own_two, above_two, low_two)), (0, (rest_one, own_one, above_one, low_one))
            ):
                part = [pl.pallas_call(
                    functools.partial(finish_rest_kernel, width=width, part=slice_at),
                    in_specs=[VMEM] * 4 + [FAR] * len(part),
                    out_specs=FAR,
                    out_shape=F32(specimen_slices.shape),
                    input_output_aliases={4: 0} if part else {},
                    scratch_shapes=[
                        pltpu.VMEM((2, tile_px, tile_px), jnp.float32), pltpu.SemaphoreType.DMA(()),
                    ],
                    compiler_params=LIMIT,
                    name="finish_rest",
                )(*operands, *map(in_hbm, part))]
            updated = pl.pallas_call(
                functools.partial(finish_quad_kernel, width=width),
                in_specs=[VMEM] * 9 + [FAR],
                out_specs=FAR,
                out_shape=F32(specimen_slices.shape),
                input_output_aliases={9: 0},
                scratch_shapes=[
                    pltpu.VMEM((2, 2, width, width), jnp.float32), pltpu.SemaphoreType.DMA(()),
                ],
                compiler_params=LIMIT,
                name="finish_quad",
            )(quad_one, quad_two, own_one, own_two, above_one, above_two, up_one, up_two, from_wrap, in_hbm(part[0]))
    return updated


def solution(mesh):
    placed = (
        P(None, None, "row", "col"),
        P(),
        P(),
        P("row", "col", None, None, None),
        P("row", "col", None, None),
        P("row", "col"),
        P("row", "col", None),
    )

    return jax.shard_map(body, mesh=mesh, in_specs=placed, out_specs=P(None, None, "row", "col"), check_vma=False)
```

profile of v0, /device:TPU:0, one launch (start us, length us, event | category | flops | bytes accessed | tf_op | source)
XLA Modules:
  0.0 94.2 jit_solution(5525671924827031326)
XLA Ops:
  1.0 3.0 %collective-permute-start.1 = (f32[4,128,128]{2,1,0:T(8,128)S(1)}, f32[4,128,128]{2,1,0:T(8,128)S(1)}, u32[]{:S(2)}, u32[]{:S(2)}) collective-permute-start(f32[4,128,128]{2,1,0:T(8,128)S(1)} %shard_map.83), channel_id=1, source_target_pairs={{1,0},{0,1},{3,2},{2,3},{5,4},{4,5},{7,6},{6,7},{9,8},{8,9},{11,10... | collective-permute-start | bytes 786440 | tf_op jit(solution)/shard_map/ppermute | solution.py:37
  5.2 3.8 %collective-permute-start = (f32[4,128,256]{2,1,0:T(8,128)S(1)}, f32[4,128,256]{2,1,0:T(8,128)S(1)}, u32[]{:S(2)}, u32[]{:S(2)}) collective-permute-start(f32[4,128,256]{2,1,0:T(8,128)S(1)} %get-tuple-element.45), channel_id=1, source_target_pairs={{2,0},{4,2},{6,4},{8,6},{10,8},{12,10},{14,12},{16,14},{18,16},{20... | collective-permute-start | bytes 1572872 | tf_op jit(solution)/shard_map/ppermute | solution.py:37
  9.0 2.8 %collective-permute-start.4 = (f32[4,128,128]{2,1,0:T(8,128)S(1)}, f32[4,128,128]{2,1,0:T(8,128)S(1)}, u32[]{:S(2)}, u32[]{:S(2)}) collective-permute-start(f32[4,128,128]{2,1,0:T(8,128)S(1)} %shard_map.83), channel_id=1, source_target_pairs={{0,31},{1,30}} | collective-permute-start | bytes 786440 | tf_op jit(solution)/shard_map/ppermute | solution.py:31
  11.9 1.6 %collective-permute-start.2 = (f32[4,128,128]{2,1,0:T(8,128)S(1)}, f32[4,128,128]{2,1,0:T(8,128)S(1)}, u32[]{:S(2)}, u32[]{:S(2)}) collective-permute-start(f32[4,128,128]{2,1,0:T(8,128)S(1)} %get-tuple-element.46), channel_id=1, source_target_pairs={{1,0},{0,1},{3,2},{2,3},{5,4},{4,5},{7,6},{6,7},{9,8},{8,9},{11,10... | collective-permute-start | bytes 786440 | tf_op jit(solution)/shard_map/ppermute | solution.py:37
  14.3 1.3 %collective-permute-start.3 = (f32[4,128,128]{2,1,0:T(8,128)S(1)}, f32[4,128,128]{2,1,0:T(8,128)S(1)}, u32[]{:S(2)}, u32[]{:S(2)}) collective-permute-start(f32[4,128,128]{2,1,0:T(8,128)S(1)} %collective-permute-done.1.upper_ref), channel_id=1, source_target_pairs={{2,0},{4,2},{6,4},{8,6},{10,8},{12,10},{14,12},{16,14},{18,16},{20... | collective-permute-start | bytes 786440 | tf_op jit(solution)/shard_map/ppermute | solution.py:24
  16.3 1.5 %stage.1 = (f32[2,2,256,256]{3,2,1,0:T(8,128)S(1)}, f32[2,128,128]{2,1,0:T(8,128)S(1)}, f32[4,128,128]{2,1,0:T(8,128)S(1)}, bf16[4,256,256]{2,1,0:T(8,128)(2,1)S(1)}) custom-call(f32[2,2,256,256]{3,2,1,0:T(8,128)} %whole_ref.3, f32[2,128,128]{2,1,0:T(8,128)} %refs_1_.1, f32[4,128,128]{2,1,0:T(8,128)} %bitcast.4, bf16[4,256,256]{2,1,0:T(8,128)(2,1)} %constant.2.clone.refs_3_), custom_call_target="tpu_custom_call" | custom-call | tf_op jit(solution)/shard_map/stage/pallas_call | solution.py:527
  18.5 3.9 %shard_map.84 = (f32[2,256,256]{2,1,0:T(8,128)S(1)}, f32[2,128,256]{2,1,0:T(8,128)S(1)}, f32[2,128,128]{2,1,0:T(8,128)S(1)}, f32[2,128,128]{2,1,0:T(8,128)S(1)},...) custom-call(s32[13]{0:T(128)S(1)} %pad_add_fusion.scalar_ref, ...), custom_call_target="tpu_custom_call" | custom-call | tf_op jit(solution)/shard_map/pallas_call | solution.py:456
  22.5 2.4 %shard_map.85 = (f32[2,256,256]{2,1,0:T(8,128)S(1)}, f32[2,128,256]{2,1,0:T(8,128)S(1)}, f32[2,128,128]{2,1,0:T(8,128)S(1)}, f32[2,128,128]{2,1,0:T(8,128)S(1)},...) custom-call(s32[13]{0:T(128)S(1)} %pad_add_fusion.scalar_ref, f32[4,2,128,128]{3,2,1,0:T(8,128)S(1)} %get-tuple-element.50.back_ref, ...), custom_call_target="tpu_custom_call" | custom-call | tf_op jit(solution)/shard_map/pallas_call | solution.py:456
  24.9 2.7 %collective-permute-start.7 = (f32[2,128,128]{2,1,0:T(8,128)S(1)}, f32[2,128,128]{2,1,0:T(8,128)S(1)}, u32[]{:S(2)}, u32[]{:S(2)}) collective-permute-start(f32[2,128,128]{2,1,0:T(8,128)S(1)} %get-tuple-element.57), channel_id=1, source_target_pairs={{0,2},{2,4},{4,6},{6,8},{8,10},{10,12},{12,14},{14,16},{16,18},{18... | collective-permute-start | bytes 393224 | tf_op jit(solution)/shard_map/ppermute | solution.py:24
  27.7 3.5 %collective-permute-start.9 = (f32[2,128,128]{2,1,0:T(8,128)S(1)}, f32[2,128,128]{2,1,0:T(8,128)S(1)}, u32[]{:S(2)}, u32[]{:S(2)}) collective-permute-start(f32[2,128,128]{2,1,0:T(8,128)S(1)} %get-tuple-element.51.other_diag_ref), channel_id=1, source_target_pairs={{0,2},{2,4},{4,6},{6,8},{8,10},{10,12},{12,14},{14,16},{16,18},{18... | collective-permute-start | bytes 393224 | tf_op jit(solution)/shard_map/ppermute | solution.py:24
  31.2 1.6 %collective-permute-start.12 = (f32[2,128,128]{2,1,0:T(8,128)S(1)}, f32[2,128,128]{2,1,0:T(8,128)S(1)}, u32[]{:S(2)}, u32[]{:S(2)}) collective-permute-start(f32[2,128,128]{2,1,0:T(8,128)S(1)} %get-tuple-element.62), channel_id=1, source_target_pairs={{1,0},{0,1},{3,2},{2,3},{5,4},{4,5},{7,6},{6,7},{9,8},{8,9},{11,10... | collective-permute-start | bytes 393224 | tf_op jit(solution)/shard_map/ppermute | solution.py:37
  34.7 2.3 %collective-permute-done.12.low_ref = f32[2,128,128]{2,1,0:T(8,128)S(1)} collective-permute-done((f32[2,128,128]{2,1,0:T(8,128)S(1)}, f32[2,128,128]{2,1,0:T(8,128)S(1)}, u32[]{:S(2)}, u32[]{:S(2)}) %collective-permute-start.12) | collective-permute-done | bytes 131104 | tf_op jit(solution)/shard_map/ppermute | solution.py:37
  37.1 1.5 %collective-permute-start.8 = (f32[2,128,128]{2,1,0:T(8,128)S(1)}, f32[2,128,128]{2,1,0:T(8,128)S(1)}, u32[]{:S(2)}, u32[]{:S(2)}) collective-permute-start(f32[2,128,128]{2,1,0:T(8,128)S(1)} %add.12), channel_id=1, source_target_pairs={{1,0},{0,1},{3,2},{2,3},{5,4},{4,5},{7,6},{6,7},{9,8},{8,9},{11,10... | collective-permute-start | bytes 393224 | tf_op jit(solution)/shard_map/ppermute | solution.py:37
  39.2 1.3 %collective-permute-done.14.low_ref = f32[2,128,128]{2,1,0:T(8,128)S(1)} collective-permute-done((f32[2,128,128]{2,1,0:T(8,128)S(1)}, f32[2,128,128]{2,1,0:T(8,128)S(1)}, u32[]{:S(2)}, u32[]{:S(2)}) %collective-permute-start.14) | collective-permute-done | bytes 131104 | tf_op jit(solution)/shard_map/ppermute | solution.py:37
  41.6 2.6 %collective-permute-done.11.wrap_ref = f32[4,128,128]{2,1,0:T(8,128)S(1)} collective-permute-done((f32[4,128,128]{2,1,0:T(8,128)S(1)}, f32[4,128,128]{2,1,0:T(8,128)S(1)}, u32[]{:S(2)}, u32[]{:S(2)}) %collective-permute-start.11) | collective-permute-done | bytes 262176 | tf_op jit(solution)/shard_map/ppermute | solution.py:31
  44.2 2.0 %collective-permute-done.10.up_two = f32[2,128,128]{2,1,0:T(8,128)S(1)} collective-permute-done((f32[2,128,128]{2,1,0:T(8,128)S(1)}, f32[2,128,128]{2,1,0:T(8,128)S(1)}, u32[]{:S(2)}, u32[]{:S(2)}) %collective-permute-start.10) | collective-permute-done | bytes 131104 | tf_op jit(solution)/shard_map/ppermute | solution.py:37
  46.3 3.8 %collective-permute-start.13 = (f32[4,128,128]{2,1,0:T(8,128)S(1)}, f32[4,128,128]{2,1,0:T(8,128)S(1)}, u32[]{:S(2)}, u32[]{:S(2)}) collective-permute-start(f32[4,128,128]{2,1,0:T(8,128)S(1)} %get-tuple-element.64), channel_id=1, source_target_pairs={{2,0},{4,2},{6,4},{8,6},{10,8},{12,10},{14,12},{16,14},{18,16},{20... | collective-permute-start | bytes 786440 | tf_op jit(solution)/shard_map/ppermute | solution.py:37
  51.3 2.9 %collective-permute-start.19 = (f32[4,128,128]{2,1,0:T(8,128)S(1)}, f32[4,128,128]{2,1,0:T(8,128)S(1)}, u32[]{:S(2)}, u32[]{:S(2)}) collective-permute-start(f32[4,128,128]{2,1,0:T(8,128)S(1)} %get-tuple-element.64), channel_id=1, source_target_pairs={{0,31},{1,30}} | collective-permute-start | bytes 786440 | tf_op jit(solution)/shard_map/ppermute | solution.py:31
  54.8 1.5 %collective-permute-start.16 = (f32[2,128,128]{2,1,0:T(8,128)S(1)}, f32[2,128,128]{2,1,0:T(8,128)S(1)}, u32[]{:S(2)}, u32[]{:S(2)}) collective-permute-start(f32[2,128,128]{2,1,0:T(8,128)S(1)} %get-tuple-element.61.quad_ref.quad_two), channel_id=1, source_target_pairs={{1,0},{0,1},{3,2},{2,3},{5,4},{4,5},{7,6},{6,7},{9,8},{8,9},{11,10... | collective-permute-start | bytes 393224 | tf_op jit(solution)/shard_map/ppermute | solution.py:37
  56.3 2.9 %collective-permute-done.20.upper_ref = f32[2,128,128]{2,1,0:T(8,128)S(1)} collective-permute-done((f32[2,128,128]{2,1,0:T(8,128)S(1)}, f32[2,128,128]{2,1,0:T(8,128)S(1)}, u32[]{:S(2)}, u32[]{:S(2)}) %collective-permute-start.20) | collective-permute-done | bytes 131104 | tf_op jit(solution)/shard_map/ppermute | solution.py:37
  62.6 2.2 %shard_map.89.moved_ref = f32[4,2,128,128]{3,2,1,0:T(8,128)S(1)} custom-call(s32[13]{0:T(128)S(1)} %pad_add_fusion.scalar_ref, f32[2,256,256]{2,1,0:T(8,128)S(1)} %get-tuple-element.69.rest_ref, f32[2,128,128]{2,1,0:T(8,128)S(1)} %get-tuple-element.60.quad_ref.quad_one, f32[4,128,128]{2,1,0:T(8,128)S(1)} %collective-permute-done.13.left_ref, ...), custom_call_target="tpu_custom_call" | custom-call | tf_op jit(solution)/shard_map/pallas_call | solution.py:456
  64.9 2.0 %collective-permute-done.17.lower_ref = f32[2,128,128]{2,1,0:T(8,128)S(1)} collective-permute-done((f32[2,128,128]{2,1,0:T(8,128)S(1)}, f32[2,128,128]{2,1,0:T(8,128)S(1)}, u32[]{:S(2)}, u32[]{:S(2)}) %collective-permute-start.17) | collective-permute-done | bytes 131104 | tf_op jit(solution)/shard_map/ppermute | solution.py:37
  66.9 2.6 %shard_map.90 = (f32[2,256,256]{2,1,0:T(8,128)S(1)}, f32[2,128,256]{2,1,0:T(8,128)S(1)}, f32[2,128,128]{2,1,0:T(8,128)S(1)}, f32[2,128,128]{2,1,0:T(8,128)S(1)},...) custom-call(s32[13]{0:T(128)S(1)} %pad_add_fusion.scalar_ref, f32[2,256,256]{2,1,0:T(8,128)S(1)} %get-tuple-element.63.rest_ref, ...), custom_call_target="tpu_custom_call" | custom-call | tf_op jit(solution)/shard_map/pallas_call | solution.py:456
  69.5 1.4 %collective-permute-start.24 = (f32[2,128,256]{2,1,0:T(8,128)S(1)}, f32[2,128,256]{2,1,0:T(8,128)S(1)}, u32[]{:S(2)}, u32[]{:S(2)}) collective-permute-start(f32[2,128,256]{2,1,0:T(8,128)S(1)} %get-tuple-element.76), channel_id=1, source_target_pairs={{30,0},{0,2},{2,4},{4,6},{6,8},{8,10},{10,12},{12,14},{14,16},{16,... | collective-permute-start | bytes 786440 | tf_op jit(solution)/shard_map/ppermute | solution.py:37
  70.9 2.4 %shard_map.91 = (f32[2,256,256]{2,1,0:T(8,128)S(1)}, f32[2,128,256]{2,1,0:T(8,128)S(1)}, f32[2,128,128]{2,1,0:T(8,128)S(1)}, f32[2,128,128]{2,1,0:T(8,128)S(1)},...) custom-call(s32[13]{0:T(128)S(1)} %pad_add_fusion.scalar_ref, f32[4,2,128,128]{3,2,1,0:T(8,128)S(1)} %get-tuple-element.71.back_ref, ...), custom_call_target="tpu_custom_call" | custom-call | tf_op jit(solution)/shard_map/pallas_call | solution.py:456
  73.3 1.9 %collective-permute-start.25 = (f32[2,128,128]{2,1,0:T(8,128)S(1)}, f32[2,128,128]{2,1,0:T(8,128)S(1)}, u32[]{:S(2)}, u32[]{:S(2)}) collective-permute-start(f32[2,128,128]{2,1,0:T(8,128)S(1)} %get-tuple-element.78), channel_id=1, source_target_pairs={{0,2},{2,4},{4,6},{6,8},{8,10},{10,12},{12,14},{14,16},{16,18},{18... | collective-permute-start | bytes 393224 | tf_op jit(solution)/shard_map/ppermute | solution.py:24
  75.3 3.1 %collective-permute-start.27 = (f32[2,128,128]{2,1,0:T(8,128)S(1)}, f32[2,128,128]{2,1,0:T(8,128)S(1)}, u32[]{:S(2)}, u32[]{:S(2)}) collective-permute-start(f32[2,128,128]{2,1,0:T(8,128)S(1)} %get-tuple-element.72.other_diag_ref), channel_id=1, source_target_pairs={{0,2},{2,4},{4,6},{6,8},{8,10},{10,12},{12,14},{14,16},{16,18},{18... | collective-permute-start | bytes 393224 | tf_op jit(solution)/shard_map/ppermute | solution.py:24
  80.4 1.5 %collective-permute-start.30 = (f32[2,128,128]{2,1,0:T(8,128)S(1)}, f32[2,128,128]{2,1,0:T(8,128)S(1)}, u32[]{:S(2)}, u32[]{:S(2)}) collective-permute-start(f32[2,128,128]{2,1,0:T(8,128)S(1)} %get-tuple-element.81), channel_id=1, source_target_pairs={{1,0},{0,1},{3,2},{2,3},{5,4},{4,5},{7,6},{6,7},{9,8},{8,9},{11,10... | collective-permute-start | bytes 393224 | tf_op jit(solution)/shard_map/ppermute | solution.py:37
  82.0 2.7 %collective-permute-done.31.low_ref = f32[2,128,128]{2,1,0:T(8,128)S(1)} collective-permute-done((f32[2,128,128]{2,1,0:T(8,128)S(1)}, f32[2,128,128]{2,1,0:T(8,128)S(1)}, u32[]{:S(2)}, u32[]{:S(2)}) %collective-permute-start.31) | collective-permute-done | bytes 131104 | tf_op jit(solution)/shard_map/ppermute | solution.py:37
  85.0 1.7 %collective-permute-start.28 = (f32[2,128,128]{2,1,0:T(8,128)S(1)}, f32[2,128,128]{2,1,0:T(8,128)S(1)}, u32[]{:S(2)}, u32[]{:S(2)}) collective-permute-start(f32[2,128,128]{2,1,0:T(8,128)S(1)} %add.15), channel_id=1, source_target_pairs={{1,0},{0,1},{3,2},{2,3},{5,4},{4,5},{7,6},{6,7},{9,8},{8,9},{11,10... | collective-permute-start | bytes 393224 | tf_op jit(solution)/shard_map/ppermute | solution.py:37
  88.5 2.6 %collective-permute-done.26.up_one = f32[2,128,128]{2,1,0:T(8,128)S(1)} collective-permute-done((f32[2,128,128]{2,1,0:T(8,128)S(1)}, f32[2,128,128]{2,1,0:T(8,128)S(1)}, u32[]{:S(2)}, u32[]{:S(2)}) %collective-permute-start.26) | collective-permute-done | bytes 131104 | tf_op jit(solution)/shard_map/ppermute | solution.py:37
  91.0 2.4 %collective-permute-done.28.up_two = f32[2,128,128]{2,1,0:T(8,128)S(1)} collective-permute-done((f32[2,128,128]{2,1,0:T(8,128)S(1)}, f32[2,128,128]{2,1,0:T(8,128)S(1)}, u32[]{:S(2)}, u32[]{:S(2)}) %collective-permute-start.28) | collective-permute-done | bytes 131104 | tf_op jit(solution)/shard_map/ppermute | solution.py:37
  (60 shorter events, 17.6 us)
Async XLA Ops:
  1.0 13.3 %collective-permute-start.1 = (f32[4,128,128]{2,1,0:T(8,128)S(1)}, f32[4,128,128]{2,1,0:T(8,128)S(1)}, u32[]{:S(2)}, u32[]{:S(2)}) collective-permute-start(f32[4,128,128]{2,1,0:T(8,128)S(1)} %shard_map.83), channel_id=1, source_target_pairs={{1,0},{0,1},{3,2},{2,3},{5,4},{4,5},{7,6},{6,7},{9,8},{8,9},{11,10... | collective-permute-start | bytes 786440 | tf_op jit(solution)/shard_map/ppermute | solution.py:37
  5.2 13.3 %collective-permute-start = (f32[4,128,256]{2,1,0:T(8,128)S(1)}, f32[4,128,256]{2,1,0:T(8,128)S(1)}, u32[]{:S(2)}, u32[]{:S(2)}) collective-permute-start(f32[4,128,256]{2,1,0:T(8,128)S(1)} %get-tuple-element.45), channel_id=1, source_target_pairs={{2,0},{4,2},{6,4},{8,6},{10,8},{12,10},{14,12},{16,14},{18,16},{20... | collective-permute-start | bytes 1572872 | tf_op jit(solution)/shard_map/ppermute | solution.py:37
  9.0 9.5 %collective-permute-start.4 = (f32[4,128,128]{2,1,0:T(8,128)S(1)}, f32[4,128,128]{2,1,0:T(8,128)S(1)}, u32[]{:S(2)}, u32[]{:S(2)}) collective-permute-start(f32[4,128,128]{2,1,0:T(8,128)S(1)} %shard_map.83), channel_id=1, source_target_pairs={{0,31},{1,30}} | collective-permute-start | bytes 786440 | tf_op jit(solution)/shard_map/ppermute | solution.py:31
  11.9 6.4 %collective-permute-start.2 = (f32[4,128,128]{2,1,0:T(8,128)S(1)}, f32[4,128,128]{2,1,0:T(8,128)S(1)}, u32[]{:S(2)}, u32[]{:S(2)}) collective-permute-start(f32[4,128,128]{2,1,0:T(8,128)S(1)} %get-tuple-element.46), channel_id=1, source_target_pairs={{1,0},{0,1},{3,2},{2,3},{5,4},{4,5},{7,6},{6,7},{9,8},{8,9},{11,10... | collective-permute-start | bytes 786440 | tf_op jit(solution)/shard_map/ppermute | solution.py:37
  14.3 4.3 %collective-permute-start.3 = (f32[4,128,128]{2,1,0:T(8,128)S(1)}, f32[4,128,128]{2,1,0:T(8,128)S(1)}, u32[]{:S(2)}, u32[]{:S(2)}) collective-permute-start(f32[4,128,128]{2,1,0:T(8,128)S(1)} %collective-permute-done.1.upper_ref), channel_id=1, source_target_pairs={{2,0},{4,2},{6,4},{8,6},{10,8},{12,10},{14,12},{16,14},{18,16},{20... | collective-permute-start | bytes 786440 | tf_op jit(solution)/shard_map/ppermute | solution.py:24
  24.9 7.9 %collective-permute-start.7 = (f32[2,128,128]{2,1,0:T(8,128)S(1)}, f32[2,128,128]{2,1,0:T(8,128)S(1)}, u32[]{:S(2)}, u32[]{:S(2)}) collective-permute-start(f32[2,128,128]{2,1,0:T(8,128)S(1)} %get-tuple-element.57), channel_id=1, source_target_pairs={{0,2},{2,4},{4,6},{6,8},{8,10},{10,12},{12,14},{14,16},{16,18},{18... | collective-permute-start | bytes 393224 | tf_op jit(solution)/shard_map/ppermute | solution.py:24
  27.6 11.0 %collective-permute-start.6 = (f32[2,128,256]{2,1,0:T(8,128)S(1)}, f32[2,128,256]{2,1,0:T(8,128)S(1)}, u32[]{:S(2)}, u32[]{:S(2)}) collective-permute-start(f32[2,128,256]{2,1,0:T(8,128)S(1)} %get-tuple-element.55), channel_id=1, source_target_pairs={{30,0},{0,2},{2,4},{4,6},{6,8},{8,10},{10,12},{12,14},{14,16},{16,... | collective-permute-start | bytes 786440 | tf_op jit(solution)/shard_map/ppermute | solution.py:37
  27.7 6.4 %collective-permute-start.9 = (f32[2,128,128]{2,1,0:T(8,128)S(1)}, f32[2,128,128]{2,1,0:T(8,128)S(1)}, u32[]{:S(2)}, u32[]{:S(2)}) collective-permute-start(f32[2,128,128]{2,1,0:T(8,128)S(1)} %get-tuple-element.51.other_diag_ref), channel_id=1, source_target_pairs={{0,2},{2,4},{4,6},{6,8},{8,10},{10,12},{12,14},{14,16},{16,18},{18... | collective-permute-start | bytes 393224 | tf_op jit(solution)/shard_map/ppermute | solution.py:24
  31.2 9.3 %collective-permute-start.5 = (f32[2,128,256]{2,1,0:T(8,128)S(1)}, f32[2,128,256]{2,1,0:T(8,128)S(1)}, u32[]{:S(2)}, u32[]{:S(2)}) collective-permute-start(f32[2,128,256]{2,1,0:T(8,128)S(1)} %get-tuple-element.54), channel_id=1, source_target_pairs={{30,0},{0,2},{2,4},{4,6},{6,8},{8,10},{10,12},{12,14},{14,16},{16,... | collective-permute-start | bytes 786440 | tf_op jit(solution)/shard_map/ppermute | solution.py:37
  31.2 5.8 %collective-permute-start.12 = (f32[2,128,128]{2,1,0:T(8,128)S(1)}, f32[2,128,128]{2,1,0:T(8,128)S(1)}, u32[]{:S(2)}, u32[]{:S(2)}) collective-permute-start(f32[2,128,128]{2,1,0:T(8,128)S(1)} %get-tuple-element.62), channel_id=1, source_target_pairs={{1,0},{0,1},{3,2},{2,3},{5,4},{4,5},{7,6},{6,7},{9,8},{8,9},{11,10... | collective-permute-start | bytes 393224 | tf_op jit(solution)/shard_map/ppermute | solution.py:37
  32.8 11.4 %collective-permute-start.11 = (f32[4,128,128]{2,1,0:T(8,128)S(1)}, f32[4,128,128]{2,1,0:T(8,128)S(1)}, u32[]{:S(2)}, u32[]{:S(2)}) collective-permute-start(f32[4,128,128]{2,1,0:T(8,128)S(1)} %get-tuple-element.59), channel_id=1, source_target_pairs={{30,1},{31,0}} | collective-permute-start | bytes 786440 | tf_op jit(solution)/shard_map/ppermute | solution.py:31
  34.1 6.4 %collective-permute-start.14 = (f32[2,128,128]{2,1,0:T(8,128)S(1)}, f32[2,128,128]{2,1,0:T(8,128)S(1)}, u32[]{:S(2)}, u32[]{:S(2)}) collective-permute-start(f32[2,128,128]{2,1,0:T(8,128)S(1)} %get-tuple-element.65), channel_id=1, source_target_pairs={{1,0},{0,1},{3,2},{2,3},{5,4},{4,5},{7,6},{6,7},{9,8},{8,9},{11,10... | collective-permute-start | bytes 393224 | tf_op jit(solution)/shard_map/ppermute | solution.py:37
  37.1 7.1 %collective-permute-start.8 = (f32[2,128,128]{2,1,0:T(8,128)S(1)}, f32[2,128,128]{2,1,0:T(8,128)S(1)}, u32[]{:S(2)}, u32[]{:S(2)}) collective-permute-start(f32[2,128,128]{2,1,0:T(8,128)S(1)} %add.12), channel_id=1, source_target_pairs={{1,0},{0,1},{3,2},{2,3},{5,4},{4,5},{7,6},{6,7},{9,8},{8,9},{11,10... | collective-permute-start | bytes 393224 | tf_op jit(solution)/shard_map/ppermute | solution.py:37
  38.6 7.6 %collective-permute-start.10 = (f32[2,128,128]{2,1,0:T(8,128)S(1)}, f32[2,128,128]{2,1,0:T(8,128)S(1)}, u32[]{:S(2)}, u32[]{:S(2)}) collective-permute-start(f32[2,128,128]{2,1,0:T(8,128)S(1)} %add.13), channel_id=1, source_target_pairs={{1,0},{0,1},{3,2},{2,3},{5,4},{4,5},{7,6},{6,7},{9,8},{8,9},{11,10... | collective-permute-start | bytes 393224 | tf_op jit(solution)/shard_map/ppermute | solution.py:37
  40.6 14.2 %collective-permute-start.21 = (f32[2,128,128]{2,1,0:T(8,128)S(1)}, f32[2,128,128]{2,1,0:T(8,128)S(1)}, u32[]{:S(2)}, u32[]{:S(2)}) collective-permute-start(f32[2,128,128]{2,1,0:T(8,128)S(1)} %get-tuple-element.70), channel_id=1, source_target_pairs={{1,0},{0,1},{3,2},{2,3},{5,4},{4,5},{7,6},{6,7},{9,8},{8,9},{11,10... | collective-permute-start | bytes 393224 | tf_op jit(solution)/shard_map/ppermute | solution.py:37
  46.3 15.1 %collective-permute-start.13 = (f32[4,128,128]{2,1,0:T(8,128)S(1)}, f32[4,128,128]{2,1,0:T(8,128)S(1)}, u32[]{:S(2)}, u32[]{:S(2)}) collective-permute-start(f32[4,128,128]{2,1,0:T(8,128)S(1)} %get-tuple-element.64), channel_id=1, source_target_pairs={{2,0},{4,2},{6,4},{8,6},{10,8},{12,10},{14,12},{16,14},{18,16},{20... | collective-permute-start | bytes 786440 | tf_op jit(solution)/shard_map/ppermute | solution.py:37
  50.0 12.6 %collective-permute-start.15 = (f32[4,128,128]{2,1,0:T(8,128)S(1)}, f32[4,128,128]{2,1,0:T(8,128)S(1)}, u32[]{:S(2)}, u32[]{:S(2)}) collective-permute-start(f32[4,128,128]{2,1,0:T(8,128)S(1)} %get-tuple-element.67), channel_id=1, source_target_pairs={{2,0},{4,2},{6,4},{8,6},{10,8},{12,10},{14,12},{16,14},{18,16},{20... | collective-permute-start | bytes 786440 | tf_op jit(solution)/shard_map/ppermute | solution.py:37
  51.3 11.3 %collective-permute-start.19 = (f32[4,128,128]{2,1,0:T(8,128)S(1)}, f32[4,128,128]{2,1,0:T(8,128)S(1)}, u32[]{:S(2)}, u32[]{:S(2)}) collective-permute-start(f32[4,128,128]{2,1,0:T(8,128)S(1)} %get-tuple-element.64), channel_id=1, source_target_pairs={{0,31},{1,30}} | collective-permute-start | bytes 786440 | tf_op jit(solution)/shard_map/ppermute | solution.py:31
  54.2 5.0 %collective-permute-start.20 = (f32[2,128,128]{2,1,0:T(8,128)S(1)}, f32[2,128,128]{2,1,0:T(8,128)S(1)}, u32[]{:S(2)}, u32[]{:S(2)}) collective-permute-start(f32[2,128,128]{2,1,0:T(8,128)S(1)} %get-tuple-element.60.quad_ref.quad_one), channel_id=1, source_target_pairs={{1,0},{0,1},{3,2},{2,3},{5,4},{4,5},{7,6},{6,7},{9,8},{8,9},{11,10... | collective-permute-start | bytes 393224 | tf_op jit(solution)/shard_map/ppermute | solution.py:37
  54.8 5.9 %collective-permute-start.16 = (f32[2,128,128]{2,1,0:T(8,128)S(1)}, f32[2,128,128]{2,1,0:T(8,128)S(1)}, u32[]{:S(2)}, u32[]{:S(2)}) collective-permute-start(f32[2,128,128]{2,1,0:T(8,128)S(1)} %get-tuple-element.61.quad_ref.quad_two), channel_id=1, source_target_pairs={{1,0},{0,1},{3,2},{2,3},{5,4},{4,5},{7,6},{6,7},{9,8},{8,9},{11,10... | collective-permute-start | bytes 393224 | tf_op jit(solution)/shard_map/ppermute | solution.py:37
  59.3 3.3 %collective-permute-start.22 = (f32[2,128,128]{2,1,0:T(8,128)S(1)}, f32[2,128,128]{2,1,0:T(8,128)S(1)}, u32[]{:S(2)}, u32[]{:S(2)}) collective-permute-start(f32[2,128,128]{2,1,0:T(8,128)S(1)} %collective-permute-done.20.upper_ref), channel_id=1, source_target_pairs={{2,0},{4,2},{6,4},{8,6},{10,8},{12,10},{14,12},{16,14},{18,16},{20... | collective-permute-start | bytes 393224 | tf_op jit(solution)/shard_map/ppermute | solution.py:24
  60.7 6.3 %collective-permute-start.17 = (f32[2,128,128]{2,1,0:T(8,128)S(1)}, f32[2,128,128]{2,1,0:T(8,128)S(1)}, u32[]{:S(2)}, u32[]{:S(2)}) collective-permute-start(f32[2,128,128]{2,1,0:T(8,128)S(1)} %get-tuple-element.68), channel_id=1, source_target_pairs={{1,0},{0,1},{3,2},{2,3},{5,4},{4,5},{7,6},{6,7},{9,8},{8,9},{11,10... | collective-permute-start | bytes 393224 | tf_op jit(solution)/shard_map/ppermute | solution.py:37
  61.3 5.6 %collective-permute-start.18 = (f32[2,128,128]{2,1,0:T(8,128)S(1)}, f32[2,128,128]{2,1,0:T(8,128)S(1)}, u32[]{:S(2)}, u32[]{:S(2)}) collective-permute-start(f32[2,128,128]{2,1,0:T(8,128)S(1)} %collective-permute-done.16.upper_ref), channel_id=1, source_target_pairs={{2,0},{4,2},{6,4},{8,6},{10,8},{12,10},{14,12},{16,14},{18,16},{20... | collective-permute-start | bytes 393224 | tf_op jit(solution)/shard_map/ppermute | solution.py:24
  69.5 15.4 %collective-permute-start.24 = (f32[2,128,256]{2,1,0:T(8,128)S(1)}, f32[2,128,256]{2,1,0:T(8,128)S(1)}, u32[]{:S(2)}, u32[]{:S(2)}) collective-permute-start(f32[2,128,256]{2,1,0:T(8,128)S(1)} %get-tuple-element.76), channel_id=1, source_target_pairs={{30,0},{0,2},{2,4},{4,6},{6,8},{8,10},{10,12},{12,14},{14,16},{16,... | collective-permute-start | bytes 786440 | tf_op jit(solution)/shard_map/ppermute | solution.py:37
  73.3 5.8 %collective-permute-start.25 = (f32[2,128,128]{2,1,0:T(8,128)S(1)}, f32[2,128,128]{2,1,0:T(8,128)S(1)}, u32[]{:S(2)}, u32[]{:S(2)}) collective-permute-start(f32[2,128,128]{2,1,0:T(8,128)S(1)} %get-tuple-element.78), channel_id=1, source_target_pairs={{0,2},{2,4},{4,6},{6,8},{8,10},{10,12},{12,14},{14,16},{16,18},{18... | collective-permute-start | bytes 393224 | tf_op jit(solution)/shard_map/ppermute | solution.py:24
  75.3 5.2 %collective-permute-start.27 = (f32[2,128,128]{2,1,0:T(8,128)S(1)}, f32[2,128,128]{2,1,0:T(8,128)S(1)}, u32[]{:S(2)}, u32[]{:S(2)}) collective-permute-start(f32[2,128,128]{2,1,0:T(8,128)S(1)} %get-tuple-element.72.other_diag_ref), channel_id=1, source_target_pairs={{0,2},{2,4},{4,6},{6,8},{8,10},{10,12},{12,14},{14,16},{16,18},{18... | collective-permute-start | bytes 393224 | tf_op jit(solution)/shard_map/ppermute | solution.py:24
  78.4 9.2 %collective-permute-start.23 = (f32[2,128,256]{2,1,0:T(8,128)S(1)}, f32[2,128,256]{2,1,0:T(8,128)S(1)}, u32[]{:S(2)}, u32[]{:S(2)}) collective-permute-start(f32[2,128,256]{2,1,0:T(8,128)S(1)} %get-tuple-element.75), channel_id=1, source_target_pairs={{30,0},{0,2},{2,4},{4,6},{6,8},{8,10},{10,12},{12,14},{14,16},{16,... | collective-permute-start | bytes 786440 | tf_op jit(solution)/shard_map/ppermute | solution.py:37
  78.5 6.2 %collective-permute-start.31 = (f32[2,128,128]{2,1,0:T(8,128)S(1)}, f32[2,128,128]{2,1,0:T(8,128)S(1)}, u32[]{:S(2)}, u32[]{:S(2)}) collective-permute-start(f32[2,128,128]{2,1,0:T(8,128)S(1)} %get-tuple-element.82), channel_id=1, source_target_pairs={{1,0},{0,1},{3,2},{2,3},{5,4},{4,5},{7,6},{6,7},{9,8},{8,9},{11,10... | collective-permute-start | bytes 393224 | tf_op jit(solution)/shard_map/ppermute | solution.py:37
  79.1 14.3 %collective-permute-start.29 = (f32[4,128,128]{2,1,0:T(8,128)S(1)}, f32[4,128,128]{2,1,0:T(8,128)S(1)}, u32[]{:S(2)}, u32[]{:S(2)}) collective-permute-start(f32[4,128,128]{2,1,0:T(8,128)S(1)} %get-tuple-element.80), channel_id=1, source_target_pairs={{30,1},{31,0}} | collective-permute-start | bytes 786440 | tf_op jit(solution)/shard_map/ppermute | solution.py:31
  80.4 7.1 %collective-permute-start.30 = (f32[2,128,128]{2,1,0:T(8,128)S(1)}, f32[2,128,128]{2,1,0:T(8,128)S(1)}, u32[]{:S(2)}, u32[]{:S(2)}) collective-permute-start(f32[2,128,128]{2,1,0:T(8,128)S(1)} %get-tuple-element.81), channel_id=1, source_target_pairs={{1,0},{0,1},{3,2},{2,3},{5,4},{4,5},{7,6},{6,7},{9,8},{8,9},{11,10... | collective-permute-start | bytes 393224 | tf_op jit(solution)/shard_map/ppermute | solution.py:37
  84.7 6.4 %collective-permute-start.26 = (f32[2,128,128]{2,1,0:T(8,128)S(1)}, f32[2,128,128]{2,1,0:T(8,128)S(1)}, u32[]{:S(2)}, u32[]{:S(2)}) collective-permute-start(f32[2,128,128]{2,1,0:T(8,128)S(1)} %add.14), channel_id=1, source_target_pairs={{1,0},{0,1},{3,2},{2,3},{5,4},{4,5},{7,6},{6,7},{9,8},{8,9},{11,10... | collective-permute-start | bytes 393224 | tf_op jit(solution)/shard_map/ppermute | solution.py:37
  85.0 8.5 %collective-permute-start.28 = (f32[2,128,128]{2,1,0:T(8,128)S(1)}, f32[2,128,128]{2,1,0:T(8,128)S(1)}, u32[]{:S(2)}, u32[]{:S(2)}) collective-permute-start(f32[2,128,128]{2,1,0:T(8,128)S(1)} %add.15), channel_id=1, source_target_pairs={{1,0},{0,1},{3,2},{2,3},{5,4},{4,5},{7,6},{6,7},{9,8},{8,9},{11,10... | collective-permute-start | bytes 393224 | tf_op jit(solution)/shard_map/ppermute | solution.py:37
  (3 other events, 4.4 us)
where the time goes:
time: 94.6 us; the launch traced here: 94.2 us
  starting transfers between devices  50.4 us (53%)
  waiting for transfers between devices  21.5 us (23%)
  Pallas kernels  20.1 us (21%)
  local copies, waits for them, and re-layouts  1.08 us (1%)
  between operations  0.97 us (1%)
    ppermute x21, starting transfers between devices, from_behind(): return lax.ppermute(block, axis, route)  27 us
    ppermute x21, waiting for transfers between devices, from_behind(): return lax.ppermute(block, axis, route)  18.6 us
    ppermute x7, starting transfers between devices, send_corner(): return lax.ppermute(block, 'row', route)  15.1 us
    pallas_call x8, Pallas kernels, call(): pl.pallas_call(functools.partial(kernel, **static), in_specs=[SMEM] * len...  13.8 us
    ppermute x4, starting transfers between devices, send_wrap(): return lax.ppermute(block, ('row', 'col'), route)  8.34 us
    ppermute x4, waiting for transfers between devices, send_wrap(): return lax.ppermute(block, ('row', 'col'), route)  2.85 us
    pallas_call x2, Pallas kernels, pack(): pl.pallas_call(functools.partial(pack_kernel, boxes=boxes), in_specs=[FAR...  2.19 us
  transfers between devices with their start and end apart: 32, of which 12 were waited for; matrix products, arithmetic and copies ran while one was open for 1% of the time, Pallas kernels for 10%

commit v1 on v0

--- a/solution.py
+++ b/solution.py
@@ -16,19 +16,6 @@
 
 step_size = 0.02
 floor_amp = 0.5
-
-
-def send_corner(block, distance):
-    count = lax.axis_size("row")
-    route = [(i, i + distance) for i in range(count) if 0 <= i + distance < count]
-    return lax.ppermute(block, "row", route)
-
-
-def send_wrap(block, distance):
-    rows, cols = lax.axis_size("row"), lax.axis_size("col")
-    start, end = (rows - 1, 0) if distance > 0 else (0, rows - 1)
-    route = [(start * cols + c, end * cols + (c + distance) % cols) for c in range(cols)]
-    return lax.ppermute(block, ("row", "col"), route)
 
 
 def from_behind(block, axis, distance):
@@ -95,15 +82,11 @@
 
 
 def fill_ext(ext_ref, pieces):
-    for row, col, *sources in pieces:
-        height, across = sources[0].shape[1:]
+    for row, col, source in pieces:
+        height, across = source.shape[1:]
         for c in range(2):
             for b in range(across // LANES):
-                lanes = slice(b * LANES, (b + 1) * LANES)
-                value = sources[0][c, :, lanes]
-                for source in sources[1:]:
-                    value += source[c, :, lanes]
-                ext_ref[c, col // LANES + b, row:row + height, :] = value
+                ext_ref[c, col // LANES + b, row:row + height, :] = source[c, :, b * LANES:(b + 1) * LANES]
 
 
 def place(scalar_ref, j):
@@ -197,21 +180,19 @@
 
 
 def whole_pieces(refs, s, tile_px, width):
-    tile_ref, below_ref, upper_ref, lower_ref, corner_ref, wrapped_ref = refs
+    tile_ref, below_ref, upper_ref, lower_ref, corner_ref = refs
     both = pl.ds(2 * s, 2)
     return [
         (0, 0, tile_ref.at[s]),
         (tile_px, 0, below_ref.at[both]),
         (0, tile_px, upper_ref.at[both]),
         (width, tile_px, lower_ref.at[both]),
-        (tile_px, tile_px, corner_ref.at[both], wrapped_ref.at[both]),
+        (tile_px, tile_px, corner_ref.at[both]),
     ]
 
 
 def slice_pieces(refs, s, tile_px, width):
-    (
-        rest_ref, quad_ref, below_left_ref, below_right_ref, upper_ref, lower_ref, corner_ref, wrapped_ref,
-    ) = refs
+    rest_ref, quad_ref, below_left_ref, below_right_ref, upper_ref, lower_ref, corner_ref = refs
     both = pl.ds(2 * s, 2)
     across = tile_px - width
     return [
@@ -222,7 +203,7 @@
         (tile_px, width, below_right_ref.at[both]),
         (0, tile_px, upper_ref),
         (width, tile_px, lower_ref),
-        (tile_px, tile_px, corner_ref, wrapped_ref.at[both]),
+        (tile_px, tile_px, corner_ref),
     ]
 
 
@@ -254,7 +235,7 @@
 
 
 def wave_kernel(
-    scalar_ref, tile_ref, below_ref, upper_ref, lower_ref, corner_ref, wrapped_ref,
+    scalar_ref, tile_ref, below_ref, upper_ref, lower_ref, corner_ref,
     cos_ref, sin_ref, probe_ref, amp_ref, table_ref,
     own_ref, down_ref, up_out_ref, low_out_ref, diag_ref, back_ref,
     ext_ref, win_ref, moved_ref, *, spots, width,
@@ -262,7 +243,7 @@
     lane = lanes_of(width)
     tile_px = own_ref.shape[1]
     spot_list = [place(scalar_ref, j) for j in range(spots)]
-    halo = (tile_ref, below_ref, upper_ref, lower_ref, corner_ref, wrapped_ref)
+    halo = (tile_ref, below_ref, upper_ref, lower_ref, corner_ref)
     fill_ext(ext_ref, whole_pieces(halo, 0, tile_px, width))
     light(ext_ref, spot_list, probe_ref, back_ref, width, lane)
     fill_ext(ext_ref, whole_pieces(halo, 1, tile_px, width))
@@ -283,12 +264,12 @@
 
 
 def forward_kernel(
-    scalar_ref, rest_ref, quad_ref, left_ref, right_ref, upper_ref, lower_ref, corner_ref, wrapped_ref,
+    scalar_ref, rest_ref, quad_ref, left_ref, right_ref, upper_ref, lower_ref, corner_ref,
     cos_ref, sin_ref, probe_ref, table_ref, moved_ref, ext_ref, enter_ref, *, spots, width,
 ):
     lane = lanes_of(width)
     spot_list = [place(scalar_ref, j) for j in range(spots)]
-    halo = (rest_ref, quad_ref, left_ref, right_ref, upper_ref, lower_ref, corner_ref, wrapped_ref)
+    halo = (rest_ref, quad_ref, left_ref, right_ref, upper_ref, lower_ref, corner_ref)
     fill_ext(ext_ref, slice_pieces(halo, 0, rest_ref.shape[1], width))
     light(ext_ref, spot_list, probe_ref, enter_ref, width, lane)
     interleave([
@@ -298,14 +279,14 @@
 
 
 def residual_kernel(
-    scalar_ref, rest_ref, quad_ref, left_ref, right_ref, upper_ref, lower_ref, corner_ref, wrapped_ref,
+    scalar_ref, rest_ref, quad_ref, left_ref, right_ref, upper_ref, lower_ref, corner_ref,
     moved_ref, amp_ref, table_ref,
     own_ref, down_ref, up_out_ref, low_out_ref, diag_ref, back_ref,
     ext_ref, win_ref, *, spots, width,
 ):
     lane = lanes_of(width)
     spot_list = [place(scalar_ref, j) for j in range(spots)]
-    halo = (rest_ref, quad_ref, left_ref, right_ref, upper_ref, lower_ref, corner_ref, wrapped_ref)
+    halo = (rest_ref, quad_ref, left_ref, right_ref, upper_ref, lower_ref, corner_ref)
     fill_ext(ext_ref, slice_pieces(halo, 1, rest_ref.shape[1], width))
     take_windows(ext_ref, spot_list, win_ref, width, lane)
     ext_ref[...] = jnp.zeros(ext_ref.shape, jnp.float32)
@@ -321,8 +302,8 @@
 
 
 def backward_kernel(
-    scalar_ref, back_ref, other_diag_ref, cos_ref, sin_ref, probe_ref, table_ref,
-    own_ref, down_ref, up_out_ref, low_out_ref, diag_ref, diags_ref, ext_ref, *, spots, width,
+    scalar_ref, back_ref, cos_ref, sin_ref, probe_ref, table_ref,
+    own_ref, down_ref, up_out_ref, low_out_ref, diag_ref, ext_ref, *, spots, width,
 ):
     lane = lanes_of(width)
     total = scalar_ref[2 * spots]
@@ -349,8 +330,6 @@
 
     interleave([chain(group) for group in groups_of(spots)], LAG)
     emit(ext_ref, own_ref, down_ref, up_out_ref, low_out_ref, diag_ref, width)
-    diags_ref[:2] = diag_ref[...]
-    diags_ref[2:] = other_diag_ref[...]
 
 
 def step(value, gradient):
@@ -366,10 +345,9 @@
     yield low, right, step(tile_ref[c, low, right], own_ref[c, low, right])
 
 
-def quad_value(quad_ref, own_ref, above_ref, upper_ref, wrap_ref, c, width):
+def quad_value(quad_ref, own_ref, above_ref, upper_ref, c, width):
     top, left = slice(0, width), slice(0, width)
-    received = above_ref[c, :, left] + upper_ref[c] + wrap_ref[c]
-    return step(quad_ref[c, top, left], own_ref[c, top, left] + received)
+    return step(quad_ref[c, top, left], own_ref[c, top, left] + above_ref[c, :, left] + upper_ref[c])
 
 
 def update_second_kernel(
@@ -396,14 +374,13 @@
 
 
 def update_quad_kernel(
-    tile_ref, own_one, own_two, above_one, above_two, up_one, up_two, wrap_ref,
+    tile_ref, own_one, own_two, above_one, above_two, up_one, up_two,
     quad_one, quad_two, left_ref, *, width,
 ):
     parts = ((own_one, above_one, up_one, quad_one), (own_two, above_two, up_two, quad_two))
     for s, (own_ref, above_ref, up_ref, quad_ref) in enumerate(parts):
         for c in range(2):
-            wrap = wrap_ref.at[pl.ds(2 * s, 2)]
-            value = quad_value(tile_ref.at[s], own_ref, above_ref, up_ref, wrap, c, width)
+            value = quad_value(tile_ref.at[s], own_ref, above_ref, up_ref, c, width)
             quad_ref[c] = value
             left_ref[2 * s + c] = value
 
@@ -420,14 +397,14 @@
 
 
 def finish_quad_kernel(
-    quad_one, quad_two, own_one, own_two, above_one, above_two, up_one, up_two, wrap_ref, part_ref, out_ref,
+    quad_one, quad_two, own_one, own_two, above_one, above_two, up_one, up_two, part_ref, out_ref,
     quads_ref, sem, *, width,
 ):
     del part_ref
     parts = ((quad_one, own_one, above_one, up_one), (quad_two, own_two, above_two, up_two))
     for s, refs in enumerate(parts):
         for c in range(2):
-            quads_ref[s, c] = quad_value(*refs, wrap_ref.at[pl.ds(2 * s, 2)], c, width)
+            quads_ref[s, c] = quad_value(*refs, c, width)
     copy = pltpu.make_async_copy(quads_ref, out_ref.at[:, :, pl.ds(0, width), pl.ds(0, width)], sem)
     copy.start()
     copy.wait()
@@ -463,28 +440,20 @@
     )(*scalars, *arrays)
 
 
-def pack_kernel(whole_ref, *refs, boxes):
-    outs, sems = refs[:-1], refs[-1]
+def pack_kernel(whole_ref, up_ref, low_ref, top_ref, sems, *, width):
+    tile_px = whole_ref.shape[2]
+    left = pl.ds(0, width)
     copies = []
-    for (rows, lanes), out_ref in zip(boxes, outs):
-        for s in range(2):
-            source = whole_ref.at[s, :, pl.ds(*rows), pl.ds(*lanes)]
-            copies.append(pltpu.make_async_copy(source, out_ref.at[pl.ds(2 * s, 2)], sems.at[len(copies)]))
+    for s in range(2):
+        both = pl.ds(2 * s, 2)
+        copies.append((whole_ref.at[s, :, pl.ds(0, width), left], up_ref.at[both]))
+        copies.append((whole_ref.at[s, :, pl.ds(width, tile_px - width), left], low_ref.at[both]))
+        copies.append((whole_ref.at[s, :, pl.ds(0, width), :], top_ref.at[both]))
+    copies = [pltpu.make_async_copy(a, b, sems.at[k]) for k, (a, b) in enumerate(copies)]
     for copy in copies:
         copy.start()
     for copy in copies:
         copy.wait()
-
-
-def pack(whole, boxes):
-    return pl.pallas_call(
-        functools.partial(pack_kernel, boxes=boxes),
-        in_specs=[FAR],
-        out_specs=[VMEM] * len(boxes),
-        out_shape=[F32((4, rows[1], lanes[1])) for rows, lanes in boxes],
-        scratch_shapes=[pltpu.SemaphoreType.DMA((2 * len(boxes),))],
-        compiler_params=LIMIT,
-    )(in_hbm(whole))
 
 
 def in_hbm(array):
@@ -517,12 +486,18 @@
     strip = F32((2, width, tile_px))
     gradient = [whole, strip, square, square, square]
 
-    (left_up,) = pack(specimen_slices, [((0, width), (0, width))])
+    left_up, left_low, top = pl.pallas_call(
+        functools.partial(pack_kernel, width=width),
+        in_specs=[FAR],
+        out_specs=[VMEM] * 3,
+        out_shape=[squares, squares, F32((4, width, tile_px))],
+        scratch_shapes=[pltpu.SemaphoreType.DMA((6,))],
+        compiler_params=LIMIT,
+        name="pack",
+    )(in_hbm(specimen_slices))
     upper = from_behind(left_up, "col", -1)
-    left_low, top = pack(specimen_slices, [((width, across), (0, width)), ((0, width), (0, tile_px))])
     lower = from_behind(left_low, "col", -1)
     below = from_behind(top, "row", -1)
-    wrapped = send_wrap(left_up, -1)
     far = (specimen_slices, illumination_probe, amplitudes[0, 0], jnp.asarray(dft_operands(width)))
     tile, probe, measured, table = pl.pallas_call(
         stage_kernel,
@@ -533,12 +508,12 @@
         compiler_params=LIMIT,
         name="stage",
     )(*[in_hbm(x) for x in far])
-    corner = send_corner(upper, -1)
+    corner = from_behind(upper, "row", -1)
     for i in range(ITERS):
         if i == 0:
             own_two, down_two, up_two, low_two, diag_two, back = call(
                 wave_kernel, scalars,
-                (tile, below, upper, lower, corner, wrapped, cos, sin, probe, measured, table),
+                (tile, below, upper, lower, corner, cos, sin, probe, measured, table),
                 [*gradient, wave], [ext_space, wave_space, wave_space], **static,
             )
         else:
@@ -551,20 +526,19 @@
                 [*gradient, wave], [ext_space, wave_space], **static,
             )
         low_two = from_behind(low_two, "col", 1)
-        corner_two = send_corner(diag_two, 1)
+        corner_two = from_behind(diag_two, "row", 1)
         above_two = from_behind(down_two, "row", 1)
-        own_one, down_one, up_one, low_one, diag_one, diags = call(
-            backward_kernel, scalars, (back, diag_two, cos, sin, probe, table),
-            [*gradient, squares], [ext_space], **static,
+        own_one, down_one, up_one, low_one, diag_one = call(
+            backward_kernel, scalars, (back, cos, sin, probe, table),
+            gradient, [ext_space], **static,
         )
         low_one = from_behind(low_one, "col", 1)
-        corner_one = send_corner(diag_one, 1)
+        corner_one = from_behind(diag_one, "row", 1)
         above_one = from_behind(down_one, "row", 1)
         up_two = up_two + corner_two
         up_one = up_one + corner_one
         up_two = from_behind(up_two, "col", 1)
         up_one = from_behind(up_one, "col", 1)
-        from_wrap = send_wrap(diags, 1)
         if i + 1 < ITERS:
             rest_two, left_two, right = call(
                 update_second_kernel, (), (tile, own_two, above_two, low_two),
@@ -578,19 +552,18 @@
             below_right = from_behind(right, "row", -1)
             quad_one, quad_two, left = call(
                 update_quad_kernel, (),
-                (tile, own_one, own_two, above_one, above_two, up_one, up_two, from_wrap),
+                (tile, own_one, own_two, above_one, above_two, up_one, up_two),
                 [square, square, squares], [], width=width,
             )
             upper_one = from_behind(quad_one, "col", -1)
             upper_two = from_behind(quad_two, "col", -1)
             below_left = from_behind(left, "row", -1)
             lower_two = from_behind(left_two, "col", -1)
-            wrapped = send_wrap(left, -1)
-            corner_one = send_corner(upper_one, -1)
-            corner_two = send_corner(upper_two, -1)
+            corner_one = from_behind(upper_one, "row", -1)
+            corner_two = from_behind(upper_two, "row", -1)
             halo = (
-                (rest_one, quad_one, below_left, below_right, upper_one, lower_one, corner_one, wrapped),
-                (rest_two, quad_two, below_left, below_right, upper_two, lower_two, corner_two, wrapped),
+                (rest_one, quad_one, below_left, below_right, upper_one, lower_one, corner_one),
+                (rest_two, quad_two, below_left, below_right, upper_two, lower_two, corner_two),
             )
         else:
             part = []
@@ -611,16 +584,16 @@
                 )(*operands, *map(in_hbm, part))]
             updated = pl.pallas_call(
                 functools.partial(finish_quad_kernel, width=width),
-                in_specs=[VMEM] * 9 + [FAR],
+                in_specs=[VMEM] * 8 + [FAR],
                 out_specs=FAR,
                 out_shape=F32(specimen_slices.shape),
-                input_output_aliases={9: 0},
+                input_output_aliases={8: 0},
                 scratch_shapes=[
                     pltpu.VMEM((2, 2, width, width), jnp.float32), pltpu.SemaphoreType.DMA(()),
                 ],
                 compiler_params=LIMIT,
                 name="finish_quad",
-            )(quad_one, quad_two, own_one, own_two, above_one, above_two, up_one, up_two, from_wrap, in_hbm(part[0]))
+            )(quad_one, quad_two, own_one, own_two, above_one, above_two, up_one, up_two, in_hbm(part[0]))
     return updated
 
 

time: 94.6 us -> 80.2 us (0.85)
  starting transfers between devices: 50.4 us -> 32.5 us
  waiting for transfers between devices: 21.5 us -> 26.3 us
  Pallas kernels: 20.1 us -> 19.1 us
    ppermute x11 -> x0, starting transfers between devices: 23.4 us -> none  [the longest x7 15.1 us: send_corner(): return lax.ppermute(block, 'row', route)]
    ppermute x21 -> x28, waiting for transfers between devices: 18.6 us -> 26.3 us  [from_behind(): return lax.ppermute(block, axis, route)]
    ppermute x21 -> x28, starting transfers between devices: 27 us -> 32.5 us  [from_behind(): return lax.ppermute(block, axis, route)]
    ppermute x11 -> x0, waiting for transfers between devices: 2.87 us -> none  [the longest x4 2.85 us: send_wrap(): return lax.ppermute(block, ('row', 'col'), route)]
    pallas_call x2 -> x1, Pallas kernels: 2.19 us -> 1.3 us  [body(): pl.pallas_call(functools.partial(pack_kernel, width=width), in_specs=[FAR...]
  transfers between devices with their start and end apart: 32 -> 28, of which waited for: 12 -> 13; matrix products, arithmetic and copies ran while one was open for 1% -> 1% of each run, Pallas kernels for 10% -> 10%
where the time goes in v1:
time: 80.2 us; the launch traced here: 80.1 us
  starting transfers between devices  32.5 us (41%)
  waiting for transfers between devices  26.3 us (33%)
  Pallas kernels  19.1 us (24%)
  local copies, waits for them, and re-layouts  1.08 us (1%)
  between operations  0.87 us (1%)
    ppermute x28, starting transfers between devices, from_behind(): return lax.ppermute(block, axis, route)  32.5 us
    ppermute x28, waiting for transfers between devices, from_behind(): return lax.ppermute(block, axis, route)  26.3 us
    pallas_call x8, Pallas kernels, call(): pl.pallas_call(functools.partial(kernel, **static), in_specs=[SMEM] * len...  13.8 us
    pallas_call x2, Pallas kernels, body(): pl.pallas_call(functools.partial(finish_rest_kernel, width=width, part=sl...  1.74 us
  transfers between devices with their start and end apart: 28, of which 13 were waited for; matrix products, arithmetic and copies ran while one was open for 1% of the time, Pallas kernels for 10%

profile of v1, /device:TPU:0, one launch (start us, length us, event | category | flops | bytes accessed | tf_op | source)
XLA Modules:
  0.0 80.1 jit_solution(7493555747568638427)
XLA Ops:
  0.0 1.3 %pack.1 = (f32[4,128,128]{2,1,0:T(8,128)S(1)}, f32[4,128,128]{2,1,0:T(8,128)S(1)}, f32[4,128,256]{2,1,0:T(8,128)S(1)}) custom-call(f32[2,2,256,256]{3,2,1,0:T(8,128)} %whole_ref.1), custom_call_target="tpu_custom_call" | custom-call | tf_op jit(solution)/shard_map/pack/pallas_call | solution.py:489
  1.3 3.0 %collective-permute-start.1 = (f32[4,128,128]{2,1,0:T(8,128)S(1)}, f32[4,128,128]{2,1,0:T(8,128)S(1)}, u32[]{:S(2)}, u32[]{:S(2)}) collective-permute-start(f32[4,128,128]{2,1,0:T(8,128)S(1)} %get-tuple-element.45), channel_id=1, source_target_pairs={{1,0},{0,1},{3,2},{2,3},{5,4},{4,5},{7,6},{6,7},{9,8},{8,9},{11,10... | collective-permute-start | bytes 786440 | tf_op jit(solution)/shard_map/ppermute | solution.py:24
  4.3 3.7 %collective-permute-start = (f32[4,128,256]{2,1,0:T(8,128)S(1)}, f32[4,128,256]{2,1,0:T(8,128)S(1)}, u32[]{:S(2)}, u32[]{:S(2)}) collective-permute-start(f32[4,128,256]{2,1,0:T(8,128)S(1)} %get-tuple-element.44), channel_id=1, source_target_pairs={{2,0},{4,2},{6,4},{8,6},{10,8},{12,10},{14,12},{16,14},{18,16},{20... | collective-permute-start | bytes 1572872 | tf_op jit(solution)/shard_map/ppermute | solution.py:24
  9.4 2.1 %collective-permute-done.1.upper_ref = f32[4,128,128]{2,1,0:T(8,128)S(1)} collective-permute-done((f32[4,128,128]{2,1,0:T(8,128)S(1)}, f32[4,128,128]{2,1,0:T(8,128)S(1)}, u32[]{:S(2)}, u32[]{:S(2)}) %collective-permute-start.1) | collective-permute-done | bytes 262176 | tf_op jit(solution)/shard_map/ppermute | solution.py:24
  11.5 2.5 %collective-permute-start.3 = (f32[4,128,128]{2,1,0:T(8,128)S(1)}, f32[4,128,128]{2,1,0:T(8,128)S(1)}, u32[]{:S(2)}, u32[]{:S(2)}) collective-permute-start(f32[4,128,128]{2,1,0:T(8,128)S(1)} %collective-permute-done.1.upper_ref), channel_id=1, source_target_pairs={{2,0},{4,2},{6,4},{8,6},{10,8},{12,10},{14,12},{16,14},{18,16},{20... | collective-permute-start | bytes 786440 | tf_op jit(solution)/shard_map/ppermute | solution.py:24
  14.8 1.5 %stage.1 = (f32[2,2,256,256]{3,2,1,0:T(8,128)S(1)}, f32[2,128,128]{2,1,0:T(8,128)S(1)}, f32[4,128,128]{2,1,0:T(8,128)S(1)}, bf16[4,256,256]{2,1,0:T(8,128)(2,1)S(1)}) custom-call(f32[2,2,256,256]{3,2,1,0:T(8,128)} %whole_ref.1, f32[2,128,128]{2,1,0:T(8,128)} %refs_1_.1, f32[4,128,128]{2,1,0:T(8,128)} %bitcast.4, bf16[4,256,256]{2,1,0:T(8,128)(2,1)} %constant.2.clone.refs_3_), custom_call_target="tpu_custom_call" | custom-call | tf_op jit(solution)/shard_map/stage/pallas_call | solution.py:502
  16.6 1.3 %collective-permute-done.3.corner_ref = f32[4,128,128]{2,1,0:T(8,128)S(1)} collective-permute-done((f32[4,128,128]{2,1,0:T(8,128)S(1)}, f32[4,128,128]{2,1,0:T(8,128)S(1)}, u32[]{:S(2)}, u32[]{:S(2)}) %collective-permute-start.3) | collective-permute-done | bytes 262176 | tf_op jit(solution)/shard_map/ppermute | solution.py:24
  17.9 3.9 %shard_map.82 = (f32[2,256,256]{2,1,0:T(8,128)S(1)}, f32[2,128,256]{2,1,0:T(8,128)S(1)}, f32[2,128,128]{2,1,0:T(8,128)S(1)}, f32[2,128,128]{2,1,0:T(8,128)S(1)},...) custom-call(s32[13]{0:T(128)S(1)} %pad_add_fusion.scalar_ref, ...), custom_call_target="tpu_custom_call" | custom-call | tf_op jit(solution)/shard_map/pallas_call | solution.py:433
  22.2 2.4 %shard_map.83 = (f32[2,256,256]{2,1,0:T(8,128)S(1)}, f32[2,128,256]{2,1,0:T(8,128)S(1)}, f32[2,128,128]{2,1,0:T(8,128)S(1)}, f32[2,128,128]{2,1,0:T(8,128)S(1)}, f32[2,128,128]{2,1,0:T(8,128)S(1)}) custom-call(s32[13]{0:T(128)S(1)} %pad_add_fusion.scalar_ref, f32[4,2,128,128]{3,2,1,0:T(8,128)S(1)} %get-tuple-element.50.back_ref, ...), custom_call_target="tpu_custom_call" | custom-call | tf_op jit(solution)/shard_map/pallas_call | solution.py:433
  24.6 1.2 %collective-permute-start.4 = (f32[2,128,256]{2,1,0:T(8,128)S(1)}, f32[2,128,256]{2,1,0:T(8,128)S(1)}, u32[]{:S(2)}, u32[]{:S(2)}) collective-permute-start(f32[2,128,256]{2,1,0:T(8,128)S(1)} %get-tuple-element.53), channel_id=1, source_target_pairs={{30,0},{0,2},{2,4},{4,6},{6,8},{8,10},{10,12},{12,14},{14,16},{16,... | collective-permute-start | bytes 786440 | tf_op jit(solution)/shard_map/ppermute | solution.py:24
  26.2 1.5 %collective-permute-start.10 = (f32[2,128,128]{2,1,0:T(8,128)S(1)}, f32[2,128,128]{2,1,0:T(8,128)S(1)}, u32[]{:S(2)}, u32[]{:S(2)}) collective-permute-start(f32[2,128,128]{2,1,0:T(8,128)S(1)} %get-tuple-element.61), channel_id=1, source_target_pairs={{1,0},{0,1},{3,2},{2,3},{5,4},{4,5},{7,6},{6,7},{9,8},{8,9},{11,10... | collective-permute-start | bytes 393224 | tf_op jit(solution)/shard_map/ppermute | solution.py:24
  27.7 1.4 %collective-permute-done.8 = f32[2,128,128]{2,1,0:T(8,128)S(1)} collective-permute-done((f32[2,128,128]{2,1,0:T(8,128)S(1)}, f32[2,128,128]{2,1,0:T(8,128)S(1)}, u32[]{:S(2)}, u32[]{:S(2)}) %collective-permute-start.8) | collective-permute-done | bytes 131104 | tf_op jit(solution)/shard_map/ppermute | solution.py:24
  29.2 1.5 %collective-permute-start.12 = (f32[2,128,128]{2,1,0:T(8,128)S(1)}, f32[2,128,128]{2,1,0:T(8,128)S(1)}, u32[]{:S(2)}, u32[]{:S(2)}) collective-permute-start(f32[2,128,128]{2,1,0:T(8,128)S(1)} %get-tuple-element.64), channel_id=1, source_target_pairs={{1,0},{0,1},{3,2},{2,3},{5,4},{4,5},{7,6},{6,7},{9,8},{8,9},{11,10... | collective-permute-start | bytes 393224 | tf_op jit(solution)/shard_map/ppermute | solution.py:24
  30.7 5.5 %collective-permute-done.6 = f32[2,128,128]{2,1,0:T(8,128)S(1)} collective-permute-done((f32[2,128,128]{2,1,0:T(8,128)S(1)}, f32[2,128,128]{2,1,0:T(8,128)S(1)}, u32[]{:S(2)}, u32[]{:S(2)}) %collective-permute-start.6) | collective-permute-done | bytes 131104 | tf_op jit(solution)/shard_map/ppermute | solution.py:24
  36.2 1.5 %collective-permute-start.9 = (f32[2,128,128]{2,1,0:T(8,128)S(1)}, f32[2,128,128]{2,1,0:T(8,128)S(1)}, u32[]{:S(2)}, u32[]{:S(2)}) collective-permute-start(f32[2,128,128]{2,1,0:T(8,128)S(1)} %add.13), channel_id=1, source_target_pairs={{1,0},{0,1},{3,2},{2,3},{5,4},{4,5},{7,6},{6,7},{9,8},{8,9},{11,10... | collective-permute-start | bytes 393224 | tf_op jit(solution)/shard_map/ppermute | solution.py:24
  38.5 1.6 %collective-permute-start.18 = (f32[2,128,128]{2,1,0:T(8,128)S(1)}, f32[2,128,128]{2,1,0:T(8,128)S(1)}, u32[]{:S(2)}, u32[]{:S(2)}) collective-permute-start(f32[2,128,128]{2,1,0:T(8,128)S(1)} %get-tuple-element.69), channel_id=1, source_target_pairs={{1,0},{0,1},{3,2},{2,3},{5,4},{4,5},{7,6},{6,7},{9,8},{8,9},{11,10... | collective-permute-start | bytes 393224 | tf_op jit(solution)/shard_map/ppermute | solution.py:24
  40.1 1.5 %collective-permute-done.9.up_two = f32[2,128,128]{2,1,0:T(8,128)S(1)} collective-permute-done((f32[2,128,128]{2,1,0:T(8,128)S(1)}, f32[2,128,128]{2,1,0:T(8,128)S(1)}, u32[]{:S(2)}, u32[]{:S(2)}) %collective-permute-start.9) | collective-permute-done | bytes 131104 | tf_op jit(solution)/shard_map/ppermute | solution.py:24
  41.6 2.4 %collective-permute-done.7.up_one = f32[2,128,128]{2,1,0:T(8,128)S(1)} collective-permute-done((f32[2,128,128]{2,1,0:T(8,128)S(1)}, f32[2,128,128]{2,1,0:T(8,128)S(1)}, u32[]{:S(2)}, u32[]{:S(2)}) %collective-permute-start.7) | collective-permute-done | bytes 131104 | tf_op jit(solution)/shard_map/ppermute | solution.py:24
  44.1 1.6 %collective-permute-start.17 = (f32[2,128,128]{2,1,0:T(8,128)S(1)}, f32[2,128,128]{2,1,0:T(8,128)S(1)}, u32[]{:S(2)}, u32[]{:S(2)}) collective-permute-start(f32[2,128,128]{2,1,0:T(8,128)S(1)} %get-tuple-element.59.quad_ref.quad_one), channel_id=1, source_target_pairs={{1,0},{0,1},{3,2},{2,3},{5,4},{4,5},{7,6},{6,7},{9,8},{8,9},{11,10... | collective-permute-start | bytes 393224 | tf_op jit(solution)/shard_map/ppermute | solution.py:24
  45.6 2.2 %collective-permute-start.11 = (f32[4,128,128]{2,1,0:T(8,128)S(1)}, f32[4,128,128]{2,1,0:T(8,128)S(1)}, u32[]{:S(2)}, u32[]{:S(2)}) collective-permute-start(f32[4,128,128]{2,1,0:T(8,128)S(1)} %get-tuple-element.63), channel_id=1, source_target_pairs={{2,0},{4,2},{6,4},{8,6},{10,8},{12,10},{14,12},{16,14},{18,16},{20... | collective-permute-start | bytes 786440 | tf_op jit(solution)/shard_map/ppermute | solution.py:24
  48.4 1.1 %collective-permute-done.17.upper_ref = f32[2,128,128]{2,1,0:T(8,128)S(1)} collective-permute-done((f32[2,128,128]{2,1,0:T(8,128)S(1)}, f32[2,128,128]{2,1,0:T(8,128)S(1)}, u32[]{:S(2)}, u32[]{:S(2)}) %collective-permute-start.17) | collective-permute-done | bytes 131104 | tf_op jit(solution)/shard_map/ppermute | solution.py:24
  49.5 2.5 %collective-permute-start.15 = (f32[2,128,128]{2,1,0:T(8,128)S(1)}, f32[2,128,128]{2,1,0:T(8,128)S(1)}, u32[]{:S(2)}, u32[]{:S(2)}) collective-permute-start(f32[2,128,128]{2,1,0:T(8,128)S(1)} %get-tuple-element.67), channel_id=1, source_target_pairs={{1,0},{0,1},{3,2},{2,3},{5,4},{4,5},{7,6},{6,7},{9,8},{8,9},{11,10... | collective-permute-start | bytes 393224 | tf_op jit(solution)/shard_map/ppermute | solution.py:24
  52.8 1.1 %collective-permute-start.16 = (f32[2,128,128]{2,1,0:T(8,128)S(1)}, f32[2,128,128]{2,1,0:T(8,128)S(1)}, u32[]{:S(2)}, u32[]{:S(2)}) collective-permute-start(f32[2,128,128]{2,1,0:T(8,128)S(1)} %collective-permute-done.14.upper_ref), channel_id=1, source_target_pairs={{2,0},{4,2},{6,4},{8,6},{10,8},{12,10},{14,12},{16,14},{18,16},{20... | collective-permute-start | bytes 393224 | tf_op jit(solution)/shard_map/ppermute | solution.py:24
  53.9 2.2 %shard_map.87.moved_ref = f32[4,2,128,128]{3,2,1,0:T(8,128)S(1)} custom-call(s32[13]{0:T(128)S(1)} %pad_add_fusion.scalar_ref, f32[2,256,256]{2,1,0:T(8,128)S(1)} %get-tuple-element.68.rest_ref, f32[2,128,128]{2,1,0:T(8,128)S(1)} %get-tuple-element.59.quad_ref.quad_one, f32[4,128,128]{2,1,0:T(8,128)S(1)} %collective-permute-done.11.left_ref, ...), custom_call_target="tpu_custom_call" | custom-call | tf_op jit(solution)/shard_map/pallas_call | solution.py:433
  56.4 2.6 %shard_map.88 = (f32[2,256,256]{2,1,0:T(8,128)S(1)}, f32[2,128,256]{2,1,0:T(8,128)S(1)}, f32[2,128,128]{2,1,0:T(8,128)S(1)}, f32[2,128,128]{2,1,0:T(8,128)S(1)},...) custom-call(s32[13]{0:T(128)S(1)} %pad_add_fusion.scalar_ref, f32[2,256,256]{2,1,0:T(8,128)S(1)} %get-tuple-element.62.rest_ref, ...), custom_call_target="tpu_custom_call" | custom-call | tf_op jit(solution)/shard_map/pallas_call | solution.py:433
  59.0 2.4 %shard_map.89 = (f32[2,256,256]{2,1,0:T(8,128)S(1)}, f32[2,128,256]{2,1,0:T(8,128)S(1)}, f32[2,128,128]{2,1,0:T(8,128)S(1)}, f32[2,128,128]{2,1,0:T(8,128)S(1)}, f32[2,128,128]{2,1,0:T(8,128)S(1)}) custom-call(s32[13]{0:T(128)S(1)} %pad_add_fusion.scalar_ref, f32[4,2,128,128]{3,2,1,0:T(8,128)S(1)} %get-tuple-element.70.back_ref, ...), custom_call_target="tpu_custom_call" | custom-call | tf_op jit(solution)/shard_map/pallas_call | solution.py:433
  62.6 1.6 %collective-permute-start.27 = (f32[2,128,128]{2,1,0:T(8,128)S(1)}, f32[2,128,128]{2,1,0:T(8,128)S(1)}, u32[]{:S(2)}, u32[]{:S(2)}) collective-permute-start(f32[2,128,128]{2,1,0:T(8,128)S(1)} %get-tuple-element.80), channel_id=1, source_target_pairs={{1,0},{0,1},{3,2},{2,3},{5,4},{4,5},{7,6},{6,7},{9,8},{8,9},{11,10... | collective-permute-start | bytes 393224 | tf_op jit(solution)/shard_map/ppermute | solution.py:24
  64.2 4.5 %collective-permute-done.22 = f32[2,128,128]{2,1,0:T(8,128)S(1)} collective-permute-done((f32[2,128,128]{2,1,0:T(8,128)S(1)}, f32[2,128,128]{2,1,0:T(8,128)S(1)}, u32[]{:S(2)}, u32[]{:S(2)}) %collective-permute-start.22) | collective-permute-done | bytes 131104 | tf_op jit(solution)/shard_map/ppermute | solution.py:24
  68.7 1.3 %collective-permute-start.26 = (f32[2,128,128]{2,1,0:T(8,128)S(1)}, f32[2,128,128]{2,1,0:T(8,128)S(1)}, u32[]{:S(2)}, u32[]{:S(2)}) collective-permute-start(f32[2,128,128]{2,1,0:T(8,128)S(1)} %get-tuple-element.79), channel_id=1, source_target_pairs={{1,0},{0,1},{3,2},{2,3},{5,4},{4,5},{7,6},{6,7},{9,8},{8,9},{11,10... | collective-permute-start | bytes 393224 | tf_op jit(solution)/shard_map/ppermute | solution.py:24
  70.0 2.9 %collective-permute-done.24 = f32[2,128,128]{2,1,0:T(8,128)S(1)} collective-permute-done((f32[2,128,128]{2,1,0:T(8,128)S(1)}, f32[2,128,128]{2,1,0:T(8,128)S(1)}, u32[]{:S(2)}, u32[]{:S(2)}) %collective-permute-start.24) | collective-permute-done | bytes 131104 | tf_op jit(solution)/shard_map/ppermute | solution.py:24
  72.9 1.3 %collective-permute-start.23 = (f32[2,128,128]{2,1,0:T(8,128)S(1)}, f32[2,128,128]{2,1,0:T(8,128)S(1)}, u32[]{:S(2)}, u32[]{:S(2)}) collective-permute-start(f32[2,128,128]{2,1,0:T(8,128)S(1)} %add.14), channel_id=1, source_target_pairs={{1,0},{0,1},{3,2},{2,3},{5,4},{4,5},{7,6},{6,7},{9,8},{8,9},{11,10... | collective-permute-start | bytes 393224 | tf_op jit(solution)/shard_map/ppermute | solution.py:24
  77.9 1.4 %collective-permute-done.25.up_two = f32[2,128,128]{2,1,0:T(8,128)S(1)} collective-permute-done((f32[2,128,128]{2,1,0:T(8,128)S(1)}, f32[2,128,128]{2,1,0:T(8,128)S(1)}, u32[]{:S(2)}, u32[]{:S(2)}) %collective-permute-start.25) | collective-permute-done | bytes 131104 | tf_op jit(solution)/shard_map/ppermute | solution.py:24
  (51 shorter events, 10.5 us)
Async XLA Ops:
  1.3 10.2 %collective-permute-start.1 = (f32[4,128,128]{2,1,0:T(8,128)S(1)}, f32[4,128,128]{2,1,0:T(8,128)S(1)}, u32[]{:S(2)}, u32[]{:S(2)}) collective-permute-start(f32[4,128,128]{2,1,0:T(8,128)S(1)} %get-tuple-element.45), channel_id=1, source_target_pairs={{1,0},{0,1},{3,2},{2,3},{5,4},{4,5},{7,6},{6,7},{9,8},{8,9},{11,10... | collective-permute-start | bytes 786440 | tf_op jit(solution)/shard_map/ppermute | solution.py:24
  4.3 13.6 %collective-permute-start = (f32[4,128,256]{2,1,0:T(8,128)S(1)}, f32[4,128,256]{2,1,0:T(8,128)S(1)}, u32[]{:S(2)}, u32[]{:S(2)}) collective-permute-start(f32[4,128,256]{2,1,0:T(8,128)S(1)} %get-tuple-element.44), channel_id=1, source_target_pairs={{2,0},{4,2},{6,4},{8,6},{10,8},{12,10},{14,12},{16,14},{18,16},{20... | collective-permute-start | bytes 1572872 | tf_op jit(solution)/shard_map/ppermute | solution.py:24
  8.1 1.2 %copy-start.1 = (s32[1,1,4,2]{2,3,1,0:T(2,128)S(1)}, s32[1,1,4,2]{2,3,1,0:T(2,128)}, u32[]{:S(2)}) copy-start(s32[1,1,4,2]{2,3,1,0:T(2,128)} %param.12) | copy-start | bytes 100
  8.1 8.5 %collective-permute-start.2 = (f32[4,128,128]{2,1,0:T(8,128)S(1)}, f32[4,128,128]{2,1,0:T(8,128)S(1)}, u32[]{:S(2)}, u32[]{:S(2)}) collective-permute-start(f32[4,128,128]{2,1,0:T(8,128)S(1)} %get-tuple-element.46), channel_id=1, source_target_pairs={{1,0},{0,1},{3,2},{2,3},{5,4},{4,5},{7,6},{6,7},{9,8},{8,9},{11,10... | collective-permute-start | bytes 786440 | tf_op jit(solution)/shard_map/ppermute | solution.py:24
  11.5 6.4 %collective-permute-start.3 = (f32[4,128,128]{2,1,0:T(8,128)S(1)}, f32[4,128,128]{2,1,0:T(8,128)S(1)}, u32[]{:S(2)}, u32[]{:S(2)}) collective-permute-start(f32[4,128,128]{2,1,0:T(8,128)S(1)} %collective-permute-done.1.upper_ref), channel_id=1, source_target_pairs={{2,0},{4,2},{6,4},{8,6},{10,8},{12,10},{14,12},{16,14},{18,16},{20... | collective-permute-start | bytes 786440 | tf_op jit(solution)/shard_map/ppermute | solution.py:24
  14.0 0.7 copy-start.2
  14.8 1.6 %copy-start = (f32[128,128]{1,0:T(8,128)S(1)}, f32[128,128]{1,0:T(8,128)}, u32[]{:S(2)}) copy-start(f32[128,128]{1,0:T(8,128)} %param.10) | copy-start | bytes 196612
  21.9 7.3 %collective-permute-start.8 = (f32[2,128,128]{2,1,0:T(8,128)S(1)}, f32[2,128,128]{2,1,0:T(8,128)S(1)}, u32[]{:S(2)}, u32[]{:S(2)}) collective-permute-start(f32[2,128,128]{2,1,0:T(8,128)S(1)} %get-tuple-element.58), channel_id=1, source_target_pairs={{30,0},{0,2},{2,4},{4,6},{6,8},{8,10},{10,12},{12,14},{14,16},{16,... | collective-permute-start | bytes 393224 | tf_op jit(solution)/shard_map/ppermute | solution.py:24
  21.9 16.4 %collective-permute-start.5 = (f32[2,128,256]{2,1,0:T(8,128)S(1)}, f32[2,128,256]{2,1,0:T(8,128)S(1)}, u32[]{:S(2)}, u32[]{:S(2)}) collective-permute-start(f32[2,128,256]{2,1,0:T(8,128)S(1)} %get-tuple-element.54), channel_id=1, source_target_pairs={{30,0},{0,2},{2,4},{4,6},{6,8},{8,10},{10,12},{12,14},{14,16},{16,... | collective-permute-start | bytes 786440 | tf_op jit(solution)/shard_map/ppermute | solution.py:24
  24.6 13.8 %collective-permute-start.4 = (f32[2,128,256]{2,1,0:T(8,128)S(1)}, f32[2,128,256]{2,1,0:T(8,128)S(1)}, u32[]{:S(2)}, u32[]{:S(2)}) collective-permute-start(f32[2,128,256]{2,1,0:T(8,128)S(1)} %get-tuple-element.53), channel_id=1, source_target_pairs={{30,0},{0,2},{2,4},{4,6},{6,8},{8,10},{10,12},{12,14},{14,16},{16,... | collective-permute-start | bytes 786440 | tf_op jit(solution)/shard_map/ppermute | solution.py:24
  25.8 10.4 %collective-permute-start.6 = (f32[2,128,128]{2,1,0:T(8,128)S(1)}, f32[2,128,128]{2,1,0:T(8,128)S(1)}, u32[]{:S(2)}, u32[]{:S(2)}) collective-permute-start(f32[2,128,128]{2,1,0:T(8,128)S(1)} %get-tuple-element.56), channel_id=1, source_target_pairs={{30,0},{0,2},{2,4},{4,6},{6,8},{8,10},{10,12},{12,14},{14,16},{16,... | collective-permute-start | bytes 393224 | tf_op jit(solution)/shard_map/ppermute | solution.py:24
  26.2 11.5 %collective-permute-start.10 = (f32[2,128,128]{2,1,0:T(8,128)S(1)}, f32[2,128,128]{2,1,0:T(8,128)S(1)}, u32[]{:S(2)}, u32[]{:S(2)}) collective-permute-start(f32[2,128,128]{2,1,0:T(8,128)S(1)} %get-tuple-element.61), channel_id=1, source_target_pairs={{1,0},{0,1},{3,2},{2,3},{5,4},{4,5},{7,6},{6,7},{9,8},{8,9},{11,10... | collective-permute-start | bytes 393224 | tf_op jit(solution)/shard_map/ppermute | solution.py:24
  29.2 9.2 %collective-permute-start.12 = (f32[2,128,128]{2,1,0:T(8,128)S(1)}, f32[2,128,128]{2,1,0:T(8,128)S(1)}, u32[]{:S(2)}, u32[]{:S(2)}) collective-permute-start(f32[2,128,128]{2,1,0:T(8,128)S(1)} %get-tuple-element.64), channel_id=1, source_target_pairs={{1,0},{0,1},{3,2},{2,3},{5,4},{4,5},{7,6},{6,7},{9,8},{8,9},{11,10... | collective-permute-start | bytes 393224 | tf_op jit(solution)/shard_map/ppermute | solution.py:24
  36.2 5.4 %collective-permute-start.9 = (f32[2,128,128]{2,1,0:T(8,128)S(1)}, f32[2,128,128]{2,1,0:T(8,128)S(1)}, u32[]{:S(2)}, u32[]{:S(2)}) collective-permute-start(f32[2,128,128]{2,1,0:T(8,128)S(1)} %add.13), channel_id=1, source_target_pairs={{1,0},{0,1},{3,2},{2,3},{5,4},{4,5},{7,6},{6,7},{9,8},{8,9},{11,10... | collective-permute-start | bytes 393224 | tf_op jit(solution)/shard_map/ppermute | solution.py:24
  37.7 6.2 %collective-permute-start.7 = (f32[2,128,128]{2,1,0:T(8,128)S(1)}, f32[2,128,128]{2,1,0:T(8,128)S(1)}, u32[]{:S(2)}, u32[]{:S(2)}) collective-permute-start(f32[2,128,128]{2,1,0:T(8,128)S(1)} %add.12), channel_id=1, source_target_pairs={{1,0},{0,1},{3,2},{2,3},{5,4},{4,5},{7,6},{6,7},{9,8},{8,9},{11,10... | collective-permute-start | bytes 393224 | tf_op jit(solution)/shard_map/ppermute | solution.py:24
  38.5 11.0 %collective-permute-start.18 = (f32[2,128,128]{2,1,0:T(8,128)S(1)}, f32[2,128,128]{2,1,0:T(8,128)S(1)}, u32[]{:S(2)}, u32[]{:S(2)}) collective-permute-start(f32[2,128,128]{2,1,0:T(8,128)S(1)} %get-tuple-element.69), channel_id=1, source_target_pairs={{1,0},{0,1},{3,2},{2,3},{5,4},{4,5},{7,6},{6,7},{9,8},{8,9},{11,10... | collective-permute-start | bytes 393224 | tf_op jit(solution)/shard_map/ppermute | solution.py:24
  44.1 5.4 %collective-permute-start.17 = (f32[2,128,128]{2,1,0:T(8,128)S(1)}, f32[2,128,128]{2,1,0:T(8,128)S(1)}, u32[]{:S(2)}, u32[]{:S(2)}) collective-permute-start(f32[2,128,128]{2,1,0:T(8,128)S(1)} %get-tuple-element.59.quad_ref.quad_one), channel_id=1, source_target_pairs={{1,0},{0,1},{3,2},{2,3},{5,4},{4,5},{7,6},{6,7},{9,8},{8,9},{11,10... | collective-permute-start | bytes 393224 | tf_op jit(solution)/shard_map/ppermute | solution.py:24
  45.6 8.3 %collective-permute-start.13 = (f32[4,128,128]{2,1,0:T(8,128)S(1)}, f32[4,128,128]{2,1,0:T(8,128)S(1)}, u32[]{:S(2)}, u32[]{:S(2)}) collective-permute-start(f32[4,128,128]{2,1,0:T(8,128)S(1)} %get-tuple-element.66), channel_id=1, source_target_pairs={{2,0},{4,2},{6,4},{8,6},{10,8},{12,10},{14,12},{16,14},{18,16},{20... | collective-permute-start | bytes 786440 | tf_op jit(solution)/shard_map/ppermute | solution.py:24
  45.6 8.3 %collective-permute-start.11 = (f32[4,128,128]{2,1,0:T(8,128)S(1)}, f32[4,128,128]{2,1,0:T(8,128)S(1)}, u32[]{:S(2)}, u32[]{:S(2)}) collective-permute-start(f32[4,128,128]{2,1,0:T(8,128)S(1)} %get-tuple-element.63), channel_id=1, source_target_pairs={{2,0},{4,2},{6,4},{8,6},{10,8},{12,10},{14,12},{16,14},{18,16},{20... | collective-permute-start | bytes 786440 | tf_op jit(solution)/shard_map/ppermute | solution.py:24
  47.8 5.0 %collective-permute-start.14 = (f32[2,128,128]{2,1,0:T(8,128)S(1)}, f32[2,128,128]{2,1,0:T(8,128)S(1)}, u32[]{:S(2)}, u32[]{:S(2)}) collective-permute-start(f32[2,128,128]{2,1,0:T(8,128)S(1)} %get-tuple-element.60.quad_ref.quad_two), channel_id=1, source_target_pairs={{1,0},{0,1},{3,2},{2,3},{5,4},{4,5},{7,6},{6,7},{9,8},{8,9},{11,10... | collective-permute-start | bytes 393224 | tf_op jit(solution)/shard_map/ppermute | solution.py:24
  49.5 4.4 %collective-permute-start.19 = (f32[2,128,128]{2,1,0:T(8,128)S(1)}, f32[2,128,128]{2,1,0:T(8,128)S(1)}, u32[]{:S(2)}, u32[]{:S(2)}) collective-permute-start(f32[2,128,128]{2,1,0:T(8,128)S(1)} %collective-permute-done.17.upper_ref), channel_id=1, source_target_pairs={{2,0},{4,2},{6,4},{8,6},{10,8},{12,10},{14,12},{16,14},{18,16},{20... | collective-permute-start | bytes 393224 | tf_op jit(solution)/shard_map/ppermute | solution.py:24
  49.5 6.7 %collective-permute-start.15 = (f32[2,128,128]{2,1,0:T(8,128)S(1)}, f32[2,128,128]{2,1,0:T(8,128)S(1)}, u32[]{:S(2)}, u32[]{:S(2)}) collective-permute-start(f32[2,128,128]{2,1,0:T(8,128)S(1)} %get-tuple-element.67), channel_id=1, source_target_pairs={{1,0},{0,1},{3,2},{2,3},{5,4},{4,5},{7,6},{6,7},{9,8},{8,9},{11,10... | collective-permute-start | bytes 393224 | tf_op jit(solution)/shard_map/ppermute | solution.py:24
  52.8 3.6 %collective-permute-start.16 = (f32[2,128,128]{2,1,0:T(8,128)S(1)}, f32[2,128,128]{2,1,0:T(8,128)S(1)}, u32[]{:S(2)}, u32[]{:S(2)}) collective-permute-start(f32[2,128,128]{2,1,0:T(8,128)S(1)} %collective-permute-done.14.upper_ref), channel_id=1, source_target_pairs={{2,0},{4,2},{6,4},{8,6},{10,8},{12,10},{14,12},{16,14},{18,16},{20... | collective-permute-start | bytes 393224 | tf_op jit(solution)/shard_map/ppermute | solution.py:24
  61.4 7.3 %collective-permute-start.22 = (f32[2,128,128]{2,1,0:T(8,128)S(1)}, f32[2,128,128]{2,1,0:T(8,128)S(1)}, u32[]{:S(2)}, u32[]{:S(2)}) collective-permute-start(f32[2,128,128]{2,1,0:T(8,128)S(1)} %get-tuple-element.76), channel_id=1, source_target_pairs={{30,0},{0,2},{2,4},{4,6},{6,8},{8,10},{10,12},{12,14},{14,16},{16,... | collective-permute-start | bytes 393224 | tf_op jit(solution)/shard_map/ppermute | solution.py:24
  61.6 13.4 %collective-permute-start.21 = (f32[2,128,256]{2,1,0:T(8,128)S(1)}, f32[2,128,256]{2,1,0:T(8,128)S(1)}, u32[]{:S(2)}, u32[]{:S(2)}) collective-permute-start(f32[2,128,256]{2,1,0:T(8,128)S(1)} %get-tuple-element.74), channel_id=1, source_target_pairs={{30,0},{0,2},{2,4},{4,6},{6,8},{8,10},{10,12},{12,14},{14,16},{16,... | collective-permute-start | bytes 786440 | tf_op jit(solution)/shard_map/ppermute | solution.py:24
  61.7 11.2 %collective-permute-start.24 = (f32[2,128,128]{2,1,0:T(8,128)S(1)}, f32[2,128,128]{2,1,0:T(8,128)S(1)}, u32[]{:S(2)}, u32[]{:S(2)}) collective-permute-start(f32[2,128,128]{2,1,0:T(8,128)S(1)} %get-tuple-element.78), channel_id=1, source_target_pairs={{30,0},{0,2},{2,4},{4,6},{6,8},{8,10},{10,12},{12,14},{14,16},{16,... | collective-permute-start | bytes 393224 | tf_op jit(solution)/shard_map/ppermute | solution.py:24
  62.5 13.4 %collective-permute-start.20 = (f32[2,128,256]{2,1,0:T(8,128)S(1)}, f32[2,128,256]{2,1,0:T(8,128)S(1)}, u32[]{:S(2)}, u32[]{:S(2)}) collective-permute-start(f32[2,128,256]{2,1,0:T(8,128)S(1)} %get-tuple-element.73), channel_id=1, source_target_pairs={{30,0},{0,2},{2,4},{4,6},{6,8},{8,10},{10,12},{12,14},{14,16},{16,... | collective-permute-start | bytes 786440 | tf_op jit(solution)/shard_map/ppermute | solution.py:24
  62.6 11.6 %collective-permute-start.27 = (f32[2,128,128]{2,1,0:T(8,128)S(1)}, f32[2,128,128]{2,1,0:T(8,128)S(1)}, u32[]{:S(2)}, u32[]{:S(2)}) collective-permute-start(f32[2,128,128]{2,1,0:T(8,128)S(1)} %get-tuple-element.80), channel_id=1, source_target_pairs={{1,0},{0,1},{3,2},{2,3},{5,4},{4,5},{7,6},{6,7},{9,8},{8,9},{11,10... | collective-permute-start | bytes 393224 | tf_op jit(solution)/shard_map/ppermute | solution.py:24
  68.7 7.2 %collective-permute-start.26 = (f32[2,128,128]{2,1,0:T(8,128)S(1)}, f32[2,128,128]{2,1,0:T(8,128)S(1)}, u32[]{:S(2)}, u32[]{:S(2)}) collective-permute-start(f32[2,128,128]{2,1,0:T(8,128)S(1)} %get-tuple-element.79), channel_id=1, source_target_pairs={{1,0},{0,1},{3,2},{2,3},{5,4},{4,5},{7,6},{6,7},{9,8},{8,9},{11,10... | collective-permute-start | bytes 393224 | tf_op jit(solution)/shard_map/ppermute | solution.py:24
  72.9 5.0 %collective-permute-start.23 = (f32[2,128,128]{2,1,0:T(8,128)S(1)}, f32[2,128,128]{2,1,0:T(8,128)S(1)}, u32[]{:S(2)}, u32[]{:S(2)}) collective-permute-start(f32[2,128,128]{2,1,0:T(8,128)S(1)} %add.14), channel_id=1, source_target_pairs={{1,0},{0,1},{3,2},{2,3},{5,4},{4,5},{7,6},{6,7},{9,8},{8,9},{11,10... | collective-permute-start | bytes 393224 | tf_op jit(solution)/shard_map/ppermute | solution.py:24
  74.2 5.0 %collective-permute-start.25 = (f32[2,128,128]{2,1,0:T(8,128)S(1)}, f32[2,128,128]{2,1,0:T(8,128)S(1)}, u32[]{:S(2)}, u32[]{:S(2)}) collective-permute-start(f32[2,128,128]{2,1,0:T(8,128)S(1)} %add.15), channel_id=1, source_target_pairs={{1,0},{0,1},{3,2},{2,3},{5,4},{4,5},{7,6},{6,7},{9,8},{8,9},{11,10... | collective-permute-start | bytes 393224 | tf_op jit(solution)/shard_map/ppermute | solution.py:24

commit v2 on v1

--- a/solution.py
+++ b/solution.py
@@ -90,8 +90,8 @@
 
 
 def place(scalar_ref, j):
-    col = scalar_ref[2 * j + 1]
-    return scalar_ref[2 * j], col // LANES, col % LANES
+    col = scalar_ref[0, 2 * j + 1]
+    return scalar_ref[0, 2 * j], col // LANES, col % LANES
 
 
 def window(ext_ref, c, spot, width, lane):
@@ -222,7 +222,7 @@
 
 
 def residual_end(scalar_ref, spots, spot_list, ext_ref, moved_ref, win_ref, back_ref, width, lane):
-    total = scalar_ref[2 * spots]
+    total = scalar_ref[0, 2 * spots]
 
     def finish(j, real, imag):
         used = j < total
@@ -235,42 +235,48 @@
 
 
 def wave_kernel(
-    scalar_ref, tile_ref, below_ref, upper_ref, lower_ref, corner_ref,
+    numbers_ref, tile_ref, below_ref, upper_ref, lower_ref, corner_ref,
     cos_ref, sin_ref, probe_ref, amp_ref, table_ref,
     own_ref, down_ref, up_out_ref, low_out_ref, diag_ref, back_ref,
-    ext_ref, win_ref, moved_ref, *, spots, width,
-):
+    ext_ref, other_ref, grad_ref, win_ref, moved_ref, scalar_ref, scalar_sem, *, spots, width,
+):
+    fetched = pltpu.make_async_copy(numbers_ref, scalar_ref, scalar_sem)
+    fetched.start()
     lane = lanes_of(width)
     tile_px = own_ref.shape[1]
-    spot_list = [place(scalar_ref, j) for j in range(spots)]
     halo = (tile_ref, below_ref, upper_ref, lower_ref, corner_ref)
     fill_ext(ext_ref, whole_pieces(halo, 0, tile_px, width))
+    fill_ext(other_ref, whole_pieces(halo, 1, tile_px, width))
+    grad_ref[...] = jnp.zeros(grad_ref.shape, jnp.float32)
+    fetched.wait()
+    spot_list = [place(scalar_ref, j) for j in range(spots)]
     light(ext_ref, spot_list, probe_ref, back_ref, width, lane)
-    fill_ext(ext_ref, whole_pieces(halo, 1, tile_px, width))
-    take_windows(ext_ref, spot_list, win_ref, width, lane)
-    ext_ref[...] = jnp.zeros(ext_ref.shape, jnp.float32)
-    finish = residual_end(scalar_ref, spots, spot_list, ext_ref, moved_ref, win_ref, back_ref, width, lane)
+    take_windows(other_ref, spot_list, win_ref, width, lane)
+    finish = residual_end(scalar_ref, spots, spot_list, grad_ref, moved_ref, win_ref, back_ref, width, lane)
     interleave([
         joined(
             forward_steps(group, back_ref, moved_ref, cos_ref, sin_ref, table_ref, width),
             residual_steps(
-                group, moved_ref, win_ref, lambda j: amp_ref[scalar_ref[2 * spots + 1 + j]],
+                group, moved_ref, win_ref, lambda j: amp_ref[scalar_ref[0, 2 * spots + 1 + j]],
                 finish, table_ref, width,
             ),
         )
         for group in groups_of(spots)
     ], LAG)
-    emit(ext_ref, own_ref, down_ref, up_out_ref, low_out_ref, diag_ref, width)
+    emit(grad_ref, own_ref, down_ref, up_out_ref, low_out_ref, diag_ref, width)
 
 
 def forward_kernel(
-    scalar_ref, rest_ref, quad_ref, left_ref, right_ref, upper_ref, lower_ref, corner_ref,
-    cos_ref, sin_ref, probe_ref, table_ref, moved_ref, ext_ref, enter_ref, *, spots, width,
-):
+    numbers_ref, rest_ref, quad_ref, left_ref, right_ref, upper_ref, lower_ref, corner_ref,
+    cos_ref, sin_ref, probe_ref, table_ref, moved_ref, ext_ref, enter_ref, scalar_ref, scalar_sem, *, spots, width,
+):
+    fetched = pltpu.make_async_copy(numbers_ref, scalar_ref, scalar_sem)
+    fetched.start()
     lane = lanes_of(width)
-    spot_list = [place(scalar_ref, j) for j in range(spots)]
     halo = (rest_ref, quad_ref, left_ref, right_ref, upper_ref, lower_ref, corner_ref)
     fill_ext(ext_ref, slice_pieces(halo, 0, rest_ref.shape[1], width))
+    fetched.wait()
+    spot_list = [place(scalar_ref, j) for j in range(spots)]
     light(ext_ref, spot_list, probe_ref, enter_ref, width, lane)
     interleave([
         forward_steps(group, enter_ref, moved_ref, cos_ref, sin_ref, table_ref, width)
@@ -279,34 +285,40 @@
 
 
 def residual_kernel(
-    scalar_ref, rest_ref, quad_ref, left_ref, right_ref, upper_ref, lower_ref, corner_ref,
+    numbers_ref, rest_ref, quad_ref, left_ref, right_ref, upper_ref, lower_ref, corner_ref,
     moved_ref, amp_ref, table_ref,
     own_ref, down_ref, up_out_ref, low_out_ref, diag_ref, back_ref,
-    ext_ref, win_ref, *, spots, width,
-):
+    ext_ref, grad_ref, win_ref, scalar_ref, scalar_sem, *, spots, width,
+):
+    fetched = pltpu.make_async_copy(numbers_ref, scalar_ref, scalar_sem)
+    fetched.start()
     lane = lanes_of(width)
-    spot_list = [place(scalar_ref, j) for j in range(spots)]
     halo = (rest_ref, quad_ref, left_ref, right_ref, upper_ref, lower_ref, corner_ref)
     fill_ext(ext_ref, slice_pieces(halo, 1, rest_ref.shape[1], width))
+    grad_ref[...] = jnp.zeros(grad_ref.shape, jnp.float32)
+    fetched.wait()
+    spot_list = [place(scalar_ref, j) for j in range(spots)]
     take_windows(ext_ref, spot_list, win_ref, width, lane)
-    ext_ref[...] = jnp.zeros(ext_ref.shape, jnp.float32)
-    finish = residual_end(scalar_ref, spots, spot_list, ext_ref, moved_ref, win_ref, back_ref, width, lane)
+    finish = residual_end(scalar_ref, spots, spot_list, grad_ref, moved_ref, win_ref, back_ref, width, lane)
     interleave([
         residual_steps(
-            group, moved_ref, win_ref, lambda j: amp_ref[scalar_ref[2 * spots + 1 + j]],
+            group, moved_ref, win_ref, lambda j: amp_ref[scalar_ref[0, 2 * spots + 1 + j]],
             finish, table_ref, width,
         )
         for group in groups_of(spots)
     ], LAG)
-    emit(ext_ref, own_ref, down_ref, up_out_ref, low_out_ref, diag_ref, width)
+    emit(grad_ref, own_ref, down_ref, up_out_ref, low_out_ref, diag_ref, width)
 
 
 def backward_kernel(
-    scalar_ref, back_ref, cos_ref, sin_ref, probe_ref, table_ref,
-    own_ref, down_ref, up_out_ref, low_out_ref, diag_ref, ext_ref, *, spots, width,
-):
+    numbers_ref, back_ref, other_down_ref, cos_ref, sin_ref, probe_ref, table_ref,
+    own_ref, down_ref, up_out_ref, low_out_ref, diag_ref, ext_ref, scalar_ref, scalar_sem, *, spots, width,
+):
+    fetched = pltpu.make_async_copy(numbers_ref, scalar_ref, scalar_sem)
+    fetched.start()
     lane = lanes_of(width)
-    total = scalar_ref[2 * spots]
+    down_ref[2:] = other_down_ref[...]
+    waiting = [fetched]
     ext_ref[...] = jnp.zeros(ext_ref.shape, jnp.float32)
 
     def chain(group):
@@ -321,6 +333,9 @@
         yield True
         pairs = left_side(half, table_ref, width)
         yield True
+        while waiting:
+            waiting.pop().wait()
+        total = scalar_ref[0, 2 * spots]
         for j, (real, negative) in zip(group, pairs):
             imag = -negative
             spot = place(scalar_ref, j)
@@ -350,61 +365,63 @@
     return step(quad_ref[c, top, left], own_ref[c, top, left] + above_ref[c, :, left] + upper_ref[c])
 
 
-def update_second_kernel(
-    tile_ref, own_ref, above_ref, low_ref, rest_ref, left_ref, right_ref, *, width,
-):
-    for c in range(2):
-        pieces = list(rest_values(tile_ref.at[1], own_ref, above_ref, low_ref, c, width))
-        for rows, lanes, value in pieces:
-            rest_ref[c, rows, lanes] = value
-        right_ref[c] = pieces[0][2]
-        left_ref[c] = pieces[1][2]
-
-
-def update_first_kernel(
-    tile_ref, own_ref, above_ref, low_ref, second_ref, rest_ref, left_ref, right_ref, *, width,
-):
-    for c in range(2):
-        pieces = list(rest_values(tile_ref.at[0], own_ref, above_ref, low_ref, c, width))
-        for rows, lanes, value in pieces:
-            rest_ref[c, rows, lanes] = value
-        right_ref[c] = pieces[0][2]
-        right_ref[2 + c] = second_ref[c]
-        left_ref[c] = pieces[1][2]
+def update_low_kernel(tile_ref, own_one, own_two, low_one, low_two, left_one, left_two, *, width):
+    tile_px = own_one.shape[1]
+    low, left = slice(width, tile_px), slice(0, width)
+    for s, (own_ref, low_ref, left_ref) in enumerate(((own_one, low_one, left_one), (own_two, low_two, left_two))):
+        for c in range(2):
+            left_ref[c] = step(tile_ref[s, c, low, left], own_ref[c, low, left] + low_ref[c])
+
+
+def update_rest_kernel(
+    tile_ref, own_one, own_two, above_ref, low_one, low_two, rest_one, rest_two, right_ref, *, width,
+):
+    parts = ((own_one, low_one, rest_one), (own_two, low_two, rest_two))
+    for s, (own_ref, low_ref, rest_ref) in enumerate(parts):
+        above = above_ref.at[pl.ds(2 * s, 2)]
+        for c in range(2):
+            pieces = list(rest_values(tile_ref.at[s], own_ref, above, low_ref, c, width))
+            for rows, lanes, value in pieces:
+                rest_ref[c, rows, lanes] = value
+            right_ref[2 * s + c] = pieces[0][2]
 
 
 def update_quad_kernel(
-    tile_ref, own_one, own_two, above_one, above_two, up_one, up_two,
-    quad_one, quad_two, left_ref, *, width,
-):
-    parts = ((own_one, above_one, up_one, quad_one), (own_two, above_two, up_two, quad_two))
-    for s, (own_ref, above_ref, up_ref, quad_ref) in enumerate(parts):
+    tile_ref, own_one, own_two, above_ref, up_one, up_two, quad_one, quad_two, left_ref, *, width,
+):
+    parts = ((own_one, up_one, quad_one), (own_two, up_two, quad_two))
+    for s, (own_ref, up_ref, quad_ref) in enumerate(parts):
+        above = above_ref.at[pl.ds(2 * s, 2)]
         for c in range(2):
-            value = quad_value(tile_ref.at[s], own_ref, above_ref, up_ref, c, width)
+            value = quad_value(tile_ref.at[s], own_ref, above, up_ref, c, width)
             quad_ref[c] = value
             left_ref[2 * s + c] = value
 
 
-def finish_rest_kernel(rest_ref, own_ref, above_ref, low_ref, *refs, width, part):
-    out_ref, tile_ref, sem = refs[-3:]
-    for c in range(2):
-        for rows, lanes, value in rest_values(rest_ref, own_ref, above_ref, low_ref, c, width):
-            tile_ref[c, rows, lanes] = value
-        tile_ref[c, :width, :width] = jnp.zeros((width, width), jnp.float32)
-    copy = pltpu.make_async_copy(tile_ref, out_ref.at[part], sem)
+def finish_rest_kernel(
+    rest_one, rest_two, own_one, own_two, above_ref, low_one, low_two, out_ref, tile_ref, sem, *, width,
+):
+    parts = ((rest_one, own_one, low_one), (rest_two, own_two, low_two))
+    for s, (rest_ref, own_ref, low_ref) in enumerate(parts):
+        above = above_ref.at[pl.ds(2 * s, 2)]
+        for c in range(2):
+            for rows, lanes, value in rest_values(rest_ref, own_ref, above, low_ref, c, width):
+                tile_ref[s, c, rows, lanes] = value
+            tile_ref[s, c, :width, :width] = jnp.zeros((width, width), jnp.float32)
+    copy = pltpu.make_async_copy(tile_ref, out_ref, sem)
     copy.start()
     copy.wait()
 
 
 def finish_quad_kernel(
-    quad_one, quad_two, own_one, own_two, above_one, above_two, up_one, up_two, part_ref, out_ref,
-    quads_ref, sem, *, width,
+    quad_one, quad_two, own_one, own_two, above_ref, up_one, up_two, part_ref, out_ref, quads_ref, sem, *, width,
 ):
     del part_ref
-    parts = ((quad_one, own_one, above_one, up_one), (quad_two, own_two, above_two, up_two))
-    for s, refs in enumerate(parts):
+    parts = ((quad_one, own_one, up_one), (quad_two, own_two, up_two))
+    for s, (quad_ref, own_ref, up_ref) in enumerate(parts):
+        above = above_ref.at[pl.ds(2 * s, 2)]
         for c in range(2):
-            quads_ref[s, c] = quad_value(*refs, c, width)
+            quads_ref[s, c] = quad_value(quad_ref, own_ref, above, up_ref, c, width)
     copy = pltpu.make_async_copy(quads_ref, out_ref.at[:, :, pl.ds(0, width), pl.ds(0, width)], sem)
     copy.start()
     copy.wait()
@@ -423,6 +440,7 @@
 F32 = functools.partial(jax.ShapeDtypeStruct, dtype=jnp.float32)
 SMEM = pl.BlockSpec(memory_space=pltpu.SMEM)
 VMEM = pl.BlockSpec(memory_space=pltpu.VMEM)
+SCALAR_SPACE = (pltpu.SMEM((1, LANES), jnp.int32), pltpu.SemaphoreType.DMA(()))
 LIMIT = pltpu.CompilerParams(vmem_limit_bytes=16 * 1024 * 1024)
 
 
@@ -432,10 +450,10 @@
 def call(kernel, scalars, arrays, outs, scratch, **static):
     return pl.pallas_call(
         functools.partial(kernel, **static),
-        in_specs=[SMEM] * len(scalars) + [VMEM] * len(arrays),
+        in_specs=[VMEM] * (len(scalars) + len(arrays)),
         out_specs=[VMEM] * len(outs),
         out_shape=outs,
-        scratch_shapes=scratch,
+        scratch_shapes=[*scratch, *(SCALAR_SPACE if scalars else ())],
         compiler_params=LIMIT,
     )(*scalars, *arrays)
 
@@ -475,7 +493,9 @@
     ext = tile_px + width
     across = tile_px - width
     cos, sin = jnp.cos(propagation_phase), jnp.sin(propagation_phase)
-    scalars = (jnp.concatenate([positions.reshape(-1), counts.reshape(-1), measurement_index.reshape(-1)]),)
+    numbers = jnp.concatenate([positions.reshape(-1), counts.reshape(-1), measurement_index.reshape(-1)])
+    numbers = jnp.pad(numbers, (0, LANES - numbers.shape[0])).reshape(1, LANES)
+    scalars = (numbers,)
     static = dict(spots=spots, width=width)
     ext_space = pltpu.VMEM((2, ext // LANES, ext, LANES), jnp.float32)
     wave_space = pltpu.VMEM((spots, 2, width, width), jnp.float32)
@@ -514,7 +534,7 @@
             own_two, down_two, up_two, low_two, diag_two, back = call(
                 wave_kernel, scalars,
                 (tile, below, upper, lower, corner, cos, sin, probe, measured, table),
-                [*gradient, wave], [ext_space, wave_space, wave_space], **static,
+                [*gradient, wave], [ext_space, ext_space, ext_space, wave_space, wave_space], **static,
             )
         else:
             (moved,) = call(
@@ -523,36 +543,35 @@
             )
             own_two, down_two, up_two, low_two, diag_two, back = call(
                 residual_kernel, scalars, (*halo[1], moved, measured, table),
-                [*gradient, wave], [ext_space, wave_space], **static,
+                [*gradient, wave], [ext_space, ext_space, wave_space], **static,
             )
         low_two = from_behind(low_two, "col", 1)
         corner_two = from_behind(diag_two, "row", 1)
-        above_two = from_behind(down_two, "row", 1)
-        own_one, down_one, up_one, low_one, diag_one = call(
-            backward_kernel, scalars, (back, cos, sin, probe, table),
-            gradient, [ext_space], **static,
+        own_one, down, up_one, low_one, diag_one = call(
+            backward_kernel, scalars, (back, down_two, cos, sin, probe, table),
+            [whole, F32((4, width, tile_px)), square, square, square], [ext_space], **static,
         )
         low_one = from_behind(low_one, "col", 1)
         corner_one = from_behind(diag_one, "row", 1)
-        above_one = from_behind(down_one, "row", 1)
+        above = from_behind(down, "row", 1)
         up_two = up_two + corner_two
         up_one = up_one + corner_one
         up_two = from_behind(up_two, "col", 1)
         up_one = from_behind(up_one, "col", 1)
         if i + 1 < ITERS:
-            rest_two, left_two, right = call(
-                update_second_kernel, (), (tile, own_two, above_two, low_two),
-                [whole, square, F32((2, width, across))], [], width=width,
-            )
-            rest_one, left_one, right = call(
-                update_first_kernel, (), (tile, own_one, above_one, low_one, right),
-                [whole, square, F32((4, width, across))], [], width=width,
+            left_one, left_two = call(
+                update_low_kernel, (), (tile, own_one, own_two, low_one, low_two),
+                [F32((2, across, width))] * 2, [], width=width,
             )
             lower_one = from_behind(left_one, "col", -1)
+            rest_one, rest_two, right = call(
+                update_rest_kernel, (), (tile, own_one, own_two, above, low_one, low_two),
+                [whole, whole, F32((4, width, across))], [], width=width,
+            )
             below_right = from_behind(right, "row", -1)
             quad_one, quad_two, left = call(
                 update_quad_kernel, (),
-                (tile, own_one, own_two, above_one, above_two, up_one, up_two),
+                (tile, own_one, own_two, above, up_one, up_two),
                 [square, square, squares], [], width=width,
             )
             upper_one = from_behind(quad_one, "col", -1)
@@ -566,34 +585,29 @@
                 (rest_two, quad_two, below_left, below_right, upper_two, lower_two, corner_two),
             )
         else:
-            part = []
-            for slice_at, operands in (
-                (1, (rest_two, own_two, above_two, low_two)), (0, (rest_one, own_one, above_one, low_one))
-            ):
-                part = [pl.pallas_call(
-                    functools.partial(finish_rest_kernel, width=width, part=slice_at),
-                    in_specs=[VMEM] * 4 + [FAR] * len(part),
-                    out_specs=FAR,
-                    out_shape=F32(specimen_slices.shape),
-                    input_output_aliases={4: 0} if part else {},
-                    scratch_shapes=[
-                        pltpu.VMEM((2, tile_px, tile_px), jnp.float32), pltpu.SemaphoreType.DMA(()),
-                    ],
-                    compiler_params=LIMIT,
-                    name="finish_rest",
-                )(*operands, *map(in_hbm, part))]
+            part = pl.pallas_call(
+                functools.partial(finish_rest_kernel, width=width),
+                in_specs=[VMEM] * 7,
+                out_specs=FAR,
+                out_shape=F32(specimen_slices.shape),
+                scratch_shapes=[
+                    pltpu.VMEM(specimen_slices.shape, jnp.float32), pltpu.SemaphoreType.DMA(()),
+                ],
+                compiler_params=LIMIT,
+                name="finish_rest",
+            )(rest_one, rest_two, own_one, own_two, above, low_one, low_two)
             updated = pl.pallas_call(
                 functools.partial(finish_quad_kernel, width=width),
-                in_specs=[VMEM] * 8 + [FAR],
+                in_specs=[VMEM] * 7 + [FAR],
                 out_specs=FAR,
                 out_shape=F32(specimen_slices.shape),
-                input_output_aliases={8: 0},
+                input_output_aliases={7: 0},
                 scratch_shapes=[
                     pltpu.VMEM((2, 2, width, width), jnp.float32), pltpu.SemaphoreType.DMA(()),
                 ],
                 compiler_params=LIMIT,
                 name="finish_quad",
-            )(quad_one, quad_two, own_one, own_two, above_one, above_two, up_one, up_two, in_hbm(part[0]))
+            )(quad_one, quad_two, own_one, own_two, above, up_one, up_two, in_hbm(part))
     return updated
 
 

time: 80.2 us -> 81 us (level)
  waiting for transfers between devices: 26.3 us -> 30.4 us
  Pallas kernels: 19.1 us -> 17.4 us
  starting transfers between devices: 32.5 us -> 31 us
    ppermute x28 -> x26, waiting for transfers between devices: 26.3 us -> 30.4 us  [from_behind(): return lax.ppermute(block, axis, route)]
    pallas_call x10 -> x9, Pallas kernels: 15.5 us -> 13.8 us  [the longest x8 12.7 us: call(): pl.pallas_call(functools.partial(kernel, **static), in_specs=[VMEM] * (le...]
    ppermute x28 -> x26, starting transfers between devices: 32.5 us -> 31 us  [from_behind(): return lax.ppermute(block, axis, route)]
  transfers between devices with their start and end apart: 28 -> 26, of which waited for: 13 -> 13; matrix products, arithmetic and copies ran while one was open for 1% -> 1% of each run, Pallas kernels for 10% -> 6%
where the time goes in v2:
time: 81 us; the launch traced here: 80.8 us
  starting transfers between devices  31 us (38%)
  waiting for transfers between devices  30.4 us (38%)
  Pallas kernels  17.4 us (21%)
  local copies, waits for them, and re-layouts  1.09 us (1%)
  between operations  0.81 us (1%)
    ppermute x26, starting transfers between devices, from_behind(): return lax.ppermute(block, axis, route)  31 us
    ppermute x26, waiting for transfers between devices, from_behind(): return lax.ppermute(block, axis, route)  30.4 us
    pallas_call x8, Pallas kernels, call(): pl.pallas_call(functools.partial(kernel, **static), in_specs=[VMEM] * (le...  12.7 us
  transfers between devices with their start and end apart: 26, of which 13 were waited for; matrix products, arithmetic and copies ran while one was open for 1% of the time, Pallas kernels for 6%

profile of v2, /device:TPU:0, one launch (start us, length us, event | category | flops | bytes accessed | tf_op | source)
XLA Modules:
  0.0 80.8 jit_solution(7463933008547058517)
XLA Ops:
  0.0 1.3 %pack.1 = (f32[4,128,128]{2,1,0:T(8,128)S(1)}, f32[4,128,128]{2,1,0:T(8,128)S(1)}, f32[4,128,256]{2,1,0:T(8,128)S(1)}) custom-call(f32[2,2,256,256]{3,2,1,0:T(8,128)} %whole_ref.1), custom_call_target="tpu_custom_call" | custom-call | tf_op jit(solution)/shard_map/pack/pallas_call | solution.py:509
  1.3 3.0 %collective-permute-start.1 = (f32[4,128,128]{2,1,0:T(8,128)S(1)}, f32[4,128,128]{2,1,0:T(8,128)S(1)}, u32[]{:S(2)}, u32[]{:S(2)}) collective-permute-start(f32[4,128,128]{2,1,0:T(8,128)S(1)} %get-tuple-element.44), channel_id=1, source_target_pairs={{1,0},{0,1},{3,2},{2,3},{5,4},{4,5},{7,6},{6,7},{9,8},{8,9},{11,10... | collective-permute-start | bytes 786440 | tf_op jit(solution)/shard_map/ppermute | solution.py:24
  4.3 3.7 %collective-permute-start = (f32[4,128,256]{2,1,0:T(8,128)S(1)}, f32[4,128,256]{2,1,0:T(8,128)S(1)}, u32[]{:S(2)}, u32[]{:S(2)}) collective-permute-start(f32[4,128,256]{2,1,0:T(8,128)S(1)} %get-tuple-element.43), channel_id=1, source_target_pairs={{2,0},{4,2},{6,4},{8,6},{10,8},{12,10},{14,12},{16,14},{18,16},{20... | collective-permute-start | bytes 1572872 | tf_op jit(solution)/shard_map/ppermute | solution.py:24
  10.2 1.3 %collective-permute-done.1.upper_ref = f32[4,128,128]{2,1,0:T(8,128)S(1)} collective-permute-done((f32[4,128,128]{2,1,0:T(8,128)S(1)}, f32[4,128,128]{2,1,0:T(8,128)S(1)}, u32[]{:S(2)}, u32[]{:S(2)}) %collective-permute-start.1) | collective-permute-done | bytes 262176 | tf_op jit(solution)/shard_map/ppermute | solution.py:24
  11.5 2.5 %collective-permute-start.3 = (f32[4,128,128]{2,1,0:T(8,128)S(1)}, f32[4,128,128]{2,1,0:T(8,128)S(1)}, u32[]{:S(2)}, u32[]{:S(2)}) collective-permute-start(f32[4,128,128]{2,1,0:T(8,128)S(1)} %collective-permute-done.1.upper_ref), channel_id=1, source_target_pairs={{2,0},{4,2},{6,4},{8,6},{10,8},{12,10},{14,12},{16,14},{18,16},{20... | collective-permute-start | bytes 786440 | tf_op jit(solution)/shard_map/ppermute | solution.py:24
  14.0 1.5 %stage.1 = (f32[2,2,256,256]{3,2,1,0:T(8,128)S(1)}, f32[2,128,128]{2,1,0:T(8,128)S(1)}, f32[4,128,128]{2,1,0:T(8,128)S(1)}, bf16[4,256,256]{2,1,0:T(8,128)(2,1)S(1)}) custom-call(f32[2,2,256,256]{3,2,1,0:T(8,128)} %whole_ref.1, f32[2,128,128]{2,1,0:T(8,128)} %refs_1_.1, f32[4,128,128]{2,1,0:T(8,128)} %bitcast.6, bf16[4,256,256]{2,1,0:T(8,128)(2,1)} %constant.4.clone.refs_3_), custom_call_target="tpu_custom_call" | custom-call | tf_op jit(solution)/shard_map/stage/pallas_call | solution.py:522
  16.3 1.7 %collective-permute-done.3.corner_ref = f32[4,128,128]{2,1,0:T(8,128)S(1)} collective-permute-done((f32[4,128,128]{2,1,0:T(8,128)S(1)}, f32[4,128,128]{2,1,0:T(8,128)S(1)}, u32[]{:S(2)}, u32[]{:S(2)}) %collective-permute-start.3) | collective-permute-done | bytes 262176 | tf_op jit(solution)/shard_map/ppermute | solution.py:24
  17.9 3.8 %shard_map.82 = (f32[2,256,256]{2,1,0:T(8,128)S(1)}, f32[2,128,256]{2,1,0:T(8,128)S(1)}, f32[2,128,128]{2,1,0:T(8,128)S(1)}, f32[2,128,128]{2,1,0:T(8,128)S(1)},...) custom-call(s32[1,128]{1,0:T(1,128)S(1)} %pad_bitcast_fusion.numbers_ref, ...), custom_call_target="tpu_custom_call" | custom-call | tf_op jit(solution)/shard_map/pallas_call | solution.py:451
  21.7 2.0 %shard_map.83 = (f32[2,256,256]{2,1,0:T(8,128)S(1)}, f32[4,128,256]{2,1,0:T(8,128)S(1)}, f32[2,128,128]{2,1,0:T(8,128)S(1)}, f32[2,128,128]{2,1,0:T(8,128)S(1)}, f32[2,128,128]{2,1,0:T(8,128)S(1)}) custom-call(s32[1,128]{1,0:T(1,128)S(1)} %pad_bitcast_fusion.numbers_ref, f32[4,2,128,128]{3,2,1,0:T(8,128)S(1)} %get-tuple-element.49.back_ref, ...), custom_call_target="tpu_custom_call" | custom-call | tf_op jit(solution)/shard_map/pallas_call | solution.py:451
  24.0 1.2 %collective-permute-start.7 = (f32[2,128,128]{2,1,0:T(8,128)S(1)}, f32[2,128,128]{2,1,0:T(8,128)S(1)}, u32[]{:S(2)}, u32[]{:S(2)}) collective-permute-start(f32[2,128,128]{2,1,0:T(8,128)S(1)} %get-tuple-element.57), channel_id=1, source_target_pairs={{30,0},{0,2},{2,4},{4,6},{6,8},{8,10},{10,12},{12,14},{14,16},{16,... | collective-permute-start | bytes 393224 | tf_op jit(solution)/shard_map/ppermute | solution.py:24
  25.2 1.5 %collective-permute-start.9 = (f32[2,128,128]{2,1,0:T(8,128)S(1)}, f32[2,128,128]{2,1,0:T(8,128)S(1)}, u32[]{:S(2)}, u32[]{:S(2)}) collective-permute-start(f32[2,128,128]{2,1,0:T(8,128)S(1)} %get-tuple-element.60), channel_id=1, source_target_pairs={{1,0},{0,1},{3,2},{2,3},{5,4},{4,5},{7,6},{6,7},{9,8},{8,9},{11,10... | collective-permute-start | bytes 393224 | tf_op jit(solution)/shard_map/ppermute | solution.py:24
  27.2 9.4 %collective-permute-done.5 = f32[2,128,128]{2,1,0:T(8,128)S(1)} collective-permute-done((f32[2,128,128]{2,1,0:T(8,128)S(1)}, f32[2,128,128]{2,1,0:T(8,128)S(1)}, u32[]{:S(2)}, u32[]{:S(2)}) %collective-permute-start.5) | collective-permute-done | bytes 131104 | tf_op jit(solution)/shard_map/ppermute | solution.py:24
  36.7 1.6 %collective-permute-start.6 = (f32[2,128,128]{2,1,0:T(8,128)S(1)}, f32[2,128,128]{2,1,0:T(8,128)S(1)}, u32[]{:S(2)}, u32[]{:S(2)}) collective-permute-start(f32[2,128,128]{2,1,0:T(8,128)S(1)} %add.14), channel_id=1, source_target_pairs={{1,0},{0,1},{3,2},{2,3},{5,4},{4,5},{7,6},{6,7},{9,8},{8,9},{11,10... | collective-permute-start | bytes 393224 | tf_op jit(solution)/shard_map/ppermute | solution.py:24
  38.3 1.4 %collective-permute-start.8 = (f32[2,128,128]{2,1,0:T(8,128)S(1)}, f32[2,128,128]{2,1,0:T(8,128)S(1)}, u32[]{:S(2)}, u32[]{:S(2)}) collective-permute-start(f32[2,128,128]{2,1,0:T(8,128)S(1)} %add.15), channel_id=1, source_target_pairs={{1,0},{0,1},{3,2},{2,3},{5,4},{4,5},{7,6},{6,7},{9,8},{8,9},{11,10... | collective-permute-start | bytes 393224 | tf_op jit(solution)/shard_map/ppermute | solution.py:24
  40.5 2.2 %collective-permute-done.6.up_one = f32[2,128,128]{2,1,0:T(8,128)S(1)} collective-permute-done((f32[2,128,128]{2,1,0:T(8,128)S(1)}, f32[2,128,128]{2,1,0:T(8,128)S(1)}, u32[]{:S(2)}, u32[]{:S(2)}) %collective-permute-start.6) | collective-permute-done | bytes 131104 | tf_op jit(solution)/shard_map/ppermute | solution.py:24
  42.7 1.4 %collective-permute-done.8.up_two = f32[2,128,128]{2,1,0:T(8,128)S(1)} collective-permute-done((f32[2,128,128]{2,1,0:T(8,128)S(1)}, f32[2,128,128]{2,1,0:T(8,128)S(1)}, u32[]{:S(2)}, u32[]{:S(2)}) %collective-permute-start.8) | collective-permute-done | bytes 131104 | tf_op jit(solution)/shard_map/ppermute | solution.py:24
  44.2 1.5 %collective-permute-start.16 = (f32[2,128,128]{2,1,0:T(8,128)S(1)}, f32[2,128,128]{2,1,0:T(8,128)S(1)}, u32[]{:S(2)}, u32[]{:S(2)}) collective-permute-start(f32[2,128,128]{2,1,0:T(8,128)S(1)} %get-tuple-element.58.quad_ref.quad_one), channel_id=1, source_target_pairs={{1,0},{0,1},{3,2},{2,3},{5,4},{4,5},{7,6},{6,7},{9,8},{8,9},{11,10... | collective-permute-start | bytes 393224 | tf_op jit(solution)/shard_map/ppermute | solution.py:24
  45.9 2.2 %collective-permute-start.12 = (f32[4,128,128]{2,1,0:T(8,128)S(1)}, f32[4,128,128]{2,1,0:T(8,128)S(1)}, u32[]{:S(2)}, u32[]{:S(2)}) collective-permute-start(f32[4,128,128]{2,1,0:T(8,128)S(1)} %get-tuple-element.64), channel_id=1, source_target_pairs={{2,0},{4,2},{6,4},{8,6},{10,8},{12,10},{14,12},{16,14},{18,16},{20... | collective-permute-start | bytes 786440 | tf_op jit(solution)/shard_map/ppermute | solution.py:24
  49.3 2.4 %collective-permute-start.14 = (f32[2,128,128]{2,1,0:T(8,128)S(1)}, f32[2,128,128]{2,1,0:T(8,128)S(1)}, u32[]{:S(2)}, u32[]{:S(2)}) collective-permute-start(f32[2,128,128]{2,1,0:T(8,128)S(1)} %get-tuple-element.65), channel_id=1, source_target_pairs={{1,0},{0,1},{3,2},{2,3},{5,4},{4,5},{7,6},{6,7},{9,8},{8,9},{11,10... | collective-permute-start | bytes 393224 | tf_op jit(solution)/shard_map/ppermute | solution.py:24
  51.7 1.3 %collective-permute-done.13.upper_ref = f32[2,128,128]{2,1,0:T(8,128)S(1)} collective-permute-done((f32[2,128,128]{2,1,0:T(8,128)S(1)}, f32[2,128,128]{2,1,0:T(8,128)S(1)}, u32[]{:S(2)}, u32[]{:S(2)}) %collective-permute-start.13) | collective-permute-done | bytes 131104 | tf_op jit(solution)/shard_map/ppermute | solution.py:24
  53.8 2.2 %shard_map.87.moved_ref = f32[4,2,128,128]{3,2,1,0:T(8,128)S(1)} custom-call(s32[1,128]{1,0:T(1,128)S(1)} %pad_bitcast_fusion.numbers_ref, f32[2,256,256]{2,1,0:T(8,128)S(1)} %get-tuple-element.66.rest_ref.rest_one, f32[2,128,128]{2,1,0:T(8,128)S(1)} %get-tuple-element.58.quad_ref.quad_one, f32[4,128,128]{2,1,0:T(8,128)S(1)} %collective-permute-done.11.left_ref, ...), custom_call_target="tpu_custom_call" | custom-call | tf_op jit(solution)/shard_map/pallas_call | solution.py:451
  56.2 2.5 %shard_map.88 = (f32[2,256,256]{2,1,0:T(8,128)S(1)}, f32[2,128,256]{2,1,0:T(8,128)S(1)}, f32[2,128,128]{2,1,0:T(8,128)S(1)}, f32[2,128,128]{2,1,0:T(8,128)S(1)},...) custom-call(s32[1,128]{1,0:T(1,128)S(1)} %pad_bitcast_fusion.numbers_ref, ...), custom_call_target="tpu_custom_call" | custom-call | tf_op jit(solution)/shard_map/pallas_call | solution.py:451
  58.6 2.0 %shard_map.89 = (f32[2,256,256]{2,1,0:T(8,128)S(1)}, f32[4,128,256]{2,1,0:T(8,128)S(1)}, f32[2,128,128]{2,1,0:T(8,128)S(1)}, f32[2,128,128]{2,1,0:T(8,128)S(1)}, f32[2,128,128]{2,1,0:T(8,128)S(1)}) custom-call(s32[1,128]{1,0:T(1,128)S(1)} %pad_bitcast_fusion.numbers_ref, f32[4,2,128,128]{3,2,1,0:T(8,128)S(1)} %get-tuple-element.68.back_ref, ...), custom_call_target="tpu_custom_call" | custom-call | tf_op jit(solution)/shard_map/pallas_call | solution.py:451
  61.2 1.2 %collective-permute-start.22 = (f32[2,128,128]{2,1,0:T(8,128)S(1)}, f32[2,128,128]{2,1,0:T(8,128)S(1)}, u32[]{:S(2)}, u32[]{:S(2)}) collective-permute-start(f32[2,128,128]{2,1,0:T(8,128)S(1)} %get-tuple-element.76), channel_id=1, source_target_pairs={{30,0},{0,2},{2,4},{4,6},{6,8},{8,10},{10,12},{12,14},{14,16},{16,... | collective-permute-start | bytes 393224 | tf_op jit(solution)/shard_map/ppermute | solution.py:24
  62.9 1.5 %collective-permute-start.25 = (f32[2,128,128]{2,1,0:T(8,128)S(1)}, f32[2,128,128]{2,1,0:T(8,128)S(1)}, u32[]{:S(2)}, u32[]{:S(2)}) collective-permute-start(f32[2,128,128]{2,1,0:T(8,128)S(1)} %get-tuple-element.78), channel_id=1, source_target_pairs={{1,0},{0,1},{3,2},{2,3},{5,4},{4,5},{7,6},{6,7},{9,8},{8,9},{11,10... | collective-permute-start | bytes 393224 | tf_op jit(solution)/shard_map/ppermute | solution.py:24
  64.4 9.1 %collective-permute-done.20 = f32[2,128,128]{2,1,0:T(8,128)S(1)} collective-permute-done((f32[2,128,128]{2,1,0:T(8,128)S(1)}, f32[2,128,128]{2,1,0:T(8,128)S(1)}, u32[]{:S(2)}, u32[]{:S(2)}) %collective-permute-start.20) | collective-permute-done | bytes 131104 | tf_op jit(solution)/shard_map/ppermute | solution.py:24
  73.5 1.4 %collective-permute-start.21 = (f32[2,128,128]{2,1,0:T(8,128)S(1)}, f32[2,128,128]{2,1,0:T(8,128)S(1)}, u32[]{:S(2)}, u32[]{:S(2)}) collective-permute-start(f32[2,128,128]{2,1,0:T(8,128)S(1)} %add.16), channel_id=1, source_target_pairs={{1,0},{0,1},{3,2},{2,3},{5,4},{4,5},{7,6},{6,7},{9,8},{8,9},{11,10... | collective-permute-start | bytes 393224 | tf_op jit(solution)/shard_map/ppermute | solution.py:24
  75.0 1.4 %collective-permute-start.23 = (f32[2,128,128]{2,1,0:T(8,128)S(1)}, f32[2,128,128]{2,1,0:T(8,128)S(1)}, u32[]{:S(2)}, u32[]{:S(2)}) collective-permute-start(f32[2,128,128]{2,1,0:T(8,128)S(1)} %add.17), channel_id=1, source_target_pairs={{1,0},{0,1},{3,2},{2,3},{5,4},{4,5},{7,6},{6,7},{9,8},{8,9},{11,10... | collective-permute-start | bytes 393224 | tf_op jit(solution)/shard_map/ppermute | solution.py:24
  76.4 1.1 %finish_rest.1.part_ref = f32[2,2,256,256]{3,2,1,0:T(8,128)} custom-call(f32[2,256,256]{2,1,0:T(8,128)S(1)} %get-tuple-element.66.rest_ref.rest_one, f32[2,256,256]{2,1,0:T(8,128)S(1)} %get-tuple-element.62.rest_ref.rest_two, f32[2,256,256]{2,1,0:T(8,128)S(1)} %get-tuple-element.70.own_one, f32[2,256,256]{2,1,0:T(8,128)S(1)} %get-tuple-element.71.own_two, ...), custom_call_target="tpu_custom_call" | custom-call | tf_op jit(solution)/shard_map/finish_rest/pallas_call | solution.py:588
  77.5 1.1 %collective-permute-done.21.up_one = f32[2,128,128]{2,1,0:T(8,128)S(1)} collective-permute-done((f32[2,128,128]{2,1,0:T(8,128)S(1)}, f32[2,128,128]{2,1,0:T(8,128)S(1)}, u32[]{:S(2)}, u32[]{:S(2)}) %collective-permute-start.21) | collective-permute-done | bytes 131104 | tf_op jit(solution)/shard_map/ppermute | solution.py:24
  78.6 1.4 %collective-permute-done.23.up_two = f32[2,128,128]{2,1,0:T(8,128)S(1)} collective-permute-done((f32[2,128,128]{2,1,0:T(8,128)S(1)}, f32[2,128,128]{2,1,0:T(8,128)S(1)}, u32[]{:S(2)}, u32[]{:S(2)}) %collective-permute-start.23) | collective-permute-done | bytes 131104 | tf_op jit(solution)/shard_map/ppermute | solution.py:24
  80.0 0.8 finish_quad.1
  (47 shorter events, 7.3 us)
Async XLA Ops:
  1.3 10.2 %collective-permute-start.1 = (f32[4,128,128]{2,1,0:T(8,128)S(1)}, f32[4,128,128]{2,1,0:T(8,128)S(1)}, u32[]{:S(2)}, u32[]{:S(2)}) collective-permute-start(f32[4,128,128]{2,1,0:T(8,128)S(1)} %get-tuple-element.44), channel_id=1, source_target_pairs={{1,0},{0,1},{3,2},{2,3},{5,4},{4,5},{7,6},{6,7},{9,8},{8,9},{11,10... | collective-permute-start | bytes 786440 | tf_op jit(solution)/shard_map/ppermute | solution.py:24
  4.3 11.9 %collective-permute-start = (f32[4,128,256]{2,1,0:T(8,128)S(1)}, f32[4,128,256]{2,1,0:T(8,128)S(1)}, u32[]{:S(2)}, u32[]{:S(2)}) collective-permute-start(f32[4,128,256]{2,1,0:T(8,128)S(1)} %get-tuple-element.43), channel_id=1, source_target_pairs={{2,0},{4,2},{6,4},{8,6},{10,8},{12,10},{14,12},{16,14},{18,16},{20... | collective-permute-start | bytes 1572872 | tf_op jit(solution)/shard_map/ppermute | solution.py:24
  8.1 1.2 %copy-start.1 = (s32[1,1,4,2]{2,3,1,0:T(2,128)S(1)}, s32[1,1,4,2]{2,3,1,0:T(2,128)}, u32[]{:S(2)}) copy-start(s32[1,1,4,2]{2,3,1,0:T(2,128)} %param.12) | copy-start | bytes 100
  8.1 8.2 %collective-permute-start.2 = (f32[4,128,128]{2,1,0:T(8,128)S(1)}, f32[4,128,128]{2,1,0:T(8,128)S(1)}, u32[]{:S(2)}, u32[]{:S(2)}) collective-permute-start(f32[4,128,128]{2,1,0:T(8,128)S(1)} %get-tuple-element.45), channel_id=1, source_target_pairs={{1,0},{0,1},{3,2},{2,3},{5,4},{4,5},{7,6},{6,7},{9,8},{8,9},{11,10... | collective-permute-start | bytes 786440 | tf_op jit(solution)/shard_map/ppermute | solution.py:24
  9.4 0.7 copy-start.2
  11.5 6.4 %collective-permute-start.3 = (f32[4,128,128]{2,1,0:T(8,128)S(1)}, f32[4,128,128]{2,1,0:T(8,128)S(1)}, u32[]{:S(2)}, u32[]{:S(2)}) collective-permute-start(f32[4,128,128]{2,1,0:T(8,128)S(1)} %collective-permute-done.1.upper_ref), channel_id=1, source_target_pairs={{2,0},{4,2},{6,4},{8,6},{10,8},{12,10},{14,12},{16,14},{18,16},{20... | collective-permute-start | bytes 786440 | tf_op jit(solution)/shard_map/ppermute | solution.py:24
  14.0 1.6 %copy-start = (f32[128,128]{1,0:T(8,128)S(1)}, f32[128,128]{1,0:T(8,128)}, u32[]{:S(2)}) copy-start(f32[128,128]{1,0:T(8,128)} %param.10) | copy-start | bytes 196612
  23.7 20.4 %collective-permute-start.4 = (f32[4,128,256]{2,1,0:T(8,128)S(1)}, f32[4,128,256]{2,1,0:T(8,128)S(1)}, u32[]{:S(2)}, u32[]{:S(2)}) collective-permute-start(f32[4,128,256]{2,1,0:T(8,128)S(1)} %get-tuple-element.53), channel_id=1, source_target_pairs={{30,0},{0,2},{2,4},{4,6},{6,8},{8,10},{10,12},{12,14},{14,16},{16,... | collective-permute-start | bytes 1572872 | tf_op jit(solution)/shard_map/ppermute | solution.py:24
  23.8 12.9 %collective-permute-start.5 = (f32[2,128,128]{2,1,0:T(8,128)S(1)}, f32[2,128,128]{2,1,0:T(8,128)S(1)}, u32[]{:S(2)}, u32[]{:S(2)}) collective-permute-start(f32[2,128,128]{2,1,0:T(8,128)S(1)} %get-tuple-element.55), channel_id=1, source_target_pairs={{30,0},{0,2},{2,4},{4,6},{6,8},{8,10},{10,12},{12,14},{14,16},{16,... | collective-permute-start | bytes 393224 | tf_op jit(solution)/shard_map/ppermute | solution.py:24
  24.0 14.2 %collective-permute-start.7 = (f32[2,128,128]{2,1,0:T(8,128)S(1)}, f32[2,128,128]{2,1,0:T(8,128)S(1)}, u32[]{:S(2)}, u32[]{:S(2)}) collective-permute-start(f32[2,128,128]{2,1,0:T(8,128)S(1)} %get-tuple-element.57), channel_id=1, source_target_pairs={{30,0},{0,2},{2,4},{4,6},{6,8},{8,10},{10,12},{12,14},{14,16},{16,... | collective-permute-start | bytes 393224 | tf_op jit(solution)/shard_map/ppermute | solution.py:24
  25.2 14.4 %collective-permute-start.9 = (f32[2,128,128]{2,1,0:T(8,128)S(1)}, f32[2,128,128]{2,1,0:T(8,128)S(1)}, u32[]{:S(2)}, u32[]{:S(2)}) collective-permute-start(f32[2,128,128]{2,1,0:T(8,128)S(1)} %get-tuple-element.60), channel_id=1, source_target_pairs={{1,0},{0,1},{3,2},{2,3},{5,4},{4,5},{7,6},{6,7},{9,8},{8,9},{11,10... | collective-permute-start | bytes 393224 | tf_op jit(solution)/shard_map/ppermute | solution.py:24
  26.7 13.0 %collective-permute-start.10 = (f32[2,128,128]{2,1,0:T(8,128)S(1)}, f32[2,128,128]{2,1,0:T(8,128)S(1)}, u32[]{:S(2)}, u32[]{:S(2)}) collective-permute-start(f32[2,128,128]{2,1,0:T(8,128)S(1)} %get-tuple-element.61), channel_id=1, source_target_pairs={{1,0},{0,1},{3,2},{2,3},{5,4},{4,5},{7,6},{6,7},{9,8},{8,9},{11,10... | collective-permute-start | bytes 393224 | tf_op jit(solution)/shard_map/ppermute | solution.py:24
  36.7 6.0 %collective-permute-start.6 = (f32[2,128,128]{2,1,0:T(8,128)S(1)}, f32[2,128,128]{2,1,0:T(8,128)S(1)}, u32[]{:S(2)}, u32[]{:S(2)}) collective-permute-start(f32[2,128,128]{2,1,0:T(8,128)S(1)} %add.14), channel_id=1, source_target_pairs={{1,0},{0,1},{3,2},{2,3},{5,4},{4,5},{7,6},{6,7},{9,8},{8,9},{11,10... | collective-permute-start | bytes 393224 | tf_op jit(solution)/shard_map/ppermute | solution.py:24
  38.3 5.8 %collective-permute-start.8 = (f32[2,128,128]{2,1,0:T(8,128)S(1)}, f32[2,128,128]{2,1,0:T(8,128)S(1)}, u32[]{:S(2)}, u32[]{:S(2)}) collective-permute-start(f32[2,128,128]{2,1,0:T(8,128)S(1)} %add.15), channel_id=1, source_target_pairs={{1,0},{0,1},{3,2},{2,3},{5,4},{4,5},{7,6},{6,7},{9,8},{8,9},{11,10... | collective-permute-start | bytes 393224 | tf_op jit(solution)/shard_map/ppermute | solution.py:24
  39.7 9.6 %collective-permute-start.17 = (f32[2,128,128]{2,1,0:T(8,128)S(1)}, f32[2,128,128]{2,1,0:T(8,128)S(1)}, u32[]{:S(2)}, u32[]{:S(2)}) collective-permute-start(f32[2,128,128]{2,1,0:T(8,128)S(1)} %get-tuple-element.67), channel_id=1, source_target_pairs={{1,0},{0,1},{3,2},{2,3},{5,4},{4,5},{7,6},{6,7},{9,8},{8,9},{11,10... | collective-permute-start | bytes 393224 | tf_op jit(solution)/shard_map/ppermute | solution.py:24
  44.2 5.1 %collective-permute-start.16 = (f32[2,128,128]{2,1,0:T(8,128)S(1)}, f32[2,128,128]{2,1,0:T(8,128)S(1)}, u32[]{:S(2)}, u32[]{:S(2)}) collective-permute-start(f32[2,128,128]{2,1,0:T(8,128)S(1)} %get-tuple-element.58.quad_ref.quad_one), channel_id=1, source_target_pairs={{1,0},{0,1},{3,2},{2,3},{5,4},{4,5},{7,6},{6,7},{9,8},{8,9},{11,10... | collective-permute-start | bytes 393224 | tf_op jit(solution)/shard_map/ppermute | solution.py:24
  45.7 8.1 %collective-permute-start.11 = (f32[4,128,128]{2,1,0:T(8,128)S(1)}, f32[4,128,128]{2,1,0:T(8,128)S(1)}, u32[]{:S(2)}, u32[]{:S(2)}) collective-permute-start(f32[4,128,128]{2,1,0:T(8,128)S(1)} %get-tuple-element.63), channel_id=1, source_target_pairs={{2,0},{4,2},{6,4},{8,6},{10,8},{12,10},{14,12},{16,14},{18,16},{20... | collective-permute-start | bytes 786440 | tf_op jit(solution)/shard_map/ppermute | solution.py:24
  45.9 8.0 %collective-permute-start.12 = (f32[4,128,128]{2,1,0:T(8,128)S(1)}, f32[4,128,128]{2,1,0:T(8,128)S(1)}, u32[]{:S(2)}, u32[]{:S(2)}) collective-permute-start(f32[4,128,128]{2,1,0:T(8,128)S(1)} %get-tuple-element.64), channel_id=1, source_target_pairs={{2,0},{4,2},{6,4},{8,6},{10,8},{12,10},{14,12},{16,14},{18,16},{20... | collective-permute-start | bytes 786440 | tf_op jit(solution)/shard_map/ppermute | solution.py:24
  48.1 5.0 %collective-permute-start.13 = (f32[2,128,128]{2,1,0:T(8,128)S(1)}, f32[2,128,128]{2,1,0:T(8,128)S(1)}, u32[]{:S(2)}, u32[]{:S(2)}) collective-permute-start(f32[2,128,128]{2,1,0:T(8,128)S(1)} %get-tuple-element.59.quad_ref.quad_two), channel_id=1, source_target_pairs={{1,0},{0,1},{3,2},{2,3},{5,4},{4,5},{7,6},{6,7},{9,8},{8,9},{11,10... | collective-permute-start | bytes 393224 | tf_op jit(solution)/shard_map/ppermute | solution.py:24
  49.3 4.5 %collective-permute-start.18 = (f32[2,128,128]{2,1,0:T(8,128)S(1)}, f32[2,128,128]{2,1,0:T(8,128)S(1)}, u32[]{:S(2)}, u32[]{:S(2)}) collective-permute-start(f32[2,128,128]{2,1,0:T(8,128)S(1)} %collective-permute-done.16.upper_ref), channel_id=1, source_target_pairs={{2,0},{4,2},{6,4},{8,6},{10,8},{12,10},{14,12},{16,14},{18,16},{20... | collective-permute-start | bytes 393224 | tf_op jit(solution)/shard_map/ppermute | solution.py:24
  49.3 6.7 %collective-permute-start.14 = (f32[2,128,128]{2,1,0:T(8,128)S(1)}, f32[2,128,128]{2,1,0:T(8,128)S(1)}, u32[]{:S(2)}, u32[]{:S(2)}) collective-permute-start(f32[2,128,128]{2,1,0:T(8,128)S(1)} %get-tuple-element.65), channel_id=1, source_target_pairs={{1,0},{0,1},{3,2},{2,3},{5,4},{4,5},{7,6},{6,7},{9,8},{8,9},{11,10... | collective-permute-start | bytes 393224 | tf_op jit(solution)/shard_map/ppermute | solution.py:24
  53.1 3.1 %collective-permute-start.15 = (f32[2,128,128]{2,1,0:T(8,128)S(1)}, f32[2,128,128]{2,1,0:T(8,128)S(1)}, u32[]{:S(2)}, u32[]{:S(2)}) collective-permute-start(f32[2,128,128]{2,1,0:T(8,128)S(1)} %collective-permute-done.13.upper_ref), channel_id=1, source_target_pairs={{2,0},{4,2},{6,4},{8,6},{10,8},{12,10},{14,12},{16,14},{18,16},{20... | collective-permute-start | bytes 393224 | tf_op jit(solution)/shard_map/ppermute | solution.py:24
  60.6 15.7 %collective-permute-start.19 = (f32[4,128,256]{2,1,0:T(8,128)S(1)}, f32[4,128,256]{2,1,0:T(8,128)S(1)}, u32[]{:S(2)}, u32[]{:S(2)}) collective-permute-start(f32[4,128,256]{2,1,0:T(8,128)S(1)} %get-tuple-element.72), channel_id=1, source_target_pairs={{30,0},{0,2},{2,4},{4,6},{6,8},{8,10},{10,12},{12,14},{14,16},{16,... | collective-permute-start | bytes 1572872 | tf_op jit(solution)/shard_map/ppermute | solution.py:24
  61.2 12.3 %collective-permute-start.20 = (f32[2,128,128]{2,1,0:T(8,128)S(1)}, f32[2,128,128]{2,1,0:T(8,128)S(1)}, u32[]{:S(2)}, u32[]{:S(2)}) collective-permute-start(f32[2,128,128]{2,1,0:T(8,128)S(1)} %get-tuple-element.74), channel_id=1, source_target_pairs={{30,0},{0,2},{2,4},{4,6},{6,8},{8,10},{10,12},{12,14},{14,16},{16,... | collective-permute-start | bytes 393224 | tf_op jit(solution)/shard_map/ppermute | solution.py:24
  61.2 13.7 %collective-permute-start.22 = (f32[2,128,128]{2,1,0:T(8,128)S(1)}, f32[2,128,128]{2,1,0:T(8,128)S(1)}, u32[]{:S(2)}, u32[]{:S(2)}) collective-permute-start(f32[2,128,128]{2,1,0:T(8,128)S(1)} %get-tuple-element.76), channel_id=1, source_target_pairs={{30,0},{0,2},{2,4},{4,6},{6,8},{8,10},{10,12},{12,14},{14,16},{16,... | collective-permute-start | bytes 393224 | tf_op jit(solution)/shard_map/ppermute | solution.py:24
  62.4 14.0 %collective-permute-start.24 = (f32[2,128,128]{2,1,0:T(8,128)S(1)}, f32[2,128,128]{2,1,0:T(8,128)S(1)}, u32[]{:S(2)}, u32[]{:S(2)}) collective-permute-start(f32[2,128,128]{2,1,0:T(8,128)S(1)} %get-tuple-element.77), channel_id=1, source_target_pairs={{1,0},{0,1},{3,2},{2,3},{5,4},{4,5},{7,6},{6,7},{9,8},{8,9},{11,10... | collective-permute-start | bytes 393224 | tf_op jit(solution)/shard_map/ppermute | solution.py:24
  62.9 13.4 %collective-permute-start.25 = (f32[2,128,128]{2,1,0:T(8,128)S(1)}, f32[2,128,128]{2,1,0:T(8,128)S(1)}, u32[]{:S(2)}, u32[]{:S(2)}) collective-permute-start(f32[2,128,128]{2,1,0:T(8,128)S(1)} %get-tuple-element.78), channel_id=1, source_target_pairs={{1,0},{0,1},{3,2},{2,3},{5,4},{4,5},{7,6},{6,7},{9,8},{8,9},{11,10... | collective-permute-start | bytes 393224 | tf_op jit(solution)/shard_map/ppermute | solution.py:24
  73.5 5.0 %collective-permute-start.21 = (f32[2,128,128]{2,1,0:T(8,128)S(1)}, f32[2,128,128]{2,1,0:T(8,128)S(1)}, u32[]{:S(2)}, u32[]{:S(2)}) collective-permute-start(f32[2,128,128]{2,1,0:T(8,128)S(1)} %add.16), channel_id=1, source_target_pairs={{1,0},{0,1},{3,2},{2,3},{5,4},{4,5},{7,6},{6,7},{9,8},{8,9},{11,10... | collective-permute-start | bytes 393224 | tf_op jit(solution)/shard_map/ppermute | solution.py:24
  75.0 5.0 %collective-permute-start.23 = (f32[2,128,128]{2,1,0:T(8,128)S(1)}, f32[2,128,128]{2,1,0:T(8,128)S(1)}, u32[]{:S(2)}, u32[]{:S(2)}) collective-permute-start(f32[2,128,128]{2,1,0:T(8,128)S(1)} %add.17), channel_id=1, source_target_pairs={{1,0},{0,1},{3,2},{2,3},{5,4},{4,5},{7,6},{6,7},{9,8},{8,9},{11,10... | collective-permute-start | bytes 393224 | tf_op jit(solution)/shard_map/ppermute | solution.py:24

commit v3 on v2

--- a/solution.py
+++ b/solution.py
@@ -89,9 +89,18 @@
                 ext_ref[c, col // LANES + b, row:row + height, :] = source[c, :, b * LANES:(b + 1) * LANES]
 
 
-def place(scalar_ref, j):
-    col = scalar_ref[0, 2 * j + 1]
-    return scalar_ref[0, 2 * j], col // LANES, col % LANES
+def pick(numbers_ref, k):
+    values = numbers_ref[...].astype(jnp.float32)
+    lane = lax.broadcasted_iota(jnp.int32, values.shape, 1)
+    return jnp.sum(jnp.where(lane == k, values, 0.0)).astype(jnp.int32)
+
+
+def places(numbers_ref, spots):
+    spot_list = []
+    for j in range(spots):
+        row, col = pick(numbers_ref, 2 * j), pick(numbers_ref, 2 * j + 1)
+        spot_list.append((row, col // LANES, col % LANES))
+    return spot_list
 
 
 def window(ext_ref, c, spot, width, lane):
@@ -221,8 +230,8 @@
         enter_ref[j, 1] = probe_ref[0] * imag + probe_ref[1] * real
 
 
-def residual_end(scalar_ref, spots, spot_list, ext_ref, moved_ref, win_ref, back_ref, width, lane):
-    total = scalar_ref[0, 2 * spots]
+def residual_end(numbers_ref, spots, spot_list, ext_ref, moved_ref, win_ref, back_ref, width, lane):
+    total = pick(numbers_ref, 2 * spots)
 
     def finish(j, real, imag):
         used = j < total
@@ -238,26 +247,23 @@
     numbers_ref, tile_ref, below_ref, upper_ref, lower_ref, corner_ref,
     cos_ref, sin_ref, probe_ref, amp_ref, table_ref,
     own_ref, down_ref, up_out_ref, low_out_ref, diag_ref, back_ref,
-    ext_ref, other_ref, grad_ref, win_ref, moved_ref, scalar_ref, scalar_sem, *, spots, width,
-):
-    fetched = pltpu.make_async_copy(numbers_ref, scalar_ref, scalar_sem)
-    fetched.start()
+    ext_ref, other_ref, grad_ref, win_ref, moved_ref, *, spots, width,
+):
     lane = lanes_of(width)
     tile_px = own_ref.shape[1]
     halo = (tile_ref, below_ref, upper_ref, lower_ref, corner_ref)
     fill_ext(ext_ref, whole_pieces(halo, 0, tile_px, width))
     fill_ext(other_ref, whole_pieces(halo, 1, tile_px, width))
     grad_ref[...] = jnp.zeros(grad_ref.shape, jnp.float32)
-    fetched.wait()
-    spot_list = [place(scalar_ref, j) for j in range(spots)]
+    spot_list = places(numbers_ref, spots)
     light(ext_ref, spot_list, probe_ref, back_ref, width, lane)
     take_windows(other_ref, spot_list, win_ref, width, lane)
-    finish = residual_end(scalar_ref, spots, spot_list, grad_ref, moved_ref, win_ref, back_ref, width, lane)
+    finish = residual_end(numbers_ref, spots, spot_list, grad_ref, moved_ref, win_ref, back_ref, width, lane)
     interleave([
         joined(
             forward_steps(group, back_ref, moved_ref, cos_ref, sin_ref, table_ref, width),
             residual_steps(
-                group, moved_ref, win_ref, lambda j: amp_ref[scalar_ref[0, 2 * spots + 1 + j]],
+                group, moved_ref, win_ref, lambda j: amp_ref[pick(numbers_ref, 2 * spots + 1 + j)],
                 finish, table_ref, width,
             ),
         )
@@ -268,15 +274,12 @@
 
 def forward_kernel(
     numbers_ref, rest_ref, quad_ref, left_ref, right_ref, upper_ref, lower_ref, corner_ref,
-    cos_ref, sin_ref, probe_ref, table_ref, moved_ref, ext_ref, enter_ref, scalar_ref, scalar_sem, *, spots, width,
-):
-    fetched = pltpu.make_async_copy(numbers_ref, scalar_ref, scalar_sem)
-    fetched.start()
+    cos_ref, sin_ref, probe_ref, table_ref, moved_ref, ext_ref, enter_ref, *, spots, width,
+):
     lane = lanes_of(width)
     halo = (rest_ref, quad_ref, left_ref, right_ref, upper_ref, lower_ref, corner_ref)
     fill_ext(ext_ref, slice_pieces(halo, 0, rest_ref.shape[1], width))
-    fetched.wait()
-    spot_list = [place(scalar_ref, j) for j in range(spots)]
+    spot_list = places(numbers_ref, spots)
     light(ext_ref, spot_list, probe_ref, enter_ref, width, lane)
     interleave([
         forward_steps(group, enter_ref, moved_ref, cos_ref, sin_ref, table_ref, width)
@@ -288,21 +291,18 @@
     numbers_ref, rest_ref, quad_ref, left_ref, right_ref, upper_ref, lower_ref, corner_ref,
     moved_ref, amp_ref, table_ref,
     own_ref, down_ref, up_out_ref, low_out_ref, diag_ref, back_ref,
-    ext_ref, grad_ref, win_ref, scalar_ref, scalar_sem, *, spots, width,
-):
-    fetched = pltpu.make_async_copy(numbers_ref, scalar_ref, scalar_sem)
-    fetched.start()
+    ext_ref, grad_ref, win_ref, *, spots, width,
+):
     lane = lanes_of(width)
     halo = (rest_ref, quad_ref, left_ref, right_ref, upper_ref, lower_ref, corner_ref)
     fill_ext(ext_ref, slice_pieces(halo, 1, rest_ref.shape[1], width))
     grad_ref[...] = jnp.zeros(grad_ref.shape, jnp.float32)
-    fetched.wait()
-    spot_list = [place(scalar_ref, j) for j in range(spots)]
+    spot_list = places(numbers_ref, spots)
     take_windows(ext_ref, spot_list, win_ref, width, lane)
-    finish = residual_end(scalar_ref, spots, spot_list, grad_ref, moved_ref, win_ref, back_ref, width, lane)
+    finish = residual_end(numbers_ref, spots, spot_list, grad_ref, moved_ref, win_ref, back_ref, width, lane)
     interleave([
         residual_steps(
-            group, moved_ref, win_ref, lambda j: amp_ref[scalar_ref[0, 2 * spots + 1 + j]],
+            group, moved_ref, win_ref, lambda j: amp_ref[pick(numbers_ref, 2 * spots + 1 + j)],
             finish, table_ref, width,
         )
         for group in groups_of(spots)
@@ -312,13 +312,12 @@
 
 def backward_kernel(
     numbers_ref, back_ref, other_down_ref, cos_ref, sin_ref, probe_ref, table_ref,
-    own_ref, down_ref, up_out_ref, low_out_ref, diag_ref, ext_ref, scalar_ref, scalar_sem, *, spots, width,
-):
-    fetched = pltpu.make_async_copy(numbers_ref, scalar_ref, scalar_sem)
-    fetched.start()
+    own_ref, down_ref, up_out_ref, low_out_ref, diag_ref, ext_ref, *, spots, width,
+):
     lane = lanes_of(width)
     down_ref[2:] = other_down_ref[...]
-    waiting = [fetched]
+    spot_list = places(numbers_ref, spots)
+    total = pick(numbers_ref, 2 * spots)
     ext_ref[...] = jnp.zeros(ext_ref.shape, jnp.float32)
 
     def chain(group):
@@ -333,12 +332,9 @@
         yield True
         pairs = left_side(half, table_ref, width)
         yield True
-        while waiting:
-            waiting.pop().wait()
-        total = scalar_ref[0, 2 * spots]
         for j, (real, negative) in zip(group, pairs):
             imag = -negative
-            spot = place(scalar_ref, j)
+            spot = spot_list[j]
             used = j < total
             scatter(ext_ref, 0, spot, width, lane, used, probe_ref[0] * real + probe_ref[1] * imag)
             scatter(ext_ref, 1, spot, width, lane, used, probe_ref[0] * imag - probe_ref[1] * real)
@@ -398,33 +394,23 @@
             left_ref[2 * s + c] = value
 
 
-def finish_rest_kernel(
-    rest_one, rest_two, own_one, own_two, above_ref, low_one, low_two, out_ref, tile_ref, sem, *, width,
-):
-    parts = ((rest_one, own_one, low_one), (rest_two, own_two, low_two))
-    for s, (rest_ref, own_ref, low_ref) in enumerate(parts):
+def finish_kernel(
+    rest_one, rest_two, quad_one, quad_two, own_one, own_two, above_ref, low_one, low_two, up_one, up_two,
+    out_ref, tile_ref, sems, *, width,
+):
+    parts = ((rest_one, quad_one, own_one, low_one, up_one), (rest_two, quad_two, own_two, low_two, up_two))
+    copies = []
+    for s in (1, 0):
+        rest_ref, quad_ref, own_ref, low_ref, up_ref = parts[s]
         above = above_ref.at[pl.ds(2 * s, 2)]
         for c in range(2):
             for rows, lanes, value in rest_values(rest_ref, own_ref, above, low_ref, c, width):
                 tile_ref[s, c, rows, lanes] = value
-            tile_ref[s, c, :width, :width] = jnp.zeros((width, width), jnp.float32)
-    copy = pltpu.make_async_copy(tile_ref, out_ref, sem)
-    copy.start()
-    copy.wait()
-
-
-def finish_quad_kernel(
-    quad_one, quad_two, own_one, own_two, above_ref, up_one, up_two, part_ref, out_ref, quads_ref, sem, *, width,
-):
-    del part_ref
-    parts = ((quad_one, own_one, up_one), (quad_two, own_two, up_two))
-    for s, (quad_ref, own_ref, up_ref) in enumerate(parts):
-        above = above_ref.at[pl.ds(2 * s, 2)]
-        for c in range(2):
-            quads_ref[s, c] = quad_value(quad_ref, own_ref, above, up_ref, c, width)
-    copy = pltpu.make_async_copy(quads_ref, out_ref.at[:, :, pl.ds(0, width), pl.ds(0, width)], sem)
-    copy.start()
-    copy.wait()
+            tile_ref[s, c, :width, :width] = quad_value(quad_ref, own_ref, above, up_ref, c, width)
+            copies.append(pltpu.make_async_copy(tile_ref.at[s, c], out_ref.at[s, c], sems.at[len(copies)]))
+            copies[-1].start()
+    for copy in copies:
+        copy.wait()
 
 
 def stage_kernel(*refs):
@@ -438,9 +424,7 @@
 
 
 F32 = functools.partial(jax.ShapeDtypeStruct, dtype=jnp.float32)
-SMEM = pl.BlockSpec(memory_space=pltpu.SMEM)
 VMEM = pl.BlockSpec(memory_space=pltpu.VMEM)
-SCALAR_SPACE = (pltpu.SMEM((1, LANES), jnp.int32), pltpu.SemaphoreType.DMA(()))
 LIMIT = pltpu.CompilerParams(vmem_limit_bytes=16 * 1024 * 1024)
 
 
@@ -453,25 +437,33 @@
         in_specs=[VMEM] * (len(scalars) + len(arrays)),
         out_specs=[VMEM] * len(outs),
         out_shape=outs,
-        scratch_shapes=[*scratch, *(SCALAR_SPACE if scalars else ())],
+        scratch_shapes=scratch,
         compiler_params=LIMIT,
     )(*scalars, *arrays)
 
 
-def pack_kernel(whole_ref, up_ref, low_ref, top_ref, sems, *, width):
-    tile_px = whole_ref.shape[2]
-    left = pl.ds(0, width)
+def pack_kernel(whole_ref, *refs, boxes):
+    outs, sems = refs[:-1], refs[-1]
     copies = []
-    for s in range(2):
-        both = pl.ds(2 * s, 2)
-        copies.append((whole_ref.at[s, :, pl.ds(0, width), left], up_ref.at[both]))
-        copies.append((whole_ref.at[s, :, pl.ds(width, tile_px - width), left], low_ref.at[both]))
-        copies.append((whole_ref.at[s, :, pl.ds(0, width), :], top_ref.at[both]))
-    copies = [pltpu.make_async_copy(a, b, sems.at[k]) for k, (a, b) in enumerate(copies)]
+    for (rows, lanes), out_ref in zip(boxes, outs):
+        for s in range(2):
+            source = whole_ref.at[s, :, pl.ds(*rows), pl.ds(*lanes)]
+            copies.append(pltpu.make_async_copy(source, out_ref.at[pl.ds(2 * s, 2)], sems.at[len(copies)]))
     for copy in copies:
         copy.start()
     for copy in copies:
         copy.wait()
+
+
+def pack(whole, boxes):
+    return pl.pallas_call(
+        functools.partial(pack_kernel, boxes=boxes),
+        in_specs=[FAR],
+        out_specs=[VMEM] * len(boxes),
+        out_shape=[F32((4, rows[1], lanes[1])) for rows, lanes in boxes],
+        scratch_shapes=[pltpu.SemaphoreType.DMA((2 * len(boxes),))],
+        compiler_params=LIMIT,
+    )(in_hbm(whole))
 
 
 def in_hbm(array):
@@ -506,16 +498,9 @@
     strip = F32((2, width, tile_px))
     gradient = [whole, strip, square, square, square]
 
-    left_up, left_low, top = pl.pallas_call(
-        functools.partial(pack_kernel, width=width),
-        in_specs=[FAR],
-        out_specs=[VMEM] * 3,
-        out_shape=[squares, squares, F32((4, width, tile_px))],
-        scratch_shapes=[pltpu.SemaphoreType.DMA((6,))],
-        compiler_params=LIMIT,
-        name="pack",
-    )(in_hbm(specimen_slices))
+    (left_up,) = pack(specimen_slices, [((0, width), (0, width))])
     upper = from_behind(left_up, "col", -1)
+    left_low, top = pack(specimen_slices, [((width, across), (0, width)), ((0, width), (0, tile_px))])
     lower = from_behind(left_low, "col", -1)
     below = from_behind(top, "row", -1)
     far = (specimen_slices, illumination_probe, amplitudes[0, 0], jnp.asarray(dft_operands(width)))
@@ -585,29 +570,20 @@
                 (rest_two, quad_two, below_left, below_right, upper_two, lower_two, corner_two),
             )
         else:
-            part = pl.pallas_call(
-                functools.partial(finish_rest_kernel, width=width),
-                in_specs=[VMEM] * 7,
+            updated = pl.pallas_call(
+                functools.partial(finish_kernel, width=width),
+                in_specs=[VMEM] * 11,
                 out_specs=FAR,
                 out_shape=F32(specimen_slices.shape),
                 scratch_shapes=[
-                    pltpu.VMEM(specimen_slices.shape, jnp.float32), pltpu.SemaphoreType.DMA(()),
+                    pltpu.VMEM(specimen_slices.shape, jnp.float32), pltpu.SemaphoreType.DMA((4,)),
                 ],
                 compiler_params=LIMIT,
-                name="finish_rest",
-            )(rest_one, rest_two, own_one, own_two, above, low_one, low_two)
-            updated = pl.pallas_call(
-                functools.partial(finish_quad_kernel, width=width),
-                in_specs=[VMEM] * 7 + [FAR],
-                out_specs=FAR,
-                out_shape=F32(specimen_slices.shape),
-                input_output_aliases={7: 0},
-                scratch_shapes=[
-                    pltpu.VMEM((2, 2, width, width), jnp.float32), pltpu.SemaphoreType.DMA(()),
-                ],
-                compiler_params=LIMIT,
-                name="finish_quad",
-            )(quad_one, quad_two, own_one, own_two, above, up_one, up_two, in_hbm(part))
+                name="finish",
+            )(
+                rest_one, rest_two, quad_one, quad_two, own_one, own_two, above,
+                low_one, low_two, up_one, up_two,
+            )
     return updated
 
 

time: 81 us -> 80 us (0.988)
  waiting for transfers between devices: 30.4 us -> 32.3 us
  starting transfers between devices: 31 us -> 29.4 us
  Pallas kernels: 17.4 us -> 16 us
    ppermute x26, waiting for transfers between devices: 30.4 us -> 32.3 us  [from_behind(): return lax.ppermute(block, axis, route)]
    ppermute x26, starting transfers between devices: 31 us -> 29.4 us  [from_behind(): return lax.ppermute(block, axis, route)]
    pallas_call x8, Pallas kernels: 12.7 us -> 11.3 us  [call(): pl.pallas_call(functools.partial(kernel, **static), in_specs=[VMEM] * (le...]
  transfers between devices with their start and end apart: 26 -> 26, of which waited for: 13 -> 14; matrix products, arithmetic and copies ran while one was open for 1% -> 1% of each run, Pallas kernels for 6% -> 6%
where the time goes in v3:
time: 80 us; the launch traced here: 79.8 us
  waiting for transfers between devices  32.3 us (40%)
  starting transfers between devices  29.4 us (37%)
  Pallas kernels  16 us (20%)
  local copies, waits for them, and re-layouts  1.09 us (1%)
  between operations  0.81 us (1%)
    ppermute x26, waiting for transfers between devices, from_behind(): return lax.ppermute(block, axis, route)  32.3 us
    ppermute x26, starting transfers between devices, from_behind(): return lax.ppermute(block, axis, route)  29.4 us
    pallas_call x8, Pallas kernels, call(): pl.pallas_call(functools.partial(kernel, **static), in_specs=[VMEM] * (le...  11.3 us
    pallas_call x2, Pallas kernels, pack(): pl.pallas_call(functools.partial(pack_kernel, boxes=boxes), in_specs=[FAR...  2.19 us
  transfers between devices with their start and end apart: 26, of which 14 were waited for; matrix products, arithmetic and copies ran while one was open for 1% of the time, Pallas kernels for 6%

profile of v3, /device:TPU:0, one launch (start us, length us, event | category | flops | bytes accessed | tf_op | source)
XLA Modules:
  0.0 79.8 jit_solution(12856840414508518922)
XLA Ops:
  0.0 1.0 %shard_map.83 = f32[4,128,128]{2,1,0:T(8,128)S(1)} custom-call(f32[2,2,256,256]{3,2,1,0:T(8,128)} %whole_ref.3), custom_call_target="tpu_custom_call" | custom-call | tf_op jit(solution)/shard_map/pallas_call | solution.py:459
  1.0 3.0 %collective-permute-start.1 = (f32[4,128,128]{2,1,0:T(8,128)S(1)}, f32[4,128,128]{2,1,0:T(8,128)S(1)}, u32[]{:S(2)}, u32[]{:S(2)}) collective-permute-start(f32[4,128,128]{2,1,0:T(8,128)S(1)} %shard_map.83), channel_id=1, source_target_pairs={{1,0},{0,1},{3,2},{2,3},{5,4},{4,5},{7,6},{6,7},{9,8},{8,9},{11,10... | collective-permute-start | bytes 786440 | tf_op jit(solution)/shard_map/ppermute | solution.py:24
  4.0 1.2 %shard_map.82 = (f32[4,128,128]{2,1,0:T(8,128)S(1)}, f32[4,128,256]{2,1,0:T(8,128)S(1)}) custom-call(f32[2,2,256,256]{3,2,1,0:T(8,128)} %whole_ref.3), custom_call_target="tpu_custom_call" | custom-call | tf_op jit(solution)/shard_map/pallas_call | solution.py:459
  5.2 3.8 %collective-permute-start = (f32[4,128,256]{2,1,0:T(8,128)S(1)}, f32[4,128,256]{2,1,0:T(8,128)S(1)}, u32[]{:S(2)}, u32[]{:S(2)}) collective-permute-start(f32[4,128,256]{2,1,0:T(8,128)S(1)} %get-tuple-element.42), channel_id=1, source_target_pairs={{2,0},{4,2},{6,4},{8,6},{10,8},{12,10},{14,12},{16,14},{18,16},{20... | collective-permute-start | bytes 1572872 | tf_op jit(solution)/shard_map/ppermute | solution.py:24
  11.2 2.5 %collective-permute-start.3 = (f32[4,128,128]{2,1,0:T(8,128)S(1)}, f32[4,128,128]{2,1,0:T(8,128)S(1)}, u32[]{:S(2)}, u32[]{:S(2)}) collective-permute-start(f32[4,128,128]{2,1,0:T(8,128)S(1)} %collective-permute-done.1.upper_ref), channel_id=1, source_target_pairs={{2,0},{4,2},{6,4},{8,6},{10,8},{12,10},{14,12},{16,14},{18,16},{20... | collective-permute-start | bytes 786440 | tf_op jit(solution)/shard_map/ppermute | solution.py:24
  13.7 1.5 %stage.1 = (f32[2,2,256,256]{3,2,1,0:T(8,128)S(1)}, f32[2,128,128]{2,1,0:T(8,128)S(1)}, f32[4,128,128]{2,1,0:T(8,128)S(1)}, bf16[4,256,256]{2,1,0:T(8,128)(2,1)S(1)}) custom-call(f32[2,2,256,256]{3,2,1,0:T(8,128)} %whole_ref.3, f32[2,128,128]{2,1,0:T(8,128)} %refs_1_.1, f32[4,128,128]{2,1,0:T(8,128)} %bitcast.6, bf16[4,256,256]{2,1,0:T(8,128)(2,1)} %constant.4.clone.refs_3_), custom_call_target="tpu_custom_call" | custom-call | tf_op jit(solution)/shard_map/stage/pallas_call | solution.py:507
  16.0 2.6 %collective-permute-done.3.corner_ref = f32[4,128,128]{2,1,0:T(8,128)S(1)} collective-permute-done((f32[4,128,128]{2,1,0:T(8,128)S(1)}, f32[4,128,128]{2,1,0:T(8,128)S(1)}, u32[]{:S(2)}, u32[]{:S(2)}) %collective-permute-start.3) | collective-permute-done | bytes 262176 | tf_op jit(solution)/shard_map/ppermute | solution.py:24
  18.5 3.5 %shard_map.84 = (f32[2,256,256]{2,1,0:T(8,128)S(1)}, f32[2,128,256]{2,1,0:T(8,128)S(1)}, f32[2,128,128]{2,1,0:T(8,128)S(1)}, f32[2,128,128]{2,1,0:T(8,128)S(1)},...) custom-call(s32[1,128]{1,0:T(1,128)S(1)} %pad_bitcast_fusion.numbers_ref, ...), custom_call_target="tpu_custom_call" | custom-call | tf_op jit(solution)/shard_map/pallas_call | solution.py:435
  22.0 1.9 %shard_map.85 = (f32[2,256,256]{2,1,0:T(8,128)S(1)}, f32[4,128,256]{2,1,0:T(8,128)S(1)}, f32[2,128,128]{2,1,0:T(8,128)S(1)}, f32[2,128,128]{2,1,0:T(8,128)S(1)}, f32[2,128,128]{2,1,0:T(8,128)S(1)}) custom-call(s32[1,128]{1,0:T(1,128)S(1)} %pad_bitcast_fusion.numbers_ref, f32[4,2,128,128]{3,2,1,0:T(8,128)S(1)} %get-tuple-element.47.back_ref, ...), custom_call_target="tpu_custom_call" | custom-call | tf_op jit(solution)/shard_map/pallas_call | solution.py:435
  24.4 1.5 %collective-permute-start.6 = (f32[2,128,128]{2,1,0:T(8,128)S(1)}, f32[2,128,128]{2,1,0:T(8,128)S(1)}, u32[]{:S(2)}, u32[]{:S(2)}) collective-permute-start(f32[2,128,128]{2,1,0:T(8,128)S(1)} %get-tuple-element.53), channel_id=1, source_target_pairs={{1,0},{0,1},{3,2},{2,3},{5,4},{4,5},{7,6},{6,7},{9,8},{8,9},{11,10... | collective-permute-start | bytes 393224 | tf_op jit(solution)/shard_map/ppermute | solution.py:24
  26.5 10.3 %collective-permute-done.9 = f32[2,128,128]{2,1,0:T(8,128)S(1)} collective-permute-done((f32[2,128,128]{2,1,0:T(8,128)S(1)}, f32[2,128,128]{2,1,0:T(8,128)S(1)}, u32[]{:S(2)}, u32[]{:S(2)}) %collective-permute-start.9) | collective-permute-done | bytes 131104 | tf_op jit(solution)/shard_map/ppermute | solution.py:24
  38.2 0.8 collective-permute-start.8
  39.0 1.4 %collective-permute-start.17 = (f32[2,128,128]{2,1,0:T(8,128)S(1)}, f32[2,128,128]{2,1,0:T(8,128)S(1)}, u32[]{:S(2)}, u32[]{:S(2)}) collective-permute-start(f32[2,128,128]{2,1,0:T(8,128)S(1)} %get-tuple-element.65), channel_id=1, source_target_pairs={{1,0},{0,1},{3,2},{2,3},{5,4},{4,5},{7,6},{6,7},{9,8},{8,9},{11,10... | collective-permute-start | bytes 393224 | tf_op jit(solution)/shard_map/ppermute | solution.py:24
  40.4 1.5 %collective-permute-done.10.up_two = f32[2,128,128]{2,1,0:T(8,128)S(1)} collective-permute-done((f32[2,128,128]{2,1,0:T(8,128)S(1)}, f32[2,128,128]{2,1,0:T(8,128)S(1)}, u32[]{:S(2)}, u32[]{:S(2)}) %collective-permute-start.10) | collective-permute-done | bytes 131104 | tf_op jit(solution)/shard_map/ppermute | solution.py:24
  41.9 1.4 %collective-permute-done.8.up_one = f32[2,128,128]{2,1,0:T(8,128)S(1)} collective-permute-done((f32[2,128,128]{2,1,0:T(8,128)S(1)}, f32[2,128,128]{2,1,0:T(8,128)S(1)}, u32[]{:S(2)}, u32[]{:S(2)}) %collective-permute-start.8) | collective-permute-done | bytes 131104 | tf_op jit(solution)/shard_map/ppermute | solution.py:24
  43.4 1.5 %collective-permute-start.16 = (f32[2,128,128]{2,1,0:T(8,128)S(1)}, f32[2,128,128]{2,1,0:T(8,128)S(1)}, u32[]{:S(2)}, u32[]{:S(2)}) collective-permute-start(f32[2,128,128]{2,1,0:T(8,128)S(1)} %get-tuple-element.60.quad_ref.quad_one), channel_id=1, source_target_pairs={{1,0},{0,1},{3,2},{2,3},{5,4},{4,5},{7,6},{6,7},{9,8},{8,9},{11,10... | collective-permute-start | bytes 393224 | tf_op jit(solution)/shard_map/ppermute | solution.py:24
  45.2 2.0 %collective-permute-start.11 = (f32[4,128,128]{2,1,0:T(8,128)S(1)}, f32[4,128,128]{2,1,0:T(8,128)S(1)}, u32[]{:S(2)}, u32[]{:S(2)}) collective-permute-start(f32[4,128,128]{2,1,0:T(8,128)S(1)} %get-tuple-element.62), channel_id=1, source_target_pairs={{2,0},{4,2},{6,4},{8,6},{10,8},{12,10},{14,12},{16,14},{18,16},{20... | collective-permute-start | bytes 786440 | tf_op jit(solution)/shard_map/ppermute | solution.py:24
  47.2 0.7 collective-permute-start.13
  48.6 2.4 %collective-permute-start.14 = (f32[2,128,128]{2,1,0:T(8,128)S(1)}, f32[2,128,128]{2,1,0:T(8,128)S(1)}, u32[]{:S(2)}, u32[]{:S(2)}) collective-permute-start(f32[2,128,128]{2,1,0:T(8,128)S(1)} %get-tuple-element.64), channel_id=1, source_target_pairs={{1,0},{0,1},{3,2},{2,3},{5,4},{4,5},{7,6},{6,7},{9,8},{8,9},{11,10... | collective-permute-start | bytes 393224 | tf_op jit(solution)/shard_map/ppermute | solution.py:24
  51.0 1.2 %collective-permute-done.13.upper_ref = f32[2,128,128]{2,1,0:T(8,128)S(1)} collective-permute-done((f32[2,128,128]{2,1,0:T(8,128)S(1)}, f32[2,128,128]{2,1,0:T(8,128)S(1)}, u32[]{:S(2)}, u32[]{:S(2)}) %collective-permute-start.13) | collective-permute-done | bytes 131104 | tf_op jit(solution)/shard_map/ppermute | solution.py:24
  53.3 1.8 %shard_map.89.moved_ref = f32[4,2,128,128]{3,2,1,0:T(8,128)S(1)} custom-call(s32[1,128]{1,0:T(1,128)S(1)} %pad_bitcast_fusion.numbers_ref, f32[2,256,256]{2,1,0:T(8,128)S(1)} %get-tuple-element.54.rest_ref.rest_one, f32[2,128,128]{2,1,0:T(8,128)S(1)} %get-tuple-element.60.quad_ref.quad_one, f32[4,128,128]{2,1,0:T(8,128)S(1)} %collective-permute-done.11.left_ref, ...), custom_call_target="tpu_custom_call" | custom-call | tf_op jit(solution)/shard_map/pallas_call | solution.py:435
  55.1 2.1 %shard_map.90 = (f32[2,256,256]{2,1,0:T(8,128)S(1)}, f32[2,128,256]{2,1,0:T(8,128)S(1)}, f32[2,128,128]{2,1,0:T(8,128)S(1)}, f32[2,128,128]{2,1,0:T(8,128)S(1)},...) custom-call(s32[1,128]{1,0:T(1,128)S(1)} %pad_bitcast_fusion.numbers_ref, ...), custom_call_target="tpu_custom_call" | custom-call | tf_op jit(solution)/shard_map/pallas_call | solution.py:435
  57.2 1.9 %shard_map.91 = (f32[2,256,256]{2,1,0:T(8,128)S(1)}, f32[4,128,256]{2,1,0:T(8,128)S(1)}, f32[2,128,128]{2,1,0:T(8,128)S(1)}, f32[2,128,128]{2,1,0:T(8,128)S(1)}, f32[2,128,128]{2,1,0:T(8,128)S(1)}) custom-call(s32[1,128]{1,0:T(1,128)S(1)} %pad_bitcast_fusion.numbers_ref, f32[4,2,128,128]{3,2,1,0:T(8,128)S(1)} %get-tuple-element.66.back_ref, ...), custom_call_target="tpu_custom_call" | custom-call | tf_op jit(solution)/shard_map/pallas_call | solution.py:435
  59.1 0.8 %collective-permute-start.19 = (f32[4,128,256]{2,1,0:T(8,128)S(1)}, f32[4,128,256]{2,1,0:T(8,128)S(1)}, u32[]{:S(2)}, u32[]{:S(2)}) collective-permute-start(f32[4,128,256]{2,1,0:T(8,128)S(1)} %get-tuple-element.70), channel_id=1, source_target_pairs={{30,0},{0,2},{2,4},{4,6},{6,8},{8,10},{10,12},{12,14},{14,16},{16,... | collective-permute-start | bytes 1572872 | tf_op jit(solution)/shard_map/ppermute | solution.py:24
  60.0 1.0 %collective-permute-start.24 = (f32[2,128,128]{2,1,0:T(8,128)S(1)}, f32[2,128,128]{2,1,0:T(8,128)S(1)}, u32[]{:S(2)}, u32[]{:S(2)}) collective-permute-start(f32[2,128,128]{2,1,0:T(8,128)S(1)} %get-tuple-element.76), channel_id=1, source_target_pairs={{30,0},{0,2},{2,4},{4,6},{6,8},{8,10},{10,12},{12,14},{14,16},{16,... | collective-permute-start | bytes 393224 | tf_op jit(solution)/shard_map/ppermute | solution.py:24
  61.4 1.5 %collective-permute-start.21 = (f32[2,128,128]{2,1,0:T(8,128)S(1)}, f32[2,128,128]{2,1,0:T(8,128)S(1)}, u32[]{:S(2)}, u32[]{:S(2)}) collective-permute-start(f32[2,128,128]{2,1,0:T(8,128)S(1)} %get-tuple-element.72), channel_id=1, source_target_pairs={{1,0},{0,1},{3,2},{2,3},{5,4},{4,5},{7,6},{6,7},{9,8},{8,9},{11,10... | collective-permute-start | bytes 393224 | tf_op jit(solution)/shard_map/ppermute | solution.py:24
  62.9 9.0 %collective-permute-done.22 = f32[2,128,128]{2,1,0:T(8,128)S(1)} collective-permute-done((f32[2,128,128]{2,1,0:T(8,128)S(1)}, f32[2,128,128]{2,1,0:T(8,128)S(1)}, u32[]{:S(2)}, u32[]{:S(2)}) %collective-permute-start.22) | collective-permute-done | bytes 131104 | tf_op jit(solution)/shard_map/ppermute | solution.py:24
  72.0 1.7 %collective-permute-start.23 = (f32[2,128,128]{2,1,0:T(8,128)S(1)}, f32[2,128,128]{2,1,0:T(8,128)S(1)}, u32[]{:S(2)}, u32[]{:S(2)}) collective-permute-start(f32[2,128,128]{2,1,0:T(8,128)S(1)} %add.16), channel_id=1, source_target_pairs={{1,0},{0,1},{3,2},{2,3},{5,4},{4,5},{7,6},{6,7},{9,8},{8,9},{11,10... | collective-permute-start | bytes 393224 | tf_op jit(solution)/shard_map/ppermute | solution.py:24
  73.7 1.4 %collective-permute-start.25 = (f32[2,128,128]{2,1,0:T(8,128)S(1)}, f32[2,128,128]{2,1,0:T(8,128)S(1)}, u32[]{:S(2)}, u32[]{:S(2)}) collective-permute-start(f32[2,128,128]{2,1,0:T(8,128)S(1)} %add.17), channel_id=1, source_target_pairs={{1,0},{0,1},{3,2},{2,3},{5,4},{4,5},{7,6},{6,7},{9,8},{8,9},{11,10... | collective-permute-start | bytes 393224 | tf_op jit(solution)/shard_map/ppermute | solution.py:24
  75.1 1.9 %collective-permute-done.23.up_one = f32[2,128,128]{2,1,0:T(8,128)S(1)} collective-permute-done((f32[2,128,128]{2,1,0:T(8,128)S(1)}, f32[2,128,128]{2,1,0:T(8,128)S(1)}, u32[]{:S(2)}, u32[]{:S(2)}) %collective-permute-start.23) | collective-permute-done | bytes 131104 | tf_op jit(solution)/shard_map/ppermute | solution.py:24
  77.0 1.7 %collective-permute-done.25.up_two = f32[2,128,128]{2,1,0:T(8,128)S(1)} collective-permute-done((f32[2,128,128]{2,1,0:T(8,128)S(1)}, f32[2,128,128]{2,1,0:T(8,128)S(1)}, u32[]{:S(2)}, u32[]{:S(2)}) %collective-permute-start.25) | collective-permute-done | bytes 131104 | tf_op jit(solution)/shard_map/ppermute | solution.py:24
  78.7 1.1 %finish.1 = f32[2,2,256,256]{3,2,1,0:T(8,128)} custom-call(f32[2,256,256]{2,1,0:T(8,128)S(1)} %get-tuple-element.54.rest_ref.rest_one, f32[2,256,256]{2,1,0:T(8,128)S(1)} %get-tuple-element.55.rest_ref.rest_two, f32[2,128,128]{2,1,0:T(8,128)S(1)} %get-tuple-element.60.quad_ref.quad_one, f32[2,128,128]{2,1,0:T(8,128)S(1)} %get-tuple-element.61.quad_ref.quad_two, ...), custom_call_target="tpu_custom_call" | custom-call | tf_op jit(solution)/shard_map/finish/pallas_call | solution.py:573
  (47 shorter events, 7.4 us)
Async XLA Ops:
  1.0 10.2 %collective-permute-start.1 = (f32[4,128,128]{2,1,0:T(8,128)S(1)}, f32[4,128,128]{2,1,0:T(8,128)S(1)}, u32[]{:S(2)}, u32[]{:S(2)}) collective-permute-start(f32[4,128,128]{2,1,0:T(8,128)S(1)} %shard_map.83), channel_id=1, source_target_pairs={{1,0},{0,1},{3,2},{2,3},{5,4},{4,5},{7,6},{6,7},{9,8},{8,9},{11,10... | collective-permute-start | bytes 786440 | tf_op jit(solution)/shard_map/ppermute | solution.py:24
  5.2 13.3 %collective-permute-start = (f32[4,128,256]{2,1,0:T(8,128)S(1)}, f32[4,128,256]{2,1,0:T(8,128)S(1)}, u32[]{:S(2)}, u32[]{:S(2)}) collective-permute-start(f32[4,128,256]{2,1,0:T(8,128)S(1)} %get-tuple-element.42), channel_id=1, source_target_pairs={{2,0},{4,2},{6,4},{8,6},{10,8},{12,10},{14,12},{16,14},{18,16},{20... | collective-permute-start | bytes 1572872 | tf_op jit(solution)/shard_map/ppermute | solution.py:24
  9.0 1.2 %copy-start.1 = (s32[1,1,4,2]{2,3,1,0:T(2,128)S(1)}, s32[1,1,4,2]{2,3,1,0:T(2,128)}, u32[]{:S(2)}) copy-start(s32[1,1,4,2]{2,3,1,0:T(2,128)} %param.12) | copy-start | bytes 100
  9.0 6.9 %collective-permute-start.2 = (f32[4,128,128]{2,1,0:T(8,128)S(1)}, f32[4,128,128]{2,1,0:T(8,128)S(1)}, u32[]{:S(2)}, u32[]{:S(2)}) collective-permute-start(f32[4,128,128]{2,1,0:T(8,128)S(1)} %get-tuple-element.43), channel_id=1, source_target_pairs={{1,0},{0,1},{3,2},{2,3},{5,4},{4,5},{7,6},{6,7},{9,8},{8,9},{11,10... | collective-permute-start | bytes 786440 | tf_op jit(solution)/shard_map/ppermute | solution.py:24
  10.4 0.7 copy-start.2
  11.2 7.3 %collective-permute-start.3 = (f32[4,128,128]{2,1,0:T(8,128)S(1)}, f32[4,128,128]{2,1,0:T(8,128)S(1)}, u32[]{:S(2)}, u32[]{:S(2)}) collective-permute-start(f32[4,128,128]{2,1,0:T(8,128)S(1)} %collective-permute-done.1.upper_ref), channel_id=1, source_target_pairs={{2,0},{4,2},{6,4},{8,6},{10,8},{12,10},{14,12},{16,14},{18,16},{20... | collective-permute-start | bytes 786440 | tf_op jit(solution)/shard_map/ppermute | solution.py:24
  13.7 1.6 %copy-start = (f32[128,128]{1,0:T(8,128)S(1)}, f32[128,128]{1,0:T(8,128)}, u32[]{:S(2)}) copy-start(f32[128,128]{1,0:T(8,128)} %param.10) | copy-start | bytes 196612
  23.9 19.5 %collective-permute-start.4 = (f32[4,128,256]{2,1,0:T(8,128)S(1)}, f32[4,128,256]{2,1,0:T(8,128)S(1)}, u32[]{:S(2)}, u32[]{:S(2)}) collective-permute-start(f32[4,128,256]{2,1,0:T(8,128)S(1)} %get-tuple-element.51), channel_id=1, source_target_pairs={{30,0},{0,2},{2,4},{4,6},{6,8},{8,10},{10,12},{12,14},{14,16},{16,... | collective-permute-start | bytes 1572872 | tf_op jit(solution)/shard_map/ppermute | solution.py:24
  23.9 12.9 %collective-permute-start.9 = (f32[2,128,128]{2,1,0:T(8,128)S(1)}, f32[2,128,128]{2,1,0:T(8,128)S(1)}, u32[]{:S(2)}, u32[]{:S(2)}) collective-permute-start(f32[2,128,128]{2,1,0:T(8,128)S(1)} %get-tuple-element.59), channel_id=1, source_target_pairs={{30,0},{0,2},{2,4},{4,6},{6,8},{8,10},{10,12},{12,14},{14,16},{16,... | collective-permute-start | bytes 393224 | tf_op jit(solution)/shard_map/ppermute | solution.py:24
  24.0 14.2 %collective-permute-start.7 = (f32[2,128,128]{2,1,0:T(8,128)S(1)}, f32[2,128,128]{2,1,0:T(8,128)S(1)}, u32[]{:S(2)}, u32[]{:S(2)}) collective-permute-start(f32[2,128,128]{2,1,0:T(8,128)S(1)} %get-tuple-element.57), channel_id=1, source_target_pairs={{30,0},{0,2},{2,4},{4,6},{6,8},{8,10},{10,12},{12,14},{14,16},{16,... | collective-permute-start | bytes 393224 | tf_op jit(solution)/shard_map/ppermute | solution.py:24
  24.4 14.5 %collective-permute-start.6 = (f32[2,128,128]{2,1,0:T(8,128)S(1)}, f32[2,128,128]{2,1,0:T(8,128)S(1)}, u32[]{:S(2)}, u32[]{:S(2)}) collective-permute-start(f32[2,128,128]{2,1,0:T(8,128)S(1)} %get-tuple-element.53), channel_id=1, source_target_pairs={{1,0},{0,1},{3,2},{2,3},{5,4},{4,5},{7,6},{6,7},{9,8},{8,9},{11,10... | collective-permute-start | bytes 393224 | tf_op jit(solution)/shard_map/ppermute | solution.py:24
  25.9 13.0 %collective-permute-start.5 = (f32[2,128,128]{2,1,0:T(8,128)S(1)}, f32[2,128,128]{2,1,0:T(8,128)S(1)}, u32[]{:S(2)}, u32[]{:S(2)}) collective-permute-start(f32[2,128,128]{2,1,0:T(8,128)S(1)} %get-tuple-element.52), channel_id=1, source_target_pairs={{1,0},{0,1},{3,2},{2,3},{5,4},{4,5},{7,6},{6,7},{9,8},{8,9},{11,10... | collective-permute-start | bytes 393224 | tf_op jit(solution)/shard_map/ppermute | solution.py:24
  36.8 5.1 %collective-permute-start.10 = (f32[2,128,128]{2,1,0:T(8,128)S(1)}, f32[2,128,128]{2,1,0:T(8,128)S(1)}, u32[]{:S(2)}, u32[]{:S(2)}) collective-permute-start(f32[2,128,128]{2,1,0:T(8,128)S(1)} %add.15), channel_id=1, source_target_pairs={{1,0},{0,1},{3,2},{2,3},{5,4},{4,5},{7,6},{6,7},{9,8},{8,9},{11,10... | collective-permute-start | bytes 393224 | tf_op jit(solution)/shard_map/ppermute | solution.py:24
  38.2 5.1 %collective-permute-start.8 = (f32[2,128,128]{2,1,0:T(8,128)S(1)}, f32[2,128,128]{2,1,0:T(8,128)S(1)}, u32[]{:S(2)}, u32[]{:S(2)}) collective-permute-start(f32[2,128,128]{2,1,0:T(8,128)S(1)} %add.14), channel_id=1, source_target_pairs={{1,0},{0,1},{3,2},{2,3},{5,4},{4,5},{7,6},{6,7},{9,8},{8,9},{11,10... | collective-permute-start | bytes 393224 | tf_op jit(solution)/shard_map/ppermute | solution.py:24
  39.0 9.5 %collective-permute-start.17 = (f32[2,128,128]{2,1,0:T(8,128)S(1)}, f32[2,128,128]{2,1,0:T(8,128)S(1)}, u32[]{:S(2)}, u32[]{:S(2)}) collective-permute-start(f32[2,128,128]{2,1,0:T(8,128)S(1)} %get-tuple-element.65), channel_id=1, source_target_pairs={{1,0},{0,1},{3,2},{2,3},{5,4},{4,5},{7,6},{6,7},{9,8},{8,9},{11,10... | collective-permute-start | bytes 393224 | tf_op jit(solution)/shard_map/ppermute | solution.py:24
  43.4 5.2 %collective-permute-start.16 = (f32[2,128,128]{2,1,0:T(8,128)S(1)}, f32[2,128,128]{2,1,0:T(8,128)S(1)}, u32[]{:S(2)}, u32[]{:S(2)}) collective-permute-start(f32[2,128,128]{2,1,0:T(8,128)S(1)} %get-tuple-element.60.quad_ref.quad_one), channel_id=1, source_target_pairs={{1,0},{0,1},{3,2},{2,3},{5,4},{4,5},{7,6},{6,7},{9,8},{8,9},{11,10... | collective-permute-start | bytes 393224 | tf_op jit(solution)/shard_map/ppermute | solution.py:24
  45.1 8.2 %collective-permute-start.12 = (f32[4,128,128]{2,1,0:T(8,128)S(1)}, f32[4,128,128]{2,1,0:T(8,128)S(1)}, u32[]{:S(2)}, u32[]{:S(2)}) collective-permute-start(f32[4,128,128]{2,1,0:T(8,128)S(1)} %get-tuple-element.63), channel_id=1, source_target_pairs={{2,0},{4,2},{6,4},{8,6},{10,8},{12,10},{14,12},{16,14},{18,16},{20... | collective-permute-start | bytes 786440 | tf_op jit(solution)/shard_map/ppermute | solution.py:24
  45.2 8.1 %collective-permute-start.11 = (f32[4,128,128]{2,1,0:T(8,128)S(1)}, f32[4,128,128]{2,1,0:T(8,128)S(1)}, u32[]{:S(2)}, u32[]{:S(2)}) collective-permute-start(f32[4,128,128]{2,1,0:T(8,128)S(1)} %get-tuple-element.62), channel_id=1, source_target_pairs={{2,0},{4,2},{6,4},{8,6},{10,8},{12,10},{14,12},{16,14},{18,16},{20... | collective-permute-start | bytes 786440 | tf_op jit(solution)/shard_map/ppermute | solution.py:24
  47.2 5.0 %collective-permute-start.13 = (f32[2,128,128]{2,1,0:T(8,128)S(1)}, f32[2,128,128]{2,1,0:T(8,128)S(1)}, u32[]{:S(2)}, u32[]{:S(2)}) collective-permute-start(f32[2,128,128]{2,1,0:T(8,128)S(1)} %get-tuple-element.61.quad_ref.quad_two), channel_id=1, source_target_pairs={{1,0},{0,1},{3,2},{2,3},{5,4},{4,5},{7,6},{6,7},{9,8},{8,9},{11,10... | collective-permute-start | bytes 393224 | tf_op jit(solution)/shard_map/ppermute | solution.py:24
  48.6 4.7 %collective-permute-start.18 = (f32[2,128,128]{2,1,0:T(8,128)S(1)}, f32[2,128,128]{2,1,0:T(8,128)S(1)}, u32[]{:S(2)}, u32[]{:S(2)}) collective-permute-start(f32[2,128,128]{2,1,0:T(8,128)S(1)} %collective-permute-done.16.upper_ref), channel_id=1, source_target_pairs={{2,0},{4,2},{6,4},{8,6},{10,8},{12,10},{14,12},{16,14},{18,16},{20... | collective-permute-start | bytes 393224 | tf_op jit(solution)/shard_map/ppermute | solution.py:24
  48.6 6.5 %collective-permute-start.14 = (f32[2,128,128]{2,1,0:T(8,128)S(1)}, f32[2,128,128]{2,1,0:T(8,128)S(1)}, u32[]{:S(2)}, u32[]{:S(2)}) collective-permute-start(f32[2,128,128]{2,1,0:T(8,128)S(1)} %get-tuple-element.64), channel_id=1, source_target_pairs={{1,0},{0,1},{3,2},{2,3},{5,4},{4,5},{7,6},{6,7},{9,8},{8,9},{11,10... | collective-permute-start | bytes 393224 | tf_op jit(solution)/shard_map/ppermute | solution.py:24
  52.2 2.9 %collective-permute-start.15 = (f32[2,128,128]{2,1,0:T(8,128)S(1)}, f32[2,128,128]{2,1,0:T(8,128)S(1)}, u32[]{:S(2)}, u32[]{:S(2)}) collective-permute-start(f32[2,128,128]{2,1,0:T(8,128)S(1)} %collective-permute-done.13.upper_ref), channel_id=1, source_target_pairs={{2,0},{4,2},{6,4},{8,6},{10,8},{12,10},{14,12},{16,14},{18,16},{20... | collective-permute-start | bytes 393224 | tf_op jit(solution)/shard_map/ppermute | solution.py:24
  59.1 19.6 %collective-permute-start.19 = (f32[4,128,256]{2,1,0:T(8,128)S(1)}, f32[4,128,256]{2,1,0:T(8,128)S(1)}, u32[]{:S(2)}, u32[]{:S(2)}) collective-permute-start(f32[4,128,256]{2,1,0:T(8,128)S(1)} %get-tuple-element.70), channel_id=1, source_target_pairs={{30,0},{0,2},{2,4},{4,6},{6,8},{8,10},{10,12},{12,14},{14,16},{16,... | collective-permute-start | bytes 1572872 | tf_op jit(solution)/shard_map/ppermute | solution.py:24
  59.9 12.1 %collective-permute-start.22 = (f32[2,128,128]{2,1,0:T(8,128)S(1)}, f32[2,128,128]{2,1,0:T(8,128)S(1)}, u32[]{:S(2)}, u32[]{:S(2)}) collective-permute-start(f32[2,128,128]{2,1,0:T(8,128)S(1)} %get-tuple-element.74), channel_id=1, source_target_pairs={{30,0},{0,2},{2,4},{4,6},{6,8},{8,10},{10,12},{12,14},{14,16},{16,... | collective-permute-start | bytes 393224 | tf_op jit(solution)/shard_map/ppermute | solution.py:24
  60.0 13.7 %collective-permute-start.24 = (f32[2,128,128]{2,1,0:T(8,128)S(1)}, f32[2,128,128]{2,1,0:T(8,128)S(1)}, u32[]{:S(2)}, u32[]{:S(2)}) collective-permute-start(f32[2,128,128]{2,1,0:T(8,128)S(1)} %get-tuple-element.76), channel_id=1, source_target_pairs={{30,0},{0,2},{2,4},{4,6},{6,8},{8,10},{10,12},{12,14},{14,16},{16,... | collective-permute-start | bytes 393224 | tf_op jit(solution)/shard_map/ppermute | solution.py:24
  60.9 14.1 %collective-permute-start.20 = (f32[2,128,128]{2,1,0:T(8,128)S(1)}, f32[2,128,128]{2,1,0:T(8,128)S(1)}, u32[]{:S(2)}, u32[]{:S(2)}) collective-permute-start(f32[2,128,128]{2,1,0:T(8,128)S(1)} %get-tuple-element.71), channel_id=1, source_target_pairs={{1,0},{0,1},{3,2},{2,3},{5,4},{4,5},{7,6},{6,7},{9,8},{8,9},{11,10... | collective-permute-start | bytes 393224 | tf_op jit(solution)/shard_map/ppermute | solution.py:24
  61.4 13.6 %collective-permute-start.21 = (f32[2,128,128]{2,1,0:T(8,128)S(1)}, f32[2,128,128]{2,1,0:T(8,128)S(1)}, u32[]{:S(2)}, u32[]{:S(2)}) collective-permute-start(f32[2,128,128]{2,1,0:T(8,128)S(1)} %get-tuple-element.72), channel_id=1, source_target_pairs={{1,0},{0,1},{3,2},{2,3},{5,4},{4,5},{7,6},{6,7},{9,8},{8,9},{11,10... | collective-permute-start | bytes 393224 | tf_op jit(solution)/shard_map/ppermute | solution.py:24
  72.0 5.0 %collective-permute-start.23 = (f32[2,128,128]{2,1,0:T(8,128)S(1)}, f32[2,128,128]{2,1,0:T(8,128)S(1)}, u32[]{:S(2)}, u32[]{:S(2)}) collective-permute-start(f32[2,128,128]{2,1,0:T(8,128)S(1)} %add.16), channel_id=1, source_target_pairs={{1,0},{0,1},{3,2},{2,3},{5,4},{4,5},{7,6},{6,7},{9,8},{8,9},{11,10... | collective-permute-start | bytes 393224 | tf_op jit(solution)/shard_map/ppermute | solution.py:24
  73.7 5.0 %collective-permute-start.25 = (f32[2,128,128]{2,1,0:T(8,128)S(1)}, f32[2,128,128]{2,1,0:T(8,128)S(1)}, u32[]{:S(2)}, u32[]{:S(2)}) collective-permute-start(f32[2,128,128]{2,1,0:T(8,128)S(1)} %add.17), channel_id=1, source_target_pairs={{1,0},{0,1},{3,2},{2,3},{5,4},{4,5},{7,6},{6,7},{9,8},{8,9},{11,10... | collective-permute-start | bytes 393224 | tf_op jit(solution)/shard_map/ppermute | solution.py:24

commit v4 on v3

--- a/solution.py
+++ b/solution.py
@@ -194,9 +194,9 @@
     return [
         (0, 0, tile_ref.at[s]),
         (tile_px, 0, below_ref.at[both]),
-        (0, tile_px, upper_ref.at[both]),
+        (0, tile_px, upper_ref),
         (width, tile_px, lower_ref.at[both]),
-        (tile_px, tile_px, corner_ref.at[both]),
+        (tile_px, tile_px, corner_ref),
     ]
 
 
@@ -244,16 +244,17 @@
 
 
 def wave_kernel(
-    numbers_ref, tile_ref, below_ref, upper_ref, lower_ref, corner_ref,
+    numbers_ref, tile_ref, below_ref, upper_one, upper_two, lower_ref, corner_one, corner_two,
     cos_ref, sin_ref, probe_ref, amp_ref, table_ref,
     own_ref, down_ref, up_out_ref, low_out_ref, diag_ref, back_ref,
     ext_ref, other_ref, grad_ref, win_ref, moved_ref, *, spots, width,
 ):
     lane = lanes_of(width)
     tile_px = own_ref.shape[1]
-    halo = (tile_ref, below_ref, upper_ref, lower_ref, corner_ref)
-    fill_ext(ext_ref, whole_pieces(halo, 0, tile_px, width))
-    fill_ext(other_ref, whole_pieces(halo, 1, tile_px, width))
+    first = (tile_ref, below_ref, upper_one, lower_ref, corner_one)
+    second = (tile_ref, below_ref, upper_two, lower_ref, corner_two)
+    fill_ext(ext_ref, whole_pieces(first, 0, tile_px, width))
+    fill_ext(other_ref, whole_pieces(second, 1, tile_px, width))
     grad_ref[...] = jnp.zeros(grad_ref.shape, jnp.float32)
     spot_list = places(numbers_ref, spots)
     light(ext_ref, spot_list, probe_ref, back_ref, width, lane)
@@ -348,10 +349,14 @@
 
 
 def rest_values(tile_ref, own_ref, above_ref, lower_ref, c, width):
+    top, right = slice(0, width), slice(width, own_ref.shape[1])
+    yield top, right, step(tile_ref[c, top, right], own_ref[c, top, right] + above_ref[c, :, right])
+    yield from low_values(tile_ref, own_ref, lower_ref, c, width)
+
+
+def low_values(tile_ref, own_ref, lower_ref, c, width):
     tile_px = own_ref.shape[1]
-    top, low = slice(0, width), slice(width, tile_px)
-    left, right = slice(0, width), slice(width, tile_px)
-    yield top, right, step(tile_ref[c, top, right], own_ref[c, top, right] + above_ref[c, :, right])
+    low, left, right = slice(width, tile_px), slice(0, width), slice(width, tile_px)
     yield low, left, step(tile_ref[c, low, left], own_ref[c, low, left] + lower_ref[c])
     yield low, right, step(tile_ref[c, low, right], own_ref[c, low, right])
 
@@ -394,23 +399,35 @@
             left_ref[2 * s + c] = value
 
 
-def finish_kernel(
-    rest_one, rest_two, quad_one, quad_two, own_one, own_two, above_ref, low_one, low_two, up_one, up_two,
-    out_ref, tile_ref, sems, *, width,
-):
-    parts = ((rest_one, quad_one, own_one, low_one, up_one), (rest_two, quad_two, own_two, low_two, up_two))
-    copies = []
-    for s in (1, 0):
-        rest_ref, quad_ref, own_ref, low_ref, up_ref = parts[s]
+def finish_low_kernel(
+    rest_one, rest_two, own_one, own_two, low_one, low_two, out_ref, rows_ref, sem, *, width,
+):
+    tile_px = own_one.shape[1]
+    for s, (rest_ref, own_ref, low_ref) in enumerate(((rest_one, own_one, low_one), (rest_two, own_two, low_two))):
+        for c in range(2):
+            for _, lanes, value in low_values(rest_ref, own_ref, low_ref, c, width):
+                rows_ref[s, c, :, lanes] = value
+    copy = pltpu.make_async_copy(rows_ref, out_ref.at[:, :, pl.ds(width, tile_px - width), :], sem)
+    copy.start()
+    copy.wait()
+
+
+def finish_top_kernel(
+    rest_one, rest_two, quad_one, quad_two, own_one, own_two, above_ref, up_one, up_two, part_ref,
+    out_ref, rows_ref, sem, *, width,
+):
+    del part_ref
+    tile_px = own_one.shape[1]
+    parts = ((rest_one, quad_one, own_one, up_one), (rest_two, quad_two, own_two, up_two))
+    for s, (rest_ref, quad_ref, own_ref, up_ref) in enumerate(parts):
         above = above_ref.at[pl.ds(2 * s, 2)]
         for c in range(2):
-            for rows, lanes, value in rest_values(rest_ref, own_ref, above, low_ref, c, width):
-                tile_ref[s, c, rows, lanes] = value
-            tile_ref[s, c, :width, :width] = quad_value(quad_ref, own_ref, above, up_ref, c, width)
-            copies.append(pltpu.make_async_copy(tile_ref.at[s, c], out_ref.at[s, c], sems.at[len(copies)]))
-            copies[-1].start()
-    for copy in copies:
-        copy.wait()
+            top, right = slice(0, width), slice(width, tile_px)
+            rows_ref[s, c, :, :width] = quad_value(quad_ref, own_ref, above, up_ref, c, width)
+            rows_ref[s, c, :, width:] = step(rest_ref[c, top, right], own_ref[c, top, right] + above[c, :, right])
+    copy = pltpu.make_async_copy(rows_ref, out_ref.at[:, :, pl.ds(0, width), :], sem)
+    copy.start()
+    copy.wait()
 
 
 def stage_kernel(*refs):
@@ -445,10 +462,10 @@
 def pack_kernel(whole_ref, *refs, boxes):
     outs, sems = refs[:-1], refs[-1]
     copies = []
-    for (rows, lanes), out_ref in zip(boxes, outs):
-        for s in range(2):
+    for (slices, rows, lanes), out_ref in zip(boxes, outs):
+        for k, s in enumerate(slices):
             source = whole_ref.at[s, :, pl.ds(*rows), pl.ds(*lanes)]
-            copies.append(pltpu.make_async_copy(source, out_ref.at[pl.ds(2 * s, 2)], sems.at[len(copies)]))
+            copies.append(pltpu.make_async_copy(source, out_ref.at[pl.ds(2 * k, 2)], sems.at[len(copies)]))
     for copy in copies:
         copy.start()
     for copy in copies:
@@ -456,12 +473,13 @@
 
 
 def pack(whole, boxes):
+    count = sum(len(slices) for slices, _, _ in boxes)
     return pl.pallas_call(
         functools.partial(pack_kernel, boxes=boxes),
         in_specs=[FAR],
         out_specs=[VMEM] * len(boxes),
-        out_shape=[F32((4, rows[1], lanes[1])) for rows, lanes in boxes],
-        scratch_shapes=[pltpu.SemaphoreType.DMA((2 * len(boxes),))],
+        out_shape=[F32((2 * len(slices), rows[1], lanes[1])) for slices, rows, lanes in boxes],
+        scratch_shapes=[pltpu.SemaphoreType.DMA((count,))],
         compiler_params=LIMIT,
     )(in_hbm(whole))
 
@@ -498,9 +516,11 @@
     strip = F32((2, width, tile_px))
     gradient = [whole, strip, square, square, square]
 
-    (left_up,) = pack(specimen_slices, [((0, width), (0, width))])
-    upper = from_behind(left_up, "col", -1)
-    left_low, top = pack(specimen_slices, [((width, across), (0, width)), ((0, width), (0, tile_px))])
+    left, low, full = (0, width), (width, across), (0, tile_px)
+    up_one, up_two = pack(specimen_slices, [((0,), left, left), ((1,), left, left)])
+    upper_one = from_behind(up_one, "col", -1)
+    upper_two = from_behind(up_two, "col", -1)
+    left_low, top = pack(specimen_slices, [((0, 1), low, left), ((0, 1), left, full)])
     lower = from_behind(left_low, "col", -1)
     below = from_behind(top, "row", -1)
     far = (specimen_slices, illumination_probe, amplitudes[0, 0], jnp.asarray(dft_operands(width)))
@@ -513,12 +533,13 @@
         compiler_params=LIMIT,
         name="stage",
     )(*[in_hbm(x) for x in far])
-    corner = from_behind(upper, "row", -1)
+    corner_one = from_behind(upper_one, "row", -1)
+    corner_two = from_behind(upper_two, "row", -1)
     for i in range(ITERS):
         if i == 0:
             own_two, down_two, up_two, low_two, diag_two, back = call(
                 wave_kernel, scalars,
-                (tile, below, upper, lower, corner, cos, sin, probe, measured, table),
+                (tile, below, upper_one, upper_two, lower, corner_one, corner_two, cos, sin, probe, measured, table),
                 [*gradient, wave], [ext_space, ext_space, ext_space, wave_space, wave_space], **static,
             )
         else:
@@ -570,19 +591,31 @@
                 (rest_two, quad_two, below_left, below_right, upper_two, lower_two, corner_two),
             )
         else:
-            updated = pl.pallas_call(
-                functools.partial(finish_kernel, width=width),
-                in_specs=[VMEM] * 11,
+            end = dict(
                 out_specs=FAR,
                 out_shape=F32(specimen_slices.shape),
+                compiler_params=LIMIT,
+            )
+            part = pl.pallas_call(
+                functools.partial(finish_low_kernel, width=width),
+                in_specs=[VMEM] * 6,
                 scratch_shapes=[
-                    pltpu.VMEM(specimen_slices.shape, jnp.float32), pltpu.SemaphoreType.DMA((4,)),
+                    pltpu.VMEM((2, 2, across, tile_px), jnp.float32), pltpu.SemaphoreType.DMA(()),
                 ],
-                compiler_params=LIMIT,
-                name="finish",
+                name="finish_low",
+                **end,
+            )(rest_one, rest_two, own_one, own_two, low_one, low_two)
+            updated = pl.pallas_call(
+                functools.partial(finish_top_kernel, width=width),
+                in_specs=[VMEM] * 9 + [FAR],
+                input_output_aliases={9: 0},
+                scratch_shapes=[
+                    pltpu.VMEM((2, 2, width, tile_px), jnp.float32), pltpu.SemaphoreType.DMA(()),
+                ],
+                name="finish_top",
+                **end,
             )(
-                rest_one, rest_two, quad_one, quad_two, own_one, own_two, above,
-                low_one, low_two, up_one, up_two,
+                rest_one, rest_two, quad_one, quad_two, own_one, own_two, above, up_one, up_two, in_hbm(part),
             )
     return updated
 

time: 80 us -> 81.8 us (1.022)
  starting transfers between devices: 29.4 us -> 30.3 us
    ppermute x26 -> x28, starting transfers between devices: 29.4 us -> 30.3 us  [from_behind(): return lax.ppermute(block, axis, route)]
    pallas_call x1 -> x2, Pallas kernels: 1.05 us -> 1.8 us  [the longest x1 0.92 us: body(): pl.pallas_call(functools.partial(finish_top_kernel, width=width), in_spec...]
    ppermute x26 -> x28, waiting for transfers between devices: 32.3 us -> 32.4 us  [from_behind(): return lax.ppermute(block, axis, route)]
  transfers between devices with their start and end apart: 26 -> 28, of which waited for: 14 -> 14; matrix products, arithmetic and copies ran while one was open for 1% -> 1% of each run, Pallas kernels for 6% -> 7%
where the time goes in v4:
time: 81.8 us; the launch traced here: 81.6 us
  waiting for transfers between devices  32.4 us (40%)
  starting transfers between devices  30.3 us (37%)
  Pallas kernels  16.8 us (21%)
  local copies, waits for them, and re-layouts  1.1 us (1%)
  between operations  0.84 us (1%)
    ppermute x28, waiting for transfers between devices, from_behind(): return lax.ppermute(block, axis, route)  32.4 us
    ppermute x28, starting transfers between devices, from_behind(): return lax.ppermute(block, axis, route)  30.3 us
    pallas_call x8, Pallas kernels, call(): pl.pallas_call(functools.partial(kernel, **static), in_specs=[VMEM] * (le...  11.3 us
    pallas_call x2, Pallas kernels, pack(): pl.pallas_call(functools.partial(pack_kernel, boxes=boxes), in_specs=[FAR...  2.19 us
  transfers between devices with their start and end apart: 28, of which 14 were waited for; matrix products, arithmetic and copies ran while one was open for 1% of the time, Pallas kernels for 7%

profile of v4, /device:TPU:0, one launch (start us, length us, event | category | flops | bytes accessed | tf_op | source)
XLA Modules:
  0.0 81.6 jit_solution(16627291228967924555)
XLA Ops:
  0.0 1.2 %shard_map.82 = (f32[4,128,128]{2,1,0:T(8,128)S(1)}, f32[4,128,256]{2,1,0:T(8,128)S(1)}) custom-call(f32[2,2,256,256]{3,2,1,0:T(8,128)} %whole_ref.3), custom_call_target="tpu_custom_call" | custom-call | tf_op jit(solution)/shard_map/pallas_call | solution.py:477
  1.2 5.5 %collective-permute-start = (f32[4,128,256]{2,1,0:T(8,128)S(1)}, f32[4,128,256]{2,1,0:T(8,128)S(1)}, u32[]{:S(2)}, u32[]{:S(2)}) collective-permute-start(f32[4,128,256]{2,1,0:T(8,128)S(1)} %get-tuple-element.44), channel_id=1, source_target_pairs={{2,0},{4,2},{6,4},{8,6},{10,8},{12,10},{14,12},{16,14},{18,16},{20... | collective-permute-start | bytes 1572872 | tf_op jit(solution)/shard_map/ppermute | solution.py:24
  6.7 1.0 %shard_map.83 = (f32[2,128,128]{2,1,0:T(8,128)S(1)}, f32[2,128,128]{2,1,0:T(8,128)S(1)}) custom-call(f32[2,2,256,256]{3,2,1,0:T(8,128)} %whole_ref.3), custom_call_target="tpu_custom_call" | custom-call | tf_op jit(solution)/shard_map/pallas_call | solution.py:477
  7.7 1.6 %collective-permute-start.1 = (f32[2,128,128]{2,1,0:T(8,128)S(1)}, f32[2,128,128]{2,1,0:T(8,128)S(1)}, u32[]{:S(2)}, u32[]{:S(2)}) collective-permute-start(f32[2,128,128]{2,1,0:T(8,128)S(1)} %get-tuple-element.45), channel_id=1, source_target_pairs={{1,0},{0,1},{3,2},{2,3},{5,4},{4,5},{7,6},{6,7},{9,8},{8,9},{11,10... | collective-permute-start | bytes 393224 | tf_op jit(solution)/shard_map/ppermute | solution.py:24
  9.8 1.5 %collective-permute-start.3 = (f32[4,128,128]{2,1,0:T(8,128)S(1)}, f32[4,128,128]{2,1,0:T(8,128)S(1)}, u32[]{:S(2)}, u32[]{:S(2)}) collective-permute-start(f32[4,128,128]{2,1,0:T(8,128)S(1)} %get-tuple-element.47), channel_id=1, source_target_pairs={{1,0},{0,1},{3,2},{2,3},{5,4},{4,5},{7,6},{6,7},{9,8},{8,9},{11,10... | collective-permute-start | bytes 786440 | tf_op jit(solution)/shard_map/ppermute | solution.py:24
  12.4 1.3 %collective-permute-done.1.upper_one = f32[2,128,128]{2,1,0:T(8,128)S(1)} collective-permute-done((f32[2,128,128]{2,1,0:T(8,128)S(1)}, f32[2,128,128]{2,1,0:T(8,128)S(1)}, u32[]{:S(2)}, u32[]{:S(2)}) %collective-permute-start.1) | collective-permute-done | bytes 131104 | tf_op jit(solution)/shard_map/ppermute | solution.py:24
  13.7 1.4 %collective-permute-done.2.upper_two = f32[2,128,128]{2,1,0:T(8,128)S(1)} collective-permute-done((f32[2,128,128]{2,1,0:T(8,128)S(1)}, f32[2,128,128]{2,1,0:T(8,128)S(1)}, u32[]{:S(2)}, u32[]{:S(2)}) %collective-permute-start.2) | collective-permute-done | bytes 131104 | tf_op jit(solution)/shard_map/ppermute | solution.py:24
  15.1 1.2 %collective-permute-start.5 = (f32[2,128,128]{2,1,0:T(8,128)S(1)}, f32[2,128,128]{2,1,0:T(8,128)S(1)}, u32[]{:S(2)}, u32[]{:S(2)}) collective-permute-start(f32[2,128,128]{2,1,0:T(8,128)S(1)} %collective-permute-done.2.upper_two), channel_id=1, source_target_pairs={{2,0},{4,2},{6,4},{8,6},{10,8},{12,10},{14,12},{16,14},{18,16},{20... | collective-permute-start | bytes 393224 | tf_op jit(solution)/shard_map/ppermute | solution.py:24
  17.1 1.5 %stage.1 = (f32[2,2,256,256]{3,2,1,0:T(8,128)S(1)}, f32[2,128,128]{2,1,0:T(8,128)S(1)}, f32[4,128,128]{2,1,0:T(8,128)S(1)}, bf16[4,256,256]{2,1,0:T(8,128)(2,1)S(1)}) custom-call(f32[2,2,256,256]{3,2,1,0:T(8,128)} %whole_ref.3, f32[2,128,128]{2,1,0:T(8,128)} %refs_1_.1, f32[4,128,128]{2,1,0:T(8,128)} %bitcast.6, bf16[4,256,256]{2,1,0:T(8,128)(2,1)} %constant.4.clone.refs_3_), custom_call_target="tpu_custom_call" | custom-call | tf_op jit(solution)/shard_map/stage/pallas_call | solution.py:527
  18.9 3.5 %shard_map.84 = (f32[2,256,256]{2,1,0:T(8,128)S(1)}, f32[2,128,256]{2,1,0:T(8,128)S(1)}, f32[2,128,128]{2,1,0:T(8,128)S(1)}, f32[2,128,128]{2,1,0:T(8,128)S(1)},...) custom-call(s32[1,128]{1,0:T(1,128)S(1)} %pad_bitcast_fusion.numbers_ref, ...), custom_call_target="tpu_custom_call" | custom-call | tf_op jit(solution)/shard_map/pallas_call | solution.py:452
  22.3 1.9 %shard_map.85 = (f32[2,256,256]{2,1,0:T(8,128)S(1)}, f32[4,128,256]{2,1,0:T(8,128)S(1)}, f32[2,128,128]{2,1,0:T(8,128)S(1)}, f32[2,128,128]{2,1,0:T(8,128)S(1)}, f32[2,128,128]{2,1,0:T(8,128)S(1)}) custom-call(s32[1,128]{1,0:T(1,128)S(1)} %pad_bitcast_fusion.numbers_ref, f32[4,2,128,128]{3,2,1,0:T(8,128)S(1)} %get-tuple-element.51.back_ref, ...), custom_call_target="tpu_custom_call" | custom-call | tf_op jit(solution)/shard_map/pallas_call | solution.py:452
  24.3 0.9 %collective-permute-start.11 = (f32[2,128,128]{2,1,0:T(8,128)S(1)}, f32[2,128,128]{2,1,0:T(8,128)S(1)}, u32[]{:S(2)}, u32[]{:S(2)}) collective-permute-start(f32[2,128,128]{2,1,0:T(8,128)S(1)} %get-tuple-element.63), channel_id=1, source_target_pairs={{30,0},{0,2},{2,4},{4,6},{6,8},{8,10},{10,12},{12,14},{14,16},{16,... | collective-permute-start | bytes 393224 | tf_op jit(solution)/shard_map/ppermute | solution.py:24
  25.3 1.5 %collective-permute-start.8 = (f32[2,128,128]{2,1,0:T(8,128)S(1)}, f32[2,128,128]{2,1,0:T(8,128)S(1)}, u32[]{:S(2)}, u32[]{:S(2)}) collective-permute-start(f32[2,128,128]{2,1,0:T(8,128)S(1)} %get-tuple-element.57), channel_id=1, source_target_pairs={{1,0},{0,1},{3,2},{2,3},{5,4},{4,5},{7,6},{6,7},{9,8},{8,9},{11,10... | collective-permute-start | bytes 393224 | tf_op jit(solution)/shard_map/ppermute | solution.py:24
  27.3 9.8 %collective-permute-done.11 = f32[2,128,128]{2,1,0:T(8,128)S(1)} collective-permute-done((f32[2,128,128]{2,1,0:T(8,128)S(1)}, f32[2,128,128]{2,1,0:T(8,128)S(1)}, u32[]{:S(2)}, u32[]{:S(2)}) %collective-permute-start.11) | collective-permute-done | bytes 131104 | tf_op jit(solution)/shard_map/ppermute | solution.py:24
  37.1 1.6 %collective-permute-start.12 = (f32[2,128,128]{2,1,0:T(8,128)S(1)}, f32[2,128,128]{2,1,0:T(8,128)S(1)}, u32[]{:S(2)}, u32[]{:S(2)}) collective-permute-start(f32[2,128,128]{2,1,0:T(8,128)S(1)} %add.15), channel_id=1, source_target_pairs={{1,0},{0,1},{3,2},{2,3},{5,4},{4,5},{7,6},{6,7},{9,8},{8,9},{11,10... | collective-permute-start | bytes 393224 | tf_op jit(solution)/shard_map/ppermute | solution.py:24
  38.7 1.4 %collective-permute-start.10 = (f32[2,128,128]{2,1,0:T(8,128)S(1)}, f32[2,128,128]{2,1,0:T(8,128)S(1)}, u32[]{:S(2)}, u32[]{:S(2)}) collective-permute-start(f32[2,128,128]{2,1,0:T(8,128)S(1)} %add.14), channel_id=1, source_target_pairs={{1,0},{0,1},{3,2},{2,3},{5,4},{4,5},{7,6},{6,7},{9,8},{8,9},{11,10... | collective-permute-start | bytes 393224 | tf_op jit(solution)/shard_map/ppermute | solution.py:24
  40.9 2.3 %collective-permute-done.12.up_two = f32[2,128,128]{2,1,0:T(8,128)S(1)} collective-permute-done((f32[2,128,128]{2,1,0:T(8,128)S(1)}, f32[2,128,128]{2,1,0:T(8,128)S(1)}, u32[]{:S(2)}, u32[]{:S(2)}) %collective-permute-start.12) | collective-permute-done | bytes 131104 | tf_op jit(solution)/shard_map/ppermute | solution.py:24
  43.2 1.8 %collective-permute-done.10.up_one = f32[2,128,128]{2,1,0:T(8,128)S(1)} collective-permute-done((f32[2,128,128]{2,1,0:T(8,128)S(1)}, f32[2,128,128]{2,1,0:T(8,128)S(1)}, u32[]{:S(2)}, u32[]{:S(2)}) %collective-permute-start.10) | collective-permute-done | bytes 131104 | tf_op jit(solution)/shard_map/ppermute | solution.py:24
  45.0 1.6 %collective-permute-start.18 = (f32[2,128,128]{2,1,0:T(8,128)S(1)}, f32[2,128,128]{2,1,0:T(8,128)S(1)}, u32[]{:S(2)}, u32[]{:S(2)}) collective-permute-start(f32[2,128,128]{2,1,0:T(8,128)S(1)} %get-tuple-element.64.quad_ref.quad_one), channel_id=1, source_target_pairs={{1,0},{0,1},{3,2},{2,3},{5,4},{4,5},{7,6},{6,7},{9,8},{8,9},{11,10... | collective-permute-start | bytes 393224 | tf_op jit(solution)/shard_map/ppermute | solution.py:24
  46.8 2.5 %collective-permute-start.14 = (f32[4,128,128]{2,1,0:T(8,128)S(1)}, f32[4,128,128]{2,1,0:T(8,128)S(1)}, u32[]{:S(2)}, u32[]{:S(2)}) collective-permute-start(f32[4,128,128]{2,1,0:T(8,128)S(1)} %get-tuple-element.67), channel_id=1, source_target_pairs={{2,0},{4,2},{6,4},{8,6},{10,8},{12,10},{14,12},{16,14},{18,16},{20... | collective-permute-start | bytes 786440 | tf_op jit(solution)/shard_map/ppermute | solution.py:24
  50.2 2.5 %collective-permute-start.16 = (f32[2,128,128]{2,1,0:T(8,128)S(1)}, f32[2,128,128]{2,1,0:T(8,128)S(1)}, u32[]{:S(2)}, u32[]{:S(2)}) collective-permute-start(f32[2,128,128]{2,1,0:T(8,128)S(1)} %get-tuple-element.68), channel_id=1, source_target_pairs={{1,0},{0,1},{3,2},{2,3},{5,4},{4,5},{7,6},{6,7},{9,8},{8,9},{11,10... | collective-permute-start | bytes 393224 | tf_op jit(solution)/shard_map/ppermute | solution.py:24
  52.7 1.8 %collective-permute-done.15.upper_ref = f32[2,128,128]{2,1,0:T(8,128)S(1)} collective-permute-done((f32[2,128,128]{2,1,0:T(8,128)S(1)}, f32[2,128,128]{2,1,0:T(8,128)S(1)}, u32[]{:S(2)}, u32[]{:S(2)}) %collective-permute-start.15) | collective-permute-done | bytes 131104 | tf_op jit(solution)/shard_map/ppermute | solution.py:24
  54.8 1.8 %shard_map.89.moved_ref = f32[4,2,128,128]{3,2,1,0:T(8,128)S(1)} custom-call(s32[1,128]{1,0:T(1,128)S(1)} %pad_bitcast_fusion.numbers_ref, f32[2,256,256]{2,1,0:T(8,128)S(1)} %get-tuple-element.58.rest_ref.rest_one, f32[2,128,128]{2,1,0:T(8,128)S(1)} %get-tuple-element.64.quad_ref.quad_one, f32[4,128,128]{2,1,0:T(8,128)S(1)} %collective-permute-done.13.left_ref, ...), custom_call_target="tpu_custom_call" | custom-call | tf_op jit(solution)/shard_map/pallas_call | solution.py:452
  57.4 2.1 %shard_map.90 = (f32[2,256,256]{2,1,0:T(8,128)S(1)}, f32[2,128,256]{2,1,0:T(8,128)S(1)}, f32[2,128,128]{2,1,0:T(8,128)S(1)}, f32[2,128,128]{2,1,0:T(8,128)S(1)},...) custom-call(s32[1,128]{1,0:T(1,128)S(1)} %pad_bitcast_fusion.numbers_ref, ...), custom_call_target="tpu_custom_call" | custom-call | tf_op jit(solution)/shard_map/pallas_call | solution.py:452
  59.4 1.9 %shard_map.91 = (f32[2,256,256]{2,1,0:T(8,128)S(1)}, f32[4,128,256]{2,1,0:T(8,128)S(1)}, f32[2,128,128]{2,1,0:T(8,128)S(1)}, f32[2,128,128]{2,1,0:T(8,128)S(1)}, f32[2,128,128]{2,1,0:T(8,128)S(1)}) custom-call(s32[1,128]{1,0:T(1,128)S(1)} %pad_bitcast_fusion.numbers_ref, f32[4,2,128,128]{3,2,1,0:T(8,128)S(1)} %get-tuple-element.70.back_ref, ...), custom_call_target="tpu_custom_call" | custom-call | tf_op jit(solution)/shard_map/pallas_call | solution.py:452
  61.4 1.2 %collective-permute-start.24 = (f32[2,128,128]{2,1,0:T(8,128)S(1)}, f32[2,128,128]{2,1,0:T(8,128)S(1)}, u32[]{:S(2)}, u32[]{:S(2)}) collective-permute-start(f32[2,128,128]{2,1,0:T(8,128)S(1)} %get-tuple-element.78), channel_id=1, source_target_pairs={{30,0},{0,2},{2,4},{4,6},{6,8},{8,10},{10,12},{12,14},{14,16},{16,... | collective-permute-start | bytes 393224 | tf_op jit(solution)/shard_map/ppermute | solution.py:24
  63.2 1.5 %collective-permute-start.27 = (f32[2,128,128]{2,1,0:T(8,128)S(1)}, f32[2,128,128]{2,1,0:T(8,128)S(1)}, u32[]{:S(2)}, u32[]{:S(2)}) collective-permute-start(f32[2,128,128]{2,1,0:T(8,128)S(1)} %get-tuple-element.80), channel_id=1, source_target_pairs={{1,0},{0,1},{3,2},{2,3},{5,4},{4,5},{7,6},{6,7},{9,8},{8,9},{11,10... | collective-permute-start | bytes 393224 | tf_op jit(solution)/shard_map/ppermute | solution.py:24
  64.7 9.5 %collective-permute-done.22 = f32[2,128,128]{2,1,0:T(8,128)S(1)} collective-permute-done((f32[2,128,128]{2,1,0:T(8,128)S(1)}, f32[2,128,128]{2,1,0:T(8,128)S(1)}, u32[]{:S(2)}, u32[]{:S(2)}) %collective-permute-start.22) | collective-permute-done | bytes 131104 | tf_op jit(solution)/shard_map/ppermute | solution.py:24
  74.2 1.2 %collective-permute-start.23 = (f32[2,128,128]{2,1,0:T(8,128)S(1)}, f32[2,128,128]{2,1,0:T(8,128)S(1)}, u32[]{:S(2)}, u32[]{:S(2)}) collective-permute-start(f32[2,128,128]{2,1,0:T(8,128)S(1)} %add.16), channel_id=1, source_target_pairs={{1,0},{0,1},{3,2},{2,3},{5,4},{4,5},{7,6},{6,7},{9,8},{8,9},{11,10... | collective-permute-start | bytes 393224 | tf_op jit(solution)/shard_map/ppermute | solution.py:24
  75.6 1.2 %collective-permute-start.25 = (f32[2,128,128]{2,1,0:T(8,128)S(1)}, f32[2,128,128]{2,1,0:T(8,128)S(1)}, u32[]{:S(2)}, u32[]{:S(2)}) collective-permute-start(f32[2,128,128]{2,1,0:T(8,128)S(1)} %add.17), channel_id=1, source_target_pairs={{1,0},{0,1},{3,2},{2,3},{5,4},{4,5},{7,6},{6,7},{9,8},{8,9},{11,10... | collective-permute-start | bytes 393224 | tf_op jit(solution)/shard_map/ppermute | solution.py:24
  77.7 1.6 %collective-permute-done.23.up_one = f32[2,128,128]{2,1,0:T(8,128)S(1)} collective-permute-done((f32[2,128,128]{2,1,0:T(8,128)S(1)}, f32[2,128,128]{2,1,0:T(8,128)S(1)}, u32[]{:S(2)}, u32[]{:S(2)}) %collective-permute-start.23) | collective-permute-done | bytes 131104 | tf_op jit(solution)/shard_map/ppermute | solution.py:24
  79.2 1.4 %collective-permute-done.25.up_two = f32[2,128,128]{2,1,0:T(8,128)S(1)} collective-permute-done((f32[2,128,128]{2,1,0:T(8,128)S(1)}, f32[2,128,128]{2,1,0:T(8,128)S(1)}, u32[]{:S(2)}, u32[]{:S(2)}) %collective-permute-start.25) | collective-permute-done | bytes 131104 | tf_op jit(solution)/shard_map/ppermute | solution.py:24
  (52 shorter events, 8.4 us)
Async XLA Ops:
  1.2 10.1 %copy-start = (f32[128,128]{1,0:T(8,128)S(1)}, f32[128,128]{1,0:T(8,128)}, u32[]{:S(2)}) copy-start(f32[128,128]{1,0:T(8,128)} %param.10) | copy-start | bytes 196612
  1.2 17.6 %collective-permute-start = (f32[4,128,256]{2,1,0:T(8,128)S(1)}, f32[4,128,256]{2,1,0:T(8,128)S(1)}, u32[]{:S(2)}, u32[]{:S(2)}) collective-permute-start(f32[4,128,256]{2,1,0:T(8,128)S(1)} %get-tuple-element.44), channel_id=1, source_target_pairs={{2,0},{4,2},{6,4},{8,6},{10,8},{12,10},{14,12},{16,14},{18,16},{20... | collective-permute-start | bytes 1572872 | tf_op jit(solution)/shard_map/ppermute | solution.py:24
  7.7 6.0 %collective-permute-start.1 = (f32[2,128,128]{2,1,0:T(8,128)S(1)}, f32[2,128,128]{2,1,0:T(8,128)S(1)}, u32[]{:S(2)}, u32[]{:S(2)}) collective-permute-start(f32[2,128,128]{2,1,0:T(8,128)S(1)} %get-tuple-element.45), channel_id=1, source_target_pairs={{1,0},{0,1},{3,2},{2,3},{5,4},{4,5},{7,6},{6,7},{9,8},{8,9},{11,10... | collective-permute-start | bytes 393224 | tf_op jit(solution)/shard_map/ppermute | solution.py:24
  9.3 5.8 %collective-permute-start.2 = (f32[2,128,128]{2,1,0:T(8,128)S(1)}, f32[2,128,128]{2,1,0:T(8,128)S(1)}, u32[]{:S(2)}, u32[]{:S(2)}) collective-permute-start(f32[2,128,128]{2,1,0:T(8,128)S(1)} %get-tuple-element.46), channel_id=1, source_target_pairs={{1,0},{0,1},{3,2},{2,3},{5,4},{4,5},{7,6},{6,7},{9,8},{8,9},{11,10... | collective-permute-start | bytes 393224 | tf_op jit(solution)/shard_map/ppermute | solution.py:24
  9.8 9.0 %collective-permute-start.3 = (f32[4,128,128]{2,1,0:T(8,128)S(1)}, f32[4,128,128]{2,1,0:T(8,128)S(1)}, u32[]{:S(2)}, u32[]{:S(2)}) collective-permute-start(f32[4,128,128]{2,1,0:T(8,128)S(1)} %get-tuple-element.47), channel_id=1, source_target_pairs={{1,0},{0,1},{3,2},{2,3},{5,4},{4,5},{7,6},{6,7},{9,8},{8,9},{11,10... | collective-permute-start | bytes 786440 | tf_op jit(solution)/shard_map/ppermute | solution.py:24
  11.6 0.7 copy-start.1
  13.7 4.8 %collective-permute-start.4 = (f32[2,128,128]{2,1,0:T(8,128)S(1)}, f32[2,128,128]{2,1,0:T(8,128)S(1)}, u32[]{:S(2)}, u32[]{:S(2)}) collective-permute-start(f32[2,128,128]{2,1,0:T(8,128)S(1)} %collective-permute-done.1.upper_one), channel_id=1, source_target_pairs={{2,0},{4,2},{6,4},{8,6},{10,8},{12,10},{14,12},{16,14},{18,16},{20... | collective-permute-start | bytes 393224 | tf_op jit(solution)/shard_map/ppermute | solution.py:24
  15.1 3.7 %collective-permute-start.5 = (f32[2,128,128]{2,1,0:T(8,128)S(1)}, f32[2,128,128]{2,1,0:T(8,128)S(1)}, u32[]{:S(2)}, u32[]{:S(2)}) collective-permute-start(f32[2,128,128]{2,1,0:T(8,128)S(1)} %collective-permute-done.2.upper_two), channel_id=1, source_target_pairs={{2,0},{4,2},{6,4},{8,6},{10,8},{12,10},{14,12},{16,14},{18,16},{20... | collective-permute-start | bytes 393224 | tf_op jit(solution)/shard_map/ppermute | solution.py:24
  16.3 0.7 copy-start.2
  24.2 20.7 %collective-permute-start.6 = (f32[4,128,256]{2,1,0:T(8,128)S(1)}, f32[4,128,256]{2,1,0:T(8,128)S(1)}, u32[]{:S(2)}, u32[]{:S(2)}) collective-permute-start(f32[4,128,256]{2,1,0:T(8,128)S(1)} %get-tuple-element.55), channel_id=1, source_target_pairs={{30,0},{0,2},{2,4},{4,6},{6,8},{8,10},{10,12},{12,14},{14,16},{16,... | collective-permute-start | bytes 1572872 | tf_op jit(solution)/shard_map/ppermute | solution.py:24
  24.3 12.8 %collective-permute-start.11 = (f32[2,128,128]{2,1,0:T(8,128)S(1)}, f32[2,128,128]{2,1,0:T(8,128)S(1)}, u32[]{:S(2)}, u32[]{:S(2)}) collective-permute-start(f32[2,128,128]{2,1,0:T(8,128)S(1)} %get-tuple-element.63), channel_id=1, source_target_pairs={{30,0},{0,2},{2,4},{4,6},{6,8},{8,10},{10,12},{12,14},{14,16},{16,... | collective-permute-start | bytes 393224 | tf_op jit(solution)/shard_map/ppermute | solution.py:24
  25.2 13.5 %collective-permute-start.9 = (f32[2,128,128]{2,1,0:T(8,128)S(1)}, f32[2,128,128]{2,1,0:T(8,128)S(1)}, u32[]{:S(2)}, u32[]{:S(2)}) collective-permute-start(f32[2,128,128]{2,1,0:T(8,128)S(1)} %get-tuple-element.61), channel_id=1, source_target_pairs={{30,0},{0,2},{2,4},{4,6},{6,8},{8,10},{10,12},{12,14},{14,16},{16,... | collective-permute-start | bytes 393224 | tf_op jit(solution)/shard_map/ppermute | solution.py:24
  25.3 14.8 %collective-permute-start.8 = (f32[2,128,128]{2,1,0:T(8,128)S(1)}, f32[2,128,128]{2,1,0:T(8,128)S(1)}, u32[]{:S(2)}, u32[]{:S(2)}) collective-permute-start(f32[2,128,128]{2,1,0:T(8,128)S(1)} %get-tuple-element.57), channel_id=1, source_target_pairs={{1,0},{0,1},{3,2},{2,3},{5,4},{4,5},{7,6},{6,7},{9,8},{8,9},{11,10... | collective-permute-start | bytes 393224 | tf_op jit(solution)/shard_map/ppermute | solution.py:24
  26.7 13.4 %collective-permute-start.7 = (f32[2,128,128]{2,1,0:T(8,128)S(1)}, f32[2,128,128]{2,1,0:T(8,128)S(1)}, u32[]{:S(2)}, u32[]{:S(2)}) collective-permute-start(f32[2,128,128]{2,1,0:T(8,128)S(1)} %get-tuple-element.56), channel_id=1, source_target_pairs={{1,0},{0,1},{3,2},{2,3},{5,4},{4,5},{7,6},{6,7},{9,8},{8,9},{11,10... | collective-permute-start | bytes 393224 | tf_op jit(solution)/shard_map/ppermute | solution.py:24
  37.1 6.1 %collective-permute-start.12 = (f32[2,128,128]{2,1,0:T(8,128)S(1)}, f32[2,128,128]{2,1,0:T(8,128)S(1)}, u32[]{:S(2)}, u32[]{:S(2)}) collective-permute-start(f32[2,128,128]{2,1,0:T(8,128)S(1)} %add.15), channel_id=1, source_target_pairs={{1,0},{0,1},{3,2},{2,3},{5,4},{4,5},{7,6},{6,7},{9,8},{8,9},{11,10... | collective-permute-start | bytes 393224 | tf_op jit(solution)/shard_map/ppermute | solution.py:24
  38.7 6.2 %collective-permute-start.10 = (f32[2,128,128]{2,1,0:T(8,128)S(1)}, f32[2,128,128]{2,1,0:T(8,128)S(1)}, u32[]{:S(2)}, u32[]{:S(2)}) collective-permute-start(f32[2,128,128]{2,1,0:T(8,128)S(1)} %add.14), channel_id=1, source_target_pairs={{1,0},{0,1},{3,2},{2,3},{5,4},{4,5},{7,6},{6,7},{9,8},{8,9},{11,10... | collective-permute-start | bytes 393224 | tf_op jit(solution)/shard_map/ppermute | solution.py:24
  40.2 10.0 %collective-permute-start.19 = (f32[2,128,128]{2,1,0:T(8,128)S(1)}, f32[2,128,128]{2,1,0:T(8,128)S(1)}, u32[]{:S(2)}, u32[]{:S(2)}) collective-permute-start(f32[2,128,128]{2,1,0:T(8,128)S(1)} %get-tuple-element.69), channel_id=1, source_target_pairs={{1,0},{0,1},{3,2},{2,3},{5,4},{4,5},{7,6},{6,7},{9,8},{8,9},{11,10... | collective-permute-start | bytes 393224 | tf_op jit(solution)/shard_map/ppermute | solution.py:24
  45.0 5.2 %collective-permute-start.18 = (f32[2,128,128]{2,1,0:T(8,128)S(1)}, f32[2,128,128]{2,1,0:T(8,128)S(1)}, u32[]{:S(2)}, u32[]{:S(2)}) collective-permute-start(f32[2,128,128]{2,1,0:T(8,128)S(1)} %get-tuple-element.64.quad_ref.quad_one), channel_id=1, source_target_pairs={{1,0},{0,1},{3,2},{2,3},{5,4},{4,5},{7,6},{6,7},{9,8},{8,9},{11,10... | collective-permute-start | bytes 393224 | tf_op jit(solution)/shard_map/ppermute | solution.py:24
  46.6 8.2 %collective-permute-start.13 = (f32[4,128,128]{2,1,0:T(8,128)S(1)}, f32[4,128,128]{2,1,0:T(8,128)S(1)}, u32[]{:S(2)}, u32[]{:S(2)}) collective-permute-start(f32[4,128,128]{2,1,0:T(8,128)S(1)} %get-tuple-element.66), channel_id=1, source_target_pairs={{2,0},{4,2},{6,4},{8,6},{10,8},{12,10},{14,12},{16,14},{18,16},{20... | collective-permute-start | bytes 786440 | tf_op jit(solution)/shard_map/ppermute | solution.py:24
  46.8 8.1 %collective-permute-start.14 = (f32[4,128,128]{2,1,0:T(8,128)S(1)}, f32[4,128,128]{2,1,0:T(8,128)S(1)}, u32[]{:S(2)}, u32[]{:S(2)}) collective-permute-start(f32[4,128,128]{2,1,0:T(8,128)S(1)} %get-tuple-element.67), channel_id=1, source_target_pairs={{2,0},{4,2},{6,4},{8,6},{10,8},{12,10},{14,12},{16,14},{18,16},{20... | collective-permute-start | bytes 786440 | tf_op jit(solution)/shard_map/ppermute | solution.py:24
  49.3 5.2 %collective-permute-start.15 = (f32[2,128,128]{2,1,0:T(8,128)S(1)}, f32[2,128,128]{2,1,0:T(8,128)S(1)}, u32[]{:S(2)}, u32[]{:S(2)}) collective-permute-start(f32[2,128,128]{2,1,0:T(8,128)S(1)} %get-tuple-element.65.quad_ref.quad_two), channel_id=1, source_target_pairs={{1,0},{0,1},{3,2},{2,3},{5,4},{4,5},{7,6},{6,7},{9,8},{8,9},{11,10... | collective-permute-start | bytes 393224 | tf_op jit(solution)/shard_map/ppermute | solution.py:24
  50.2 4.7 %collective-permute-start.20 = (f32[2,128,128]{2,1,0:T(8,128)S(1)}, f32[2,128,128]{2,1,0:T(8,128)S(1)}, u32[]{:S(2)}, u32[]{:S(2)}) collective-permute-start(f32[2,128,128]{2,1,0:T(8,128)S(1)} %collective-permute-done.18.upper_ref), channel_id=1, source_target_pairs={{2,0},{4,2},{6,4},{8,6},{10,8},{12,10},{14,12},{16,14},{18,16},{20... | collective-permute-start | bytes 393224 | tf_op jit(solution)/shard_map/ppermute | solution.py:24
  50.2 6.9 %collective-permute-start.16 = (f32[2,128,128]{2,1,0:T(8,128)S(1)}, f32[2,128,128]{2,1,0:T(8,128)S(1)}, u32[]{:S(2)}, u32[]{:S(2)}) collective-permute-start(f32[2,128,128]{2,1,0:T(8,128)S(1)} %get-tuple-element.68), channel_id=1, source_target_pairs={{1,0},{0,1},{3,2},{2,3},{5,4},{4,5},{7,6},{6,7},{9,8},{8,9},{11,10... | collective-permute-start | bytes 393224 | tf_op jit(solution)/shard_map/ppermute | solution.py:24
  54.5 2.9 %collective-permute-start.17 = (f32[2,128,128]{2,1,0:T(8,128)S(1)}, f32[2,128,128]{2,1,0:T(8,128)S(1)}, u32[]{:S(2)}, u32[]{:S(2)}) collective-permute-start(f32[2,128,128]{2,1,0:T(8,128)S(1)} %collective-permute-done.15.upper_ref), channel_id=1, source_target_pairs={{2,0},{4,2},{6,4},{8,6},{10,8},{12,10},{14,12},{16,14},{18,16},{20... | collective-permute-start | bytes 393224 | tf_op jit(solution)/shard_map/ppermute | solution.py:24
  61.3 19.4 %collective-permute-start.21 = (f32[4,128,256]{2,1,0:T(8,128)S(1)}, f32[4,128,256]{2,1,0:T(8,128)S(1)}, u32[]{:S(2)}, u32[]{:S(2)}) collective-permute-start(f32[4,128,256]{2,1,0:T(8,128)S(1)} %get-tuple-element.74), channel_id=1, source_target_pairs={{30,0},{0,2},{2,4},{4,6},{6,8},{8,10},{10,12},{12,14},{14,16},{16,... | collective-permute-start | bytes 1572872 | tf_op jit(solution)/shard_map/ppermute | solution.py:24
  61.4 12.8 %collective-permute-start.22 = (f32[2,128,128]{2,1,0:T(8,128)S(1)}, f32[2,128,128]{2,1,0:T(8,128)S(1)}, u32[]{:S(2)}, u32[]{:S(2)}) collective-permute-start(f32[2,128,128]{2,1,0:T(8,128)S(1)} %get-tuple-element.76), channel_id=1, source_target_pairs={{30,0},{0,2},{2,4},{4,6},{6,8},{8,10},{10,12},{12,14},{14,16},{16,... | collective-permute-start | bytes 393224 | tf_op jit(solution)/shard_map/ppermute | solution.py:24
  61.4 14.2 %collective-permute-start.24 = (f32[2,128,128]{2,1,0:T(8,128)S(1)}, f32[2,128,128]{2,1,0:T(8,128)S(1)}, u32[]{:S(2)}, u32[]{:S(2)}) collective-permute-start(f32[2,128,128]{2,1,0:T(8,128)S(1)} %get-tuple-element.78), channel_id=1, source_target_pairs={{30,0},{0,2},{2,4},{4,6},{6,8},{8,10},{10,12},{12,14},{14,16},{16,... | collective-permute-start | bytes 393224 | tf_op jit(solution)/shard_map/ppermute | solution.py:24
  62.7 14.1 %collective-permute-start.26 = (f32[2,128,128]{2,1,0:T(8,128)S(1)}, f32[2,128,128]{2,1,0:T(8,128)S(1)}, u32[]{:S(2)}, u32[]{:S(2)}) collective-permute-start(f32[2,128,128]{2,1,0:T(8,128)S(1)} %get-tuple-element.79), channel_id=1, source_target_pairs={{1,0},{0,1},{3,2},{2,3},{5,4},{4,5},{7,6},{6,7},{9,8},{8,9},{11,10... | collective-permute-start | bytes 393224 | tf_op jit(solution)/shard_map/ppermute | solution.py:24
  63.2 13.6 %collective-permute-start.27 = (f32[2,128,128]{2,1,0:T(8,128)S(1)}, f32[2,128,128]{2,1,0:T(8,128)S(1)}, u32[]{:S(2)}, u32[]{:S(2)}) collective-permute-start(f32[2,128,128]{2,1,0:T(8,128)S(1)} %get-tuple-element.80), channel_id=1, source_target_pairs={{1,0},{0,1},{3,2},{2,3},{5,4},{4,5},{7,6},{6,7},{9,8},{8,9},{11,10... | collective-permute-start | bytes 393224 | tf_op jit(solution)/shard_map/ppermute | solution.py:24
  74.2 5.0 %collective-permute-start.23 = (f32[2,128,128]{2,1,0:T(8,128)S(1)}, f32[2,128,128]{2,1,0:T(8,128)S(1)}, u32[]{:S(2)}, u32[]{:S(2)}) collective-permute-start(f32[2,128,128]{2,1,0:T(8,128)S(1)} %add.16), channel_id=1, source_target_pairs={{1,0},{0,1},{3,2},{2,3},{5,4},{4,5},{7,6},{6,7},{9,8},{8,9},{11,10... | collective-permute-start | bytes 393224 | tf_op jit(solution)/shard_map/ppermute | solution.py:24
  75.6 5.0 %collective-permute-start.25 = (f32[2,128,128]{2,1,0:T(8,128)S(1)}, f32[2,128,128]{2,1,0:T(8,128)S(1)}, u32[]{:S(2)}, u32[]{:S(2)}) collective-permute-start(f32[2,128,128]{2,1,0:T(8,128)S(1)} %add.17), channel_id=1, source_target_pairs={{1,0},{0,1},{3,2},{2,3},{5,4},{4,5},{7,6},{6,7},{9,8},{8,9},{11,10... | collective-permute-start | bytes 393224 | tf_op jit(solution)/shard_map/ppermute | solution.py:24

commit v5 on v4

--- a/solution.py
+++ b/solution.py
@@ -517,10 +517,11 @@
     gradient = [whole, strip, square, square, square]
 
     left, low, full = (0, width), (width, across), (0, tile_px)
-    up_one, up_two = pack(specimen_slices, [((0,), left, left), ((1,), left, left)])
+    up_one, up_two, left_low, top = pack(
+        specimen_slices, [((0,), left, left), ((1,), left, left), ((0, 1), low, left), ((0, 1), left, full)]
+    )
     upper_one = from_behind(up_one, "col", -1)
     upper_two = from_behind(up_two, "col", -1)
-    left_low, top = pack(specimen_slices, [((0, 1), low, left), ((0, 1), left, full)])
     lower = from_behind(left_low, "col", -1)
     below = from_behind(top, "row", -1)
     far = (specimen_slices, illumination_probe, amplitudes[0, 0], jnp.asarray(dft_operands(width)))

time: 81.8 us -> 80.8 us (0.988)
    pallas_call x2 -> x1, Pallas kernels: 2.19 us -> 1.37 us  [pack(): pl.pallas_call(functools.partial(pack_kernel, boxes=boxes), in_specs=[FAR...]
  transfers between devices with their start and end apart: 28 -> 28, of which waited for: 14 -> 14; matrix products, arithmetic and copies ran while one was open for 1% -> 1% of each run, Pallas kernels for 7% -> 5%
where the time goes in v5:
time: 80.8 us; the launch traced here: 80.7 us
  waiting for transfers between devices  32.5 us (40%)
  starting transfers between devices  30.2 us (37%)
  Pallas kernels  16 us (20%)
  local copies, waits for them, and re-layouts  1.09 us (1%)
  between operations  0.83 us (1%)
    ppermute x28, waiting for transfers between devices, from_behind(): return lax.ppermute(block, axis, route)  32.5 us
    ppermute x28, starting transfers between devices, from_behind(): return lax.ppermute(block, axis, route)  30.2 us
    pallas_call x8, Pallas kernels, call(): pl.pallas_call(functools.partial(kernel, **static), in_specs=[VMEM] * (le...  11.3 us
  transfers between devices with their start and end apart: 28, of which 14 were waited for; matrix products, arithmetic and copies ran while one was open for 1% of the time, Pallas kernels for 5%

profile of v5, /device:TPU:0, one launch (start us, length us, event | category | flops | bytes accessed | tf_op | source)
XLA Modules:
  0.0 80.7 jit_solution(10569711194641477804)
XLA Ops:
  0.0 1.4 %shard_map.82 = (f32[2,128,128]{2,1,0:T(8,128)S(1)}, f32[2,128,128]{2,1,0:T(8,128)S(1)}, f32[4,128,128]{2,1,0:T(8,128)S(1)}, f32[4,128,256]{2,1,0:T(8,128)S(1)}) custom-call(f32[2,2,256,256]{3,2,1,0:T(8,128)} %whole_ref.1), custom_call_target="tpu_custom_call" | custom-call | tf_op jit(solution)/shard_map/pallas_call | solution.py:477
  1.4 5.5 %collective-permute-start = (f32[4,128,256]{2,1,0:T(8,128)S(1)}, f32[4,128,256]{2,1,0:T(8,128)S(1)}, u32[]{:S(2)}, u32[]{:S(2)}) collective-permute-start(f32[4,128,256]{2,1,0:T(8,128)S(1)} %get-tuple-element.44), channel_id=1, source_target_pairs={{2,0},{4,2},{6,4},{8,6},{10,8},{12,10},{14,12},{16,14},{18,16},{20... | collective-permute-start | bytes 1572872 | tf_op jit(solution)/shard_map/ppermute | solution.py:24
  6.9 1.5 %collective-permute-start.1 = (f32[2,128,128]{2,1,0:T(8,128)S(1)}, f32[2,128,128]{2,1,0:T(8,128)S(1)}, u32[]{:S(2)}, u32[]{:S(2)}) collective-permute-start(f32[2,128,128]{2,1,0:T(8,128)S(1)} %get-tuple-element.45), channel_id=1, source_target_pairs={{1,0},{0,1},{3,2},{2,3},{5,4},{4,5},{7,6},{6,7},{9,8},{8,9},{11,10... | collective-permute-start | bytes 393224 | tf_op jit(solution)/shard_map/ppermute | solution.py:24
  8.9 1.5 %collective-permute-start.3 = (f32[4,128,128]{2,1,0:T(8,128)S(1)}, f32[4,128,128]{2,1,0:T(8,128)S(1)}, u32[]{:S(2)}, u32[]{:S(2)}) collective-permute-start(f32[4,128,128]{2,1,0:T(8,128)S(1)} %get-tuple-element.47), channel_id=1, source_target_pairs={{1,0},{0,1},{3,2},{2,3},{5,4},{4,5},{7,6},{6,7},{9,8},{8,9},{11,10... | collective-permute-start | bytes 786440 | tf_op jit(solution)/shard_map/ppermute | solution.py:24
  11.5 1.3 %collective-permute-done.1.upper_one = f32[2,128,128]{2,1,0:T(8,128)S(1)} collective-permute-done((f32[2,128,128]{2,1,0:T(8,128)S(1)}, f32[2,128,128]{2,1,0:T(8,128)S(1)}, u32[]{:S(2)}, u32[]{:S(2)}) %collective-permute-start.1) | collective-permute-done | bytes 131104 | tf_op jit(solution)/shard_map/ppermute | solution.py:24
  12.8 1.4 %collective-permute-done.2.upper_two = f32[2,128,128]{2,1,0:T(8,128)S(1)} collective-permute-done((f32[2,128,128]{2,1,0:T(8,128)S(1)}, f32[2,128,128]{2,1,0:T(8,128)S(1)}, u32[]{:S(2)}, u32[]{:S(2)}) %collective-permute-start.2) | collective-permute-done | bytes 131104 | tf_op jit(solution)/shard_map/ppermute | solution.py:24
  14.2 1.1 %collective-permute-start.5 = (f32[2,128,128]{2,1,0:T(8,128)S(1)}, f32[2,128,128]{2,1,0:T(8,128)S(1)}, u32[]{:S(2)}, u32[]{:S(2)}) collective-permute-start(f32[2,128,128]{2,1,0:T(8,128)S(1)} %collective-permute-done.2.upper_two), channel_id=1, source_target_pairs={{2,0},{4,2},{6,4},{8,6},{10,8},{12,10},{14,12},{16,14},{18,16},{20... | collective-permute-start | bytes 393224 | tf_op jit(solution)/shard_map/ppermute | solution.py:24
  16.1 1.5 %stage.1 = (f32[2,2,256,256]{3,2,1,0:T(8,128)S(1)}, f32[2,128,128]{2,1,0:T(8,128)S(1)}, f32[4,128,128]{2,1,0:T(8,128)S(1)}, bf16[4,256,256]{2,1,0:T(8,128)(2,1)S(1)}) custom-call(f32[2,2,256,256]{3,2,1,0:T(8,128)} %whole_ref.1, f32[2,128,128]{2,1,0:T(8,128)} %refs_1_.1, f32[4,128,128]{2,1,0:T(8,128)} %bitcast.6, bf16[4,256,256]{2,1,0:T(8,128)(2,1)} %constant.4.clone.refs_3_), custom_call_target="tpu_custom_call" | custom-call | tf_op jit(solution)/shard_map/stage/pallas_call | solution.py:528
  17.9 3.5 %shard_map.83 = (f32[2,256,256]{2,1,0:T(8,128)S(1)}, f32[2,128,256]{2,1,0:T(8,128)S(1)}, f32[2,128,128]{2,1,0:T(8,128)S(1)}, f32[2,128,128]{2,1,0:T(8,128)S(1)},...) custom-call(s32[1,128]{1,0:T(1,128)S(1)} %pad_bitcast_fusion.numbers_ref, ...), custom_call_target="tpu_custom_call" | custom-call | tf_op jit(solution)/shard_map/pallas_call | solution.py:452
  21.4 1.9 %shard_map.84 = (f32[2,256,256]{2,1,0:T(8,128)S(1)}, f32[4,128,256]{2,1,0:T(8,128)S(1)}, f32[2,128,128]{2,1,0:T(8,128)S(1)}, f32[2,128,128]{2,1,0:T(8,128)S(1)}, f32[2,128,128]{2,1,0:T(8,128)S(1)}) custom-call(s32[1,128]{1,0:T(1,128)S(1)} %pad_bitcast_fusion.numbers_ref, f32[4,2,128,128]{3,2,1,0:T(8,128)S(1)} %get-tuple-element.51.back_ref, ...), custom_call_target="tpu_custom_call" | custom-call | tf_op jit(solution)/shard_map/pallas_call | solution.py:452
  23.3 1.0 %collective-permute-start.11 = (f32[2,128,128]{2,1,0:T(8,128)S(1)}, f32[2,128,128]{2,1,0:T(8,128)S(1)}, u32[]{:S(2)}, u32[]{:S(2)}) collective-permute-start(f32[2,128,128]{2,1,0:T(8,128)S(1)} %get-tuple-element.63), channel_id=1, source_target_pairs={{30,0},{0,2},{2,4},{4,6},{6,8},{8,10},{10,12},{12,14},{14,16},{16,... | collective-permute-start | bytes 393224 | tf_op jit(solution)/shard_map/ppermute | solution.py:24
  24.4 1.5 %collective-permute-start.8 = (f32[2,128,128]{2,1,0:T(8,128)S(1)}, f32[2,128,128]{2,1,0:T(8,128)S(1)}, u32[]{:S(2)}, u32[]{:S(2)}) collective-permute-start(f32[2,128,128]{2,1,0:T(8,128)S(1)} %get-tuple-element.57), channel_id=1, source_target_pairs={{1,0},{0,1},{3,2},{2,3},{5,4},{4,5},{7,6},{6,7},{9,8},{8,9},{11,10... | collective-permute-start | bytes 393224 | tf_op jit(solution)/shard_map/ppermute | solution.py:24
  26.4 9.7 %collective-permute-done.11 = f32[2,128,128]{2,1,0:T(8,128)S(1)} collective-permute-done((f32[2,128,128]{2,1,0:T(8,128)S(1)}, f32[2,128,128]{2,1,0:T(8,128)S(1)}, u32[]{:S(2)}, u32[]{:S(2)}) %collective-permute-start.11) | collective-permute-done | bytes 131104 | tf_op jit(solution)/shard_map/ppermute | solution.py:24
  36.1 1.6 %collective-permute-start.12 = (f32[2,128,128]{2,1,0:T(8,128)S(1)}, f32[2,128,128]{2,1,0:T(8,128)S(1)}, u32[]{:S(2)}, u32[]{:S(2)}) collective-permute-start(f32[2,128,128]{2,1,0:T(8,128)S(1)} %add.15), channel_id=1, source_target_pairs={{1,0},{0,1},{3,2},{2,3},{5,4},{4,5},{7,6},{6,7},{9,8},{8,9},{11,10... | collective-permute-start | bytes 393224 | tf_op jit(solution)/shard_map/ppermute | solution.py:24
  37.8 1.4 %collective-permute-start.10 = (f32[2,128,128]{2,1,0:T(8,128)S(1)}, f32[2,128,128]{2,1,0:T(8,128)S(1)}, u32[]{:S(2)}, u32[]{:S(2)}) collective-permute-start(f32[2,128,128]{2,1,0:T(8,128)S(1)} %add.14), channel_id=1, source_target_pairs={{1,0},{0,1},{3,2},{2,3},{5,4},{4,5},{7,6},{6,7},{9,8},{8,9},{11,10... | collective-permute-start | bytes 393224 | tf_op jit(solution)/shard_map/ppermute | solution.py:24
  40.0 2.2 %collective-permute-done.12.up_two = f32[2,128,128]{2,1,0:T(8,128)S(1)} collective-permute-done((f32[2,128,128]{2,1,0:T(8,128)S(1)}, f32[2,128,128]{2,1,0:T(8,128)S(1)}, u32[]{:S(2)}, u32[]{:S(2)}) %collective-permute-start.12) | collective-permute-done | bytes 131104 | tf_op jit(solution)/shard_map/ppermute | solution.py:24
  42.2 1.8 %collective-permute-done.10.up_one = f32[2,128,128]{2,1,0:T(8,128)S(1)} collective-permute-done((f32[2,128,128]{2,1,0:T(8,128)S(1)}, f32[2,128,128]{2,1,0:T(8,128)S(1)}, u32[]{:S(2)}, u32[]{:S(2)}) %collective-permute-start.10) | collective-permute-done | bytes 131104 | tf_op jit(solution)/shard_map/ppermute | solution.py:24
  44.1 1.6 %collective-permute-start.18 = (f32[2,128,128]{2,1,0:T(8,128)S(1)}, f32[2,128,128]{2,1,0:T(8,128)S(1)}, u32[]{:S(2)}, u32[]{:S(2)}) collective-permute-start(f32[2,128,128]{2,1,0:T(8,128)S(1)} %get-tuple-element.64.quad_ref.quad_one), channel_id=1, source_target_pairs={{1,0},{0,1},{3,2},{2,3},{5,4},{4,5},{7,6},{6,7},{9,8},{8,9},{11,10... | collective-permute-start | bytes 393224 | tf_op jit(solution)/shard_map/ppermute | solution.py:24
  45.8 2.6 %collective-permute-start.14 = (f32[4,128,128]{2,1,0:T(8,128)S(1)}, f32[4,128,128]{2,1,0:T(8,128)S(1)}, u32[]{:S(2)}, u32[]{:S(2)}) collective-permute-start(f32[4,128,128]{2,1,0:T(8,128)S(1)} %get-tuple-element.67), channel_id=1, source_target_pairs={{2,0},{4,2},{6,4},{8,6},{10,8},{12,10},{14,12},{16,14},{18,16},{20... | collective-permute-start | bytes 786440 | tf_op jit(solution)/shard_map/ppermute | solution.py:24
  49.2 2.5 %collective-permute-start.16 = (f32[2,128,128]{2,1,0:T(8,128)S(1)}, f32[2,128,128]{2,1,0:T(8,128)S(1)}, u32[]{:S(2)}, u32[]{:S(2)}) collective-permute-start(f32[2,128,128]{2,1,0:T(8,128)S(1)} %get-tuple-element.68), channel_id=1, source_target_pairs={{1,0},{0,1},{3,2},{2,3},{5,4},{4,5},{7,6},{6,7},{9,8},{8,9},{11,10... | collective-permute-start | bytes 393224 | tf_op jit(solution)/shard_map/ppermute | solution.py:24
  51.7 1.9 %collective-permute-done.15.upper_ref = f32[2,128,128]{2,1,0:T(8,128)S(1)} collective-permute-done((f32[2,128,128]{2,1,0:T(8,128)S(1)}, f32[2,128,128]{2,1,0:T(8,128)S(1)}, u32[]{:S(2)}, u32[]{:S(2)}) %collective-permute-start.15) | collective-permute-done | bytes 131104 | tf_op jit(solution)/shard_map/ppermute | solution.py:24
  53.9 1.8 %shard_map.88.moved_ref = f32[4,2,128,128]{3,2,1,0:T(8,128)S(1)} custom-call(s32[1,128]{1,0:T(1,128)S(1)} %pad_bitcast_fusion.numbers_ref, f32[2,256,256]{2,1,0:T(8,128)S(1)} %get-tuple-element.58.rest_ref.rest_one, f32[2,128,128]{2,1,0:T(8,128)S(1)} %get-tuple-element.64.quad_ref.quad_one, f32[4,128,128]{2,1,0:T(8,128)S(1)} %collective-permute-done.13.left_ref, ...), custom_call_target="tpu_custom_call" | custom-call | tf_op jit(solution)/shard_map/pallas_call | solution.py:452
  56.4 2.1 %shard_map.89 = (f32[2,256,256]{2,1,0:T(8,128)S(1)}, f32[2,128,256]{2,1,0:T(8,128)S(1)}, f32[2,128,128]{2,1,0:T(8,128)S(1)}, f32[2,128,128]{2,1,0:T(8,128)S(1)},...) custom-call(s32[1,128]{1,0:T(1,128)S(1)} %pad_bitcast_fusion.numbers_ref, ...), custom_call_target="tpu_custom_call" | custom-call | tf_op jit(solution)/shard_map/pallas_call | solution.py:452
  58.5 1.9 %shard_map.90 = (f32[2,256,256]{2,1,0:T(8,128)S(1)}, f32[4,128,256]{2,1,0:T(8,128)S(1)}, f32[2,128,128]{2,1,0:T(8,128)S(1)}, f32[2,128,128]{2,1,0:T(8,128)S(1)}, f32[2,128,128]{2,1,0:T(8,128)S(1)}) custom-call(s32[1,128]{1,0:T(1,128)S(1)} %pad_bitcast_fusion.numbers_ref, f32[4,2,128,128]{3,2,1,0:T(8,128)S(1)} %get-tuple-element.70.back_ref, ...), custom_call_target="tpu_custom_call" | custom-call | tf_op jit(solution)/shard_map/pallas_call | solution.py:452
  60.5 1.2 %collective-permute-start.24 = (f32[2,128,128]{2,1,0:T(8,128)S(1)}, f32[2,128,128]{2,1,0:T(8,128)S(1)}, u32[]{:S(2)}, u32[]{:S(2)}) collective-permute-start(f32[2,128,128]{2,1,0:T(8,128)S(1)} %get-tuple-element.78), channel_id=1, source_target_pairs={{30,0},{0,2},{2,4},{4,6},{6,8},{8,10},{10,12},{12,14},{14,16},{16,... | collective-permute-start | bytes 393224 | tf_op jit(solution)/shard_map/ppermute | solution.py:24
  62.3 1.5 %collective-permute-start.27 = (f32[2,128,128]{2,1,0:T(8,128)S(1)}, f32[2,128,128]{2,1,0:T(8,128)S(1)}, u32[]{:S(2)}, u32[]{:S(2)}) collective-permute-start(f32[2,128,128]{2,1,0:T(8,128)S(1)} %get-tuple-element.80), channel_id=1, source_target_pairs={{1,0},{0,1},{3,2},{2,3},{5,4},{4,5},{7,6},{6,7},{9,8},{8,9},{11,10... | collective-permute-start | bytes 393224 | tf_op jit(solution)/shard_map/ppermute | solution.py:24
  63.8 9.5 %collective-permute-done.22 = f32[2,128,128]{2,1,0:T(8,128)S(1)} collective-permute-done((f32[2,128,128]{2,1,0:T(8,128)S(1)}, f32[2,128,128]{2,1,0:T(8,128)S(1)}, u32[]{:S(2)}, u32[]{:S(2)}) %collective-permute-start.22) | collective-permute-done | bytes 131104 | tf_op jit(solution)/shard_map/ppermute | solution.py:24
  73.3 1.1 %collective-permute-start.23 = (f32[2,128,128]{2,1,0:T(8,128)S(1)}, f32[2,128,128]{2,1,0:T(8,128)S(1)}, u32[]{:S(2)}, u32[]{:S(2)}) collective-permute-start(f32[2,128,128]{2,1,0:T(8,128)S(1)} %add.16), channel_id=1, source_target_pairs={{1,0},{0,1},{3,2},{2,3},{5,4},{4,5},{7,6},{6,7},{9,8},{8,9},{11,10... | collective-permute-start | bytes 393224 | tf_op jit(solution)/shard_map/ppermute | solution.py:24
  74.7 1.1 %collective-permute-start.25 = (f32[2,128,128]{2,1,0:T(8,128)S(1)}, f32[2,128,128]{2,1,0:T(8,128)S(1)}, u32[]{:S(2)}, u32[]{:S(2)}) collective-permute-start(f32[2,128,128]{2,1,0:T(8,128)S(1)} %add.17), channel_id=1, source_target_pairs={{1,0},{0,1},{3,2},{2,3},{5,4},{4,5},{7,6},{6,7},{9,8},{8,9},{11,10... | collective-permute-start | bytes 393224 | tf_op jit(solution)/shard_map/ppermute | solution.py:24
  76.7 1.6 %collective-permute-done.23.up_one = f32[2,128,128]{2,1,0:T(8,128)S(1)} collective-permute-done((f32[2,128,128]{2,1,0:T(8,128)S(1)}, f32[2,128,128]{2,1,0:T(8,128)S(1)}, u32[]{:S(2)}, u32[]{:S(2)}) %collective-permute-start.23) | collective-permute-done | bytes 131104 | tf_op jit(solution)/shard_map/ppermute | solution.py:24
  78.3 1.4 %collective-permute-done.25.up_two = f32[2,128,128]{2,1,0:T(8,128)S(1)} collective-permute-done((f32[2,128,128]{2,1,0:T(8,128)S(1)}, f32[2,128,128]{2,1,0:T(8,128)S(1)}, u32[]{:S(2)}, u32[]{:S(2)}) %collective-permute-start.25) | collective-permute-done | bytes 131104 | tf_op jit(solution)/shard_map/ppermute | solution.py:24
  79.7 0.9 %finish_top.1 = f32[2,2,256,256]{3,2,1,0:T(8,128)} custom-call(f32[2,256,256]{2,1,0:T(8,128)S(1)} %get-tuple-element.58.rest_ref.rest_one, f32[2,256,256]{2,1,0:T(8,128)S(1)} %get-tuple-element.59.rest_ref.rest_two, f32[2,128,128]{2,1,0:T(8,128)S(1)} %get-tuple-element.64.quad_ref.quad_one, ...), custom_call_target="tpu_custom_call", output_to_operand_aliasing={{}: (9, {})} | custom-call | tf_op jit(solution)/shard_map/finish_top/pallas_call | solution.py:609
  (51 shorter events, 7.4 us)
Async XLA Ops:
  0.0 10.4 %copy-start = (f32[128,128]{1,0:T(8,128)S(1)}, f32[128,128]{1,0:T(8,128)}, u32[]{:S(2)}) copy-start(f32[128,128]{1,0:T(8,128)} %param.10) | copy-start | bytes 196612
  1.4 16.5 %collective-permute-start = (f32[4,128,256]{2,1,0:T(8,128)S(1)}, f32[4,128,256]{2,1,0:T(8,128)S(1)}, u32[]{:S(2)}, u32[]{:S(2)}) collective-permute-start(f32[4,128,256]{2,1,0:T(8,128)S(1)} %get-tuple-element.44), channel_id=1, source_target_pairs={{2,0},{4,2},{6,4},{8,6},{10,8},{12,10},{14,12},{16,14},{18,16},{20... | collective-permute-start | bytes 1572872 | tf_op jit(solution)/shard_map/ppermute | solution.py:24
  6.9 5.9 %collective-permute-start.1 = (f32[2,128,128]{2,1,0:T(8,128)S(1)}, f32[2,128,128]{2,1,0:T(8,128)S(1)}, u32[]{:S(2)}, u32[]{:S(2)}) collective-permute-start(f32[2,128,128]{2,1,0:T(8,128)S(1)} %get-tuple-element.45), channel_id=1, source_target_pairs={{1,0},{0,1},{3,2},{2,3},{5,4},{4,5},{7,6},{6,7},{9,8},{8,9},{11,10... | collective-permute-start | bytes 393224 | tf_op jit(solution)/shard_map/ppermute | solution.py:24
  8.4 5.8 %collective-permute-start.2 = (f32[2,128,128]{2,1,0:T(8,128)S(1)}, f32[2,128,128]{2,1,0:T(8,128)S(1)}, u32[]{:S(2)}, u32[]{:S(2)}) collective-permute-start(f32[2,128,128]{2,1,0:T(8,128)S(1)} %get-tuple-element.46), channel_id=1, source_target_pairs={{1,0},{0,1},{3,2},{2,3},{5,4},{4,5},{7,6},{6,7},{9,8},{8,9},{11,10... | collective-permute-start | bytes 393224 | tf_op jit(solution)/shard_map/ppermute | solution.py:24
  8.9 9.0 %collective-permute-start.3 = (f32[4,128,128]{2,1,0:T(8,128)S(1)}, f32[4,128,128]{2,1,0:T(8,128)S(1)}, u32[]{:S(2)}, u32[]{:S(2)}) collective-permute-start(f32[4,128,128]{2,1,0:T(8,128)S(1)} %get-tuple-element.47), channel_id=1, source_target_pairs={{1,0},{0,1},{3,2},{2,3},{5,4},{4,5},{7,6},{6,7},{9,8},{8,9},{11,10... | collective-permute-start | bytes 786440 | tf_op jit(solution)/shard_map/ppermute | solution.py:24
  10.7 0.7 copy-start.1
  12.8 4.8 %collective-permute-start.4 = (f32[2,128,128]{2,1,0:T(8,128)S(1)}, f32[2,128,128]{2,1,0:T(8,128)S(1)}, u32[]{:S(2)}, u32[]{:S(2)}) collective-permute-start(f32[2,128,128]{2,1,0:T(8,128)S(1)} %collective-permute-done.1.upper_one), channel_id=1, source_target_pairs={{2,0},{4,2},{6,4},{8,6},{10,8},{12,10},{14,12},{16,14},{18,16},{20... | collective-permute-start | bytes 393224 | tf_op jit(solution)/shard_map/ppermute | solution.py:24
  14.2 3.6 %collective-permute-start.5 = (f32[2,128,128]{2,1,0:T(8,128)S(1)}, f32[2,128,128]{2,1,0:T(8,128)S(1)}, u32[]{:S(2)}, u32[]{:S(2)}) collective-permute-start(f32[2,128,128]{2,1,0:T(8,128)S(1)} %collective-permute-done.2.upper_two), channel_id=1, source_target_pairs={{2,0},{4,2},{6,4},{8,6},{10,8},{12,10},{14,12},{16,14},{18,16},{20... | collective-permute-start | bytes 393224 | tf_op jit(solution)/shard_map/ppermute | solution.py:24
  15.4 0.7 copy-start.2
  23.2 20.7 %collective-permute-start.6 = (f32[4,128,256]{2,1,0:T(8,128)S(1)}, f32[4,128,256]{2,1,0:T(8,128)S(1)}, u32[]{:S(2)}, u32[]{:S(2)}) collective-permute-start(f32[4,128,256]{2,1,0:T(8,128)S(1)} %get-tuple-element.55), channel_id=1, source_target_pairs={{30,0},{0,2},{2,4},{4,6},{6,8},{8,10},{10,12},{12,14},{14,16},{16,... | collective-permute-start | bytes 1572872 | tf_op jit(solution)/shard_map/ppermute | solution.py:24
  23.3 12.8 %collective-permute-start.11 = (f32[2,128,128]{2,1,0:T(8,128)S(1)}, f32[2,128,128]{2,1,0:T(8,128)S(1)}, u32[]{:S(2)}, u32[]{:S(2)}) collective-permute-start(f32[2,128,128]{2,1,0:T(8,128)S(1)} %get-tuple-element.63), channel_id=1, source_target_pairs={{30,0},{0,2},{2,4},{4,6},{6,8},{8,10},{10,12},{12,14},{14,16},{16,... | collective-permute-start | bytes 393224 | tf_op jit(solution)/shard_map/ppermute | solution.py:24
  24.3 13.4 %collective-permute-start.9 = (f32[2,128,128]{2,1,0:T(8,128)S(1)}, f32[2,128,128]{2,1,0:T(8,128)S(1)}, u32[]{:S(2)}, u32[]{:S(2)}) collective-permute-start(f32[2,128,128]{2,1,0:T(8,128)S(1)} %get-tuple-element.61), channel_id=1, source_target_pairs={{30,0},{0,2},{2,4},{4,6},{6,8},{8,10},{10,12},{12,14},{14,16},{16,... | collective-permute-start | bytes 393224 | tf_op jit(solution)/shard_map/ppermute | solution.py:24
  24.4 14.8 %collective-permute-start.8 = (f32[2,128,128]{2,1,0:T(8,128)S(1)}, f32[2,128,128]{2,1,0:T(8,128)S(1)}, u32[]{:S(2)}, u32[]{:S(2)}) collective-permute-start(f32[2,128,128]{2,1,0:T(8,128)S(1)} %get-tuple-element.57), channel_id=1, source_target_pairs={{1,0},{0,1},{3,2},{2,3},{5,4},{4,5},{7,6},{6,7},{9,8},{8,9},{11,10... | collective-permute-start | bytes 393224 | tf_op jit(solution)/shard_map/ppermute | solution.py:24
  25.8 13.3 %collective-permute-start.7 = (f32[2,128,128]{2,1,0:T(8,128)S(1)}, f32[2,128,128]{2,1,0:T(8,128)S(1)}, u32[]{:S(2)}, u32[]{:S(2)}) collective-permute-start(f32[2,128,128]{2,1,0:T(8,128)S(1)} %get-tuple-element.56), channel_id=1, source_target_pairs={{1,0},{0,1},{3,2},{2,3},{5,4},{4,5},{7,6},{6,7},{9,8},{8,9},{11,10... | collective-permute-start | bytes 393224 | tf_op jit(solution)/shard_map/ppermute | solution.py:24
  36.1 6.0 %collective-permute-start.12 = (f32[2,128,128]{2,1,0:T(8,128)S(1)}, f32[2,128,128]{2,1,0:T(8,128)S(1)}, u32[]{:S(2)}, u32[]{:S(2)}) collective-permute-start(f32[2,128,128]{2,1,0:T(8,128)S(1)} %add.15), channel_id=1, source_target_pairs={{1,0},{0,1},{3,2},{2,3},{5,4},{4,5},{7,6},{6,7},{9,8},{8,9},{11,10... | collective-permute-start | bytes 393224 | tf_op jit(solution)/shard_map/ppermute | solution.py:24
  37.8 6.2 %collective-permute-start.10 = (f32[2,128,128]{2,1,0:T(8,128)S(1)}, f32[2,128,128]{2,1,0:T(8,128)S(1)}, u32[]{:S(2)}, u32[]{:S(2)}) collective-permute-start(f32[2,128,128]{2,1,0:T(8,128)S(1)} %add.14), channel_id=1, source_target_pairs={{1,0},{0,1},{3,2},{2,3},{5,4},{4,5},{7,6},{6,7},{9,8},{8,9},{11,10... | collective-permute-start | bytes 393224 | tf_op jit(solution)/shard_map/ppermute | solution.py:24
  39.2 10.0 %collective-permute-start.19 = (f32[2,128,128]{2,1,0:T(8,128)S(1)}, f32[2,128,128]{2,1,0:T(8,128)S(1)}, u32[]{:S(2)}, u32[]{:S(2)}) collective-permute-start(f32[2,128,128]{2,1,0:T(8,128)S(1)} %get-tuple-element.69), channel_id=1, source_target_pairs={{1,0},{0,1},{3,2},{2,3},{5,4},{4,5},{7,6},{6,7},{9,8},{8,9},{11,10... | collective-permute-start | bytes 393224 | tf_op jit(solution)/shard_map/ppermute | solution.py:24
  44.1 5.2 %collective-permute-start.18 = (f32[2,128,128]{2,1,0:T(8,128)S(1)}, f32[2,128,128]{2,1,0:T(8,128)S(1)}, u32[]{:S(2)}, u32[]{:S(2)}) collective-permute-start(f32[2,128,128]{2,1,0:T(8,128)S(1)} %get-tuple-element.64.quad_ref.quad_one), channel_id=1, source_target_pairs={{1,0},{0,1},{3,2},{2,3},{5,4},{4,5},{7,6},{6,7},{9,8},{8,9},{11,10... | collective-permute-start | bytes 393224 | tf_op jit(solution)/shard_map/ppermute | solution.py:24
  45.6 8.3 %collective-permute-start.13 = (f32[4,128,128]{2,1,0:T(8,128)S(1)}, f32[4,128,128]{2,1,0:T(8,128)S(1)}, u32[]{:S(2)}, u32[]{:S(2)}) collective-permute-start(f32[4,128,128]{2,1,0:T(8,128)S(1)} %get-tuple-element.66), channel_id=1, source_target_pairs={{2,0},{4,2},{6,4},{8,6},{10,8},{12,10},{14,12},{16,14},{18,16},{20... | collective-permute-start | bytes 786440 | tf_op jit(solution)/shard_map/ppermute | solution.py:24
  45.8 8.1 %collective-permute-start.14 = (f32[4,128,128]{2,1,0:T(8,128)S(1)}, f32[4,128,128]{2,1,0:T(8,128)S(1)}, u32[]{:S(2)}, u32[]{:S(2)}) collective-permute-start(f32[4,128,128]{2,1,0:T(8,128)S(1)} %get-tuple-element.67), channel_id=1, source_target_pairs={{2,0},{4,2},{6,4},{8,6},{10,8},{12,10},{14,12},{16,14},{18,16},{20... | collective-permute-start | bytes 786440 | tf_op jit(solution)/shard_map/ppermute | solution.py:24
  48.4 5.3 %collective-permute-start.15 = (f32[2,128,128]{2,1,0:T(8,128)S(1)}, f32[2,128,128]{2,1,0:T(8,128)S(1)}, u32[]{:S(2)}, u32[]{:S(2)}) collective-permute-start(f32[2,128,128]{2,1,0:T(8,128)S(1)} %get-tuple-element.65.quad_ref.quad_two), channel_id=1, source_target_pairs={{1,0},{0,1},{3,2},{2,3},{5,4},{4,5},{7,6},{6,7},{9,8},{8,9},{11,10... | collective-permute-start | bytes 393224 | tf_op jit(solution)/shard_map/ppermute | solution.py:24
  49.2 4.7 %collective-permute-start.20 = (f32[2,128,128]{2,1,0:T(8,128)S(1)}, f32[2,128,128]{2,1,0:T(8,128)S(1)}, u32[]{:S(2)}, u32[]{:S(2)}) collective-permute-start(f32[2,128,128]{2,1,0:T(8,128)S(1)} %collective-permute-done.18.upper_ref), channel_id=1, source_target_pairs={{2,0},{4,2},{6,4},{8,6},{10,8},{12,10},{14,12},{16,14},{18,16},{20... | collective-permute-start | bytes 393224 | tf_op jit(solution)/shard_map/ppermute | solution.py:24
  49.2 6.9 %collective-permute-start.16 = (f32[2,128,128]{2,1,0:T(8,128)S(1)}, f32[2,128,128]{2,1,0:T(8,128)S(1)}, u32[]{:S(2)}, u32[]{:S(2)}) collective-permute-start(f32[2,128,128]{2,1,0:T(8,128)S(1)} %get-tuple-element.68), channel_id=1, source_target_pairs={{1,0},{0,1},{3,2},{2,3},{5,4},{4,5},{7,6},{6,7},{9,8},{8,9},{11,10... | collective-permute-start | bytes 393224 | tf_op jit(solution)/shard_map/ppermute | solution.py:24
  53.6 2.8 %collective-permute-start.17 = (f32[2,128,128]{2,1,0:T(8,128)S(1)}, f32[2,128,128]{2,1,0:T(8,128)S(1)}, u32[]{:S(2)}, u32[]{:S(2)}) collective-permute-start(f32[2,128,128]{2,1,0:T(8,128)S(1)} %collective-permute-done.15.upper_ref), channel_id=1, source_target_pairs={{2,0},{4,2},{6,4},{8,6},{10,8},{12,10},{14,12},{16,14},{18,16},{20... | collective-permute-start | bytes 393224 | tf_op jit(solution)/shard_map/ppermute | solution.py:24
  60.4 19.4 %collective-permute-start.21 = (f32[4,128,256]{2,1,0:T(8,128)S(1)}, f32[4,128,256]{2,1,0:T(8,128)S(1)}, u32[]{:S(2)}, u32[]{:S(2)}) collective-permute-start(f32[4,128,256]{2,1,0:T(8,128)S(1)} %get-tuple-element.74), channel_id=1, source_target_pairs={{30,0},{0,2},{2,4},{4,6},{6,8},{8,10},{10,12},{12,14},{14,16},{16,... | collective-permute-start | bytes 1572872 | tf_op jit(solution)/shard_map/ppermute | solution.py:24
  60.4 12.8 %collective-permute-start.22 = (f32[2,128,128]{2,1,0:T(8,128)S(1)}, f32[2,128,128]{2,1,0:T(8,128)S(1)}, u32[]{:S(2)}, u32[]{:S(2)}) collective-permute-start(f32[2,128,128]{2,1,0:T(8,128)S(1)} %get-tuple-element.76), channel_id=1, source_target_pairs={{30,0},{0,2},{2,4},{4,6},{6,8},{8,10},{10,12},{12,14},{14,16},{16,... | collective-permute-start | bytes 393224 | tf_op jit(solution)/shard_map/ppermute | solution.py:24
  60.5 14.2 %collective-permute-start.24 = (f32[2,128,128]{2,1,0:T(8,128)S(1)}, f32[2,128,128]{2,1,0:T(8,128)S(1)}, u32[]{:S(2)}, u32[]{:S(2)}) collective-permute-start(f32[2,128,128]{2,1,0:T(8,128)S(1)} %get-tuple-element.78), channel_id=1, source_target_pairs={{30,0},{0,2},{2,4},{4,6},{6,8},{8,10},{10,12},{12,14},{14,16},{16,... | collective-permute-start | bytes 393224 | tf_op jit(solution)/shard_map/ppermute | solution.py:24
  61.8 14.1 %collective-permute-start.26 = (f32[2,128,128]{2,1,0:T(8,128)S(1)}, f32[2,128,128]{2,1,0:T(8,128)S(1)}, u32[]{:S(2)}, u32[]{:S(2)}) collective-permute-start(f32[2,128,128]{2,1,0:T(8,128)S(1)} %get-tuple-element.79), channel_id=1, source_target_pairs={{1,0},{0,1},{3,2},{2,3},{5,4},{4,5},{7,6},{6,7},{9,8},{8,9},{11,10... | collective-permute-start | bytes 393224 | tf_op jit(solution)/shard_map/ppermute | solution.py:24
  62.3 13.5 %collective-permute-start.27 = (f32[2,128,128]{2,1,0:T(8,128)S(1)}, f32[2,128,128]{2,1,0:T(8,128)S(1)}, u32[]{:S(2)}, u32[]{:S(2)}) collective-permute-start(f32[2,128,128]{2,1,0:T(8,128)S(1)} %get-tuple-element.80), channel_id=1, source_target_pairs={{1,0},{0,1},{3,2},{2,3},{5,4},{4,5},{7,6},{6,7},{9,8},{8,9},{11,10... | collective-permute-start | bytes 393224 | tf_op jit(solution)/shard_map/ppermute | solution.py:24
  73.3 5.0 %collective-permute-start.23 = (f32[2,128,128]{2,1,0:T(8,128)S(1)}, f32[2,128,128]{2,1,0:T(8,128)S(1)}, u32[]{:S(2)}, u32[]{:S(2)}) collective-permute-start(f32[2,128,128]{2,1,0:T(8,128)S(1)} %add.16), channel_id=1, source_target_pairs={{1,0},{0,1},{3,2},{2,3},{5,4},{4,5},{7,6},{6,7},{9,8},{8,9},{11,10... | collective-permute-start | bytes 393224 | tf_op jit(solution)/shard_map/ppermute | solution.py:24
  74.7 5.0 %collective-permute-start.25 = (f32[2,128,128]{2,1,0:T(8,128)S(1)}, f32[2,128,128]{2,1,0:T(8,128)S(1)}, u32[]{:S(2)}, u32[]{:S(2)}) collective-permute-start(f32[2,128,128]{2,1,0:T(8,128)S(1)} %add.17), channel_id=1, source_target_pairs={{1,0},{0,1},{3,2},{2,3},{5,4},{4,5},{7,6},{6,7},{9,8},{8,9},{11,10... | collective-permute-start | bytes 393224 | tf_op jit(solution)/shard_map/ppermute | solution.py:24

commit v6 on v5

--- a/solution.py
+++ b/solution.py
@@ -65,7 +65,8 @@
     parts = [half[rows_of(k, width)] for k in range(count)]
     tall = [jnp.concatenate([part[:, :width], part[:, width:]], 0) for part in parts]
     high, low = split(jnp.concatenate(tall, 1))
-    full = product(table_ref[2], high) + product(table_ref[2], low) + product(table_ref[3], high)
+    both = product(table_ref[2], jnp.concatenate([high, low], 1))
+    full = both[:, :high.shape[1]] + both[:, high.shape[1]:] + product(table_ref[3], high)
     return [(full[:width, rows_of(k, width)], full[width:, rows_of(k, width)]) for k in range(count)]
 
 
@@ -135,11 +136,11 @@
     return lax.broadcasted_iota(jnp.int32, (width, LANES), 1)
 
 
-LAG = 1
+LAG = 0
 
 
 def groups_of(spots):
-    return [range(j, min(j + 2, spots)) for j in range(0, spots, 2)]
+    return [range(j, j + 1) for j in range(spots)]
 
 
 def forward_steps(group, enter_ref, leave_ref, cos_ref, sin_ref, table_ref, width):
@@ -181,6 +182,22 @@
     yield True
     for j, (real, negative) in zip(group, pairs):
         finish(j, real, -negative)
+
+
+def by_count(total, spots, run):
+    groups = groups_of(spots)
+    first = (len(groups) + 1) // 2
+    if first == len(groups):
+        run(groups)
+        return
+
+    @pl.when(total > first)
+    def _():
+        run(groups)
+
+    @pl.when(total <= first)
+    def _():
+        run(groups[:first])
 
 
 def joined(*parts):
@@ -216,23 +233,23 @@
     ]
 
 
-def take_windows(ext_ref, spot_list, win_ref, width, lane):
-    for j, spot in enumerate(spot_list):
+def take_windows(ext_ref, spot_list, probes, win_ref, width, lane):
+    for j in probes:
+        spot = spot_list[j]
         win_ref[j, 0] = window(ext_ref, 0, spot, width, lane)
         win_ref[j, 1] = window(ext_ref, 1, spot, width, lane)
 
 
-def light(ext_ref, spot_list, probe_ref, enter_ref, width, lane):
-    for j, spot in enumerate(spot_list):
+def light(ext_ref, spot_list, probes, probe_ref, enter_ref, width, lane):
+    for j in probes:
+        spot = spot_list[j]
         real = window(ext_ref, 0, spot, width, lane)
         imag = window(ext_ref, 1, spot, width, lane)
         enter_ref[j, 0] = probe_ref[0] * real - probe_ref[1] * imag
         enter_ref[j, 1] = probe_ref[0] * imag + probe_ref[1] * real
 
 
-def residual_end(numbers_ref, spots, spot_list, ext_ref, moved_ref, win_ref, back_ref, width, lane):
-    total = pick(numbers_ref, 2 * spots)
-
+def residual_end(total, spot_list, ext_ref, moved_ref, win_ref, back_ref, width, lane):
     def finish(j, real, imag):
         used = j < total
         scatter(ext_ref, 0, spot_list[j], width, lane, used, moved_ref[j, 0] * real + moved_ref[j, 1] * imag)
@@ -257,19 +274,23 @@
     fill_ext(other_ref, whole_pieces(second, 1, tile_px, width))
     grad_ref[...] = jnp.zeros(grad_ref.shape, jnp.float32)
     spot_list = places(numbers_ref, spots)
-    light(ext_ref, spot_list, probe_ref, back_ref, width, lane)
-    take_windows(other_ref, spot_list, win_ref, width, lane)
-    finish = residual_end(numbers_ref, spots, spot_list, grad_ref, moved_ref, win_ref, back_ref, width, lane)
-    interleave([
-        joined(
-            forward_steps(group, back_ref, moved_ref, cos_ref, sin_ref, table_ref, width),
-            residual_steps(
-                group, moved_ref, win_ref, lambda j: amp_ref[pick(numbers_ref, 2 * spots + 1 + j)],
-                finish, table_ref, width,
-            ),
-        )
-        for group in groups_of(spots)
-    ], LAG)
+    total = pick(numbers_ref, 2 * spots)
+    finish = residual_end(total, spot_list, grad_ref, moved_ref, win_ref, back_ref, width, lane)
+    measured_of = lambda j: amp_ref[pick(numbers_ref, 2 * spots + 1 + j)]
+
+    def run(groups):
+        probes = [j for group in groups for j in group]
+        light(ext_ref, spot_list, probes, probe_ref, back_ref, width, lane)
+        take_windows(other_ref, spot_list, probes, win_ref, width, lane)
+        interleave([
+            joined(
+                forward_steps(group, back_ref, moved_ref, cos_ref, sin_ref, table_ref, width),
+                residual_steps(group, moved_ref, win_ref, measured_of, finish, table_ref, width),
+            )
+            for group in groups
+        ], LAG)
+
+    by_count(total, spots, run)
     emit(grad_ref, own_ref, down_ref, up_out_ref, low_out_ref, diag_ref, width)
 
 
@@ -281,11 +302,14 @@
     halo = (rest_ref, quad_ref, left_ref, right_ref, upper_ref, lower_ref, corner_ref)
     fill_ext(ext_ref, slice_pieces(halo, 0, rest_ref.shape[1], width))
     spot_list = places(numbers_ref, spots)
-    light(ext_ref, spot_list, probe_ref, enter_ref, width, lane)
-    interleave([
-        forward_steps(group, enter_ref, moved_ref, cos_ref, sin_ref, table_ref, width)
-        for group in groups_of(spots)
-    ], LAG)
+
+    def run(groups):
+        light(ext_ref, spot_list, [j for group in groups for j in group], probe_ref, enter_ref, width, lane)
+        interleave([
+            forward_steps(group, enter_ref, moved_ref, cos_ref, sin_ref, table_ref, width) for group in groups
+        ], LAG)
+
+    by_count(pick(numbers_ref, 2 * spots), spots, run)
 
 
 def residual_kernel(
@@ -299,15 +323,17 @@
     fill_ext(ext_ref, slice_pieces(halo, 1, rest_ref.shape[1], width))
     grad_ref[...] = jnp.zeros(grad_ref.shape, jnp.float32)
     spot_list = places(numbers_ref, spots)
-    take_windows(ext_ref, spot_list, win_ref, width, lane)
-    finish = residual_end(numbers_ref, spots, spot_list, grad_ref, moved_ref, win_ref, back_ref, width, lane)
-    interleave([
-        residual_steps(
-            group, moved_ref, win_ref, lambda j: amp_ref[pick(numbers_ref, 2 * spots + 1 + j)],
-            finish, table_ref, width,
-        )
-        for group in groups_of(spots)
-    ], LAG)
+    total = pick(numbers_ref, 2 * spots)
+    finish = residual_end(total, spot_list, grad_ref, moved_ref, win_ref, back_ref, width, lane)
+    measured_of = lambda j: amp_ref[pick(numbers_ref, 2 * spots + 1 + j)]
+
+    def run(groups):
+        take_windows(ext_ref, spot_list, [j for group in groups for j in group], win_ref, width, lane)
+        interleave([
+            residual_steps(group, moved_ref, win_ref, measured_of, finish, table_ref, width) for group in groups
+        ], LAG)
+
+    by_count(total, spots, run)
     emit(grad_ref, own_ref, down_ref, up_out_ref, low_out_ref, diag_ref, width)
 
 
@@ -340,7 +366,7 @@
             scatter(ext_ref, 0, spot, width, lane, used, probe_ref[0] * real + probe_ref[1] * imag)
             scatter(ext_ref, 1, spot, width, lane, used, probe_ref[0] * imag - probe_ref[1] * real)
 
-    interleave([chain(group) for group in groups_of(spots)], LAG)
+    by_count(total, spots, lambda groups: interleave([chain(group) for group in groups], LAG))
     emit(ext_ref, own_ref, down_ref, up_out_ref, low_out_ref, diag_ref, width)
 
 

time: 80.8 us -> 78.4 us (0.970)
  waiting for transfers between devices: 32.5 us -> 37.4 us
  starting transfers between devices: 30.2 us -> 25.9 us
  Pallas kernels: 16 us -> 12.6 us
    ppermute x28, waiting for transfers between devices: 32.5 us -> 37.4 us  [from_behind(): return lax.ppermute(block, axis, route)]
    ppermute x28, starting transfers between devices: 30.2 us -> 25.9 us  [from_behind(): return lax.ppermute(block, axis, route)]
    pallas_call x8, Pallas kernels: 11.3 us -> 7.97 us  [call(): pl.pallas_call(functools.partial(kernel, **static), in_specs=[VMEM] * (le...]
  transfers between devices with their start and end apart: 28 -> 28, of which waited for: 14 -> 15; matrix products, arithmetic and copies ran while one was open for 1% -> 1% of each run, Pallas kernels for 5% -> 5%
where the time goes in v6:
time: 78.4 us; the launch traced here: 78.2 us
  waiting for transfers between devices  37.4 us (48%)
  starting transfers between devices  25.9 us (33%)
  Pallas kernels  12.6 us (16%)
  local copies, waits for them, and re-layouts  1.09 us (1%)
  between operations  0.98 us (1%)
    ppermute x28, waiting for transfers between devices, from_behind(): return lax.ppermute(block, axis, route)  37.4 us
    ppermute x28, starting transfers between devices, from_behind(): return lax.ppermute(block, axis, route)  25.9 us
    pallas_call x8, Pallas kernels, call(): pl.pallas_call(functools.partial(kernel, **static), in_specs=[VMEM] * (le...  7.97 us
  transfers between devices with their start and end apart: 28, of which 15 were waited for; matrix products, arithmetic and copies ran while one was open for 1% of the time, Pallas kernels for 5%

profile of v6, /device:TPU:0, one launch (start us, length us, event | category | flops | bytes accessed | tf_op | source)
XLA Modules:
  0.0 78.2 jit_solution(761226670666486952)
XLA Ops:
  0.0 1.4 %shard_map.82 = (f32[2,128,128]{2,1,0:T(8,128)S(1)}, f32[2,128,128]{2,1,0:T(8,128)S(1)}, f32[4,128,128]{2,1,0:T(8,128)S(1)}, f32[4,128,256]{2,1,0:T(8,128)S(1)}) custom-call(f32[2,2,256,256]{3,2,1,0:T(8,128)} %whole_ref.1), custom_call_target="tpu_custom_call" | custom-call | tf_op jit(solution)/shard_map/pallas_call | solution.py:503
  1.4 5.5 %collective-permute-start = (f32[4,128,256]{2,1,0:T(8,128)S(1)}, f32[4,128,256]{2,1,0:T(8,128)S(1)}, u32[]{:S(2)}, u32[]{:S(2)}) collective-permute-start(f32[4,128,256]{2,1,0:T(8,128)S(1)} %get-tuple-element.44), channel_id=1, source_target_pairs={{2,0},{4,2},{6,4},{8,6},{10,8},{12,10},{14,12},{16,14},{18,16},{20... | collective-permute-start | bytes 1572872 | tf_op jit(solution)/shard_map/ppermute | solution.py:24
  6.9 1.5 %collective-permute-start.1 = (f32[2,128,128]{2,1,0:T(8,128)S(1)}, f32[2,128,128]{2,1,0:T(8,128)S(1)}, u32[]{:S(2)}, u32[]{:S(2)}) collective-permute-start(f32[2,128,128]{2,1,0:T(8,128)S(1)} %get-tuple-element.45), channel_id=1, source_target_pairs={{1,0},{0,1},{3,2},{2,3},{5,4},{4,5},{7,6},{6,7},{9,8},{8,9},{11,10... | collective-permute-start | bytes 393224 | tf_op jit(solution)/shard_map/ppermute | solution.py:24
  8.9 1.5 %collective-permute-start.3 = (f32[4,128,128]{2,1,0:T(8,128)S(1)}, f32[4,128,128]{2,1,0:T(8,128)S(1)}, u32[]{:S(2)}, u32[]{:S(2)}) collective-permute-start(f32[4,128,128]{2,1,0:T(8,128)S(1)} %get-tuple-element.47), channel_id=1, source_target_pairs={{1,0},{0,1},{3,2},{2,3},{5,4},{4,5},{7,6},{6,7},{9,8},{8,9},{11,10... | collective-permute-start | bytes 786440 | tf_op jit(solution)/shard_map/ppermute | solution.py:24
  11.5 1.3 %collective-permute-done.1.upper_one = f32[2,128,128]{2,1,0:T(8,128)S(1)} collective-permute-done((f32[2,128,128]{2,1,0:T(8,128)S(1)}, f32[2,128,128]{2,1,0:T(8,128)S(1)}, u32[]{:S(2)}, u32[]{:S(2)}) %collective-permute-start.1) | collective-permute-done | bytes 131104 | tf_op jit(solution)/shard_map/ppermute | solution.py:24
  12.8 1.4 %collective-permute-done.2.upper_two = f32[2,128,128]{2,1,0:T(8,128)S(1)} collective-permute-done((f32[2,128,128]{2,1,0:T(8,128)S(1)}, f32[2,128,128]{2,1,0:T(8,128)S(1)}, u32[]{:S(2)}, u32[]{:S(2)}) %collective-permute-start.2) | collective-permute-done | bytes 131104 | tf_op jit(solution)/shard_map/ppermute | solution.py:24
  14.2 1.1 %collective-permute-start.5 = (f32[2,128,128]{2,1,0:T(8,128)S(1)}, f32[2,128,128]{2,1,0:T(8,128)S(1)}, u32[]{:S(2)}, u32[]{:S(2)}) collective-permute-start(f32[2,128,128]{2,1,0:T(8,128)S(1)} %collective-permute-done.2.upper_two), channel_id=1, source_target_pairs={{2,0},{4,2},{6,4},{8,6},{10,8},{12,10},{14,12},{16,14},{18,16},{20... | collective-permute-start | bytes 393224 | tf_op jit(solution)/shard_map/ppermute | solution.py:24
  16.1 1.5 %stage.1 = (f32[2,2,256,256]{3,2,1,0:T(8,128)S(1)}, f32[2,128,128]{2,1,0:T(8,128)S(1)}, f32[4,128,128]{2,1,0:T(8,128)S(1)}, bf16[4,256,256]{2,1,0:T(8,128)(2,1)S(1)}) custom-call(f32[2,2,256,256]{3,2,1,0:T(8,128)} %whole_ref.1, f32[2,128,128]{2,1,0:T(8,128)} %refs_1_.1, f32[4,128,128]{2,1,0:T(8,128)} %bitcast.6, bf16[4,256,256]{2,1,0:T(8,128)(2,1)} %constant.4.clone.refs_3_), custom_call_target="tpu_custom_call" | custom-call | tf_op jit(solution)/shard_map/stage/pallas_call | solution.py:554
  17.9 2.3 %shard_map.83 = (f32[2,256,256]{2,1,0:T(8,128)S(1)}, f32[2,128,256]{2,1,0:T(8,128)S(1)}, f32[2,128,128]{2,1,0:T(8,128)S(1)}, f32[2,128,128]{2,1,0:T(8,128)S(1)},...) custom-call(s32[1,128]{1,0:T(1,128)S(1)} %pad_bitcast_fusion.numbers_ref, ...), custom_call_target="tpu_custom_call" | custom-call | tf_op jit(solution)/shard_map/pallas_call | solution.py:478
  20.2 1.3 %shard_map.84 = (f32[2,256,256]{2,1,0:T(8,128)S(1)}, f32[4,128,256]{2,1,0:T(8,128)S(1)}, f32[2,128,128]{2,1,0:T(8,128)S(1)}, f32[2,128,128]{2,1,0:T(8,128)S(1)}, f32[2,128,128]{2,1,0:T(8,128)S(1)}) custom-call(s32[1,128]{1,0:T(1,128)S(1)} %pad_bitcast_fusion.numbers_ref, f32[4,2,128,128]{3,2,1,0:T(8,128)S(1)} %get-tuple-element.51.back_ref, ...), custom_call_target="tpu_custom_call" | custom-call | tf_op jit(solution)/shard_map/pallas_call | solution.py:478
  21.6 1.8 %collective-permute-start.11 = (f32[2,128,128]{2,1,0:T(8,128)S(1)}, f32[2,128,128]{2,1,0:T(8,128)S(1)}, u32[]{:S(2)}, u32[]{:S(2)}) collective-permute-start(f32[2,128,128]{2,1,0:T(8,128)S(1)} %get-tuple-element.63), channel_id=1, source_target_pairs={{30,0},{0,2},{2,4},{4,6},{6,8},{8,10},{10,12},{12,14},{14,16},{16,... | collective-permute-start | bytes 393224 | tf_op jit(solution)/shard_map/ppermute | solution.py:24
  24.1 1.4 %collective-permute-start.7 = (f32[2,128,128]{2,1,0:T(8,128)S(1)}, f32[2,128,128]{2,1,0:T(8,128)S(1)}, u32[]{:S(2)}, u32[]{:S(2)}) collective-permute-start(f32[2,128,128]{2,1,0:T(8,128)S(1)} %get-tuple-element.56), channel_id=1, source_target_pairs={{1,0},{0,1},{3,2},{2,3},{5,4},{4,5},{7,6},{6,7},{9,8},{8,9},{11,10... | collective-permute-start | bytes 393224 | tf_op jit(solution)/shard_map/ppermute | solution.py:24
  25.5 9.7 %collective-permute-done.11 = f32[2,128,128]{2,1,0:T(8,128)S(1)} collective-permute-done((f32[2,128,128]{2,1,0:T(8,128)S(1)}, f32[2,128,128]{2,1,0:T(8,128)S(1)}, u32[]{:S(2)}, u32[]{:S(2)}) %collective-permute-start.11) | collective-permute-done | bytes 131104 | tf_op jit(solution)/shard_map/ppermute | solution.py:24
  37.5 1.4 %collective-permute-start.19 = (f32[2,128,128]{2,1,0:T(8,128)S(1)}, f32[2,128,128]{2,1,0:T(8,128)S(1)}, u32[]{:S(2)}, u32[]{:S(2)}) collective-permute-start(f32[2,128,128]{2,1,0:T(8,128)S(1)} %get-tuple-element.69), channel_id=1, source_target_pairs={{1,0},{0,1},{3,2},{2,3},{5,4},{4,5},{7,6},{6,7},{9,8},{8,9},{11,10... | collective-permute-start | bytes 393224 | tf_op jit(solution)/shard_map/ppermute | solution.py:24
  38.8 2.4 %collective-permute-done.12.up_two = f32[2,128,128]{2,1,0:T(8,128)S(1)} collective-permute-done((f32[2,128,128]{2,1,0:T(8,128)S(1)}, f32[2,128,128]{2,1,0:T(8,128)S(1)}, u32[]{:S(2)}, u32[]{:S(2)}) %collective-permute-start.12) | collective-permute-done | bytes 131104 | tf_op jit(solution)/shard_map/ppermute | solution.py:24
  41.2 1.8 %collective-permute-done.10.up_one = f32[2,128,128]{2,1,0:T(8,128)S(1)} collective-permute-done((f32[2,128,128]{2,1,0:T(8,128)S(1)}, f32[2,128,128]{2,1,0:T(8,128)S(1)}, u32[]{:S(2)}, u32[]{:S(2)}) %collective-permute-start.10) | collective-permute-done | bytes 131104 | tf_op jit(solution)/shard_map/ppermute | solution.py:24
  44.1 2.3 %collective-permute-start.14 = (f32[4,128,128]{2,1,0:T(8,128)S(1)}, f32[4,128,128]{2,1,0:T(8,128)S(1)}, u32[]{:S(2)}, u32[]{:S(2)}) collective-permute-start(f32[4,128,128]{2,1,0:T(8,128)S(1)} %get-tuple-element.67), channel_id=1, source_target_pairs={{2,0},{4,2},{6,4},{8,6},{10,8},{12,10},{14,12},{16,14},{18,16},{20... | collective-permute-start | bytes 786440 | tf_op jit(solution)/shard_map/ppermute | solution.py:24
  46.3 0.9 %collective-permute-start.15 = (f32[2,128,128]{2,1,0:T(8,128)S(1)}, f32[2,128,128]{2,1,0:T(8,128)S(1)}, u32[]{:S(2)}, u32[]{:S(2)}) collective-permute-start(f32[2,128,128]{2,1,0:T(8,128)S(1)} %get-tuple-element.65.quad_ref.quad_two), channel_id=1, source_target_pairs={{1,0},{0,1},{3,2},{2,3},{5,4},{4,5},{7,6},{6,7},{9,8},{8,9},{11,10... | collective-permute-start | bytes 393224 | tf_op jit(solution)/shard_map/ppermute | solution.py:24
  47.2 1.8 %collective-permute-done.18.upper_ref = f32[2,128,128]{2,1,0:T(8,128)S(1)} collective-permute-done((f32[2,128,128]{2,1,0:T(8,128)S(1)}, f32[2,128,128]{2,1,0:T(8,128)S(1)}, u32[]{:S(2)}, u32[]{:S(2)}) %collective-permute-start.18) | collective-permute-done | bytes 131104 | tf_op jit(solution)/shard_map/ppermute | solution.py:24
  49.2 2.1 %collective-permute-done.15.upper_ref = f32[2,128,128]{2,1,0:T(8,128)S(1)} collective-permute-done((f32[2,128,128]{2,1,0:T(8,128)S(1)}, f32[2,128,128]{2,1,0:T(8,128)S(1)}, u32[]{:S(2)}, u32[]{:S(2)}) %collective-permute-start.15) | collective-permute-done | bytes 131104 | tf_op jit(solution)/shard_map/ppermute | solution.py:24
  52.0 1.2 %shard_map.88.moved_ref = f32[4,2,128,128]{3,2,1,0:T(8,128)S(1)} custom-call(s32[1,128]{1,0:T(1,128)S(1)} %pad_bitcast_fusion.numbers_ref, f32[2,256,256]{2,1,0:T(8,128)S(1)} %get-tuple-element.58.rest_ref.rest_one, f32[2,128,128]{2,1,0:T(8,128)S(1)} %get-tuple-element.64.quad_ref.quad_one, f32[4,128,128]{2,1,0:T(8,128)S(1)} %collective-permute-done.13.left_ref, ...), custom_call_target="tpu_custom_call" | custom-call | tf_op jit(solution)/shard_map/pallas_call | solution.py:478
  53.2 1.7 %collective-permute-done.16.lower_ref = f32[2,128,128]{2,1,0:T(8,128)S(1)} collective-permute-done((f32[2,128,128]{2,1,0:T(8,128)S(1)}, f32[2,128,128]{2,1,0:T(8,128)S(1)}, u32[]{:S(2)}, u32[]{:S(2)}) %collective-permute-start.16) | collective-permute-done | bytes 131104 | tf_op jit(solution)/shard_map/ppermute | solution.py:24
  54.9 1.6 %shard_map.89 = (f32[2,256,256]{2,1,0:T(8,128)S(1)}, f32[2,128,256]{2,1,0:T(8,128)S(1)}, f32[2,128,128]{2,1,0:T(8,128)S(1)}, f32[2,128,128]{2,1,0:T(8,128)S(1)},...) custom-call(s32[1,128]{1,0:T(1,128)S(1)} %pad_bitcast_fusion.numbers_ref, ...), custom_call_target="tpu_custom_call" | custom-call | tf_op jit(solution)/shard_map/pallas_call | solution.py:478
  56.6 1.3 %shard_map.90 = (f32[2,256,256]{2,1,0:T(8,128)S(1)}, f32[4,128,256]{2,1,0:T(8,128)S(1)}, f32[2,128,128]{2,1,0:T(8,128)S(1)}, f32[2,128,128]{2,1,0:T(8,128)S(1)}, f32[2,128,128]{2,1,0:T(8,128)S(1)}) custom-call(s32[1,128]{1,0:T(1,128)S(1)} %pad_bitcast_fusion.numbers_ref, f32[4,2,128,128]{3,2,1,0:T(8,128)S(1)} %get-tuple-element.70.back_ref, ...), custom_call_target="tpu_custom_call" | custom-call | tf_op jit(solution)/shard_map/pallas_call | solution.py:478
  58.0 1.2 %collective-permute-start.24 = (f32[2,128,128]{2,1,0:T(8,128)S(1)}, f32[2,128,128]{2,1,0:T(8,128)S(1)}, u32[]{:S(2)}, u32[]{:S(2)}) collective-permute-start(f32[2,128,128]{2,1,0:T(8,128)S(1)} %get-tuple-element.78), channel_id=1, source_target_pairs={{30,0},{0,2},{2,4},{4,6},{6,8},{8,10},{10,12},{12,14},{14,16},{16,... | collective-permute-start | bytes 393224 | tf_op jit(solution)/shard_map/ppermute | solution.py:24
  59.4 1.9 %collective-permute-start.27 = (f32[2,128,128]{2,1,0:T(8,128)S(1)}, f32[2,128,128]{2,1,0:T(8,128)S(1)}, u32[]{:S(2)}, u32[]{:S(2)}) collective-permute-start(f32[2,128,128]{2,1,0:T(8,128)S(1)} %get-tuple-element.80), channel_id=1, source_target_pairs={{1,0},{0,1},{3,2},{2,3},{5,4},{4,5},{7,6},{6,7},{9,8},{8,9},{11,10... | collective-permute-start | bytes 393224 | tf_op jit(solution)/shard_map/ppermute | solution.py:24
  61.3 9.4 %collective-permute-done.22 = f32[2,128,128]{2,1,0:T(8,128)S(1)} collective-permute-done((f32[2,128,128]{2,1,0:T(8,128)S(1)}, f32[2,128,128]{2,1,0:T(8,128)S(1)}, u32[]{:S(2)}, u32[]{:S(2)}) %collective-permute-start.22) | collective-permute-done | bytes 131104 | tf_op jit(solution)/shard_map/ppermute | solution.py:24
  71.0 1.0 %collective-permute-done.24 = f32[2,128,128]{2,1,0:T(8,128)S(1)} collective-permute-done((f32[2,128,128]{2,1,0:T(8,128)S(1)}, f32[2,128,128]{2,1,0:T(8,128)S(1)}, u32[]{:S(2)}, u32[]{:S(2)}) %collective-permute-start.24) | collective-permute-done | bytes 131104 | tf_op jit(solution)/shard_map/ppermute | solution.py:24
  72.9 0.9 %finish_low.1.part_ref = f32[2,2,256,256]{3,2,1,0:T(8,128)} custom-call(f32[2,256,256]{2,1,0:T(8,128)S(1)} %get-tuple-element.58.rest_ref.rest_one, f32[2,256,256]{2,1,0:T(8,128)S(1)} %get-tuple-element.59.rest_ref.rest_two, f32[2,256,256]{2,1,0:T(8,128)S(1)} %get-tuple-element.72.own_one, f32[2,256,256]{2,1,0:T(8,128)S(1)} %get-tuple-element.73.own_two, ...), custom_call_target="tpu_custom_call" | custom-call | tf_op jit(solution)/shard_map/finish_low/pallas_call | solution.py:626
  73.7 2.0 %collective-permute-done.23.up_one = f32[2,128,128]{2,1,0:T(8,128)S(1)} collective-permute-done((f32[2,128,128]{2,1,0:T(8,128)S(1)}, f32[2,128,128]{2,1,0:T(8,128)S(1)}, u32[]{:S(2)}, u32[]{:S(2)}) %collective-permute-start.23) | collective-permute-done | bytes 131104 | tf_op jit(solution)/shard_map/ppermute | solution.py:24
  75.7 1.4 %collective-permute-done.25.up_two = f32[2,128,128]{2,1,0:T(8,128)S(1)} collective-permute-done((f32[2,128,128]{2,1,0:T(8,128)S(1)}, f32[2,128,128]{2,1,0:T(8,128)S(1)}, u32[]{:S(2)}, u32[]{:S(2)}) %collective-permute-start.25) | collective-permute-done | bytes 131104 | tf_op jit(solution)/shard_map/ppermute | solution.py:24
  77.1 0.9 %finish_top.1 = f32[2,2,256,256]{3,2,1,0:T(8,128)} custom-call(f32[2,256,256]{2,1,0:T(8,128)S(1)} %get-tuple-element.58.rest_ref.rest_one, f32[2,256,256]{2,1,0:T(8,128)S(1)} %get-tuple-element.59.rest_ref.rest_two, f32[2,128,128]{2,1,0:T(8,128)S(1)} %get-tuple-element.64.quad_ref.quad_one, ...), custom_call_target="tpu_custom_call", output_to_operand_aliasing={{}: (9, {})} | custom-call | tf_op jit(solution)/shard_map/finish_top/pallas_call | solution.py:635
  (51 shorter events, 8.3 us)
Async XLA Ops:
  0.0 10.4 %copy-start = (f32[128,128]{1,0:T(8,128)S(1)}, f32[128,128]{1,0:T(8,128)}, u32[]{:S(2)}) copy-start(f32[128,128]{1,0:T(8,128)} %param.10) | copy-start | bytes 196612
  1.4 16.5 %collective-permute-start = (f32[4,128,256]{2,1,0:T(8,128)S(1)}, f32[4,128,256]{2,1,0:T(8,128)S(1)}, u32[]{:S(2)}, u32[]{:S(2)}) collective-permute-start(f32[4,128,256]{2,1,0:T(8,128)S(1)} %get-tuple-element.44), channel_id=1, source_target_pairs={{2,0},{4,2},{6,4},{8,6},{10,8},{12,10},{14,12},{16,14},{18,16},{20... | collective-permute-start | bytes 1572872 | tf_op jit(solution)/shard_map/ppermute | solution.py:24
  6.9 5.9 %collective-permute-start.1 = (f32[2,128,128]{2,1,0:T(8,128)S(1)}, f32[2,128,128]{2,1,0:T(8,128)S(1)}, u32[]{:S(2)}, u32[]{:S(2)}) collective-permute-start(f32[2,128,128]{2,1,0:T(8,128)S(1)} %get-tuple-element.45), channel_id=1, source_target_pairs={{1,0},{0,1},{3,2},{2,3},{5,4},{4,5},{7,6},{6,7},{9,8},{8,9},{11,10... | collective-permute-start | bytes 393224 | tf_op jit(solution)/shard_map/ppermute | solution.py:24
  8.4 5.8 %collective-permute-start.2 = (f32[2,128,128]{2,1,0:T(8,128)S(1)}, f32[2,128,128]{2,1,0:T(8,128)S(1)}, u32[]{:S(2)}, u32[]{:S(2)}) collective-permute-start(f32[2,128,128]{2,1,0:T(8,128)S(1)} %get-tuple-element.46), channel_id=1, source_target_pairs={{1,0},{0,1},{3,2},{2,3},{5,4},{4,5},{7,6},{6,7},{9,8},{8,9},{11,10... | collective-permute-start | bytes 393224 | tf_op jit(solution)/shard_map/ppermute | solution.py:24
  8.9 9.0 %collective-permute-start.3 = (f32[4,128,128]{2,1,0:T(8,128)S(1)}, f32[4,128,128]{2,1,0:T(8,128)S(1)}, u32[]{:S(2)}, u32[]{:S(2)}) collective-permute-start(f32[4,128,128]{2,1,0:T(8,128)S(1)} %get-tuple-element.47), channel_id=1, source_target_pairs={{1,0},{0,1},{3,2},{2,3},{5,4},{4,5},{7,6},{6,7},{9,8},{8,9},{11,10... | collective-permute-start | bytes 786440 | tf_op jit(solution)/shard_map/ppermute | solution.py:24
  10.7 0.7 copy-start.1
  12.8 4.8 %collective-permute-start.4 = (f32[2,128,128]{2,1,0:T(8,128)S(1)}, f32[2,128,128]{2,1,0:T(8,128)S(1)}, u32[]{:S(2)}, u32[]{:S(2)}) collective-permute-start(f32[2,128,128]{2,1,0:T(8,128)S(1)} %collective-permute-done.1.upper_one), channel_id=1, source_target_pairs={{2,0},{4,2},{6,4},{8,6},{10,8},{12,10},{14,12},{16,14},{18,16},{20... | collective-permute-start | bytes 393224 | tf_op jit(solution)/shard_map/ppermute | solution.py:24
  14.2 3.6 %collective-permute-start.5 = (f32[2,128,128]{2,1,0:T(8,128)S(1)}, f32[2,128,128]{2,1,0:T(8,128)S(1)}, u32[]{:S(2)}, u32[]{:S(2)}) collective-permute-start(f32[2,128,128]{2,1,0:T(8,128)S(1)} %collective-permute-done.2.upper_two), channel_id=1, source_target_pairs={{2,0},{4,2},{6,4},{8,6},{10,8},{12,10},{14,12},{16,14},{18,16},{20... | collective-permute-start | bytes 393224 | tf_op jit(solution)/shard_map/ppermute | solution.py:24
  15.4 0.7 copy-start.2
  21.5 21.5 %collective-permute-start.6 = (f32[4,128,256]{2,1,0:T(8,128)S(1)}, f32[4,128,256]{2,1,0:T(8,128)S(1)}, u32[]{:S(2)}, u32[]{:S(2)}) collective-permute-start(f32[4,128,256]{2,1,0:T(8,128)S(1)} %get-tuple-element.55), channel_id=1, source_target_pairs={{30,0},{0,2},{2,4},{4,6},{6,8},{8,10},{10,12},{12,14},{14,16},{16,... | collective-permute-start | bytes 1572872 | tf_op jit(solution)/shard_map/ppermute | solution.py:24
  21.6 13.6 %collective-permute-start.11 = (f32[2,128,128]{2,1,0:T(8,128)S(1)}, f32[2,128,128]{2,1,0:T(8,128)S(1)}, u32[]{:S(2)}, u32[]{:S(2)}) collective-permute-start(f32[2,128,128]{2,1,0:T(8,128)S(1)} %get-tuple-element.63), channel_id=1, source_target_pairs={{30,0},{0,2},{2,4},{4,6},{6,8},{8,10},{10,12},{12,14},{14,16},{16,... | collective-permute-start | bytes 393224 | tf_op jit(solution)/shard_map/ppermute | solution.py:24
  23.4 13.2 %collective-permute-start.9 = (f32[2,128,128]{2,1,0:T(8,128)S(1)}, f32[2,128,128]{2,1,0:T(8,128)S(1)}, u32[]{:S(2)}, u32[]{:S(2)}) collective-permute-start(f32[2,128,128]{2,1,0:T(8,128)S(1)} %get-tuple-element.61), channel_id=1, source_target_pairs={{30,0},{0,2},{2,4},{4,6},{6,8},{8,10},{10,12},{12,14},{14,16},{16,... | collective-permute-start | bytes 393224 | tf_op jit(solution)/shard_map/ppermute | solution.py:24
  23.5 13.9 %collective-permute-start.8 = (f32[2,128,128]{2,1,0:T(8,128)S(1)}, f32[2,128,128]{2,1,0:T(8,128)S(1)}, u32[]{:S(2)}, u32[]{:S(2)}) collective-permute-start(f32[2,128,128]{2,1,0:T(8,128)S(1)} %get-tuple-element.57), channel_id=1, source_target_pairs={{1,0},{0,1},{3,2},{2,3},{5,4},{4,5},{7,6},{6,7},{9,8},{8,9},{11,10... | collective-permute-start | bytes 393224 | tf_op jit(solution)/shard_map/ppermute | solution.py:24
  24.1 13.3 %collective-permute-start.7 = (f32[2,128,128]{2,1,0:T(8,128)S(1)}, f32[2,128,128]{2,1,0:T(8,128)S(1)}, u32[]{:S(2)}, u32[]{:S(2)}) collective-permute-start(f32[2,128,128]{2,1,0:T(8,128)S(1)} %get-tuple-element.56), channel_id=1, source_target_pairs={{1,0},{0,1},{3,2},{2,3},{5,4},{4,5},{7,6},{6,7},{9,8},{8,9},{11,10... | collective-permute-start | bytes 393224 | tf_op jit(solution)/shard_map/ppermute | solution.py:24
  35.2 6.0 %collective-permute-start.12 = (f32[2,128,128]{2,1,0:T(8,128)S(1)}, f32[2,128,128]{2,1,0:T(8,128)S(1)}, u32[]{:S(2)}, u32[]{:S(2)}) collective-permute-start(f32[2,128,128]{2,1,0:T(8,128)S(1)} %add.15), channel_id=1, source_target_pairs={{1,0},{0,1},{3,2},{2,3},{5,4},{4,5},{7,6},{6,7},{9,8},{8,9},{11,10... | collective-permute-start | bytes 393224 | tf_op jit(solution)/shard_map/ppermute | solution.py:24
  36.6 6.4 %collective-permute-start.10 = (f32[2,128,128]{2,1,0:T(8,128)S(1)}, f32[2,128,128]{2,1,0:T(8,128)S(1)}, u32[]{:S(2)}, u32[]{:S(2)}) collective-permute-start(f32[2,128,128]{2,1,0:T(8,128)S(1)} %add.14), channel_id=1, source_target_pairs={{1,0},{0,1},{3,2},{2,3},{5,4},{4,5},{7,6},{6,7},{9,8},{8,9},{11,10... | collective-permute-start | bytes 393224 | tf_op jit(solution)/shard_map/ppermute | solution.py:24
  37.5 11.6 %collective-permute-start.19 = (f32[2,128,128]{2,1,0:T(8,128)S(1)}, f32[2,128,128]{2,1,0:T(8,128)S(1)}, u32[]{:S(2)}, u32[]{:S(2)}) collective-permute-start(f32[2,128,128]{2,1,0:T(8,128)S(1)} %get-tuple-element.69), channel_id=1, source_target_pairs={{1,0},{0,1},{3,2},{2,3},{5,4},{4,5},{7,6},{6,7},{9,8},{8,9},{11,10... | collective-permute-start | bytes 393224 | tf_op jit(solution)/shard_map/ppermute | solution.py:24
  43.1 5.9 %collective-permute-start.18 = (f32[2,128,128]{2,1,0:T(8,128)S(1)}, f32[2,128,128]{2,1,0:T(8,128)S(1)}, u32[]{:S(2)}, u32[]{:S(2)}) collective-permute-start(f32[2,128,128]{2,1,0:T(8,128)S(1)} %get-tuple-element.64.quad_ref.quad_one), channel_id=1, source_target_pairs={{1,0},{0,1},{3,2},{2,3},{5,4},{4,5},{7,6},{6,7},{9,8},{8,9},{11,10... | collective-permute-start | bytes 393224 | tf_op jit(solution)/shard_map/ppermute | solution.py:24
  43.9 8.1 %collective-permute-start.13 = (f32[4,128,128]{2,1,0:T(8,128)S(1)}, f32[4,128,128]{2,1,0:T(8,128)S(1)}, u32[]{:S(2)}, u32[]{:S(2)}) collective-permute-start(f32[4,128,128]{2,1,0:T(8,128)S(1)} %get-tuple-element.66), channel_id=1, source_target_pairs={{2,0},{4,2},{6,4},{8,6},{10,8},{12,10},{14,12},{16,14},{18,16},{20... | collective-permute-start | bytes 786440 | tf_op jit(solution)/shard_map/ppermute | solution.py:24
  44.1 8.0 %collective-permute-start.14 = (f32[4,128,128]{2,1,0:T(8,128)S(1)}, f32[4,128,128]{2,1,0:T(8,128)S(1)}, u32[]{:S(2)}, u32[]{:S(2)}) collective-permute-start(f32[4,128,128]{2,1,0:T(8,128)S(1)} %get-tuple-element.67), channel_id=1, source_target_pairs={{2,0},{4,2},{6,4},{8,6},{10,8},{12,10},{14,12},{16,14},{18,16},{20... | collective-permute-start | bytes 786440 | tf_op jit(solution)/shard_map/ppermute | solution.py:24
  46.3 5.0 %collective-permute-start.15 = (f32[2,128,128]{2,1,0:T(8,128)S(1)}, f32[2,128,128]{2,1,0:T(8,128)S(1)}, u32[]{:S(2)}, u32[]{:S(2)}) collective-permute-start(f32[2,128,128]{2,1,0:T(8,128)S(1)} %get-tuple-element.65.quad_ref.quad_two), channel_id=1, source_target_pairs={{1,0},{0,1},{3,2},{2,3},{5,4},{4,5},{7,6},{6,7},{9,8},{8,9},{11,10... | collective-permute-start | bytes 393224 | tf_op jit(solution)/shard_map/ppermute | solution.py:24
  49.0 3.0 %collective-permute-start.20 = (f32[2,128,128]{2,1,0:T(8,128)S(1)}, f32[2,128,128]{2,1,0:T(8,128)S(1)}, u32[]{:S(2)}, u32[]{:S(2)}) collective-permute-start(f32[2,128,128]{2,1,0:T(8,128)S(1)} %collective-permute-done.18.upper_ref), channel_id=1, source_target_pairs={{2,0},{4,2},{6,4},{8,6},{10,8},{12,10},{14,12},{16,14},{18,16},{20... | collective-permute-start | bytes 393224 | tf_op jit(solution)/shard_map/ppermute | solution.py:24
  49.0 5.9 %collective-permute-start.16 = (f32[2,128,128]{2,1,0:T(8,128)S(1)}, f32[2,128,128]{2,1,0:T(8,128)S(1)}, u32[]{:S(2)}, u32[]{:S(2)}) collective-permute-start(f32[2,128,128]{2,1,0:T(8,128)S(1)} %get-tuple-element.68), channel_id=1, source_target_pairs={{1,0},{0,1},{3,2},{2,3},{5,4},{4,5},{7,6},{6,7},{9,8},{8,9},{11,10... | collective-permute-start | bytes 393224 | tf_op jit(solution)/shard_map/ppermute | solution.py:24
  51.3 3.6 %collective-permute-start.17 = (f32[2,128,128]{2,1,0:T(8,128)S(1)}, f32[2,128,128]{2,1,0:T(8,128)S(1)}, u32[]{:S(2)}, u32[]{:S(2)}) collective-permute-start(f32[2,128,128]{2,1,0:T(8,128)S(1)} %collective-permute-done.15.upper_ref), channel_id=1, source_target_pairs={{2,0},{4,2},{6,4},{8,6},{10,8},{12,10},{14,12},{16,14},{18,16},{20... | collective-permute-start | bytes 393224 | tf_op jit(solution)/shard_map/ppermute | solution.py:24
  57.9 19.2 %collective-permute-start.21 = (f32[4,128,256]{2,1,0:T(8,128)S(1)}, f32[4,128,256]{2,1,0:T(8,128)S(1)}, u32[]{:S(2)}, u32[]{:S(2)}) collective-permute-start(f32[4,128,256]{2,1,0:T(8,128)S(1)} %get-tuple-element.74), channel_id=1, source_target_pairs={{30,0},{0,2},{2,4},{4,6},{6,8},{8,10},{10,12},{12,14},{14,16},{16,... | collective-permute-start | bytes 1572872 | tf_op jit(solution)/shard_map/ppermute | solution.py:24
  58.0 12.7 %collective-permute-start.22 = (f32[2,128,128]{2,1,0:T(8,128)S(1)}, f32[2,128,128]{2,1,0:T(8,128)S(1)}, u32[]{:S(2)}, u32[]{:S(2)}) collective-permute-start(f32[2,128,128]{2,1,0:T(8,128)S(1)} %get-tuple-element.76), channel_id=1, source_target_pairs={{30,0},{0,2},{2,4},{4,6},{6,8},{8,10},{10,12},{12,14},{14,16},{16,... | collective-permute-start | bytes 393224 | tf_op jit(solution)/shard_map/ppermute | solution.py:24
  58.0 14.0 %collective-permute-start.24 = (f32[2,128,128]{2,1,0:T(8,128)S(1)}, f32[2,128,128]{2,1,0:T(8,128)S(1)}, u32[]{:S(2)}, u32[]{:S(2)}) collective-permute-start(f32[2,128,128]{2,1,0:T(8,128)S(1)} %get-tuple-element.78), channel_id=1, source_target_pairs={{30,0},{0,2},{2,4},{4,6},{6,8},{8,10},{10,12},{12,14},{14,16},{16,... | collective-permute-start | bytes 393224 | tf_op jit(solution)/shard_map/ppermute | solution.py:24
  59.3 13.6 %collective-permute-start.26 = (f32[2,128,128]{2,1,0:T(8,128)S(1)}, f32[2,128,128]{2,1,0:T(8,128)S(1)}, u32[]{:S(2)}, u32[]{:S(2)}) collective-permute-start(f32[2,128,128]{2,1,0:T(8,128)S(1)} %get-tuple-element.79), channel_id=1, source_target_pairs={{1,0},{0,1},{3,2},{2,3},{5,4},{4,5},{7,6},{6,7},{9,8},{8,9},{11,10... | collective-permute-start | bytes 393224 | tf_op jit(solution)/shard_map/ppermute | solution.py:24
  59.4 13.5 %collective-permute-start.27 = (f32[2,128,128]{2,1,0:T(8,128)S(1)}, f32[2,128,128]{2,1,0:T(8,128)S(1)}, u32[]{:S(2)}, u32[]{:S(2)}) collective-permute-start(f32[2,128,128]{2,1,0:T(8,128)S(1)} %get-tuple-element.80), channel_id=1, source_target_pairs={{1,0},{0,1},{3,2},{2,3},{5,4},{4,5},{7,6},{6,7},{9,8},{8,9},{11,10... | collective-permute-start | bytes 393224 | tf_op jit(solution)/shard_map/ppermute | solution.py:24
  70.7 5.0 %collective-permute-start.23 = (f32[2,128,128]{2,1,0:T(8,128)S(1)}, f32[2,128,128]{2,1,0:T(8,128)S(1)}, u32[]{:S(2)}, u32[]{:S(2)}) collective-permute-start(f32[2,128,128]{2,1,0:T(8,128)S(1)} %add.16), channel_id=1, source_target_pairs={{1,0},{0,1},{3,2},{2,3},{5,4},{4,5},{7,6},{6,7},{9,8},{8,9},{11,10... | collective-permute-start | bytes 393224 | tf_op jit(solution)/shard_map/ppermute | solution.py:24
  72.1 5.0 %collective-permute-start.25 = (f32[2,128,128]{2,1,0:T(8,128)S(1)}, f32[2,128,128]{2,1,0:T(8,128)S(1)}, u32[]{:S(2)}, u32[]{:S(2)}) collective-permute-start(f32[2,128,128]{2,1,0:T(8,128)S(1)} %add.17), channel_id=1, source_target_pairs={{1,0},{0,1},{3,2},{2,3},{5,4},{4,5},{7,6},{6,7},{9,8},{8,9},{11,10... | collective-permute-start | bytes 393224 | tf_op jit(solution)/shard_map/ppermute | solution.py:24

commit v7 on v6

--- a/solution.py
+++ b/solution.py
@@ -440,10 +440,11 @@
 
 def finish_top_kernel(
     rest_one, rest_two, quad_one, quad_two, own_one, own_two, above_ref, up_one, up_two, part_ref,
-    out_ref, rows_ref, sem, *, width,
+    out_ref, rows_ref, sems, *, width,
 ):
     del part_ref
     tile_px = own_one.shape[1]
+    copies = []
     parts = ((rest_one, quad_one, own_one, up_one), (rest_two, quad_two, own_two, up_two))
     for s, (rest_ref, quad_ref, own_ref, up_ref) in enumerate(parts):
         above = above_ref.at[pl.ds(2 * s, 2)]
@@ -451,9 +452,12 @@
             top, right = slice(0, width), slice(width, tile_px)
             rows_ref[s, c, :, :width] = quad_value(quad_ref, own_ref, above, up_ref, c, width)
             rows_ref[s, c, :, width:] = step(rest_ref[c, top, right], own_ref[c, top, right] + above[c, :, right])
-    copy = pltpu.make_async_copy(rows_ref, out_ref.at[:, :, pl.ds(0, width), :], sem)
-    copy.start()
-    copy.wait()
+            copies.append(
+                pltpu.make_async_copy(rows_ref.at[s, c], out_ref.at[s, c, pl.ds(0, width), :], sems.at[2 * s + c])
+            )
+            copies[-1].start()
+    for copy in copies:
+        copy.wait()
 
 
 def stage_kernel(*refs):
@@ -543,13 +547,12 @@
     gradient = [whole, strip, square, square, square]
 
     left, low, full = (0, width), (width, across), (0, tile_px)
-    up_one, up_two, left_low, top = pack(
-        specimen_slices, [((0,), left, left), ((1,), left, left), ((0, 1), low, left), ((0, 1), left, full)]
-    )
+    up_one, top = pack(specimen_slices, [((0,), left, left), ((0, 1), left, full)])
     upper_one = from_behind(up_one, "col", -1)
+    below = from_behind(top, "row", -1)
+    up_two, left_low = pack(specimen_slices, [((1,), left, left), ((0, 1), low, left)])
     upper_two = from_behind(up_two, "col", -1)
     lower = from_behind(left_low, "col", -1)
-    below = from_behind(top, "row", -1)
     far = (specimen_slices, illumination_probe, amplitudes[0, 0], jnp.asarray(dft_operands(width)))
     tile, probe, measured, table = pl.pallas_call(
         stage_kernel,
@@ -637,7 +640,7 @@
                 in_specs=[VMEM] * 9 + [FAR],
                 input_output_aliases={9: 0},
                 scratch_shapes=[
-                    pltpu.VMEM((2, 2, width, tile_px), jnp.float32), pltpu.SemaphoreType.DMA(()),
+                    pltpu.VMEM((2, 2, width, tile_px), jnp.float32), pltpu.SemaphoreType.DMA((4,)),
                 ],
                 name="finish_top",
                 **end,

time: 78.4 us -> 83.6 us (1.066)
  starting transfers between devices: 25.9 us -> 28.9 us
  waiting for transfers between devices: 37.4 us -> 38.8 us
    ppermute x28, starting transfers between devices: 25.9 us -> 28.9 us  [from_behind(): return lax.ppermute(block, axis, route)]
    ppermute x28, waiting for transfers between devices: 37.4 us -> 38.8 us  [from_behind(): return lax.ppermute(block, axis, route)]
    pallas_call x1 -> x2, Pallas kernels: 1.37 us -> 2.19 us  [pack(): pl.pallas_call(functools.partial(pack_kernel, boxes=boxes), in_specs=[FAR...]
  transfers between devices with their start and end apart: 28 -> 28, of which waited for: 15 -> 15; matrix products, arithmetic and copies ran while one was open for 1% -> 1% of each run, Pallas kernels for 5% -> 6%
where the time goes in v7:
time: 83.6 us; the launch traced here: 83.4 us
  waiting for transfers between devices  38.8 us (46%)
  starting transfers between devices  28.9 us (35%)
  Pallas kernels  13.4 us (16%)
  local copies, waits for them, and re-layouts  1.1 us (1%)
  between operations  1 us (1%)
    ppermute x28, waiting for transfers between devices, from_behind(): return lax.ppermute(block, axis, route)  38.8 us
    ppermute x28, starting transfers between devices, from_behind(): return lax.ppermute(block, axis, route)  28.9 us
    pallas_call x8, Pallas kernels, call(): pl.pallas_call(functools.partial(kernel, **static), in_specs=[VMEM] * (le...  7.97 us
    pallas_call x2, Pallas kernels, pack(): pl.pallas_call(functools.partial(pack_kernel, boxes=boxes), in_specs=[FAR...  2.19 us
  transfers between devices with their start and end apart: 28, of which 15 were waited for; matrix products, arithmetic and copies ran while one was open for 1% of the time, Pallas kernels for 6%

profile of v7, /device:TPU:0, one launch (start us, length us, event | category | flops | bytes accessed | tf_op | source)
XLA Modules:
  0.0 83.4 jit_solution(6813072868114111810)
XLA Ops:
  0.0 1.1 %shard_map.82 = (f32[2,128,128]{2,1,0:T(8,128)S(1)}, f32[4,128,256]{2,1,0:T(8,128)S(1)}) custom-call(f32[2,2,256,256]{3,2,1,0:T(8,128)} %whole_ref.3), custom_call_target="tpu_custom_call" | custom-call | tf_op jit(solution)/shard_map/pallas_call | solution.py:507
  1.1 5.5 %collective-permute-start = (f32[4,128,256]{2,1,0:T(8,128)S(1)}, f32[4,128,256]{2,1,0:T(8,128)S(1)}, u32[]{:S(2)}, u32[]{:S(2)}) collective-permute-start(f32[4,128,256]{2,1,0:T(8,128)S(1)} %get-tuple-element.44), channel_id=1, source_target_pairs={{2,0},{4,2},{6,4},{8,6},{10,8},{12,10},{14,12},{16,14},{18,16},{20... | collective-permute-start | bytes 1572872 | tf_op jit(solution)/shard_map/ppermute | solution.py:24
  6.7 1.1 %shard_map.83 = (f32[2,128,128]{2,1,0:T(8,128)S(1)}, f32[4,128,128]{2,1,0:T(8,128)S(1)}) custom-call(f32[2,2,256,256]{3,2,1,0:T(8,128)} %whole_ref.3), custom_call_target="tpu_custom_call" | custom-call | tf_op jit(solution)/shard_map/pallas_call | solution.py:507
  7.7 1.6 %collective-permute-start.2 = (f32[2,128,128]{2,1,0:T(8,128)S(1)}, f32[2,128,128]{2,1,0:T(8,128)S(1)}, u32[]{:S(2)}, u32[]{:S(2)}) collective-permute-start(f32[2,128,128]{2,1,0:T(8,128)S(1)} %get-tuple-element.46), channel_id=1, source_target_pairs={{1,0},{0,1},{3,2},{2,3},{5,4},{4,5},{7,6},{6,7},{9,8},{8,9},{11,10... | collective-permute-start | bytes 393224 | tf_op jit(solution)/shard_map/ppermute | solution.py:24
  9.8 1.5 %collective-permute-start.1 = (f32[2,128,128]{2,1,0:T(8,128)S(1)}, f32[2,128,128]{2,1,0:T(8,128)S(1)}, u32[]{:S(2)}, u32[]{:S(2)}) collective-permute-start(f32[2,128,128]{2,1,0:T(8,128)S(1)} %get-tuple-element.45), channel_id=1, source_target_pairs={{1,0},{0,1},{3,2},{2,3},{5,4},{4,5},{7,6},{6,7},{9,8},{8,9},{11,10... | collective-permute-start | bytes 393224 | tf_op jit(solution)/shard_map/ppermute | solution.py:24
  12.4 1.3 %collective-permute-done.2.upper_two = f32[2,128,128]{2,1,0:T(8,128)S(1)} collective-permute-done((f32[2,128,128]{2,1,0:T(8,128)S(1)}, f32[2,128,128]{2,1,0:T(8,128)S(1)}, u32[]{:S(2)}, u32[]{:S(2)}) %collective-permute-start.2) | collective-permute-done | bytes 131104 | tf_op jit(solution)/shard_map/ppermute | solution.py:24
  13.7 4.2 %collective-permute-done.1.upper_one = f32[2,128,128]{2,1,0:T(8,128)S(1)} collective-permute-done((f32[2,128,128]{2,1,0:T(8,128)S(1)}, f32[2,128,128]{2,1,0:T(8,128)S(1)}, u32[]{:S(2)}, u32[]{:S(2)}) %collective-permute-start.1) | collective-permute-done | bytes 131104 | tf_op jit(solution)/shard_map/ppermute | solution.py:24
  18.0 4.0 %collective-permute-start.4 = (f32[2,128,128]{2,1,0:T(8,128)S(1)}, f32[2,128,128]{2,1,0:T(8,128)S(1)}, u32[]{:S(2)}, u32[]{:S(2)}) collective-permute-start(f32[2,128,128]{2,1,0:T(8,128)S(1)} %collective-permute-done.1.upper_one), channel_id=1, source_target_pairs={{2,0},{4,2},{6,4},{8,6},{10,8},{12,10},{14,12},{16,14},{18,16},{20... | collective-permute-start | bytes 393224 | tf_op jit(solution)/shard_map/ppermute | solution.py:24
  22.7 1.5 %stage.1 = (f32[2,2,256,256]{3,2,1,0:T(8,128)S(1)}, f32[2,128,128]{2,1,0:T(8,128)S(1)}, f32[4,128,128]{2,1,0:T(8,128)S(1)}, bf16[4,256,256]{2,1,0:T(8,128)(2,1)S(1)}) custom-call(f32[2,2,256,256]{3,2,1,0:T(8,128)} %whole_ref.3, f32[2,128,128]{2,1,0:T(8,128)} %refs_1_.1, f32[4,128,128]{2,1,0:T(8,128)} %bitcast.6, bf16[4,256,256]{2,1,0:T(8,128)(2,1)} %constant.4.clone.refs_3_), custom_call_target="tpu_custom_call" | custom-call | tf_op jit(solution)/shard_map/stage/pallas_call | solution.py:557
  24.5 2.3 %shard_map.84 = (f32[2,256,256]{2,1,0:T(8,128)S(1)}, f32[2,128,256]{2,1,0:T(8,128)S(1)}, f32[2,128,128]{2,1,0:T(8,128)S(1)}, f32[2,128,128]{2,1,0:T(8,128)S(1)},...) custom-call(s32[1,128]{1,0:T(1,128)S(1)} %pad_bitcast_fusion.numbers_ref, ...), custom_call_target="tpu_custom_call" | custom-call | tf_op jit(solution)/shard_map/pallas_call | solution.py:482
  26.8 1.3 %shard_map.85 = (f32[2,256,256]{2,1,0:T(8,128)S(1)}, f32[4,128,256]{2,1,0:T(8,128)S(1)}, f32[2,128,128]{2,1,0:T(8,128)S(1)}, f32[2,128,128]{2,1,0:T(8,128)S(1)}, f32[2,128,128]{2,1,0:T(8,128)S(1)}) custom-call(s32[1,128]{1,0:T(1,128)S(1)} %pad_bitcast_fusion.numbers_ref, f32[4,2,128,128]{3,2,1,0:T(8,128)S(1)} %get-tuple-element.51.back_ref, ...), custom_call_target="tpu_custom_call" | custom-call | tf_op jit(solution)/shard_map/pallas_call | solution.py:482
  28.2 1.0 %collective-permute-start.9 = (f32[2,128,128]{2,1,0:T(8,128)S(1)}, f32[2,128,128]{2,1,0:T(8,128)S(1)}, u32[]{:S(2)}, u32[]{:S(2)}) collective-permute-start(f32[2,128,128]{2,1,0:T(8,128)S(1)} %get-tuple-element.61), channel_id=1, source_target_pairs={{30,0},{0,2},{2,4},{4,6},{6,8},{8,10},{10,12},{12,14},{14,16},{16,... | collective-permute-start | bytes 393224 | tf_op jit(solution)/shard_map/ppermute | solution.py:24
  29.9 1.3 %collective-permute-start.7 = (f32[2,128,128]{2,1,0:T(8,128)S(1)}, f32[2,128,128]{2,1,0:T(8,128)S(1)}, u32[]{:S(2)}, u32[]{:S(2)}) collective-permute-start(f32[2,128,128]{2,1,0:T(8,128)S(1)} %get-tuple-element.56), channel_id=1, source_target_pairs={{1,0},{0,1},{3,2},{2,3},{5,4},{4,5},{7,6},{6,7},{9,8},{8,9},{11,10... | collective-permute-start | bytes 393224 | tf_op jit(solution)/shard_map/ppermute | solution.py:24
  31.2 10.5 %collective-permute-done.11 = f32[2,128,128]{2,1,0:T(8,128)S(1)} collective-permute-done((f32[2,128,128]{2,1,0:T(8,128)S(1)}, f32[2,128,128]{2,1,0:T(8,128)S(1)}, u32[]{:S(2)}, u32[]{:S(2)}) %collective-permute-start.11) | collective-permute-done | bytes 131104 | tf_op jit(solution)/shard_map/ppermute | solution.py:24
  44.0 1.4 %collective-permute-start.19 = (f32[2,128,128]{2,1,0:T(8,128)S(1)}, f32[2,128,128]{2,1,0:T(8,128)S(1)}, u32[]{:S(2)}, u32[]{:S(2)}) collective-permute-start(f32[2,128,128]{2,1,0:T(8,128)S(1)} %get-tuple-element.69), channel_id=1, source_target_pairs={{1,0},{0,1},{3,2},{2,3},{5,4},{4,5},{7,6},{6,7},{9,8},{8,9},{11,10... | collective-permute-start | bytes 393224 | tf_op jit(solution)/shard_map/ppermute | solution.py:24
  45.4 1.4 %collective-permute-done.12.up_two = f32[2,128,128]{2,1,0:T(8,128)S(1)} collective-permute-done((f32[2,128,128]{2,1,0:T(8,128)S(1)}, f32[2,128,128]{2,1,0:T(8,128)S(1)}, u32[]{:S(2)}, u32[]{:S(2)}) %collective-permute-start.12) | collective-permute-done | bytes 131104 | tf_op jit(solution)/shard_map/ppermute | solution.py:24
  46.8 1.4 %collective-permute-done.10.up_one = f32[2,128,128]{2,1,0:T(8,128)S(1)} collective-permute-done((f32[2,128,128]{2,1,0:T(8,128)S(1)}, f32[2,128,128]{2,1,0:T(8,128)S(1)}, u32[]{:S(2)}, u32[]{:S(2)}) %collective-permute-start.10) | collective-permute-done | bytes 131104 | tf_op jit(solution)/shard_map/ppermute | solution.py:24
  50.0 1.1 %collective-permute-start.14 = (f32[4,128,128]{2,1,0:T(8,128)S(1)}, f32[4,128,128]{2,1,0:T(8,128)S(1)}, u32[]{:S(2)}, u32[]{:S(2)}) collective-permute-start(f32[4,128,128]{2,1,0:T(8,128)S(1)} %get-tuple-element.67), channel_id=1, source_target_pairs={{2,0},{4,2},{6,4},{8,6},{10,8},{12,10},{14,12},{16,14},{18,16},{20... | collective-permute-start | bytes 786440 | tf_op jit(solution)/shard_map/ppermute | solution.py:24
  51.6 1.9 %collective-permute-done.18.upper_ref = f32[2,128,128]{2,1,0:T(8,128)S(1)} collective-permute-done((f32[2,128,128]{2,1,0:T(8,128)S(1)}, f32[2,128,128]{2,1,0:T(8,128)S(1)}, u32[]{:S(2)}, u32[]{:S(2)}) %collective-permute-start.18) | collective-permute-done | bytes 131104 | tf_op jit(solution)/shard_map/ppermute | solution.py:24
  53.5 1.1 %collective-permute-start.20 = (f32[2,128,128]{2,1,0:T(8,128)S(1)}, f32[2,128,128]{2,1,0:T(8,128)S(1)}, u32[]{:S(2)}, u32[]{:S(2)}) collective-permute-start(f32[2,128,128]{2,1,0:T(8,128)S(1)} %collective-permute-done.18.upper_ref), channel_id=1, source_target_pairs={{2,0},{4,2},{6,4},{8,6},{10,8},{12,10},{14,12},{16,14},{18,16},{20... | collective-permute-start | bytes 393224 | tf_op jit(solution)/shard_map/ppermute | solution.py:24
  54.7 1.5 %collective-permute-done.15.upper_ref = f32[2,128,128]{2,1,0:T(8,128)S(1)} collective-permute-done((f32[2,128,128]{2,1,0:T(8,128)S(1)}, f32[2,128,128]{2,1,0:T(8,128)S(1)}, u32[]{:S(2)}, u32[]{:S(2)}) %collective-permute-start.15) | collective-permute-done | bytes 131104 | tf_op jit(solution)/shard_map/ppermute | solution.py:24
  57.0 0.9 %collective-permute-done.20.corner_ref = f32[2,128,128]{2,1,0:T(8,128)S(1)} collective-permute-done((f32[2,128,128]{2,1,0:T(8,128)S(1)}, f32[2,128,128]{2,1,0:T(8,128)S(1)}, u32[]{:S(2)}, u32[]{:S(2)}) %collective-permute-start.20) | collective-permute-done | bytes 131104 | tf_op jit(solution)/shard_map/ppermute | solution.py:24
  57.9 1.2 %shard_map.89.moved_ref = f32[4,2,128,128]{3,2,1,0:T(8,128)S(1)} custom-call(s32[1,128]{1,0:T(1,128)S(1)} %pad_bitcast_fusion.numbers_ref, f32[2,256,256]{2,1,0:T(8,128)S(1)} %get-tuple-element.58.rest_ref.rest_one, f32[2,128,128]{2,1,0:T(8,128)S(1)} %get-tuple-element.64.quad_ref.quad_one, f32[4,128,128]{2,1,0:T(8,128)S(1)} %collective-permute-done.13.left_ref, ...), custom_call_target="tpu_custom_call" | custom-call | tf_op jit(solution)/shard_map/pallas_call | solution.py:482
  59.6 1.6 %shard_map.90 = (f32[2,256,256]{2,1,0:T(8,128)S(1)}, f32[2,128,256]{2,1,0:T(8,128)S(1)}, f32[2,128,128]{2,1,0:T(8,128)S(1)}, f32[2,128,128]{2,1,0:T(8,128)S(1)},...) custom-call(s32[1,128]{1,0:T(1,128)S(1)} %pad_bitcast_fusion.numbers_ref, ...), custom_call_target="tpu_custom_call" | custom-call | tf_op jit(solution)/shard_map/pallas_call | solution.py:482
  61.2 1.3 %shard_map.91 = (f32[2,256,256]{2,1,0:T(8,128)S(1)}, f32[4,128,256]{2,1,0:T(8,128)S(1)}, f32[2,128,128]{2,1,0:T(8,128)S(1)}, f32[2,128,128]{2,1,0:T(8,128)S(1)}, f32[2,128,128]{2,1,0:T(8,128)S(1)}) custom-call(s32[1,128]{1,0:T(1,128)S(1)} %pad_bitcast_fusion.numbers_ref, f32[4,2,128,128]{3,2,1,0:T(8,128)S(1)} %get-tuple-element.70.back_ref, ...), custom_call_target="tpu_custom_call" | custom-call | tf_op jit(solution)/shard_map/pallas_call | solution.py:482
  63.3 1.4 %collective-permute-start.26 = (f32[2,128,128]{2,1,0:T(8,128)S(1)}, f32[2,128,128]{2,1,0:T(8,128)S(1)}, u32[]{:S(2)}, u32[]{:S(2)}) collective-permute-start(f32[2,128,128]{2,1,0:T(8,128)S(1)} %get-tuple-element.79), channel_id=1, source_target_pairs={{1,0},{0,1},{3,2},{2,3},{5,4},{4,5},{7,6},{6,7},{9,8},{8,9},{11,10... | collective-permute-start | bytes 393224 | tf_op jit(solution)/shard_map/ppermute | solution.py:24
  65.3 10.6 %collective-permute-done.22 = f32[2,128,128]{2,1,0:T(8,128)S(1)} collective-permute-done((f32[2,128,128]{2,1,0:T(8,128)S(1)}, f32[2,128,128]{2,1,0:T(8,128)S(1)}, u32[]{:S(2)}, u32[]{:S(2)}) %collective-permute-start.22) | collective-permute-done | bytes 131104 | tf_op jit(solution)/shard_map/ppermute | solution.py:24
  75.9 0.9 %collective-permute-start.23 = (f32[2,128,128]{2,1,0:T(8,128)S(1)}, f32[2,128,128]{2,1,0:T(8,128)S(1)}, u32[]{:S(2)}, u32[]{:S(2)}) collective-permute-start(f32[2,128,128]{2,1,0:T(8,128)S(1)} %add.16), channel_id=1, source_target_pairs={{1,0},{0,1},{3,2},{2,3},{5,4},{4,5},{7,6},{6,7},{9,8},{8,9},{11,10... | collective-permute-start | bytes 393224 | tf_op jit(solution)/shard_map/ppermute | solution.py:24
  77.3 0.9 %collective-permute-start.25 = (f32[2,128,128]{2,1,0:T(8,128)S(1)}, f32[2,128,128]{2,1,0:T(8,128)S(1)}, u32[]{:S(2)}, u32[]{:S(2)}) collective-permute-start(f32[2,128,128]{2,1,0:T(8,128)S(1)} %add.17), channel_id=1, source_target_pairs={{1,0},{0,1},{3,2},{2,3},{5,4},{4,5},{7,6},{6,7},{9,8},{8,9},{11,10... | collective-permute-start | bytes 393224 | tf_op jit(solution)/shard_map/ppermute | solution.py:24
  78.2 0.9 %finish_low.1.part_ref = f32[2,2,256,256]{3,2,1,0:T(8,128)} custom-call(f32[2,256,256]{2,1,0:T(8,128)S(1)} %get-tuple-element.58.rest_ref.rest_one, f32[2,256,256]{2,1,0:T(8,128)S(1)} %get-tuple-element.59.rest_ref.rest_two, f32[2,256,256]{2,1,0:T(8,128)S(1)} %get-tuple-element.72.own_one, f32[2,256,256]{2,1,0:T(8,128)S(1)} %get-tuple-element.73.own_two, ...), custom_call_target="tpu_custom_call" | custom-call | tf_op jit(solution)/shard_map/finish_low/pallas_call | solution.py:629
  79.1 1.8 %collective-permute-done.23.up_one = f32[2,128,128]{2,1,0:T(8,128)S(1)} collective-permute-done((f32[2,128,128]{2,1,0:T(8,128)S(1)}, f32[2,128,128]{2,1,0:T(8,128)S(1)}, u32[]{:S(2)}, u32[]{:S(2)}) %collective-permute-start.23) | collective-permute-done | bytes 131104 | tf_op jit(solution)/shard_map/ppermute | solution.py:24
  80.9 1.4 %collective-permute-done.25.up_two = f32[2,128,128]{2,1,0:T(8,128)S(1)} collective-permute-done((f32[2,128,128]{2,1,0:T(8,128)S(1)}, f32[2,128,128]{2,1,0:T(8,128)S(1)}, u32[]{:S(2)}, u32[]{:S(2)}) %collective-permute-start.25) | collective-permute-done | bytes 131104 | tf_op jit(solution)/shard_map/ppermute | solution.py:24
  (52 shorter events, 11.4 us)
Async XLA Ops:
  1.1 10.2 %copy-start = (f32[128,128]{1,0:T(8,128)S(1)}, f32[128,128]{1,0:T(8,128)}, u32[]{:S(2)}) copy-start(f32[128,128]{1,0:T(8,128)} %param.10) | copy-start | bytes 196612
  1.1 23.3 %collective-permute-start = (f32[4,128,256]{2,1,0:T(8,128)S(1)}, f32[4,128,256]{2,1,0:T(8,128)S(1)}, u32[]{:S(2)}, u32[]{:S(2)}) collective-permute-start(f32[4,128,256]{2,1,0:T(8,128)S(1)} %get-tuple-element.44), channel_id=1, source_target_pairs={{2,0},{4,2},{6,4},{8,6},{10,8},{12,10},{14,12},{16,14},{18,16},{20... | collective-permute-start | bytes 1572872 | tf_op jit(solution)/shard_map/ppermute | solution.py:24
  7.7 6.0 %collective-permute-start.2 = (f32[2,128,128]{2,1,0:T(8,128)S(1)}, f32[2,128,128]{2,1,0:T(8,128)S(1)}, u32[]{:S(2)}, u32[]{:S(2)}) collective-permute-start(f32[2,128,128]{2,1,0:T(8,128)S(1)} %get-tuple-element.46), channel_id=1, source_target_pairs={{1,0},{0,1},{3,2},{2,3},{5,4},{4,5},{7,6},{6,7},{9,8},{8,9},{11,10... | collective-permute-start | bytes 393224 | tf_op jit(solution)/shard_map/ppermute | solution.py:24
  9.3 14.9 %collective-permute-start.3 = (f32[4,128,128]{2,1,0:T(8,128)S(1)}, f32[4,128,128]{2,1,0:T(8,128)S(1)}, u32[]{:S(2)}, u32[]{:S(2)}) collective-permute-start(f32[4,128,128]{2,1,0:T(8,128)S(1)} %get-tuple-element.47), channel_id=1, source_target_pairs={{1,0},{0,1},{3,2},{2,3},{5,4},{4,5},{7,6},{6,7},{9,8},{8,9},{11,10... | collective-permute-start | bytes 786440 | tf_op jit(solution)/shard_map/ppermute | solution.py:24
  9.8 8.1 %collective-permute-start.1 = (f32[2,128,128]{2,1,0:T(8,128)S(1)}, f32[2,128,128]{2,1,0:T(8,128)S(1)}, u32[]{:S(2)}, u32[]{:S(2)}) collective-permute-start(f32[2,128,128]{2,1,0:T(8,128)S(1)} %get-tuple-element.45), channel_id=1, source_target_pairs={{1,0},{0,1},{3,2},{2,3},{5,4},{4,5},{7,6},{6,7},{9,8},{8,9},{11,10... | collective-permute-start | bytes 393224 | tf_op jit(solution)/shard_map/ppermute | solution.py:24
  11.6 0.7 copy-start.1
  13.7 10.5 %collective-permute-start.5 = (f32[2,128,128]{2,1,0:T(8,128)S(1)}, f32[2,128,128]{2,1,0:T(8,128)S(1)}, u32[]{:S(2)}, u32[]{:S(2)}) collective-permute-start(f32[2,128,128]{2,1,0:T(8,128)S(1)} %collective-permute-done.2.upper_two), channel_id=1, source_target_pairs={{2,0},{4,2},{6,4},{8,6},{10,8},{12,10},{14,12},{16,14},{18,16},{20... | collective-permute-start | bytes 393224 | tf_op jit(solution)/shard_map/ppermute | solution.py:24
  18.0 6.5 %collective-permute-start.4 = (f32[2,128,128]{2,1,0:T(8,128)S(1)}, f32[2,128,128]{2,1,0:T(8,128)S(1)}, u32[]{:S(2)}, u32[]{:S(2)}) collective-permute-start(f32[2,128,128]{2,1,0:T(8,128)S(1)} %collective-permute-done.1.upper_one), channel_id=1, source_target_pairs={{2,0},{4,2},{6,4},{8,6},{10,8},{12,10},{14,12},{16,14},{18,16},{20... | collective-permute-start | bytes 393224 | tf_op jit(solution)/shard_map/ppermute | solution.py:24
  21.9 0.7 copy-start.2
  28.1 20.1 %collective-permute-start.6 = (f32[4,128,256]{2,1,0:T(8,128)S(1)}, f32[4,128,256]{2,1,0:T(8,128)S(1)}, u32[]{:S(2)}, u32[]{:S(2)}) collective-permute-start(f32[4,128,256]{2,1,0:T(8,128)S(1)} %get-tuple-element.55), channel_id=1, source_target_pairs={{30,0},{0,2},{2,4},{4,6},{6,8},{8,10},{10,12},{12,14},{14,16},{16,... | collective-permute-start | bytes 1572872 | tf_op jit(solution)/shard_map/ppermute | solution.py:24
  28.2 13.6 %collective-permute-start.11 = (f32[2,128,128]{2,1,0:T(8,128)S(1)}, f32[2,128,128]{2,1,0:T(8,128)S(1)}, u32[]{:S(2)}, u32[]{:S(2)}) collective-permute-start(f32[2,128,128]{2,1,0:T(8,128)S(1)} %get-tuple-element.63), channel_id=1, source_target_pairs={{30,0},{0,2},{2,4},{4,6},{6,8},{8,10},{10,12},{12,14},{14,16},{16,... | collective-permute-start | bytes 393224 | tf_op jit(solution)/shard_map/ppermute | solution.py:24
  28.2 14.9 %collective-permute-start.9 = (f32[2,128,128]{2,1,0:T(8,128)S(1)}, f32[2,128,128]{2,1,0:T(8,128)S(1)}, u32[]{:S(2)}, u32[]{:S(2)}) collective-permute-start(f32[2,128,128]{2,1,0:T(8,128)S(1)} %get-tuple-element.61), channel_id=1, source_target_pairs={{30,0},{0,2},{2,4},{4,6},{6,8},{8,10},{10,12},{12,14},{14,16},{16,... | collective-permute-start | bytes 393224 | tf_op jit(solution)/shard_map/ppermute | solution.py:24
  29.2 14.8 %collective-permute-start.8 = (f32[2,128,128]{2,1,0:T(8,128)S(1)}, f32[2,128,128]{2,1,0:T(8,128)S(1)}, u32[]{:S(2)}, u32[]{:S(2)}) collective-permute-start(f32[2,128,128]{2,1,0:T(8,128)S(1)} %get-tuple-element.57), channel_id=1, source_target_pairs={{1,0},{0,1},{3,2},{2,3},{5,4},{4,5},{7,6},{6,7},{9,8},{8,9},{11,10... | collective-permute-start | bytes 393224 | tf_op jit(solution)/shard_map/ppermute | solution.py:24
  29.9 14.1 %collective-permute-start.7 = (f32[2,128,128]{2,1,0:T(8,128)S(1)}, f32[2,128,128]{2,1,0:T(8,128)S(1)}, u32[]{:S(2)}, u32[]{:S(2)}) collective-permute-start(f32[2,128,128]{2,1,0:T(8,128)S(1)} %get-tuple-element.56), channel_id=1, source_target_pairs={{1,0},{0,1},{3,2},{2,3},{5,4},{4,5},{7,6},{6,7},{9,8},{8,9},{11,10... | collective-permute-start | bytes 393224 | tf_op jit(solution)/shard_map/ppermute | solution.py:24
  41.8 5.0 %collective-permute-start.12 = (f32[2,128,128]{2,1,0:T(8,128)S(1)}, f32[2,128,128]{2,1,0:T(8,128)S(1)}, u32[]{:S(2)}, u32[]{:S(2)}) collective-permute-start(f32[2,128,128]{2,1,0:T(8,128)S(1)} %add.15), channel_id=1, source_target_pairs={{1,0},{0,1},{3,2},{2,3},{5,4},{4,5},{7,6},{6,7},{9,8},{8,9},{11,10... | collective-permute-start | bytes 393224 | tf_op jit(solution)/shard_map/ppermute | solution.py:24
  43.2 5.0 %collective-permute-start.10 = (f32[2,128,128]{2,1,0:T(8,128)S(1)}, f32[2,128,128]{2,1,0:T(8,128)S(1)}, u32[]{:S(2)}, u32[]{:S(2)}) collective-permute-start(f32[2,128,128]{2,1,0:T(8,128)S(1)} %add.14), channel_id=1, source_target_pairs={{1,0},{0,1},{3,2},{2,3},{5,4},{4,5},{7,6},{6,7},{9,8},{8,9},{11,10... | collective-permute-start | bytes 393224 | tf_op jit(solution)/shard_map/ppermute | solution.py:24
  44.0 10.6 %collective-permute-start.19 = (f32[2,128,128]{2,1,0:T(8,128)S(1)}, f32[2,128,128]{2,1,0:T(8,128)S(1)}, u32[]{:S(2)}, u32[]{:S(2)}) collective-permute-start(f32[2,128,128]{2,1,0:T(8,128)S(1)} %get-tuple-element.69), channel_id=1, source_target_pairs={{1,0},{0,1},{3,2},{2,3},{5,4},{4,5},{7,6},{6,7},{9,8},{8,9},{11,10... | collective-permute-start | bytes 393224 | tf_op jit(solution)/shard_map/ppermute | solution.py:24
  48.3 5.2 %collective-permute-start.18 = (f32[2,128,128]{2,1,0:T(8,128)S(1)}, f32[2,128,128]{2,1,0:T(8,128)S(1)}, u32[]{:S(2)}, u32[]{:S(2)}) collective-permute-start(f32[2,128,128]{2,1,0:T(8,128)S(1)} %get-tuple-element.64.quad_ref.quad_one), channel_id=1, source_target_pairs={{1,0},{0,1},{3,2},{2,3},{5,4},{4,5},{7,6},{6,7},{9,8},{8,9},{11,10... | collective-permute-start | bytes 393224 | tf_op jit(solution)/shard_map/ppermute | solution.py:24
  49.1 8.8 %collective-permute-start.13 = (f32[4,128,128]{2,1,0:T(8,128)S(1)}, f32[4,128,128]{2,1,0:T(8,128)S(1)}, u32[]{:S(2)}, u32[]{:S(2)}) collective-permute-start(f32[4,128,128]{2,1,0:T(8,128)S(1)} %get-tuple-element.66), channel_id=1, source_target_pairs={{2,0},{4,2},{6,4},{8,6},{10,8},{12,10},{14,12},{16,14},{18,16},{20... | collective-permute-start | bytes 786440 | tf_op jit(solution)/shard_map/ppermute | solution.py:24
  50.0 8.0 %collective-permute-start.14 = (f32[4,128,128]{2,1,0:T(8,128)S(1)}, f32[4,128,128]{2,1,0:T(8,128)S(1)}, u32[]{:S(2)}, u32[]{:S(2)}) collective-permute-start(f32[4,128,128]{2,1,0:T(8,128)S(1)} %get-tuple-element.67), channel_id=1, source_target_pairs={{2,0},{4,2},{6,4},{8,6},{10,8},{12,10},{14,12},{16,14},{18,16},{20... | collective-permute-start | bytes 786440 | tf_op jit(solution)/shard_map/ppermute | solution.py:24
  51.1 5.1 %collective-permute-start.15 = (f32[2,128,128]{2,1,0:T(8,128)S(1)}, f32[2,128,128]{2,1,0:T(8,128)S(1)}, u32[]{:S(2)}, u32[]{:S(2)}) collective-permute-start(f32[2,128,128]{2,1,0:T(8,128)S(1)} %get-tuple-element.65.quad_ref.quad_two), channel_id=1, source_target_pairs={{1,0},{0,1},{3,2},{2,3},{5,4},{4,5},{7,6},{6,7},{9,8},{8,9},{11,10... | collective-permute-start | bytes 393224 | tf_op jit(solution)/shard_map/ppermute | solution.py:24
  53.5 4.4 %collective-permute-start.20 = (f32[2,128,128]{2,1,0:T(8,128)S(1)}, f32[2,128,128]{2,1,0:T(8,128)S(1)}, u32[]{:S(2)}, u32[]{:S(2)}) collective-permute-start(f32[2,128,128]{2,1,0:T(8,128)S(1)} %collective-permute-done.18.upper_ref), channel_id=1, source_target_pairs={{2,0},{4,2},{6,4},{8,6},{10,8},{12,10},{14,12},{16,14},{18,16},{20... | collective-permute-start | bytes 393224 | tf_op jit(solution)/shard_map/ppermute | solution.py:24
  54.6 5.0 %collective-permute-start.16 = (f32[2,128,128]{2,1,0:T(8,128)S(1)}, f32[2,128,128]{2,1,0:T(8,128)S(1)}, u32[]{:S(2)}, u32[]{:S(2)}) collective-permute-start(f32[2,128,128]{2,1,0:T(8,128)S(1)} %get-tuple-element.68), channel_id=1, source_target_pairs={{1,0},{0,1},{3,2},{2,3},{5,4},{4,5},{7,6},{6,7},{9,8},{8,9},{11,10... | collective-permute-start | bytes 393224 | tf_op jit(solution)/shard_map/ppermute | solution.py:24
  56.1 3.4 %collective-permute-start.17 = (f32[2,128,128]{2,1,0:T(8,128)S(1)}, f32[2,128,128]{2,1,0:T(8,128)S(1)}, u32[]{:S(2)}, u32[]{:S(2)}) collective-permute-start(f32[2,128,128]{2,1,0:T(8,128)S(1)} %collective-permute-done.15.upper_ref), channel_id=1, source_target_pairs={{2,0},{4,2},{6,4},{8,6},{10,8},{12,10},{14,12},{16,14},{18,16},{20... | collective-permute-start | bytes 393224 | tf_op jit(solution)/shard_map/ppermute | solution.py:24
  62.5 19.8 %collective-permute-start.21 = (f32[4,128,256]{2,1,0:T(8,128)S(1)}, f32[4,128,256]{2,1,0:T(8,128)S(1)}, u32[]{:S(2)}, u32[]{:S(2)}) collective-permute-start(f32[4,128,256]{2,1,0:T(8,128)S(1)} %get-tuple-element.74), channel_id=1, source_target_pairs={{30,0},{0,2},{2,4},{4,6},{6,8},{8,10},{10,12},{12,14},{14,16},{16,... | collective-permute-start | bytes 1572872 | tf_op jit(solution)/shard_map/ppermute | solution.py:24
  62.7 13.2 %collective-permute-start.22 = (f32[2,128,128]{2,1,0:T(8,128)S(1)}, f32[2,128,128]{2,1,0:T(8,128)S(1)}, u32[]{:S(2)}, u32[]{:S(2)}) collective-permute-start(f32[2,128,128]{2,1,0:T(8,128)S(1)} %get-tuple-element.76), channel_id=1, source_target_pairs={{30,0},{0,2},{2,4},{4,6},{6,8},{8,10},{10,12},{12,14},{14,16},{16,... | collective-permute-start | bytes 393224 | tf_op jit(solution)/shard_map/ppermute | solution.py:24
  63.2 14.1 %collective-permute-start.24 = (f32[2,128,128]{2,1,0:T(8,128)S(1)}, f32[2,128,128]{2,1,0:T(8,128)S(1)}, u32[]{:S(2)}, u32[]{:S(2)}) collective-permute-start(f32[2,128,128]{2,1,0:T(8,128)S(1)} %get-tuple-element.78), channel_id=1, source_target_pairs={{30,0},{0,2},{2,4},{4,6},{6,8},{8,10},{10,12},{12,14},{14,16},{16,... | collective-permute-start | bytes 393224 | tf_op jit(solution)/shard_map/ppermute | solution.py:24
  63.3 14.9 %collective-permute-start.26 = (f32[2,128,128]{2,1,0:T(8,128)S(1)}, f32[2,128,128]{2,1,0:T(8,128)S(1)}, u32[]{:S(2)}, u32[]{:S(2)}) collective-permute-start(f32[2,128,128]{2,1,0:T(8,128)S(1)} %get-tuple-element.79), channel_id=1, source_target_pairs={{1,0},{0,1},{3,2},{2,3},{5,4},{4,5},{7,6},{6,7},{9,8},{8,9},{11,10... | collective-permute-start | bytes 393224 | tf_op jit(solution)/shard_map/ppermute | solution.py:24
  64.7 13.5 %collective-permute-start.27 = (f32[2,128,128]{2,1,0:T(8,128)S(1)}, f32[2,128,128]{2,1,0:T(8,128)S(1)}, u32[]{:S(2)}, u32[]{:S(2)}) collective-permute-start(f32[2,128,128]{2,1,0:T(8,128)S(1)} %get-tuple-element.80), channel_id=1, source_target_pairs={{1,0},{0,1},{3,2},{2,3},{5,4},{4,5},{7,6},{6,7},{9,8},{8,9},{11,10... | collective-permute-start | bytes 393224 | tf_op jit(solution)/shard_map/ppermute | solution.py:24
  75.9 5.0 %collective-permute-start.23 = (f32[2,128,128]{2,1,0:T(8,128)S(1)}, f32[2,128,128]{2,1,0:T(8,128)S(1)}, u32[]{:S(2)}, u32[]{:S(2)}) collective-permute-start(f32[2,128,128]{2,1,0:T(8,128)S(1)} %add.16), channel_id=1, source_target_pairs={{1,0},{0,1},{3,2},{2,3},{5,4},{4,5},{7,6},{6,7},{9,8},{8,9},{11,10... | collective-permute-start | bytes 393224 | tf_op jit(solution)/shard_map/ppermute | solution.py:24
  77.3 5.0 %collective-permute-start.25 = (f32[2,128,128]{2,1,0:T(8,128)S(1)}, f32[2,128,128]{2,1,0:T(8,128)S(1)}, u32[]{:S(2)}, u32[]{:S(2)}) collective-permute-start(f32[2,128,128]{2,1,0:T(8,128)S(1)} %add.17), channel_id=1, source_target_pairs={{1,0},{0,1},{3,2},{2,3},{5,4},{4,5},{7,6},{6,7},{9,8},{8,9},{11,10... | collective-permute-start | bytes 393224 | tf_op jit(solution)/shard_map/ppermute | solution.py:24

commit v8 on v7

--- a/solution.py
+++ b/solution.py
@@ -186,18 +186,11 @@
 
 def by_count(total, spots, run):
     groups = groups_of(spots)
-    first = (len(groups) + 1) // 2
-    if first == len(groups):
-        run(groups)
-        return
-
-    @pl.when(total > first)
-    def _():
-        run(groups)
-
-    @pl.when(total <= first)
-    def _():
-        run(groups[:first])
+    lower = 0
+    for size in sorted({1, (len(groups) + 1) // 2, len(groups)}):
+        fits = (total > lower) if size == len(groups) else (total > lower) & (total <= size)
+        pl.when(fits)(functools.partial(run, groups[:size]))
+        lower = size
 
 
 def joined(*parts):

time: 83.6 us -> 83.4 us (level)
  no operation moved by 1% of the time
where the time goes in v8:
time: 83.4 us; the launch traced here: 83.2 us
  waiting for transfers between devices  39.5 us (47%)
  starting transfers between devices  28.1 us (34%)
  Pallas kernels  13.4 us (16%)
  local copies, waits for them, and re-layouts  1.1 us (1%)
  between operations  1 us (1%)
    ppermute x28, waiting for transfers between devices, from_behind(): return lax.ppermute(block, axis, route)  39.5 us
    ppermute x28, starting transfers between devices, from_behind(): return lax.ppermute(block, axis, route)  28.1 us
    pallas_call x8, Pallas kernels, call(): pl.pallas_call(functools.partial(kernel, **static), in_specs=[VMEM] * (le...  7.97 us
    pallas_call x2, Pallas kernels, pack(): pl.pallas_call(functools.partial(pack_kernel, boxes=boxes), in_specs=[FAR...  2.19 us
  transfers between devices with their start and end apart: 28, of which 15 were waited for; matrix products, arithmetic and copies ran while one was open for 1% of the time, Pallas kernels for 6%

profile of v8, /device:TPU:0, one launch (start us, length us, event | category | flops | bytes accessed | tf_op | source)
XLA Modules:
  0.0 83.2 jit_solution(11105999792359972388)
XLA Ops:
  0.0 1.1 %shard_map.82 = (f32[2,128,128]{2,1,0:T(8,128)S(1)}, f32[4,128,256]{2,1,0:T(8,128)S(1)}) custom-call(f32[2,2,256,256]{3,2,1,0:T(8,128)} %whole_ref.3), custom_call_target="tpu_custom_call" | custom-call | tf_op jit(solution)/shard_map/pallas_call | solution.py:500
  1.1 5.5 %collective-permute-start = (f32[4,128,256]{2,1,0:T(8,128)S(1)}, f32[4,128,256]{2,1,0:T(8,128)S(1)}, u32[]{:S(2)}, u32[]{:S(2)}) collective-permute-start(f32[4,128,256]{2,1,0:T(8,128)S(1)} %get-tuple-element.44), channel_id=1, source_target_pairs={{2,0},{4,2},{6,4},{8,6},{10,8},{12,10},{14,12},{16,14},{18,16},{20... | collective-permute-start | bytes 1572872 | tf_op jit(solution)/shard_map/ppermute | solution.py:24
  6.7 1.1 %shard_map.83 = (f32[2,128,128]{2,1,0:T(8,128)S(1)}, f32[4,128,128]{2,1,0:T(8,128)S(1)}) custom-call(f32[2,2,256,256]{3,2,1,0:T(8,128)} %whole_ref.3), custom_call_target="tpu_custom_call" | custom-call | tf_op jit(solution)/shard_map/pallas_call | solution.py:500
  7.7 1.6 %collective-permute-start.2 = (f32[2,128,128]{2,1,0:T(8,128)S(1)}, f32[2,128,128]{2,1,0:T(8,128)S(1)}, u32[]{:S(2)}, u32[]{:S(2)}) collective-permute-start(f32[2,128,128]{2,1,0:T(8,128)S(1)} %get-tuple-element.46), channel_id=1, source_target_pairs={{1,0},{0,1},{3,2},{2,3},{5,4},{4,5},{7,6},{6,7},{9,8},{8,9},{11,10... | collective-permute-start | bytes 393224 | tf_op jit(solution)/shard_map/ppermute | solution.py:24
  9.8 1.5 %collective-permute-start.1 = (f32[2,128,128]{2,1,0:T(8,128)S(1)}, f32[2,128,128]{2,1,0:T(8,128)S(1)}, u32[]{:S(2)}, u32[]{:S(2)}) collective-permute-start(f32[2,128,128]{2,1,0:T(8,128)S(1)} %get-tuple-element.45), channel_id=1, source_target_pairs={{1,0},{0,1},{3,2},{2,3},{5,4},{4,5},{7,6},{6,7},{9,8},{8,9},{11,10... | collective-permute-start | bytes 393224 | tf_op jit(solution)/shard_map/ppermute | solution.py:24
  12.4 1.3 %collective-permute-done.2.upper_two = f32[2,128,128]{2,1,0:T(8,128)S(1)} collective-permute-done((f32[2,128,128]{2,1,0:T(8,128)S(1)}, f32[2,128,128]{2,1,0:T(8,128)S(1)}, u32[]{:S(2)}, u32[]{:S(2)}) %collective-permute-start.2) | collective-permute-done | bytes 131104 | tf_op jit(solution)/shard_map/ppermute | solution.py:24
  13.7 4.2 %collective-permute-done.1.upper_one = f32[2,128,128]{2,1,0:T(8,128)S(1)} collective-permute-done((f32[2,128,128]{2,1,0:T(8,128)S(1)}, f32[2,128,128]{2,1,0:T(8,128)S(1)}, u32[]{:S(2)}, u32[]{:S(2)}) %collective-permute-start.1) | collective-permute-done | bytes 131104 | tf_op jit(solution)/shard_map/ppermute | solution.py:24
  18.0 4.0 %collective-permute-start.4 = (f32[2,128,128]{2,1,0:T(8,128)S(1)}, f32[2,128,128]{2,1,0:T(8,128)S(1)}, u32[]{:S(2)}, u32[]{:S(2)}) collective-permute-start(f32[2,128,128]{2,1,0:T(8,128)S(1)} %collective-permute-done.1.upper_one), channel_id=1, source_target_pairs={{2,0},{4,2},{6,4},{8,6},{10,8},{12,10},{14,12},{16,14},{18,16},{20... | collective-permute-start | bytes 393224 | tf_op jit(solution)/shard_map/ppermute | solution.py:24
  22.7 1.5 %stage.1 = (f32[2,2,256,256]{3,2,1,0:T(8,128)S(1)}, f32[2,128,128]{2,1,0:T(8,128)S(1)}, f32[4,128,128]{2,1,0:T(8,128)S(1)}, bf16[4,256,256]{2,1,0:T(8,128)(2,1)S(1)}) custom-call(f32[2,2,256,256]{3,2,1,0:T(8,128)} %whole_ref.3, f32[2,128,128]{2,1,0:T(8,128)} %refs_1_.1, f32[4,128,128]{2,1,0:T(8,128)} %bitcast.6, bf16[4,256,256]{2,1,0:T(8,128)(2,1)} %constant.4.clone.refs_3_), custom_call_target="tpu_custom_call" | custom-call | tf_op jit(solution)/shard_map/stage/pallas_call | solution.py:550
  24.5 2.3 %shard_map.84 = (f32[2,256,256]{2,1,0:T(8,128)S(1)}, f32[2,128,256]{2,1,0:T(8,128)S(1)}, f32[2,128,128]{2,1,0:T(8,128)S(1)}, f32[2,128,128]{2,1,0:T(8,128)S(1)},...) custom-call(s32[1,128]{1,0:T(1,128)S(1)} %pad_bitcast_fusion.numbers_ref, ...), custom_call_target="tpu_custom_call" | custom-call | tf_op jit(solution)/shard_map/pallas_call | solution.py:475
  26.8 1.3 %shard_map.85 = (f32[2,256,256]{2,1,0:T(8,128)S(1)}, f32[4,128,256]{2,1,0:T(8,128)S(1)}, f32[2,128,128]{2,1,0:T(8,128)S(1)}, f32[2,128,128]{2,1,0:T(8,128)S(1)}, f32[2,128,128]{2,1,0:T(8,128)S(1)}) custom-call(s32[1,128]{1,0:T(1,128)S(1)} %pad_bitcast_fusion.numbers_ref, f32[4,2,128,128]{3,2,1,0:T(8,128)S(1)} %get-tuple-element.51.back_ref, ...), custom_call_target="tpu_custom_call" | custom-call | tf_op jit(solution)/shard_map/pallas_call | solution.py:475
  28.2 1.0 %collective-permute-start.9 = (f32[2,128,128]{2,1,0:T(8,128)S(1)}, f32[2,128,128]{2,1,0:T(8,128)S(1)}, u32[]{:S(2)}, u32[]{:S(2)}) collective-permute-start(f32[2,128,128]{2,1,0:T(8,128)S(1)} %get-tuple-element.61), channel_id=1, source_target_pairs={{30,0},{0,2},{2,4},{4,6},{6,8},{8,10},{10,12},{12,14},{14,16},{16,... | collective-permute-start | bytes 393224 | tf_op jit(solution)/shard_map/ppermute | solution.py:24
  29.8 1.4 %collective-permute-start.7 = (f32[2,128,128]{2,1,0:T(8,128)S(1)}, f32[2,128,128]{2,1,0:T(8,128)S(1)}, u32[]{:S(2)}, u32[]{:S(2)}) collective-permute-start(f32[2,128,128]{2,1,0:T(8,128)S(1)} %get-tuple-element.56), channel_id=1, source_target_pairs={{1,0},{0,1},{3,2},{2,3},{5,4},{4,5},{7,6},{6,7},{9,8},{8,9},{11,10... | collective-permute-start | bytes 393224 | tf_op jit(solution)/shard_map/ppermute | solution.py:24
  31.2 10.5 %collective-permute-done.11 = f32[2,128,128]{2,1,0:T(8,128)S(1)} collective-permute-done((f32[2,128,128]{2,1,0:T(8,128)S(1)}, f32[2,128,128]{2,1,0:T(8,128)S(1)}, u32[]{:S(2)}, u32[]{:S(2)}) %collective-permute-start.11) | collective-permute-done | bytes 131104 | tf_op jit(solution)/shard_map/ppermute | solution.py:24
  44.0 1.4 %collective-permute-start.19 = (f32[2,128,128]{2,1,0:T(8,128)S(1)}, f32[2,128,128]{2,1,0:T(8,128)S(1)}, u32[]{:S(2)}, u32[]{:S(2)}) collective-permute-start(f32[2,128,128]{2,1,0:T(8,128)S(1)} %get-tuple-element.69), channel_id=1, source_target_pairs={{1,0},{0,1},{3,2},{2,3},{5,4},{4,5},{7,6},{6,7},{9,8},{8,9},{11,10... | collective-permute-start | bytes 393224 | tf_op jit(solution)/shard_map/ppermute | solution.py:24
  45.4 1.4 %collective-permute-done.12.up_two = f32[2,128,128]{2,1,0:T(8,128)S(1)} collective-permute-done((f32[2,128,128]{2,1,0:T(8,128)S(1)}, f32[2,128,128]{2,1,0:T(8,128)S(1)}, u32[]{:S(2)}, u32[]{:S(2)}) %collective-permute-start.12) | collective-permute-done | bytes 131104 | tf_op jit(solution)/shard_map/ppermute | solution.py:24
  46.8 1.4 %collective-permute-done.10.up_one = f32[2,128,128]{2,1,0:T(8,128)S(1)} collective-permute-done((f32[2,128,128]{2,1,0:T(8,128)S(1)}, f32[2,128,128]{2,1,0:T(8,128)S(1)}, u32[]{:S(2)}, u32[]{:S(2)}) %collective-permute-start.10) | collective-permute-done | bytes 131104 | tf_op jit(solution)/shard_map/ppermute | solution.py:24
  48.3 0.8 collective-permute-start.18
  49.8 1.3 %collective-permute-start.14 = (f32[4,128,128]{2,1,0:T(8,128)S(1)}, f32[4,128,128]{2,1,0:T(8,128)S(1)}, u32[]{:S(2)}, u32[]{:S(2)}) collective-permute-start(f32[4,128,128]{2,1,0:T(8,128)S(1)} %get-tuple-element.67), channel_id=1, source_target_pairs={{2,0},{4,2},{6,4},{8,6},{10,8},{12,10},{14,12},{16,14},{18,16},{20... | collective-permute-start | bytes 786440 | tf_op jit(solution)/shard_map/ppermute | solution.py:24
  51.6 2.1 %collective-permute-done.18.upper_ref = f32[2,128,128]{2,1,0:T(8,128)S(1)} collective-permute-done((f32[2,128,128]{2,1,0:T(8,128)S(1)}, f32[2,128,128]{2,1,0:T(8,128)S(1)}, u32[]{:S(2)}, u32[]{:S(2)}) %collective-permute-start.18) | collective-permute-done | bytes 131104 | tf_op jit(solution)/shard_map/ppermute | solution.py:24
  53.7 0.9 %collective-permute-start.20 = (f32[2,128,128]{2,1,0:T(8,128)S(1)}, f32[2,128,128]{2,1,0:T(8,128)S(1)}, u32[]{:S(2)}, u32[]{:S(2)}) collective-permute-start(f32[2,128,128]{2,1,0:T(8,128)S(1)} %collective-permute-done.18.upper_ref), channel_id=1, source_target_pairs={{2,0},{4,2},{6,4},{8,6},{10,8},{12,10},{14,12},{16,14},{18,16},{20... | collective-permute-start | bytes 393224 | tf_op jit(solution)/shard_map/ppermute | solution.py:24
  54.6 1.5 %collective-permute-done.15.upper_ref = f32[2,128,128]{2,1,0:T(8,128)S(1)} collective-permute-done((f32[2,128,128]{2,1,0:T(8,128)S(1)}, f32[2,128,128]{2,1,0:T(8,128)S(1)}, u32[]{:S(2)}, u32[]{:S(2)}) %collective-permute-start.15) | collective-permute-done | bytes 131104 | tf_op jit(solution)/shard_map/ppermute | solution.py:24
  56.2 0.8 %collective-permute-start.17 = (f32[2,128,128]{2,1,0:T(8,128)S(1)}, f32[2,128,128]{2,1,0:T(8,128)S(1)}, u32[]{:S(2)}, u32[]{:S(2)}) collective-permute-start(f32[2,128,128]{2,1,0:T(8,128)S(1)} %collective-permute-done.15.upper_ref), channel_id=1, source_target_pairs={{2,0},{4,2},{6,4},{8,6},{10,8},{12,10},{14,12},{16,14},{18,16},{20... | collective-permute-start | bytes 393224 | tf_op jit(solution)/shard_map/ppermute | solution.py:24
  57.8 1.4 %shard_map.89.moved_ref = f32[4,2,128,128]{3,2,1,0:T(8,128)S(1)} custom-call(s32[1,128]{1,0:T(1,128)S(1)} %pad_bitcast_fusion.numbers_ref, f32[2,256,256]{2,1,0:T(8,128)S(1)} %get-tuple-element.58.rest_ref.rest_one, f32[2,128,128]{2,1,0:T(8,128)S(1)} %get-tuple-element.64.quad_ref.quad_one, f32[4,128,128]{2,1,0:T(8,128)S(1)} %collective-permute-done.13.left_ref, ...), custom_call_target="tpu_custom_call" | custom-call | tf_op jit(solution)/shard_map/pallas_call | solution.py:475
  59.7 1.4 %shard_map.90 = (f32[2,256,256]{2,1,0:T(8,128)S(1)}, f32[2,128,256]{2,1,0:T(8,128)S(1)}, f32[2,128,128]{2,1,0:T(8,128)S(1)}, f32[2,128,128]{2,1,0:T(8,128)S(1)},...) custom-call(s32[1,128]{1,0:T(1,128)S(1)} %pad_bitcast_fusion.numbers_ref, ...), custom_call_target="tpu_custom_call" | custom-call | tf_op jit(solution)/shard_map/pallas_call | solution.py:475
  61.1 1.3 %shard_map.91 = (f32[2,256,256]{2,1,0:T(8,128)S(1)}, f32[4,128,256]{2,1,0:T(8,128)S(1)}, f32[2,128,128]{2,1,0:T(8,128)S(1)}, f32[2,128,128]{2,1,0:T(8,128)S(1)}, f32[2,128,128]{2,1,0:T(8,128)S(1)}) custom-call(s32[1,128]{1,0:T(1,128)S(1)} %pad_bitcast_fusion.numbers_ref, f32[4,2,128,128]{3,2,1,0:T(8,128)S(1)} %get-tuple-element.70.back_ref, ...), custom_call_target="tpu_custom_call" | custom-call | tf_op jit(solution)/shard_map/pallas_call | solution.py:475
  63.1 1.3 %collective-permute-start.26 = (f32[2,128,128]{2,1,0:T(8,128)S(1)}, f32[2,128,128]{2,1,0:T(8,128)S(1)}, u32[]{:S(2)}, u32[]{:S(2)}) collective-permute-start(f32[2,128,128]{2,1,0:T(8,128)S(1)} %get-tuple-element.79), channel_id=1, source_target_pairs={{1,0},{0,1},{3,2},{2,3},{5,4},{4,5},{7,6},{6,7},{9,8},{8,9},{11,10... | collective-permute-start | bytes 393224 | tf_op jit(solution)/shard_map/ppermute | solution.py:24
  65.2 10.6 %collective-permute-done.22 = f32[2,128,128]{2,1,0:T(8,128)S(1)} collective-permute-done((f32[2,128,128]{2,1,0:T(8,128)S(1)}, f32[2,128,128]{2,1,0:T(8,128)S(1)}, u32[]{:S(2)}, u32[]{:S(2)}) %collective-permute-start.22) | collective-permute-done | bytes 131104 | tf_op jit(solution)/shard_map/ppermute | solution.py:24
  77.9 0.9 %finish_low.1.part_ref = f32[2,2,256,256]{3,2,1,0:T(8,128)} custom-call(f32[2,256,256]{2,1,0:T(8,128)S(1)} %get-tuple-element.58.rest_ref.rest_one, f32[2,256,256]{2,1,0:T(8,128)S(1)} %get-tuple-element.59.rest_ref.rest_two, f32[2,256,256]{2,1,0:T(8,128)S(1)} %get-tuple-element.72.own_one, f32[2,256,256]{2,1,0:T(8,128)S(1)} %get-tuple-element.73.own_two, ...), custom_call_target="tpu_custom_call" | custom-call | tf_op jit(solution)/shard_map/finish_low/pallas_call | solution.py:622
  78.8 2.0 %collective-permute-done.23.up_one = f32[2,128,128]{2,1,0:T(8,128)S(1)} collective-permute-done((f32[2,128,128]{2,1,0:T(8,128)S(1)}, f32[2,128,128]{2,1,0:T(8,128)S(1)}, u32[]{:S(2)}, u32[]{:S(2)}) %collective-permute-start.23) | collective-permute-done | bytes 131104 | tf_op jit(solution)/shard_map/ppermute | solution.py:24
  80.8 1.4 %collective-permute-done.25.up_two = f32[2,128,128]{2,1,0:T(8,128)S(1)} collective-permute-done((f32[2,128,128]{2,1,0:T(8,128)S(1)}, f32[2,128,128]{2,1,0:T(8,128)S(1)}, u32[]{:S(2)}, u32[]{:S(2)}) %collective-permute-start.25) | collective-permute-done | bytes 131104 | tf_op jit(solution)/shard_map/ppermute | solution.py:24
  82.2 0.9 %finish_top.1 = f32[2,2,256,256]{3,2,1,0:T(8,128)} custom-call(f32[2,256,256]{2,1,0:T(8,128)S(1)} %get-tuple-element.58.rest_ref.rest_one, f32[2,256,256]{2,1,0:T(8,128)S(1)} %get-tuple-element.59.rest_ref.rest_two, f32[2,128,128]{2,1,0:T(8,128)S(1)} %get-tuple-element.64.quad_ref.quad_one, ...), custom_call_target="tpu_custom_call", output_to_operand_aliasing={{}: (9, {})} | custom-call | tf_op jit(solution)/shard_map/finish_top/pallas_call | solution.py:631
  (52 shorter events, 11.2 us)
Async XLA Ops:
  1.1 10.2 %copy-start = (f32[128,128]{1,0:T(8,128)S(1)}, f32[128,128]{1,0:T(8,128)}, u32[]{:S(2)}) copy-start(f32[128,128]{1,0:T(8,128)} %param.10) | copy-start | bytes 196612
  1.1 23.3 %collective-permute-start = (f32[4,128,256]{2,1,0:T(8,128)S(1)}, f32[4,128,256]{2,1,0:T(8,128)S(1)}, u32[]{:S(2)}, u32[]{:S(2)}) collective-permute-start(f32[4,128,256]{2,1,0:T(8,128)S(1)} %get-tuple-element.44), channel_id=1, source_target_pairs={{2,0},{4,2},{6,4},{8,6},{10,8},{12,10},{14,12},{16,14},{18,16},{20... | collective-permute-start | bytes 1572872 | tf_op jit(solution)/shard_map/ppermute | solution.py:24
  7.7 6.0 %collective-permute-start.2 = (f32[2,128,128]{2,1,0:T(8,128)S(1)}, f32[2,128,128]{2,1,0:T(8,128)S(1)}, u32[]{:S(2)}, u32[]{:S(2)}) collective-permute-start(f32[2,128,128]{2,1,0:T(8,128)S(1)} %get-tuple-element.46), channel_id=1, source_target_pairs={{1,0},{0,1},{3,2},{2,3},{5,4},{4,5},{7,6},{6,7},{9,8},{8,9},{11,10... | collective-permute-start | bytes 393224 | tf_op jit(solution)/shard_map/ppermute | solution.py:24
  9.3 14.9 %collective-permute-start.3 = (f32[4,128,128]{2,1,0:T(8,128)S(1)}, f32[4,128,128]{2,1,0:T(8,128)S(1)}, u32[]{:S(2)}, u32[]{:S(2)}) collective-permute-start(f32[4,128,128]{2,1,0:T(8,128)S(1)} %get-tuple-element.47), channel_id=1, source_target_pairs={{1,0},{0,1},{3,2},{2,3},{5,4},{4,5},{7,6},{6,7},{9,8},{8,9},{11,10... | collective-permute-start | bytes 786440 | tf_op jit(solution)/shard_map/ppermute | solution.py:24
  9.8 8.1 %collective-permute-start.1 = (f32[2,128,128]{2,1,0:T(8,128)S(1)}, f32[2,128,128]{2,1,0:T(8,128)S(1)}, u32[]{:S(2)}, u32[]{:S(2)}) collective-permute-start(f32[2,128,128]{2,1,0:T(8,128)S(1)} %get-tuple-element.45), channel_id=1, source_target_pairs={{1,0},{0,1},{3,2},{2,3},{5,4},{4,5},{7,6},{6,7},{9,8},{8,9},{11,10... | collective-permute-start | bytes 393224 | tf_op jit(solution)/shard_map/ppermute | solution.py:24
  11.6 0.7 copy-start.1
  13.7 10.5 %collective-permute-start.5 = (f32[2,128,128]{2,1,0:T(8,128)S(1)}, f32[2,128,128]{2,1,0:T(8,128)S(1)}, u32[]{:S(2)}, u32[]{:S(2)}) collective-permute-start(f32[2,128,128]{2,1,0:T(8,128)S(1)} %collective-permute-done.2.upper_two), channel_id=1, source_target_pairs={{2,0},{4,2},{6,4},{8,6},{10,8},{12,10},{14,12},{16,14},{18,16},{20... | collective-permute-start | bytes 393224 | tf_op jit(solution)/shard_map/ppermute | solution.py:24
  18.0 6.5 %collective-permute-start.4 = (f32[2,128,128]{2,1,0:T(8,128)S(1)}, f32[2,128,128]{2,1,0:T(8,128)S(1)}, u32[]{:S(2)}, u32[]{:S(2)}) collective-permute-start(f32[2,128,128]{2,1,0:T(8,128)S(1)} %collective-permute-done.1.upper_one), channel_id=1, source_target_pairs={{2,0},{4,2},{6,4},{8,6},{10,8},{12,10},{14,12},{16,14},{18,16},{20... | collective-permute-start | bytes 393224 | tf_op jit(solution)/shard_map/ppermute | solution.py:24
  21.9 0.7 copy-start.2
  28.1 20.2 %collective-permute-start.6 = (f32[4,128,256]{2,1,0:T(8,128)S(1)}, f32[4,128,256]{2,1,0:T(8,128)S(1)}, u32[]{:S(2)}, u32[]{:S(2)}) collective-permute-start(f32[4,128,256]{2,1,0:T(8,128)S(1)} %get-tuple-element.55), channel_id=1, source_target_pairs={{30,0},{0,2},{2,4},{4,6},{6,8},{8,10},{10,12},{12,14},{14,16},{16,... | collective-permute-start | bytes 1572872 | tf_op jit(solution)/shard_map/ppermute | solution.py:24
  28.1 13.6 %collective-permute-start.11 = (f32[2,128,128]{2,1,0:T(8,128)S(1)}, f32[2,128,128]{2,1,0:T(8,128)S(1)}, u32[]{:S(2)}, u32[]{:S(2)}) collective-permute-start(f32[2,128,128]{2,1,0:T(8,128)S(1)} %get-tuple-element.63), channel_id=1, source_target_pairs={{30,0},{0,2},{2,4},{4,6},{6,8},{8,10},{10,12},{12,14},{14,16},{16,... | collective-permute-start | bytes 393224 | tf_op jit(solution)/shard_map/ppermute | solution.py:24
  28.2 15.0 %collective-permute-start.9 = (f32[2,128,128]{2,1,0:T(8,128)S(1)}, f32[2,128,128]{2,1,0:T(8,128)S(1)}, u32[]{:S(2)}, u32[]{:S(2)}) collective-permute-start(f32[2,128,128]{2,1,0:T(8,128)S(1)} %get-tuple-element.61), channel_id=1, source_target_pairs={{30,0},{0,2},{2,4},{4,6},{6,8},{8,10},{10,12},{12,14},{14,16},{16,... | collective-permute-start | bytes 393224 | tf_op jit(solution)/shard_map/ppermute | solution.py:24
  29.2 14.8 %collective-permute-start.8 = (f32[2,128,128]{2,1,0:T(8,128)S(1)}, f32[2,128,128]{2,1,0:T(8,128)S(1)}, u32[]{:S(2)}, u32[]{:S(2)}) collective-permute-start(f32[2,128,128]{2,1,0:T(8,128)S(1)} %get-tuple-element.57), channel_id=1, source_target_pairs={{1,0},{0,1},{3,2},{2,3},{5,4},{4,5},{7,6},{6,7},{9,8},{8,9},{11,10... | collective-permute-start | bytes 393224 | tf_op jit(solution)/shard_map/ppermute | solution.py:24
  29.8 14.1 %collective-permute-start.7 = (f32[2,128,128]{2,1,0:T(8,128)S(1)}, f32[2,128,128]{2,1,0:T(8,128)S(1)}, u32[]{:S(2)}, u32[]{:S(2)}) collective-permute-start(f32[2,128,128]{2,1,0:T(8,128)S(1)} %get-tuple-element.56), channel_id=1, source_target_pairs={{1,0},{0,1},{3,2},{2,3},{5,4},{4,5},{7,6},{6,7},{9,8},{8,9},{11,10... | collective-permute-start | bytes 393224 | tf_op jit(solution)/shard_map/ppermute | solution.py:24
  41.8 5.0 %collective-permute-start.12 = (f32[2,128,128]{2,1,0:T(8,128)S(1)}, f32[2,128,128]{2,1,0:T(8,128)S(1)}, u32[]{:S(2)}, u32[]{:S(2)}) collective-permute-start(f32[2,128,128]{2,1,0:T(8,128)S(1)} %add.15), channel_id=1, source_target_pairs={{1,0},{0,1},{3,2},{2,3},{5,4},{4,5},{7,6},{6,7},{9,8},{8,9},{11,10... | collective-permute-start | bytes 393224 | tf_op jit(solution)/shard_map/ppermute | solution.py:24
  43.2 5.0 %collective-permute-start.10 = (f32[2,128,128]{2,1,0:T(8,128)S(1)}, f32[2,128,128]{2,1,0:T(8,128)S(1)}, u32[]{:S(2)}, u32[]{:S(2)}) collective-permute-start(f32[2,128,128]{2,1,0:T(8,128)S(1)} %add.14), channel_id=1, source_target_pairs={{1,0},{0,1},{3,2},{2,3},{5,4},{4,5},{7,6},{6,7},{9,8},{8,9},{11,10... | collective-permute-start | bytes 393224 | tf_op jit(solution)/shard_map/ppermute | solution.py:24
  44.0 10.6 %collective-permute-start.19 = (f32[2,128,128]{2,1,0:T(8,128)S(1)}, f32[2,128,128]{2,1,0:T(8,128)S(1)}, u32[]{:S(2)}, u32[]{:S(2)}) collective-permute-start(f32[2,128,128]{2,1,0:T(8,128)S(1)} %get-tuple-element.69), channel_id=1, source_target_pairs={{1,0},{0,1},{3,2},{2,3},{5,4},{4,5},{7,6},{6,7},{9,8},{8,9},{11,10... | collective-permute-start | bytes 393224 | tf_op jit(solution)/shard_map/ppermute | solution.py:24
  48.3 5.4 %collective-permute-start.18 = (f32[2,128,128]{2,1,0:T(8,128)S(1)}, f32[2,128,128]{2,1,0:T(8,128)S(1)}, u32[]{:S(2)}, u32[]{:S(2)}) collective-permute-start(f32[2,128,128]{2,1,0:T(8,128)S(1)} %get-tuple-element.64.quad_ref.quad_one), channel_id=1, source_target_pairs={{1,0},{0,1},{3,2},{2,3},{5,4},{4,5},{7,6},{6,7},{9,8},{8,9},{11,10... | collective-permute-start | bytes 393224 | tf_op jit(solution)/shard_map/ppermute | solution.py:24
  49.1 8.7 %collective-permute-start.13 = (f32[4,128,128]{2,1,0:T(8,128)S(1)}, f32[4,128,128]{2,1,0:T(8,128)S(1)}, u32[]{:S(2)}, u32[]{:S(2)}) collective-permute-start(f32[4,128,128]{2,1,0:T(8,128)S(1)} %get-tuple-element.66), channel_id=1, source_target_pairs={{2,0},{4,2},{6,4},{8,6},{10,8},{12,10},{14,12},{16,14},{18,16},{20... | collective-permute-start | bytes 786440 | tf_op jit(solution)/shard_map/ppermute | solution.py:24
  49.8 8.0 %collective-permute-start.14 = (f32[4,128,128]{2,1,0:T(8,128)S(1)}, f32[4,128,128]{2,1,0:T(8,128)S(1)}, u32[]{:S(2)}, u32[]{:S(2)}) collective-permute-start(f32[4,128,128]{2,1,0:T(8,128)S(1)} %get-tuple-element.67), channel_id=1, source_target_pairs={{2,0},{4,2},{6,4},{8,6},{10,8},{12,10},{14,12},{16,14},{18,16},{20... | collective-permute-start | bytes 786440 | tf_op jit(solution)/shard_map/ppermute | solution.py:24
  51.1 5.1 %collective-permute-start.15 = (f32[2,128,128]{2,1,0:T(8,128)S(1)}, f32[2,128,128]{2,1,0:T(8,128)S(1)}, u32[]{:S(2)}, u32[]{:S(2)}) collective-permute-start(f32[2,128,128]{2,1,0:T(8,128)S(1)} %get-tuple-element.65.quad_ref.quad_two), channel_id=1, source_target_pairs={{1,0},{0,1},{3,2},{2,3},{5,4},{4,5},{7,6},{6,7},{9,8},{8,9},{11,10... | collective-permute-start | bytes 393224 | tf_op jit(solution)/shard_map/ppermute | solution.py:24
  53.7 4.0 %collective-permute-start.20 = (f32[2,128,128]{2,1,0:T(8,128)S(1)}, f32[2,128,128]{2,1,0:T(8,128)S(1)}, u32[]{:S(2)}, u32[]{:S(2)}) collective-permute-start(f32[2,128,128]{2,1,0:T(8,128)S(1)} %collective-permute-done.18.upper_ref), channel_id=1, source_target_pairs={{2,0},{4,2},{6,4},{8,6},{10,8},{12,10},{14,12},{16,14},{18,16},{20... | collective-permute-start | bytes 393224 | tf_op jit(solution)/shard_map/ppermute | solution.py:24
  54.6 5.0 %collective-permute-start.16 = (f32[2,128,128]{2,1,0:T(8,128)S(1)}, f32[2,128,128]{2,1,0:T(8,128)S(1)}, u32[]{:S(2)}, u32[]{:S(2)}) collective-permute-start(f32[2,128,128]{2,1,0:T(8,128)S(1)} %get-tuple-element.68), channel_id=1, source_target_pairs={{1,0},{0,1},{3,2},{2,3},{5,4},{4,5},{7,6},{6,7},{9,8},{8,9},{11,10... | collective-permute-start | bytes 393224 | tf_op jit(solution)/shard_map/ppermute | solution.py:24
  56.2 3.5 %collective-permute-start.17 = (f32[2,128,128]{2,1,0:T(8,128)S(1)}, f32[2,128,128]{2,1,0:T(8,128)S(1)}, u32[]{:S(2)}, u32[]{:S(2)}) collective-permute-start(f32[2,128,128]{2,1,0:T(8,128)S(1)} %collective-permute-done.15.upper_ref), channel_id=1, source_target_pairs={{2,0},{4,2},{6,4},{8,6},{10,8},{12,10},{14,12},{16,14},{18,16},{20... | collective-permute-start | bytes 393224 | tf_op jit(solution)/shard_map/ppermute | solution.py:24
  62.4 19.8 %collective-permute-start.21 = (f32[4,128,256]{2,1,0:T(8,128)S(1)}, f32[4,128,256]{2,1,0:T(8,128)S(1)}, u32[]{:S(2)}, u32[]{:S(2)}) collective-permute-start(f32[4,128,256]{2,1,0:T(8,128)S(1)} %get-tuple-element.74), channel_id=1, source_target_pairs={{30,0},{0,2},{2,4},{4,6},{6,8},{8,10},{10,12},{12,14},{14,16},{16,... | collective-permute-start | bytes 1572872 | tf_op jit(solution)/shard_map/ppermute | solution.py:24
  62.6 13.2 %collective-permute-start.22 = (f32[2,128,128]{2,1,0:T(8,128)S(1)}, f32[2,128,128]{2,1,0:T(8,128)S(1)}, u32[]{:S(2)}, u32[]{:S(2)}) collective-permute-start(f32[2,128,128]{2,1,0:T(8,128)S(1)} %get-tuple-element.76), channel_id=1, source_target_pairs={{30,0},{0,2},{2,4},{4,6},{6,8},{8,10},{10,12},{12,14},{14,16},{16,... | collective-permute-start | bytes 393224 | tf_op jit(solution)/shard_map/ppermute | solution.py:24
  63.0 14.2 %collective-permute-start.24 = (f32[2,128,128]{2,1,0:T(8,128)S(1)}, f32[2,128,128]{2,1,0:T(8,128)S(1)}, u32[]{:S(2)}, u32[]{:S(2)}) collective-permute-start(f32[2,128,128]{2,1,0:T(8,128)S(1)} %get-tuple-element.78), channel_id=1, source_target_pairs={{30,0},{0,2},{2,4},{4,6},{6,8},{8,10},{10,12},{12,14},{14,16},{16,... | collective-permute-start | bytes 393224 | tf_op jit(solution)/shard_map/ppermute | solution.py:24
  63.1 14.8 %collective-permute-start.26 = (f32[2,128,128]{2,1,0:T(8,128)S(1)}, f32[2,128,128]{2,1,0:T(8,128)S(1)}, u32[]{:S(2)}, u32[]{:S(2)}) collective-permute-start(f32[2,128,128]{2,1,0:T(8,128)S(1)} %get-tuple-element.79), channel_id=1, source_target_pairs={{1,0},{0,1},{3,2},{2,3},{5,4},{4,5},{7,6},{6,7},{9,8},{8,9},{11,10... | collective-permute-start | bytes 393224 | tf_op jit(solution)/shard_map/ppermute | solution.py:24
  64.4 13.5 %collective-permute-start.27 = (f32[2,128,128]{2,1,0:T(8,128)S(1)}, f32[2,128,128]{2,1,0:T(8,128)S(1)}, u32[]{:S(2)}, u32[]{:S(2)}) collective-permute-start(f32[2,128,128]{2,1,0:T(8,128)S(1)} %get-tuple-element.80), channel_id=1, source_target_pairs={{1,0},{0,1},{3,2},{2,3},{5,4},{4,5},{7,6},{6,7},{9,8},{8,9},{11,10... | collective-permute-start | bytes 393224 | tf_op jit(solution)/shard_map/ppermute | solution.py:24
  75.8 5.0 %collective-permute-start.23 = (f32[2,128,128]{2,1,0:T(8,128)S(1)}, f32[2,128,128]{2,1,0:T(8,128)S(1)}, u32[]{:S(2)}, u32[]{:S(2)}) collective-permute-start(f32[2,128,128]{2,1,0:T(8,128)S(1)} %add.16), channel_id=1, source_target_pairs={{1,0},{0,1},{3,2},{2,3},{5,4},{4,5},{7,6},{6,7},{9,8},{8,9},{11,10... | collective-permute-start | bytes 393224 | tf_op jit(solution)/shard_map/ppermute | solution.py:24
  77.2 5.0 %collective-permute-start.25 = (f32[2,128,128]{2,1,0:T(8,128)S(1)}, f32[2,128,128]{2,1,0:T(8,128)S(1)}, u32[]{:S(2)}, u32[]{:S(2)}) collective-permute-start(f32[2,128,128]{2,1,0:T(8,128)S(1)} %add.17), channel_id=1, source_target_pairs={{1,0},{0,1},{3,2},{2,3},{5,4},{4,5},{7,6},{6,7},{9,8},{8,9},{11,10... | collective-permute-start | bytes 393224 | tf_op jit(solution)/shard_map/ppermute | solution.py:24
